TPU v7x, 512 devices: a whole 4x8x8 slice. The times are simulated.
512 devices in a mesh: replica: 16 (over x, z_lo), expert: 32 (over y, z_hi, core).
Axes of the slice: x: 4, y: 8, z: 8 (z_hi: 2, z_lo: 4; z = z_hi * 4 + z_lo), core: 2. Of those that a mesh axis runs over, the one named last changes fastest.
Arguments:
- moe_input: bfloat16 [8192, 2048], P(('replica', 'expert')), may hold values from -6 to 6
- expert_ids: int32 [8192, 8], P(('replica', 'expert')), may hold values from 0 to 127, all different within a row; in each aligned block of 16 rows (0 to 15, 16 to 31, ...) at most 2 rows name the same one
- route_weight: float32 [8192, 8], P(('replica', 'expert')), may hold values from 0.05 to 0.5
- expert_slot: int32 [128], replicated, may hold values from 0 to 127, each once
- w_gate_up: bfloat16 [2048, 196608], P(None, ('replica', 'expert')), may hold values from -0.125 to 0.125
- w_down: bfloat16 [98304, 2048], P(('replica', 'expert')), may hold values from -0.21875 to 0.21875
- queries: bfloat16 [1024, 8192], P(('replica', 'expert')), may hold values from -80 to 80
- incoming_key_value: bfloat16 [1024, 1024], P(('replica', 'expert')), may hold values from -4 to 4
- key_value_pool: bfloat16 [8192, 64, 1024], P(('replica', 'expert')), may hold values from -4 to 4
- block_owner: int32 [8192], P(('replica', 'expert')), may hold values from 0 to 31, as said below
- block_tokens: int32 [8192], P(('replica', 'expert')), may hold values from 1 to 64
Outputs:
- moe_out: bfloat16 [8192, 2048], P(('replica', 'expert'))
- attn_out: bfloat16 [1024, 8192], P(('replica', 'expert'))
Inputs may be any that keep to these rules, and one draw needn't show every extreme that they name: `expert_ids`: in the rows of one device no expert is named by more than 2 rows, a bound that some block reaches. `expert_slot`: each slot hosts one expert. `block_owner`: on every device at most 2 blocks are owned by requests of any one other replica, and exactly 2 for some other replica.
All inputs are finite; a program needn't handle non-finite values.
Results may differ from a plain program's by a relative error of at most 0.0058.
Values may be sent and summed in bfloat16 or wider, within the bound.
No kernel may reach another device: no remote copies, remote signals or barrier semaphores. Data moves between devices by JAX's collectives and lax.ppermute only.
A program may use at most 64 MiB of HBM per device.

v0:
```python
import math

import jax
import jax.numpy as jnp
from jax import lax
from jax.sharding import PartitionSpec as P

QUART = 4
QUERY_HEADS = 64
KEY_VALUE_HEADS = 4
HEAD_DIMENSION = 128
DEVICE_REQUESTS = 2
DEVICE_BLOCKS = 16
BLOCK_SLOTS = 64
MIG = 2


HIGHEST = lax.Precision.HIGHEST


def partial_state(query_rows, rows, mask, scale):
    heads_kv = query_rows.shape[1]
    head_size = query_rows.shape[3]
    maxima = []
    totals = []
    weighted = []
    for head in range(heads_kv):
        cached_key_rows = rows[:, head * head_size : (head + 1) * head_size]
        cached_value_rows = rows[
            :, (heads_kv + head) * head_size : (heads_kv + head + 1) * head_size
        ].astype(jnp.float32)
        scores = (
            jnp.einsum(
                "rjd,nd->rjn",
                query_rows[:, head],
                cached_key_rows,
                preferred_element_type=jnp.float32,
            )
            * scale
        )
        keep = mask[:, None, :]
        largest = jnp.max(jnp.where(keep, scores, -1e30), axis=2)
        weights = jnp.where(keep, jnp.exp(scores - largest[:, :, None]), 0.0)
        maxima.append(largest)
        totals.append(jnp.sum(weights, axis=2))
        weighted.append(jnp.einsum("rjn,nd->rjd", weights, cached_value_rows, precision=HIGHEST))
    return (jnp.stack(maxima, 1), jnp.stack(totals, 1), jnp.stack(weighted, 1))


def finish(maxima, totals, weighted, new_score, incoming_values):
    best = jnp.maximum(jnp.max(maxima, axis=0), new_score)
    own_weight = jnp.exp(new_score - best)
    factor = jnp.exp(maxima - best[None])
    denom = own_weight + jnp.sum(factor * totals, axis=0)
    mixed = own_weight[..., None] * incoming_values + jnp.sum(factor[..., None] * weighted, axis=0)
    return mixed / denom[..., None]


def attend_migrate(query_rows, key_value_pool, block_owner, block_tokens, scale):
    replicas = lax.axis_size("replica")
    mine = lax.axis_index("replica")
    kv_width = key_value_pool.shape[2]
    target = block_owner // DEVICE_REQUESTS
    request = block_owner % DEVICE_REQUESTS
    leaving = target != mine
    to_replica = (
        (target[:, None] == jnp.arange(replicas, dtype=jnp.int32)[None, :]) & leaving[:, None]
    ).astype(jnp.int32)
    before = jnp.cumsum(to_replica, axis=0) - to_replica
    place = target * MIG + jnp.sum(before * to_replica, axis=1)
    select = (place[None, :] == jnp.arange(replicas * MIG, dtype=jnp.int32)[:, None]) & leaving[
        None, :
    ]
    chosen = select.astype(jnp.int32)
    send_blocks = jnp.dot(
        select.astype(jnp.bfloat16),
        key_value_pool.reshape(DEVICE_BLOCKS, BLOCK_SLOTS * kv_width),
        preferred_element_type=jnp.float32,
    ).astype(jnp.bfloat16)
    send_request = jnp.sum(chosen * request[None, :], axis=1)
    send_count = jnp.sum(chosen * block_tokens[None, :], axis=1)
    got_blocks, got_request, got_count = (
        lax.all_to_all(
            send_blocks.reshape(replicas, MIG, BLOCK_SLOTS * kv_width),
            "replica",
            split_axis=0,
            concat_axis=0,
            tiled=True,
        ),
        lax.all_to_all(
            send_request.reshape(replicas, MIG), "replica", split_axis=0, concat_axis=0, tiled=True
        ),
        lax.all_to_all(
            send_count.reshape(replicas, MIG), "replica", split_axis=0, concat_axis=0, tiled=True
        ),
    )
    positions = jnp.arange(BLOCK_SLOTS, dtype=jnp.int32)
    requests = jnp.arange(DEVICE_REQUESTS, dtype=jnp.int32)
    local_valid = (positions[None, :] < block_tokens[:, None]).reshape(-1)
    local_owner = jnp.repeat(block_owner, BLOCK_SLOTS)
    local_mask = (local_owner[None, :] == mine * DEVICE_REQUESTS + requests[:, None]) & local_valid[
        None, :
    ]
    local_state = partial_state(
        query_rows, key_value_pool.reshape(DEVICE_BLOCKS * BLOCK_SLOTS, kv_width), local_mask, scale
    )
    got_valid = (positions[None, :] < got_count.reshape(-1)[:, None]).reshape(-1)
    got_owner = jnp.repeat(got_request.reshape(-1), BLOCK_SLOTS)
    got_mask = (got_owner[None, :] == requests[:, None]) & got_valid[None, :]
    got_state = partial_state(query_rows, got_blocks.reshape(-1, kv_width), got_mask, scale)
    maxima = jnp.stack([local_state[0], got_state[0]], axis=0)
    totals = jnp.stack([local_state[1], got_state[1]], axis=0)
    weighted = jnp.stack([local_state[2], got_state[2]], axis=0)
    return (maxima, totals, weighted)


def expert_local(rows, w_gate_up, w_down):
    quarter = w_down.shape[0]
    halves = jnp.dot(rows, w_gate_up, preferred_element_type=jnp.float32)
    activation = (jax.nn.silu(halves[:, :quarter]) * halves[:, quarter:]).astype(jnp.bfloat16)
    return jnp.dot(activation, w_down, preferred_element_type=jnp.float32).astype(jnp.bfloat16)


def mixture(moe_input, expert_ids, route_weight, expert_slot, w_gate_up, w_down):
    token_rows = moe_input.shape[0]
    width = moe_input.shape[1]
    top_k = expert_ids.shape[1]
    experts = expert_slot.shape[0]
    replicas = lax.axis_size("replica")
    columns = lax.axis_size("expert")
    capacity = min(token_rows, max(2, 2 * token_rows * top_k // experts))
    flat_ids = expert_ids.reshape(-1)
    onehot = (flat_ids[:, None] == jnp.arange(experts, dtype=jnp.int32)[None, :]).astype(jnp.int32)
    before = jnp.cumsum(onehot, axis=0) - onehot
    position = jnp.sum(before * onehot, axis=1)
    slot_of = jnp.sum(onehot * expert_slot[None, :], axis=1)
    target = slot_of * capacity + position
    assign = (target[:, None] == jnp.arange(experts * capacity, dtype=jnp.int32)[None, :]).reshape(
        token_rows, top_k, experts * capacity
    )
    dispatch_map = jnp.sum(assign.astype(jnp.int32), axis=1).astype(jnp.bfloat16)
    send_rows = jnp.einsum(
        "tc,td->cd", dispatch_map, moe_input, preferred_element_type=jnp.float32
    ).astype(jnp.bfloat16)
    send = jnp.broadcast_to(
        send_rows.reshape(experts, 1, capacity, width), (experts, QUART, capacity, width)
    )
    send = send.reshape(replicas, columns, capacity, width)
    received = lax.all_to_all(
        lax.all_to_all(send, "replica", split_axis=0, concat_axis=0, tiled=True),
        "expert",
        split_axis=1,
        concat_axis=1,
        tiled=True,
    )
    quarter_part = expert_local(received.reshape(-1, width), w_gate_up, w_down)
    returned = lax.all_to_all(
        lax.all_to_all(
            quarter_part.reshape(send.shape), "replica", split_axis=0, concat_axis=0, tiled=True
        ),
        "expert",
        split_axis=1,
        concat_axis=1,
        tiled=True,
    )
    expert_out = jnp.sum(
        returned.reshape(experts, QUART, capacity, width).astype(jnp.float32), axis=1
    ).reshape(experts * capacity, width)
    mixing = jnp.sum(assign.astype(jnp.float32) * route_weight[:, :, None], axis=1)
    return jnp.dot(
        mixing, expert_out, precision=HIGHEST, preferred_element_type=jnp.float32
    ).astype(jnp.bfloat16)


def shards(
    moe_input,
    expert_ids,
    route_weight,
    expert_slot,
    w_gate_up,
    w_down,
    queries,
    incoming_key_value,
    key_value_pool,
    block_owner,
    block_tokens,
):
    moe_out = mixture(moe_input, expert_ids, route_weight, expert_slot, w_gate_up, w_down)
    scale = 1.0 / math.sqrt(HEAD_DIMENSION)
    query_rows = queries.reshape(
        DEVICE_REQUESTS, KEY_VALUE_HEADS, QUERY_HEADS // KEY_VALUE_HEADS, HEAD_DIMENSION
    )
    latest_keys = incoming_key_value[:, : KEY_VALUE_HEADS * HEAD_DIMENSION].reshape(
        DEVICE_REQUESTS, KEY_VALUE_HEADS, HEAD_DIMENSION
    )
    new_score = (
        jnp.einsum("rgjd,rgd->rgj", query_rows, latest_keys, preferred_element_type=jnp.float32)
        * scale
    )
    incoming_values = (
        incoming_key_value[:, KEY_VALUE_HEADS * HEAD_DIMENSION :]
        .reshape(DEVICE_REQUESTS, KEY_VALUE_HEADS, 1, HEAD_DIMENSION)
        .astype(jnp.float32)
    )
    maxima, totals, weighted = attend_migrate(
        query_rows, key_value_pool, block_owner, block_tokens, scale
    )
    attn_out = (
        finish(maxima, totals, weighted, new_score, incoming_values)
        .reshape(DEVICE_REQUESTS, QUERY_HEADS * HEAD_DIMENSION)
        .astype(jnp.bfloat16)
    )
    return (moe_out, attn_out)


def solution(mesh):
    placed = (
        P(("replica", "expert"), None),
        P(("replica", "expert"), None),
        P(("replica", "expert"), None),
        P(),
        P(None, ("replica", "expert")),
        P(("replica", "expert"), None),
        P(("replica", "expert"), None),
        P(("replica", "expert"), None),
        P(("replica", "expert"), None, None),
        P(("replica", "expert")),
        P(("replica", "expert")),
    )
    return jax.shard_map(
        shards,
        mesh=mesh,
        in_specs=placed,
        out_specs=(P(("replica", "expert"), None), P(("replica", "expert"), None)),
        check_vma=False,
    )
```

profile of v0, /device:TPU:48, one launch (start us, length us, event | category | flops | bytes accessed | tf_op | source)
XLA Modules:
  0.0 654.8 jit_solution(11600248471869123241)
XLA Ops:
  2.9 2.3 convolution_convert_fusion.2
  5.2 1.7 broadcast_in_dim.135
  7.0 4.5 broadcast_in_dim.136
  11.5 105.0 %all_to_all.43 = bf16[16,32,2,2048]{3,2,1,0:T(2,128)(2,1)S(1)} all-to-all(bf16[16,32,2,2048]{3,2,1,0:T(2,128)(2,1)} %bitcast.188), channel_id=1, replica_groups=mesh['replica'=16,'expert'=32] {'replica'}, dimensions={0} | all-to-all | bytes 8388608 | tf_op jit(solution)/shard_map/all_to_all | solution.py:150
  116.5 6.5 copy.143
  123.0 13.1 %all-to-all-start.1 = ((bf16[16,32,2,2048]{3,2,0,1:T(2,128)(2,1)}), bf16[16,32,2,2048]{3,2,0,1:T(2,128)(2,1)}, u32[]{:S(2)}, u32[]{:S(2)}) async-start(bf16[16,32,2,2048]{3,2,0,1:T(2,128)(2,1)} %copy.143), calls=%async_computation.1 | async-start | bytes 8388608 | tf_op jit(solution)/shard_map/all_to_all | solution.py:149
  138.0 108.5 %all-to-all-done.1 = bf16[16,32,2,2048]{3,2,0,1:T(2,128)(2,1)} async-done(((bf16[16,32,2,2048]{3,2,0,1:T(2,128)(2,1)}), bf16[16,32,2,2048]{3,2,0,1:T(2,128)(2,1)}, u32[]{:S(2)}, u32[]{:S(2)}) %all-to-all-start.1) | async-done | bytes 4194336 | tf_op jit(solution)/shard_map/all_to_all | solution.py:149
  246.4 3.9 all-to-all-start.5
  250.4 8.0 %copy.144 = bf16[16,32,2,2048]{3,2,1,0:T(2,128)(2,1)} copy(bf16[16,32,2,2048]{3,2,0,1:T(2,128)(2,1)} %all-to-all-done.1) | data formatting | bytes 8388608 | tf_op jit(solution)/shard_map/all_to_all | solution.py:149
  258.4 7.2 %reshape.239 = bf16[1024,2048]{1,0:T(8,128)(2,1)} reshape(bf16[16,32,2,2048]{3,2,1,0:T(2,128)(2,1)} %copy.144) | data formatting | bytes 8388608 | tf_op jit(solution)/shard_map/reshape | solution.py:156
  265.6 5.3 fusion.63
  270.9 7.6 %all-to-all-start.4 = ((s32[16,1,2]{2,1,0:T(1,128)}), s32[16,1,2]{2,1,0:T(1,128)S(1)}, u32[]{:S(2)}, u32[]{:S(2)}) async-start(s32[16,1,2]{2,1,0:T(1,128)} %bitcast.21), calls=%async_computation.4 | async-start | bytes 16384 | tf_op jit(solution)/shard_map/all_to_all | solution.py:90
  278.5 4.6 convolution_convert_fusion.1
  283.1 7.6 %reshape.240 = bf16[16,32,2,2048]{3,2,1,0:T(2,128)(2,1)} reshape(bf16[1024,2048]{1,0:T(8,128)(2,1)} %convolution_convert_fusion.1) | data formatting | bytes 8388608 | tf_op jit(solution)/shard_map/reshape | solution.py:159
  290.7 7.6 %all-to-all-start.2 = ((bf16[16,32,2,2048]{3,2,1,0:T(2,128)(2,1)}), bf16[16,32,2,2048]{3,2,1,0:T(2,128)(2,1)}, u32[]{:S(2)}, u32[]{:S(2)}) async-start(bf16[16,32,2,2048]{3,2,1,0:T(2,128)(2,1)} %reshape.240), calls=%async_computation.2 | async-start | bytes 8388608 | tf_op jit(solution)/shard_map/all_to_all | solution.py:158
  298.3 2.7 copy.176
  301.0 3.3 convolution_convert_fusion
  304.4 5.9 reshape.247
  310.2 81.6 %all-to-all-done.2 = bf16[16,32,2,2048]{3,2,1,0:T(2,128)(2,1)} async-done(((bf16[16,32,2,2048]{3,2,1,0:T(2,128)(2,1)}), bf16[16,32,2,2048]{3,2,1,0:T(2,128)(2,1)}, u32[]{:S(2)}, u32[]{:S(2)}) %all-to-all-start.2) | async-done | bytes 4194336 | tf_op jit(solution)/shard_map/all_to_all | solution.py:158
  391.8 4.7 all-to-all-start.6
  396.5 8.7 %copy.145 = bf16[16,32,2,2048]{3,2,0,1:T(2,128)(2,1)} copy(bf16[16,32,2,2048]{3,2,1,0:T(2,128)(2,1)} %all-to-all-done.2) | data formatting | bytes 8388608 | tf_op jit(solution)/shard_map/all_to_all | solution.py:158
  405.2 88.1 %all-to-all-done.6 = bf16[16,2,65536]{2,1,0:T(2,128)(2,1)} async-done(((bf16[16,2,65536]{2,1,0:T(2,128)(2,1)}), bf16[16,2,65536]{2,1,0:T(2,128)(2,1)}, u32[]{:S(2)}, u32[]{:S(2)}) %all-to-all-start.6) | async-done | bytes 4194336 | tf_op jit(solution)/shard_map/all_to_all | solution.py:83
  493.3 15.3 %all-to-all-start.3 = ((bf16[16,32,2,2048]{3,2,0,1:T(2,128)(2,1)}), bf16[16,32,2,2048]{3,2,0,1:T(2,128)(2,1)}, u32[]{:S(2)}, u32[]{:S(2)}) async-start(bf16[16,32,2,2048]{3,2,0,1:T(2,128)(2,1)} %copy.145), calls=%async_computation.3 | async-start | bytes 8388608 | tf_op jit(solution)/shard_map/all_to_all | solution.py:157
  521.9 11.5 %reshape.248 = bf16[2048,1024]{1,0:T(8,128)(2,1)} reshape(bf16[16,2,65536]{2,1,0:T(2,128)(2,1)} %all-to-all-done.6) | data formatting | bytes 8388608 | tf_op jit(solution)/shard_map/reshape | solution.py:110
  533.4 1.5 fusion
  537.6 1.4 fusion.7
  542.3 81.4 %all-to-all-done.3 = bf16[16,32,2,2048]{3,2,0,1:T(2,128)(2,1)} async-done(((bf16[16,32,2,2048]{3,2,0,1:T(2,128)(2,1)}), bf16[16,32,2,2048]{3,2,0,1:T(2,128)(2,1)}, u32[]{:S(2)}, u32[]{:S(2)}) %all-to-all-start.3) | async-done | bytes 4194336 | tf_op jit(solution)/shard_map/all_to_all | solution.py:157
  623.7 4.6 copy_convert_fusion
  628.3 8.3 %copy.147 = f32[16,32,2,2048]{3,2,1,0:T(2,128)} copy(f32[16,32,2,2048]{3,1,2,0:T(8,128)S(1)} %copy_convert_fusion) | data formatting | bytes 16777216 | tf_op jit(solution)/shard_map/convert_element_type | solution.py:167
  636.6 10.9 %reduce_sum.166 = f32[128,2,2048]{2,1,0:T(2,128)} reduce(f32[128,4,2,2048]{3,2,1,0:T(2,128)} %bitcast.187, f32[]{:T(128)} %constant.51.clone.1), dimensions={1}, to_apply=%region_5.6 | reduce | flops 1572864 | bytes 10485764 | tf_op jit(solution)/shard_map/reduce_sum | solution.py:166
  647.5 3.7 reshape.241
  651.2 3.3 convolution_convert_fusion.3
  (90 shorter events, 23.1 us)
Async XLA Ops:
  0.6 265.0 %copy-start = (bf16[2048,384]{1,0:T(8,128)(2,1)S(1)}, bf16[2048,384]{1,0:T(8,128)(2,1)}, u32[]{:S(2)}) copy-start(bf16[2048,384]{1,0:T(8,128)(2,1)} %param.15) | copy-start | bytes 4718596
  123.0 13.1 %copy-start.4 = (s32[16]{0:T(128)S(1)}, s32[16]{0:T(128)}, u32[]{:S(2)}) copy-start(s32[16]{0:T(128)} %param.20) | copy-start | bytes 196
  123.0 13.5 %copy-start.7 = (s32[16]{0:T(128)S(1)}, s32[16]{0:T(128)}, u32[]{:S(2)}) copy-start(s32[16]{0:T(128)} %param.21) | copy-start | bytes 196
  123.0 123.4 %all-to-all-start.1 = ((bf16[16,32,2,2048]{3,2,0,1:T(2,128)(2,1)}), bf16[16,32,2,2048]{3,2,0,1:T(2,128)(2,1)}, u32[]{:S(2)}, u32[]{:S(2)}) async-start(bf16[16,32,2,2048]{3,2,0,1:T(2,128)(2,1)} %copy.143), calls=%async_computation.1 | async-start | bytes 8388608 | tf_op jit(solution)/shard_map/all_to_all | solution.py:149
  246.4 24.5 %all-to-all-start.5 = ((s32[16,1,2]{2,1,0:T(1,128)}), s32[16,1,2]{2,1,0:T(1,128)S(1)}, u32[]{:S(2)}, u32[]{:S(2)}) async-start(s32[16,1,2]{2,1,0:T(1,128)} %bitcast.22), calls=%async_computation.5 | async-start | bytes 16384 | tf_op jit(solution)/shard_map/all_to_all | solution.py:93
  265.6 12.8 %copy-start.8 = (bf16[192,2048]{1,0:T(8,128)(2,1)S(1)}, bf16[192,2048]{1,0:T(8,128)(2,1)}, u32[]{:S(2)}) copy-start(bf16[192,2048]{1,0:T(8,128)(2,1)} %param.16) | copy-start | bytes 2359300
  270.9 19.8 %all-to-all-start.4 = ((s32[16,1,2]{2,1,0:T(1,128)}), s32[16,1,2]{2,1,0:T(1,128)S(1)}, u32[]{:S(2)}, u32[]{:S(2)}) async-start(s32[16,1,2]{2,1,0:T(1,128)} %bitcast.21), calls=%async_computation.4 | async-start | bytes 16384 | tf_op jit(solution)/shard_map/all_to_all | solution.py:90
  290.7 101.1 %all-to-all-start.2 = ((bf16[16,32,2,2048]{3,2,1,0:T(2,128)(2,1)}), bf16[16,32,2,2048]{3,2,1,0:T(2,128)(2,1)}, u32[]{:S(2)}, u32[]{:S(2)}) async-start(bf16[16,32,2,2048]{3,2,1,0:T(2,128)(2,1)} %reshape.240), calls=%async_computation.2 | async-start | bytes 8388608 | tf_op jit(solution)/shard_map/all_to_all | solution.py:158
  391.8 101.5 %all-to-all-start.6 = ((bf16[16,2,65536]{2,1,0:T(2,128)(2,1)}), bf16[16,2,65536]{2,1,0:T(2,128)(2,1)}, u32[]{:S(2)}, u32[]{:S(2)}) async-start(bf16[16,2,65536]{2,1,0:T(2,128)(2,1)} %reshape.247), calls=%async_computation.6 | async-start | bytes 8388608 | tf_op jit(solution)/shard_map/all_to_all | solution.py:83
  405.2 103.4 %copy-start.5 = (f32[16,8]{0,1:T(8,128)S(1)}, f32[16,8]{0,1:T(8,128)}, u32[]{:S(2)}) copy-start(f32[16,8]{0,1:T(8,128)} %param.13) | copy-start | bytes 1540
  405.2 103.5 %copy-start.3 = (bf16[2,8192]{1,0:T(2,128)(2,1)S(1)}, bf16[2,8192]{1,0:T(2,128)(2,1)}, u32[]{:S(2)}) copy-start(bf16[2,8192]{1,0:T(2,128)(2,1)} %param.17) | copy-start | bytes 98308
  405.2 108.9 %copy-start.6 = (bf16[2,1024]{1,0:T(2,128)(2,1)S(1)}, bf16[2,1024]{1,0:T(2,128)(2,1)}, u32[]{:S(2)}) copy-start(bf16[2,1024]{1,0:T(2,128)(2,1)} %param.18) | copy-start | bytes 12292
  493.3 130.4 %all-to-all-start.3 = ((bf16[16,32,2,2048]{3,2,0,1:T(2,128)(2,1)}), bf16[16,32,2,2048]{3,2,0,1:T(2,128)(2,1)}, u32[]{:S(2)}, u32[]{:S(2)}) async-start(bf16[16,32,2,2048]{3,2,0,1:T(2,128)(2,1)} %copy.145), calls=%async_computation.3 | async-start | bytes 8388608 | tf_op jit(solution)/shard_map/all_to_all | solution.py:157
  533.4 6.1 copy-start.2
  636.6 17.9 %copy-start.1 = (bf16[2048,384]{1,0:T(8,128)(2,1)S(1)}, bf16[2048,384]{1,0:T(8,128)(2,1)}, u32[]{:S(2)}) copy-start(bf16[2048,384]{1,0:T(8,128)(2,1)} %param.15) | copy-start | bytes 4718596
where the time goes:
time: 662 us; the launch traced here: 655 us
  waiting for transfers between devices  360 us (54%)
  blocking collectives  105 us (16%)
  local copies, waits for them, and re-layouts  80.8 us (12%)
  starting transfers between devices  52.2 us (8%)
  matrix products  36.3 us (5%)
  other arithmetic  19.7 us (3%)
    all_to_all x1, waiting for transfers between devices, mixture(): lax.all_to_all(lax.all_to_all(send, 'replica', split_axis=0, concat_axis=...  108 us
    all_to_all x1, blocking collectives, mixture(): lax.all_to_all(send, 'replica', split_axis=0, concat_axis=0, tiled=True)  105 us
    all_to_all x1, waiting for transfers between devices, attend_migrate(): lax.all_to_all(send_blocks.reshape(replicas, MIG, BLOCK_SLOTS * kv_width)...  88.1 us
    all_to_all x1, waiting for transfers between devices, mixture(): lax.all_to_all(quarter_part.reshape(send.shape), 'replica', split_axis=0,...  81.6 us
    all_to_all x1, waiting for transfers between devices, mixture(): lax.all_to_all(lax.all_to_all(quarter_part.reshape(send.shape), 'replica'...  81.4 us
    all_to_all x1, starting transfers between devices, mixture(): lax.all_to_all(lax.all_to_all(quarter_part.reshape(send.shape), 'replica'...  15.3 us
  transfers between devices with their start and end apart: 6, of which 4 were waited for; matrix products, arithmetic and copies ran while one was open for 13% of the time, Pallas kernels for 0%

commit v1 on v0

v1 whole, which is shorter than its diff:
```python
import functools
import math

import jax
import jax.numpy as jnp
from jax import lax
from jax.experimental import pallas as pl
from jax.experimental.pallas import tpu as pltpu
from jax.sharding import Mesh
from jax.sharding import PartitionSpec as P

D = 2048
TOK = 16
TOP = 8
SLOTS = 128
CAP = 2
PIECES = 8
WIDE = D // PIECES
HALF = 192
HEADS = 64
GROUPS = 4
HEAD = 128
REPLICAS = 16
REQUESTS = 2
BLOCKS = 16
LEN = 64
KV = GROUPS * HEAD
NEG = -1e30
STAT = 16
MESSAGE = REQUESTS * HEADS + STAT

F32 = jnp.float32
BF16 = jnp.bfloat16
VMEM_LIMIT = 56 * 1024 * 1024

AXES = ("x", "zl", "y", "zh", "c")
CHIPS = ("x", "zl", "y", "zh")
REPLICA = ("x", "zl")


def iota(shape, dim):
    return lax.broadcasted_iota(jnp.int32, shape, dim)


def whole(count):
    return [pl.BlockSpec(memory_space=pltpu.VMEM)] * count


def params():
    return pltpu.CompilerParams(vmem_limit_bytes=VMEM_LIMIT)


def routing(ids, weight, slot_row):
    lane = iota((TOK, SLOTS), 1)
    chosen = jnp.zeros((TOK, SLOTS), F32)
    scale = jnp.zeros((TOK, SLOTS), F32)
    slots = slot_row.astype(F32)
    for k in range(TOP):
        slot = jnp.sum(jnp.where(ids[:, k : k + 1] == lane, slots, 0.0), axis=1, keepdims=True)
        hit = slot == lane.astype(F32)
        chosen = chosen + jnp.where(hit, 1.0, 0.0)
        scale = scale + jnp.where(hit, weight[:, k : k + 1], 0.0)
    earlier = jnp.where(iota((TOK, TOK), 1) < iota((TOK, TOK), 0), 1.0, 0.0).astype(BF16)
    rank = jnp.dot(earlier, chosen.astype(BF16), preferred_element_type=F32)
    taken = [jnp.where(rank == float(j), chosen, 0.0) for j in range(CAP)]
    return taken, scale


def dispatch_kernel(ids_ref, weight_ref, slot_ref, rows_ref, send_ref):
    taken, _ = routing(ids_ref[...], weight_ref[...], slot_ref[...])
    spread = jnp.where(iota((TOK, TOK * PIECES), 1) // PIECES == iota((TOK, TOK * PIECES), 0), 1.0, 0.0)
    same = (
        iota((1, PIECES, TOK * PIECES), 2) % PIECES == iota((1, PIECES, TOK * PIECES), 1)
    )
    picks = []
    for j in range(CAP):
        wide = lax.dot_general(
            taken[j].astype(BF16),
            spread.astype(BF16),
            (((0,), (0,)), ((), ())),
            preferred_element_type=F32,
        )
        picks.append(jnp.where(same, wide[:, None, :], 0.0))
    pick = jnp.concatenate(picks, axis=1).reshape(SLOTS * CAP * PIECES, TOK * PIECES)
    rows = jnp.dot(pick.astype(BF16), rows_ref[...], preferred_element_type=F32).astype(BF16)
    rows = rows.reshape(SLOTS, CAP * PIECES, WIDE)
    send_ref[:, 0] = rows
    send_ref[:, 1] = rows


def dispatch(ids, weight, slot_row, rows):
    return pl.pallas_call(
        dispatch_kernel,
        name="dispatch",
        out_shape=jax.ShapeDtypeStruct((SLOTS, 2, CAP * PIECES, WIDE), BF16),
        in_specs=whole(4),
        out_specs=whole(1)[0],
        compiler_params=params(),
    )(ids, weight, slot_row, rows)


MIX_CHUNK = 512
MIX_WIDTH = SLOTS * 2 * CAP * PIECES


def mixing_kernel(ids_ref, weight_ref, slot_ref, mix_ref):
    taken, scale = routing(ids_ref[...], weight_ref[...], slot_ref[...])
    parts = []
    for j in range(CAP):
        exact = taken[j] * scale
        high = exact.astype(BF16)
        low = (exact - high.astype(F32)).astype(BF16)
        parts.append(jnp.concatenate([high, low], axis=0))
    for start in range(0, MIX_WIDTH, MIX_CHUNK):
        place = iota((SLOTS, MIX_CHUNK), 1) + start
        mine = place // (2 * CAP * PIECES) == iota((SLOTS, MIX_CHUNK), 0)
        total = jnp.zeros((2 * TOK, MIX_CHUNK), F32)
        for j in range(CAP):
            use = mine & ((place // PIECES) % CAP == j)
            total = total + jnp.dot(
                parts[j], jnp.where(use, 1.0, 0.0).astype(BF16), preferred_element_type=F32
            )
        same = iota((1, PIECES, MIX_CHUNK), 2) % PIECES == iota((1, PIECES, MIX_CHUNK), 1)
        spread = jnp.where(same, total[:, None, :], 0.0)
        mix_ref[:, start : start + MIX_CHUNK] = spread.reshape(
            2 * TOK * PIECES, MIX_CHUNK
        ).astype(BF16)


def mixing(ids, weight, slot_row):
    return pl.pallas_call(
        mixing_kernel,
        name="mixing",
        out_shape=jax.ShapeDtypeStruct((2 * TOK * PIECES, MIX_WIDTH), BF16),
        in_specs=whole(3),
        out_specs=whole(1)[0],
        compiler_params=params(),
    )(ids, weight, slot_row)


def combine_kernel(mix_ref, rows_ref, out_ref):
    both = jnp.dot(mix_ref[...], rows_ref[...], preferred_element_type=F32)
    half = TOK * PIECES
    out_ref[...] = (both[:half] + both[half:]).astype(BF16)


def combine(mix, rows):
    return pl.pallas_call(
        combine_kernel,
        name="combine",
        out_shape=jax.ShapeDtypeStruct((TOK * PIECES, WIDE), BF16),
        in_specs=whole(2),
        out_specs=whole(1)[0],
        compiler_params=params(),
    )(mix, rows)


ROW_STEP = 128
PERM = 128


def expert_kernel(rows_ref, gate_ref, up_ref, down_ref, out_ref):
    near = PERM // PIECES
    one, two = iota((PERM, PERM), 0), iota((PERM, PERM), 1)
    apart = jnp.where(two == (one % near) * PIECES + one // near, 1.0, 0.0).astype(BF16)
    back = jnp.where(two == (one % PIECES) * near + one // PIECES, 1.0, 0.0).astype(BF16)
    tall = []
    for block in range(ROW_STEP // near):
        turned = jnp.dot(
            apart, rows_ref[block * PERM : (block + 1) * PERM], preferred_element_type=F32
        ).astype(BF16)
        tall.append(
            jnp.concatenate([turned[p * near : (p + 1) * near] for p in range(PIECES)], axis=1)
        )
    x = jnp.concatenate(tall, axis=0)
    gate = jnp.dot(x, gate_ref[...], preferred_element_type=F32)
    up = jnp.dot(x, up_ref[...], preferred_element_type=F32)
    act = (gate / (1.0 + jnp.exp(-gate)) * up).astype(BF16)
    y = jnp.dot(act, down_ref[...], preferred_element_type=F32).astype(BF16)
    for block in range(ROW_STEP // near):
        rows = y[block * near : (block + 1) * near]
        stacked = jnp.concatenate(
            [rows[:, p * WIDE : (p + 1) * WIDE] for p in range(PIECES)], axis=0
        )
        out_ref[block * PERM : (block + 1) * PERM] = jnp.dot(
            back, stacked, preferred_element_type=F32
        ).astype(BF16)


def expert(rows, gate, up, down):
    step = ROW_STEP * PIECES
    return pl.pallas_call(
        expert_kernel,
        name="expert",
        grid=(rows.shape[0] // step,),
        out_shape=jax.ShapeDtypeStruct(rows.shape, BF16),
        in_specs=[
            pl.BlockSpec((step, WIDE), lambda i: (i, 0)),
            pl.BlockSpec(gate.shape, lambda i: (0, 0)),
            pl.BlockSpec(up.shape, lambda i: (0, 0)),
            pl.BlockSpec(down.shape, lambda i: (0, 0)),
        ],
        out_specs=pl.BlockSpec((step, WIDE), lambda i: (i, 0)),
        compiler_params=params(),
    )(rows, gate, up, down)


def partial_kernel(owner_ref, count_ref, query_ref, pool_ref, send_ref, top_ref, sum_ref, acc_ref):
    scale = 1.0 / math.sqrt(HEAD)
    top_ref[...] = jnp.full(top_ref.shape, NEG, F32)
    sum_ref[...] = jnp.zeros(sum_ref.shape, F32)
    acc_ref[...] = jnp.zeros(acc_ref.shape, F32)
    per = HEADS // GROUPS
    own = iota((HEADS, KV), 1) // HEAD == iota((HEADS, KV), 0) // per
    slot = iota((HEADS, LEN), 1)
    for b in range(BLOCKS):
        owner = owner_ref[b]
        rows = pl.ds(pl.multiple_of(owner * HEADS, HEADS), HEADS)
        query = query_ref[rows, :]
        wide = jnp.where(own, jnp.concatenate([query] * GROUPS, axis=1), jnp.zeros((), BF16))
        score = (
            lax.dot_general(
                wide, pool_ref[b, :, :KV], (((1,), (1,)), ((), ())), preferred_element_type=F32
            )
            * scale
        )
        keep = slot < count_ref[b]
        score = jnp.where(keep, score, NEG)
        top = jnp.max(score, axis=1, keepdims=True)
        weight = jnp.where(keep, jnp.exp(score - top), 0.0)
        total = jnp.sum(weight, axis=1, keepdims=True)
        high = weight.astype(BF16)
        low = (weight - high.astype(F32)).astype(BF16)
        mixed = jnp.dot(
            jnp.concatenate([high, low], axis=0), pool_ref[b, :, KV:], preferred_element_type=F32
        )
        mixed = mixed[:HEADS] + mixed[HEADS:]
        mixed = jnp.concatenate(
            [
                mixed[g * per : (g + 1) * per, g * HEAD : (g + 1) * HEAD]
                for g in range(GROUPS)
            ],
            axis=0,
        )
        old = top_ref[rows, :]
        best = jnp.maximum(old, top)
        keep_old, add_new = jnp.exp(old - best), jnp.exp(top - best)
        top_ref[rows, :] = best
        sum_ref[rows, :] = keep_old * sum_ref[rows, :] + add_new * total
        acc_ref[rows, :] = keep_old * acc_ref[rows, :] + add_new * mixed
    lane, row = iota((HEADS, HEAD), 1), iota((HEADS, HEAD), 0)
    line = iota((STAT, HEAD), 0)
    for r in range(REPLICAS):
        stats = jnp.zeros((STAT, HEAD), F32)
        for i in range(REQUESTS):
            at = (r * REQUESTS + i) * HEADS
            send_ref[r, i * HEADS : (i + 1) * HEADS, :] = acc_ref[at : at + HEADS, :].astype(BF16)
            flat = jnp.where(lane == row, top_ref[at : at + HEADS, :], 0.0) + jnp.where(
                lane == row + HEADS, sum_ref[at : at + HEADS, :], 0.0
            )
            flat = jnp.sum(flat, axis=0, keepdims=True)
            high = flat.astype(BF16).astype(F32)
            middle = (flat - high).astype(BF16).astype(F32)
            for part, value in enumerate((high, middle, flat - high - middle)):
                stats = jnp.where(line == i * 3 + part, value, stats)
        send_ref[r, REQUESTS * HEADS :, :] = stats.astype(BF16)


def partial_attention(owner, count, queries, pool):
    smem = pl.BlockSpec(memory_space=pltpu.SMEM)
    wide = (REPLICAS * REQUESTS * HEADS, HEAD)
    return pl.pallas_call(
        partial_kernel,
        name="partial_attention",
        out_shape=jax.ShapeDtypeStruct((REPLICAS, MESSAGE, HEAD), BF16),
        in_specs=[smem, smem] + whole(2),
        out_specs=whole(1)[0],
        scratch_shapes=[pltpu.VMEM(wide, F32)] * 3,
        compiler_params=params(),
    )(owner, count, queries, pool)


def finish_kernel(got_ref, query_ref, new_ref, out_ref):
    scale = 1.0 / math.sqrt(HEAD)
    per = HEADS // GROUPS
    lane, row = iota((HEADS, HEAD), 1), iota((HEADS, HEAD), 0)

    def by_head(line):
        return jnp.concatenate(
            [
                jnp.broadcast_to(line[:, g * HEAD : (g + 1) * HEAD], (per, HEAD))
                for g in range(GROUPS)
            ],
            axis=0,
        )

    for i in range(REQUESTS):
        query = query_ref[i * HEADS : (i + 1) * HEADS, :].astype(F32)
        key = by_head(new_ref[i : i + 1, :KV].astype(F32))
        value = by_head(new_ref[i : i + 1, KV:].astype(F32))
        own = jnp.sum(query * key, axis=1, keepdims=True) * scale
        tops, sums = [], []
        best = own
        for r in range(REPLICAS):
            stats = got_ref[r, REQUESTS * HEADS :, :].astype(F32)
            flat = stats[i * 3 : i * 3 + 1] + stats[i * 3 + 1 : i * 3 + 2]
            flat = flat + stats[i * 3 + 2 : i * 3 + 3]
            tops.append(jnp.sum(jnp.where(lane == row, flat, 0.0), axis=1, keepdims=True))
            sums.append(jnp.sum(jnp.where(lane == row + HEADS, flat, 0.0), axis=1, keepdims=True))
            best = jnp.maximum(best, tops[-1])
        weight = jnp.exp(own - best)
        total = weight
        mixed = weight * value
        for r in range(REPLICAS):
            factor = jnp.exp(tops[r] - best)
            total = total + factor * sums[r]
            mixed = mixed + factor * got_ref[r, i * HEADS : (i + 1) * HEADS, :].astype(F32)
        out_ref[i * HEADS : (i + 1) * HEADS, :] = (mixed / total).astype(BF16)


def finish(got, queries, incoming):
    return pl.pallas_call(
        finish_kernel,
        name="finish",
        out_shape=jax.ShapeDtypeStruct((REQUESTS * HEADS, HEAD), BF16),
        in_specs=whole(3),
        out_specs=whole(1)[0],
        compiler_params=params(),
    )(got, queries, incoming)


def exchange(array, axes):
    return lax.all_to_all(array, axes, split_axis=0, concat_axis=0, tiled=True)


def swap(array):
    return lax.ppermute(array, "c", [(0, 1), (1, 0)])


def shards(
    moe_input,
    expert_ids,
    route_weight,
    expert_slot,
    w_gate_up,
    w_down,
    queries,
    incoming_key_value,
    key_value_pool,
    block_owner,
    block_tokens,
):
    slot_row = expert_slot.reshape(1, SLOTS)
    query_rows = queries.reshape(REQUESTS * HEADS, HEAD)
    all_queries = lax.all_gather(query_rows, REPLICA, axis=0, tiled=True)

    send = dispatch(
        expert_ids, route_weight, slot_row, moe_input.reshape(TOK * PIECES, WIDE)
    )
    received = exchange(send.reshape(SLOTS * 2, CAP * PIECES, WIDE), CHIPS)

    other_gate_up, other_down = swap(w_gate_up), swap(w_down)
    gate = jnp.concatenate([w_gate_up[:, :HALF], other_gate_up[:, :HALF]], axis=1)
    up = jnp.concatenate([w_gate_up[:, HALF:], other_gate_up[:, HALF:]], axis=1)
    down = jnp.concatenate([w_down, other_down], axis=0)
    mix = mixing(expert_ids, route_weight, slot_row)
    partials = partial_attention(block_owner, block_tokens, all_queries, key_value_pool)

    rows = expert(received.reshape(-1, WIDE), gate, up, down)
    returned = exchange(rows.reshape(SLOTS * 2, CAP * PIECES, WIDE), CHIPS)
    got = exchange(partials, REPLICA)
    moe_out = combine(mix, returned.reshape(-1, WIDE)).reshape(TOK, D)
    attn_out = finish(got, query_rows, incoming_key_value).reshape(REQUESTS, HEADS * HEAD)
    return (moe_out, attn_out)


def solution(mesh):
    fine = Mesh(mesh.devices.reshape(4, 4, 8, 2, 2), AXES)
    rows = P(AXES, None)
    placed = (
        rows,
        rows,
        rows,
        P(),
        P(None, AXES),
        rows,
        rows,
        rows,
        P(AXES, None, None),
        P(AXES),
        P(AXES),
    )
    return jax.shard_map(
        shards, mesh=fine, in_specs=placed, out_specs=(rows, rows), check_vma=False
    )
```

time: 662 us -> 221 us (0.33)
  the two profiles are of different devices: /device:TPU:48 before, /device:TPU:2 now
where the time goes in v1:
time: 221 us; the launch traced here: 220 us
  blocking collectives  74.1 us (34%)
  starting transfers between devices  54.8 us (25%)
  waiting for transfers between devices  42.4 us (19%)
  Pallas kernels  29.2 us (13%)
  local copies, waits for them, and re-layouts  13.3 us (6%)
  other arithmetic  5.28 us (2%)
    all_gather x1, blocking collectives, shards(): all_queries = lax.all_gather(query_rows, REPLICA, axis=0, tiled=True)  74.1 us
    all_to_all x3, starting transfers between devices, exchange(): return lax.all_to_all(array, axes, split_axis=0, concat_axis=0, tiled=True)  50.4 us
    all_to_all x3, waiting for transfers between devices, exchange(): return lax.all_to_all(array, axes, split_axis=0, concat_axis=0, tiled=True)  42.4 us
    pallas_call x1, Pallas kernels, expert(): pl.pallas_call(expert_kernel, name='expert', grid=(rows.shape[0] // step,...  9.63 us
    pallas_call x1, Pallas kernels, partial_attention(): pl.pallas_call(partial_kernel, name='partial_attention', out_shape=jax.Sh...  7.36 us
    unnamed x14, local copies, waits for them, and re-layouts  4.87 us
  transfers between devices with their start and end apart: 5, of which 1 were waited for; matrix products, arithmetic and copies ran while one was open for 5% of the time, Pallas kernels for 10%

profile of v1, /device:TPU:2, one launch (start us, length us, event | category | flops | bytes accessed | tf_op | source)
XLA Modules:
  0.0 219.8 jit_solution(16211500964644154840)
XLA Ops:
  0.6 1.3 copy.13.ids_ref
  2.0 1.4 copy.14.weight_ref
  3.3 1.5 reshape.32.rows_ref
  4.8 3.1 %dispatch.1 = bf16[128,2,16,256]{3,2,1,0:T(8,128)(2,1)} custom-call(s32[16,8]{1,0:T(8,128)} %copy.13.ids_ref, f32[16,8]{1,0:T(8,128)} %copy.14.weight_ref, s32[1,128]{1,0:T(1,128)} %bitcast.9, bf16[128,256]{1,0:T(8,128)(2,1)} %reshape.32.rows_ref), custom_call_target="tpu_custom_call" | custom-call | tf_op jit(solution)/shard_map/dispatch/pallas_call | solution.py:92
  7.9 21.9 %all-to-all-start = ((bf16[256,16,256]{2,1,0:T(8,128)(2,1)}), bf16[256,16,256]{2,1,0:T(8,128)(2,1)S(1)}, u32[]{:S(2)}, u32[]{:S(2)}) async-start(bf16[256,16,256]{2,1,0:T(8,128)(2,1)} %bitcast.7), calls=%async_computation | async-start | bytes 4194304 | tf_op jit(solution)/shard_map/all_to_all | solution.py:333
  29.8 1.9 collective-permute-start
  31.7 0.0 copy-done.3
  31.7 2.4 %collective-permute-start.1 = (bf16[192,2048]{1,0:T(8,128)(2,1)S(1)}, bf16[192,2048]{1,0:T(8,128)(2,1)}, u32[]{:S(2)}, u32[]{:S(2)}) collective-permute-start(bf16[192,2048]{1,0:T(8,128)(2,1)S(1)} %copy-done.3), channel_id=1, source_target_pairs={{0,1},{1,0},{2,3},{3,2},{4,5},{5,4},{6,7},{7,6},{8,9},{9,8},{10,11... | collective-permute-start | bytes 2359304 | tf_op jit(solution)/shard_map/ppermute | solution.py:337
  34.2 0.0 copy-done.5
  34.2 0.0 copy-start.4
  34.2 74.1 %all_gather.3.query_ref = bf16[2048,128]{1,0:T(8,128)(2,1)} all-gather(bf16[128,128]{1,0:T(8,128)(2,1)S(1)} %reshape.38.query_ref), channel_id=1, replica_groups=mesh['x'=4,'zl'=4,'y'=8,'zh'=2,'c'=2] {'x','zl'}, dimensions={0}, use_global_device_ids=true | all-gather | bytes 557056 | tf_op jit(solution)/shard_map/all_gather | solution.py:355
  108.3 7.4 %partial_attention.1 = bf16[16,144,128]{2,1,0:T(8,128)(2,1)} custom-call(s32[16]{0:T(128)} %owner_ref.1, s32[16]{0:T(128)} %count_ref.1, bf16[2048,128]{1,0:T(8,128)(2,1)} %all_gather.3.query_ref, bf16[16,64,1024]{2,1,0:T(8,128)(2,1)} %pool_ref.1), custom_call_target="tpu_custom_call" | custom-call | tf_op jit(solution)/shard_map/partial_attention/pallas_call | solution.py:272
  115.6 0.0 copy-done.4
  115.6 0.0 all-to-all-done
  115.6 11.6 %all-to-all-start.2 = ((bf16[16,144,128]{2,1,0:T(8,128)(2,1)}), bf16[16,144,128]{2,1,0:T(8,128)(2,1)S(1)}, u32[]{:S(2)}, u32[]{:S(2)}) async-start(bf16[16,144,128]{2,1,0:T(8,128)(2,1)} %partial_attention.1), calls=%async_computation.2 | async-start | bytes 1179648 | tf_op jit(solution)/shard_map/all_to_all | solution.py:333
  127.2 2.0 fusion
  129.3 0.0 collective-permute-done.1
  129.3 2.4 %pad_maximum_fusion.2.down_ref = bf16[384,2048]{1,0:T(8,128)(2,1)} fusion(bf16[192,2048]{1,0:T(8,128)(2,1)} %collective-permute-done.1, bf16[192,2048]{1,0:T(8,128)(2,1)S(1)} %copy-done.3), kind=kLoop, calls=%fused_computation.2 | loop fusion | flops 3145728 | bytes 3145728 | tf_op jit(solution)/shard_map/concatenate | solution.py:365
  131.7 0.0 collective-permute-done
  131.7 2.0 fusion.1
  133.7 2.8 %pad_maximum_fusion = (bf16[2048,384]{1,0:T(8,128)(2,1)}, bf16[2048,384]{1,0:T(8,128)(2,1)}) fusion(bf16[2048,192]{1,0:T(8,128)(2,1)S(1)} %get-tuple-element.5, bf16[2048,192]{1,0:T(8,128)(2,1)S(1)} %get-tuple-element.3, bf16[2048,192]{1,0:T(8,128)(2,1)S(1)} %get-tuple-element.4, bf16[2048,192]{1,0:T(8,128)(2,1)S(1)} %get-tuple-element.2), kind=kLoop, calls=%fused_computation | loop fusion | flops 6291456 | bytes 6291456 | tf_op jit(solution)/shard_map/concatenate | solution.py:363
  136.6 9.6 %expert.1 = bf16[4096,256]{1,0:T(8,128)(2,1)} custom-call(bf16[4096,256]{1,0:T(8,128)(2,1)} %bitcast.5, bf16[2048,384]{1,0:T(8,128)(2,1)} %get-tuple-element.6.gate_ref, bf16[2048,384]{1,0:T(8,128)(2,1)} %get-tuple-element.7.up_ref, bf16[384,2048]{1,0:T(8,128)(2,1)} %pad_maximum_fusion.2.down_ref), custom_call_target="tpu_custom_call" | custom-call | tf_op jit(solution)/shard_map/expert/pallas_call | solution.py:192
  146.2 0.0 all-to-all-done.2.got_ref
  146.2 0.8 copy-done.2
  147.0 17.0 %all-to-all-start.1 = ((bf16[256,16,256]{2,1,0:T(8,128)(2,1)}), bf16[256,16,256]{2,1,0:T(8,128)(2,1)S(1)}, u32[]{:S(2)}, u32[]{:S(2)}) async-start(bf16[256,16,256]{2,1,0:T(8,128)(2,1)} %bitcast.6), calls=%async_computation.1 | async-start | bytes 4194304 | tf_op jit(solution)/shard_map/all_to_all | solution.py:333
  164.0 3.0 %mixing.1.mix_ref = bf16[256,4096]{1,0:T(8,128)(2,1)} custom-call(s32[16,8]{1,0:T(8,128)} %copy.13.ids_ref, f32[16,8]{1,0:T(8,128)} %copy.14.weight_ref, s32[1,128]{1,0:T(1,128)} %bitcast.10), custom_call_target="tpu_custom_call" | custom-call | tf_op jit(solution)/shard_map/mixing/pallas_call | solution.py:131
  167.0 2.6 %finish.1 = bf16[128,128]{1,0:T(8,128)(2,1)} custom-call(bf16[16,144,128]{2,1,0:T(8,128)(2,1)} %copy-done.2, bf16[128,128]{1,0:T(8,128)(2,1)} %copy-done.4, bf16[2,1024]{1,0:T(2,128)(2,1)} %new_ref.1), custom_call_target="tpu_custom_call" | custom-call | tf_op jit(solution)/shard_map/finish/pallas_call | solution.py:322
  169.6 1.4 reshape.39
  170.9 42.4 %all-to-all-done.1 = bf16[256,16,256]{2,1,0:T(8,128)(2,1)S(1)} async-done(((bf16[256,16,256]{2,1,0:T(8,128)(2,1)}), bf16[256,16,256]{2,1,0:T(8,128)(2,1)S(1)}, u32[]{:S(2)}, u32[]{:S(2)}) %all-to-all-start.1) | async-done | bytes 2097184 | tf_op jit(solution)/shard_map/all_to_all | solution.py:333
  213.4 1.3 copy-done.1
  214.7 3.6 %combine.1 = bf16[128,256]{1,0:T(8,128)(2,1)} custom-call(bf16[256,4096]{1,0:T(8,128)(2,1)} %mixing.1.mix_ref, bf16[4096,256]{1,0:T(8,128)(2,1)} %bitcast.8), custom_call_target="tpu_custom_call" | custom-call | tf_op jit(solution)/shard_map/combine/pallas_call | solution.py:148
  218.2 1.5 reshape.37
  (7 shorter events, 0.0 us)
Async XLA Ops:
  7.9 23.8 %copy-start.3 = (bf16[192,2048]{1,0:T(8,128)(2,1)S(1)}, bf16[192,2048]{1,0:T(8,128)(2,1)}, u32[]{:S(2)}) copy-start(bf16[192,2048]{1,0:T(8,128)(2,1)} %param.16) | copy-start | bytes 2359300
  7.9 26.2 %copy-start.5 = (bf16[2,8192]{1,0:T(2,128)(2,1)S(1)}, bf16[2,8192]{1,0:T(2,128)(2,1)}, u32[]{:S(2)}) copy-start(bf16[2,8192]{1,0:T(2,128)(2,1)} %param.17) | copy-start | bytes 98308
  7.9 107.7 %all-to-all-start = ((bf16[256,16,256]{2,1,0:T(8,128)(2,1)}), bf16[256,16,256]{2,1,0:T(8,128)(2,1)S(1)}, u32[]{:S(2)}, u32[]{:S(2)}) async-start(bf16[256,16,256]{2,1,0:T(8,128)(2,1)} %bitcast.7), calls=%async_computation | async-start | bytes 4194304 | tf_op jit(solution)/shard_map/all_to_all | solution.py:333
  29.8 101.9 %collective-permute-start = (bf16[2048,384]{1,0:T(8,128)(2,1)}, bf16[2048,384]{1,0:T(8,128)(2,1)}, u32[]{:S(2)}, u32[]{:S(2)}) collective-permute-start(bf16[2048,384]{1,0:T(8,128)(2,1)} %param.15), channel_id=1, source_target_pairs={{0,1},{1,0},{2,3},{3,2},{4,5},{5,4},{6,7},{7,6},{8,9},{9,8},{10,11... | collective-permute-start | bytes 4718600 | tf_op jit(solution)/shard_map/ppermute | solution.py:337
  31.7 97.5 %collective-permute-start.1 = (bf16[192,2048]{1,0:T(8,128)(2,1)S(1)}, bf16[192,2048]{1,0:T(8,128)(2,1)}, u32[]{:S(2)}, u32[]{:S(2)}) collective-permute-start(bf16[192,2048]{1,0:T(8,128)(2,1)S(1)} %copy-done.3), channel_id=1, source_target_pairs={{0,1},{1,0},{2,3},{3,2},{4,5},{5,4},{6,7},{7,6},{8,9},{9,8},{10,11... | collective-permute-start | bytes 2359304 | tf_op jit(solution)/shard_map/ppermute | solution.py:337
  34.2 81.4 %copy-start.4 = (bf16[128,128]{1,0:T(8,128)(2,1)}, bf16[128,128]{1,0:T(8,128)(2,1)S(1)}, u32[]{:S(2)}) copy-start(bf16[128,128]{1,0:T(8,128)(2,1)S(1)} %reshape.38.query_ref) | copy-start | bytes 98308
  115.6 13.6 %copy-start = (bf16[256,16,256]{2,1,0:T(8,128)(2,1)}, bf16[256,16,256]{2,1,0:T(8,128)(2,1)S(1)}, u32[]{:S(2)}) copy-start(bf16[256,16,256]{2,1,0:T(8,128)(2,1)S(1)} %all-to-all-done) | copy-start | bytes 6291460
  115.6 30.6 %all-to-all-start.2 = ((bf16[16,144,128]{2,1,0:T(8,128)(2,1)}), bf16[16,144,128]{2,1,0:T(8,128)(2,1)S(1)}, u32[]{:S(2)}, u32[]{:S(2)}) async-start(bf16[16,144,128]{2,1,0:T(8,128)(2,1)} %partial_attention.1), calls=%async_computation.2 | async-start | bytes 1179648 | tf_op jit(solution)/shard_map/all_to_all | solution.py:333
  146.2 0.8 copy-start.2
  147.0 66.3 %all-to-all-start.1 = ((bf16[256,16,256]{2,1,0:T(8,128)(2,1)}), bf16[256,16,256]{2,1,0:T(8,128)(2,1)S(1)}, u32[]{:S(2)}, u32[]{:S(2)}) async-start(bf16[256,16,256]{2,1,0:T(8,128)(2,1)} %bitcast.6), calls=%async_computation.1 | async-start | bytes 4194304 | tf_op jit(solution)/shard_map/all_to_all | solution.py:333
  213.4 1.3 copy-start.1

commit v2 on v1

v2 whole, which is shorter than its diff:
```python
import math

import jax
import jax.numpy as jnp
from jax import lax
from jax.experimental import pallas as pl
from jax.experimental.pallas import tpu as pltpu
from jax.sharding import Mesh
from jax.sharding import PartitionSpec as P

D = 2048
TOK = 16
TOP = 8
SLOTS = 128
RING = 8
REACH = 32
ROWS = 16
NEAR = RING * TOK
EXTRA = 256
HALF = 192
HEADS = 64
GROUPS = 4
HEAD = 128
REQUESTS = 2
SIDE = 4
BLOCKS = 16
LEN = 64
KV = GROUPS * HEAD
NEG = -1e30
STAT = 16
MESSAGE = REQUESTS * HEADS + STAT

F32 = jnp.float32
BF16 = jnp.bfloat16
VMEM_LIMIT = 56 * 1024 * 1024
AXIS = "d"


def number(x, zl, y, zh, c):
    return (x * 4 + zl) * 32 + y * 4 + zh * 2 + c


def position(device):
    return device >> 7, (device >> 5) & 3, (device >> 2) & 7, (device >> 1) & 1, device & 1


RING_GROUPS = [
    [number(x, z % 4, y, z // 4, 0) for z in range(8)] for x in range(4) for y in range(8)
] + [
    [number(x, z % 4, y, z // 4, 1) for y in range(8)] for x in range(4) for z in range(8)
]
REACH_GROUPS = [
    [number(x, z % 4, y, z // 4, 0) for x in range(4) for y in range(8)] for z in range(8)
] + [
    [number(x, z % 4, y, z // 4, 1) for x in range(4) for z in range(8)] for y in range(8)
]


def exchange(array, groups):
    return lax.all_to_all(
        array, AXIS, split_axis=0, concat_axis=0, axis_index_groups=groups, tiled=True
    )


def moved(array, dx=0, dz=0, dc=0):
    pairs = []
    for device in range(512):
        x, zl, y, zh, c = position(device)
        pairs.append((device, number((x + dx) % 4, (zl + dz) % 4, y, zh, (c + dc) % 2)))
    return lax.ppermute(array, AXIS, pairs)


def iota(shape, dim):
    return lax.broadcasted_iota(jnp.int32, shape, dim)


def whole(count):
    return [pl.BlockSpec(memory_space=pltpu.VMEM)] * count


def one(condition):
    return jnp.where(condition, 1.0, 0.0).astype(BF16)


def split(value):
    high = value.astype(BF16)
    rest = value - high.astype(F32)
    middle = rest.astype(BF16)
    return high, middle, (rest - middle.astype(F32)).astype(BF16)


def call(kernel, name, shapes, inputs, **more):
    return pl.pallas_call(
        kernel,
        name=name,
        out_shape=shapes,
        in_specs=more.pop("in_specs", whole(inputs)),
        out_specs=more.pop("out_specs", whole(1)[0]),
        compiler_params=pltpu.CompilerParams(vmem_limit_bytes=VMEM_LIMIT),
        **more,
    )


def shape(dims, kind=BF16):
    return jax.ShapeDtypeStruct(dims, kind)


def pack_kernel(token_ref, ids_ref, weight_ref, out_ref):
    x, zl, y, zh, c = position(lax.axis_index(AXIS))
    mine = jnp.where(c == 0, zh * 4 + zl, y)
    put = one(iota((TOK, NEAR), 1) == iota((TOK, NEAR), 0) + mine * TOK)
    ids = ids_ref[...].astype(F32).astype(BF16)
    parts = [jnp.dot(p, put, preferred_element_type=F32) for p in (ids,) + split(weight_ref[...])]
    left = jnp.concatenate(parts[:2], axis=0).astype(BF16)
    right = jnp.concatenate(parts[2:], axis=0).astype(BF16)
    for u in range(RING):
        out_ref[u, :, :D] = token_ref[...]
        out_ref[u, :, D : D + NEAR] = left
        out_ref[u, :, D + NEAR :] = right


def reached(slot_ref):
    x, zl, y, zh, c = position(lax.axis_index(AXIS))
    d = iota((REACH, SLOTS), 0)
    across, along = d >> 3, d & 7
    at_zl = jnp.where(c == 0, zl, along & 3)
    at_y = jnp.where(c == 0, along, y)
    return one(slot_ref[...] == (across * 4 + at_zl) * 8 + at_y)


def routing(near_ref, slot_ref):
    head = jnp.sum(near_ref[:, :, D:].astype(F32), axis=0)
    ids, weights = head[:TOP, :NEAR], (head[TOP:, :NEAR], head[:TOP, NEAR:], head[TOP:, NEAR:])
    expert = iota((SLOTS, NEAR), 0).astype(F32)
    hits = [ids[k : k + 1] == expert for k in range(TOP)]
    chosen = jnp.zeros((SLOTS, NEAR), F32)
    for hit in hits:
        chosen = chosen + jnp.where(hit, 1.0, 0.0)
    here = reached(slot_ref)
    mine = jnp.dot(here, chosen.astype(BF16), preferred_element_type=F32)
    earlier = one(iota((NEAR, NEAR), 0) < iota((NEAR, NEAR), 1))
    rank = jnp.dot(mine.astype(BF16), earlier, preferred_element_type=F32)
    place = jnp.where(mine > 0.5, rank, -1.0)
    taken = place[:, None, :] == iota((1, ROWS, NEAR), 1).astype(F32)
    return hits, weights, here, taken


def dispatch_kernel(near_ref, slot_ref, out_ref):
    _, _, _, taken = routing(near_ref, slot_ref)
    pick = jnp.where(taken, 1.0, 0.0).reshape(REACH * ROWS, NEAR).astype(BF16)
    tokens = near_ref[:, :, :D].reshape(NEAR, D)
    rows = jnp.dot(pick, tokens, preferred_element_type=F32)
    out_ref[...] = rows.astype(BF16).reshape(REACH, ROWS, D)


def mixing_kernel(near_ref, slot_ref, out_ref):
    hits, weights, here, taken = routing(near_ref, slot_ref)
    total = jnp.zeros((REACH, NEAR), F32)
    for part in weights:
        spread = jnp.zeros((SLOTS, NEAR), F32)
        for k in range(TOP):
            spread = spread + jnp.where(hits[k], part[k : k + 1], 0.0)
        total = total + jnp.dot(here, spread.astype(BF16), preferred_element_type=F32)
    mix = jnp.where(taken, total[:, None, :], 0.0).reshape(REACH * ROWS, NEAR).T
    high, low, _ = split(mix)
    out_ref[:NEAR] = high
    out_ref[NEAR:] = low


def combine_kernel(mix_ref, rows_ref, out_ref):
    rows = rows_ref[...].reshape(REACH * ROWS, D)
    both = jnp.dot(mix_ref[...], rows, preferred_element_type=F32)
    out_ref[...] = (both[:NEAR] + both[NEAR:]).astype(BF16).reshape(RING, TOK, D)


def total_kernel(parts_ref, out_ref):
    out_ref[...] = jnp.sum(parts_ref[...].astype(F32), axis=0).astype(BF16)


ROW_STEP = 128


def expert_kernel(rows_ref, gate_ref, up_ref, down_ref, out_ref):
    x = rows_ref[...]
    gate = jnp.dot(x, gate_ref[...], preferred_element_type=F32)
    up = jnp.dot(x, up_ref[...], preferred_element_type=F32)
    act = (gate / (1.0 + jnp.exp(-gate)) * up).astype(BF16)
    out_ref[...] = jnp.dot(act, down_ref[...], preferred_element_type=F32).astype(BF16)


def expert(rows, gate, up, down):
    step = pl.BlockSpec((ROW_STEP, D), lambda i: (i, 0))
    fixed = [pl.BlockSpec(w.shape, lambda i: (0, 0)) for w in (gate, up, down)]
    return call(
        expert_kernel,
        "expert",
        shape(rows.shape),
        4,
        grid=(rows.shape[0] // ROW_STEP,),
        in_specs=[step] + fixed,
        out_specs=step,
    )(rows, gate, up, down)


def partial_kernel(owner_ref, count_ref, query_ref, pool_ref, send_ref, top_ref, sum_ref, acc_ref):
    scale = 1.0 / math.sqrt(HEAD)
    top_ref[...] = jnp.full(top_ref.shape, NEG, F32)
    sum_ref[...] = jnp.zeros(sum_ref.shape, F32)
    acc_ref[...] = jnp.zeros(acc_ref.shape, F32)
    x, zl, _, _, _ = position(lax.axis_index(AXIS))
    per = HEADS // GROUPS
    own = iota((HEADS, KV), 1) // HEAD == iota((HEADS, KV), 0) // per
    slot = iota((HEADS, LEN), 1)
    for b in range(BLOCKS):
        owner = owner_ref[b]
        ax, az, request = owner >> 3, (owner >> 1) & 3, owner & 1
        asked = ((zl - az) & 3) * 8 + ((x - ax) & 3) * 2 + request
        state = ((az - zl) & 3) * 8 + ((ax - x) & 3) * 2 + request
        rows = pl.ds(pl.multiple_of(state * HEADS, HEADS), HEADS)
        query = query_ref[pl.ds(pl.multiple_of(asked * HEADS, HEADS), HEADS), :]
        wide = jnp.where(own, jnp.concatenate([query] * GROUPS, axis=1), jnp.zeros((), BF16))
        score = (
            lax.dot_general(
                wide, pool_ref[b, :, :KV], (((1,), (1,)), ((), ())), preferred_element_type=F32
            )
            * scale
        )
        keep = slot < count_ref[b]
        score = jnp.where(keep, score, NEG)
        top = jnp.max(score, axis=1, keepdims=True)
        weight = jnp.where(keep, jnp.exp(score - top), 0.0)
        total = jnp.sum(weight, axis=1, keepdims=True)
        high, low, _ = split(weight)
        mixed = jnp.dot(
            jnp.concatenate([high, low], axis=0), pool_ref[b, :, KV:], preferred_element_type=F32
        )
        mixed = mixed[:HEADS] + mixed[HEADS:]
        mixed = jnp.concatenate(
            [mixed[g * per : (g + 1) * per, g * HEAD : (g + 1) * HEAD] for g in range(GROUPS)],
            axis=0,
        )
        old = top_ref[rows, :]
        best = jnp.maximum(old, top)
        keep_old, add_new = jnp.exp(old - best), jnp.exp(top - best)
        top_ref[rows, :] = best
        sum_ref[rows, :] = keep_old * sum_ref[rows, :] + add_new * total
        acc_ref[rows, :] = keep_old * acc_ref[rows, :] + add_new * mixed
    lane, row = iota((HEADS, HEAD), 1), iota((HEADS, HEAD), 0)
    line = iota((STAT, HEAD), 0)
    for r in range(SIDE * SIDE):
        stats = jnp.zeros((STAT, HEAD), F32)
        for i in range(REQUESTS):
            at = (r * REQUESTS + i) * HEADS
            send_ref[r, i * HEADS : (i + 1) * HEADS, :] = acc_ref[at : at + HEADS, :].astype(BF16)
            flat = jnp.where(lane == row, top_ref[at : at + HEADS, :], 0.0) + jnp.where(
                lane == row + HEADS, sum_ref[at : at + HEADS, :], 0.0
            )
            flat = jnp.sum(flat, axis=0, keepdims=True)
            for part, value in enumerate(split(flat)):
                stats = jnp.where(line == i * 3 + part, value.astype(F32), stats)
        send_ref[r, REQUESTS * HEADS :, :] = stats.astype(BF16)


def partial_attention(owner, count, queries, pool):
    smem = pl.BlockSpec(memory_space=pltpu.SMEM)
    return call(
        partial_kernel,
        "partial_attention",
        shape((SIDE * SIDE, MESSAGE, HEAD)),
        4,
        in_specs=[smem, smem] + whole(2),
        scratch_shapes=[pltpu.VMEM((SIDE * SIDE * REQUESTS * HEADS, HEAD), F32)] * 3,
    )(owner, count, queries, pool)


def finish_kernel(got0_ref, got1_ref, got2_ref, got3_ref, query_ref, new_ref, out_ref):
    scale = 1.0 / math.sqrt(HEAD)
    per = HEADS // GROUPS
    lane, row = iota((HEADS, HEAD), 1), iota((HEADS, HEAD), 0)
    parts = [(ref, r) for ref in (got0_ref, got1_ref, got2_ref, got3_ref) for r in range(SIDE)]

    def by_head(line):
        return jnp.concatenate(
            [
                jnp.broadcast_to(line[:, g * HEAD : (g + 1) * HEAD], (per, HEAD))
                for g in range(GROUPS)
            ],
            axis=0,
        )

    for i in range(REQUESTS):
        query = query_ref[i * HEADS : (i + 1) * HEADS, :].astype(F32)
        key = by_head(new_ref[i : i + 1, :KV].astype(F32))
        value = by_head(new_ref[i : i + 1, KV:].astype(F32))
        own = jnp.sum(query * key, axis=1, keepdims=True) * scale
        tops, sums = [], []
        best = own
        for ref, r in parts:
            stats = ref[r, REQUESTS * HEADS :, :].astype(F32)
            flat = stats[i * 3 : i * 3 + 1] + stats[i * 3 + 1 : i * 3 + 2]
            flat = flat + stats[i * 3 + 2 : i * 3 + 3]
            tops.append(jnp.sum(jnp.where(lane == row, flat, 0.0), axis=1, keepdims=True))
            sums.append(jnp.sum(jnp.where(lane == row + HEADS, flat, 0.0), axis=1, keepdims=True))
            best = jnp.maximum(best, tops[-1])
        weight = jnp.exp(own - best)
        total = weight
        mixed = weight * value
        for (ref, r), top, part in zip(parts, tops, sums):
            factor = jnp.exp(top - best)
            total = total + factor * part
            mixed = mixed + factor * ref[r, i * HEADS : (i + 1) * HEADS, :].astype(F32)
        out_ref[i * HEADS : (i + 1) * HEADS, :] = (mixed / total).astype(BF16)


def ask(queries, pool, owner, count):
    own = queries.reshape(REQUESTS * HEADS, HEAD)
    line = jnp.concatenate([own] + [moved(own, dx=k) for k in range(1, SIDE)], axis=0)
    square = jnp.concatenate([line] + [moved(line, dz=k) for k in range(1, SIDE)], axis=0)
    return own, partial_attention(owner, count, square, pool)


def answer(own, partials, incoming):
    partials = partials.reshape(SIDE, SIDE, MESSAGE, HEAD)
    columns = [partials[0]] + [moved(partials[k], dz=k) for k in range(1, SIDE)]
    got = []
    for k in range(SIDE):
        piece = jnp.stack([column[k] for column in columns])
        got.append(moved(piece, dx=k) if k else piece)
    out = call(finish_kernel, "finish", shape((REQUESTS * HEADS, HEAD)), 6)(*got, own, incoming)
    return out.reshape(REQUESTS, HEADS * HEAD)


def shards(
    moe_input,
    expert_ids,
    route_weight,
    expert_slot,
    w_gate_up,
    w_down,
    queries,
    incoming_key_value,
    key_value_pool,
    block_owner,
    block_tokens,
):
    slot_row = expert_slot.reshape(1, SLOTS)
    packed = call(pack_kernel, "pack", shape((RING, TOK, D + EXTRA)), 3)(
        moe_input, expert_ids.T, route_weight.T
    )
    near = exchange(packed, RING_GROUPS)
    send = call(dispatch_kernel, "dispatch", shape((REACH, ROWS, D)), 2)(near, slot_row)
    received = exchange(send, REACH_GROUPS)

    own, partials = ask(queries, key_value_pool, block_owner, block_tokens)
    other_gate_up, other_down = moved(w_gate_up, dc=1), moved(w_down, dc=1)
    gate = jnp.concatenate([w_gate_up[:, :HALF], other_gate_up[:, :HALF]], axis=1)
    up = jnp.concatenate([w_gate_up[:, HALF:], other_gate_up[:, HALF:]], axis=1)
    down = jnp.concatenate([w_down, other_down], axis=0)
    received, partials = lax.optimization_barrier((received, partials))

    rows = expert(received.reshape(REACH * ROWS, D), gate, up, down)
    returned = exchange(rows.reshape(REACH, ROWS, D), REACH_GROUPS)
    attn_out = answer(own, partials, incoming_key_value)
    mix = call(mixing_kernel, "mixing", shape((2 * NEAR, REACH * ROWS)), 2)(near, slot_row)
    parts = call(combine_kernel, "combine", shape((RING, TOK, D)), 2)(mix, returned)
    parts = exchange(parts, RING_GROUPS)
    moe_out = call(total_kernel, "total", shape((TOK, D)), 1)(parts)
    return (moe_out, attn_out)


def solution(mesh):
    flat = Mesh(mesh.devices.reshape(-1), (AXIS,))
    rows = P(AXIS, None)
    placed = (
        rows,
        rows,
        rows,
        P(),
        P(None, AXIS),
        rows,
        rows,
        rows,
        P(AXIS, None, None),
        P(AXIS),
        P(AXIS),
    )
    return jax.shard_map(
        shards, mesh=flat, in_specs=placed, out_specs=(rows, rows), check_vma=False
    )
```

time: 221 us -> 182 us (0.82)
  the two profiles are of different devices: /device:TPU:2 before, /device:TPU:201 now
where the time goes in v2:
time: 182 us; the launch traced here: 181 us
  starting transfers between devices  67.1 us (37%)
  waiting for transfers between devices  48.1 us (26%)
  Pallas kernels  30.3 us (17%)
  blocking collectives  18.8 us (10%)
  local copies, waits for them, and re-layouts  10.6 us (6%)
  other arithmetic  4.88 us (3%)
    ppermute x14, starting transfers between devices, moved(): return lax.ppermute(array, AXIS, pairs)  40.8 us
    ppermute x14, waiting for transfers between devices, moved(): return lax.ppermute(array, AXIS, pairs)  38.4 us
    all_to_all x3, starting transfers between devices, exchange(): lax.all_to_all(array, AXIS, split_axis=0, concat_axis=0, axis_index_group...  26.4 us
    all_to_all x1, blocking collectives, exchange(): lax.all_to_all(array, AXIS, split_axis=0, concat_axis=0, axis_index_group...  18.8 us
    all_to_all x3, waiting for transfers between devices, exchange(): lax.all_to_all(array, AXIS, split_axis=0, concat_axis=0, axis_index_group...  9.77 us
    pallas_call x1, Pallas kernels, expert(): call(expert_kernel, 'expert', shape(rows.shape), 4, grid=(rows.shape[0] /...  7.9 us
    pallas_call x1, Pallas kernels, partial_attention(): call(partial_kernel, 'partial_attention', shape((SIDE * SIDE, MESSAGE, HE...  7.34 us
    unnamed x27, local copies, waits for them, and re-layouts  5.02 us
  transfers between devices with their start and end apart: 17, of which 8 were waited for; matrix products, arithmetic and copies ran while one was open for 6% of the time, Pallas kernels for 9%

profile of v2, /device:TPU:201, one launch (start us, length us, event | category | flops | bytes accessed | tf_op | source)
XLA Modules:
  0.0 180.8 jit_solution(17967348249781735797)
XLA Ops:
  2.5 18.8 %all_to_all.20.near_ref = bf16[8,16,2304]{2,1,0:T(8,128)(2,1)} all-to-all(bf16[8,16,2304]{2,1,0:T(8,128)(2,1)} %pack.1), channel_id=1, replica_groups={{0,32,64,96,2,34,66,98},{4,36,68,100,6,38,70,102},{8,40,72,104,10,42,74..., dimensions={0} | all-to-all | bytes 1179648 | tf_op jit(solution)/shard_map/all_to_all | solution.py:60
  21.2 3.4 %dispatch.1 = bf16[32,16,2048]{2,1,0:T(8,128)(2,1)} custom-call(bf16[8,16,2304]{2,1,0:T(8,128)(2,1)} %all_to_all.20.near_ref, s32[1,128]{1,0:T(1,128)} %bitcast.9), custom_call_target="tpu_custom_call" | custom-call | tf_op jit(solution)/shard_map/dispatch/pallas_call | solution.py:351
  24.7 10.3 %all-to-all-start.1 = ((bf16[32,16,2048]{2,1,0:T(8,128)(2,1)}), bf16[32,16,2048]{2,1,0:T(8,128)(2,1)S(1)}, u32[]{:S(2)}, u32[]{:S(2)}) async-start(bf16[32,16,2048]{2,1,0:T(8,128)(2,1)} %dispatch.1), calls=%async_computation.1 | async-start | bytes 4194304 | tf_op jit(solution)/shard_map/all_to_all | solution.py:60
  35.0 3.1 %collective-permute-start = (bf16[128,128]{1,0:T(8,128)(2,1)S(1)}, bf16[128,128]{1,0:T(8,128)(2,1)S(1)}, u32[]{:S(2)}, u32[]{:S(2)}) collective-permute-start(bf16[128,128]{1,0:T(8,128)(2,1)S(1)} %reshape.30.query_ref), channel_id=1, source_target_pairs={{0,128},{1,129},{2,130},{3,131},{4,132},{5,133},{6,134},{7,135},{8... | collective-permute-start | bytes 98312 | tf_op jit(solution)/shard_map/ppermute | solution.py:70
  38.1 4.4 %collective-permute-start.1 = (bf16[128,128]{1,0:T(8,128)(2,1)S(1)}, bf16[128,128]{1,0:T(8,128)(2,1)S(1)}, u32[]{:S(2)}, u32[]{:S(2)}) collective-permute-start(bf16[128,128]{1,0:T(8,128)(2,1)S(1)} %reshape.30.query_ref), channel_id=1, source_target_pairs={{0,256},{1,257},{2,258},{3,259},{4,260},{5,261},{6,262},{7,263},{8... | collective-permute-start | bytes 98312 | tf_op jit(solution)/shard_map/ppermute | solution.py:70
  42.5 3.0 %collective-permute-start.2 = (bf16[128,128]{1,0:T(8,128)(2,1)S(1)}, bf16[128,128]{1,0:T(8,128)(2,1)S(1)}, u32[]{:S(2)}, u32[]{:S(2)}) collective-permute-start(bf16[128,128]{1,0:T(8,128)(2,1)S(1)} %reshape.30.query_ref), channel_id=1, source_target_pairs={{0,384},{1,385},{2,386},{3,387},{4,388},{5,389},{6,390},{7,391},{8... | collective-permute-start | bytes 98312 | tf_op jit(solution)/shard_map/ppermute | solution.py:70
  45.5 3.4 %collective-permute-start.6 = (bf16[2048,384]{1,0:T(8,128)(2,1)}, bf16[2048,384]{1,0:T(8,128)(2,1)}, u32[]{:S(2)}, u32[]{:S(2)}) collective-permute-start(bf16[2048,384]{1,0:T(8,128)(2,1)} %param.15), channel_id=1, source_target_pairs={{0,1},{1,0},{2,3},{3,2},{4,5},{5,4},{6,7},{7,6},{8,9},{9,8},{10,11... | collective-permute-start | bytes 4718600 | tf_op jit(solution)/shard_map/ppermute | solution.py:70
  49.0 1.9 %collective-permute-start.7 = (bf16[192,2048]{1,0:T(8,128)(2,1)S(1)}, bf16[192,2048]{1,0:T(8,128)(2,1)S(1)}, u32[]{:S(2)}, u32[]{:S(2)}) collective-permute-start(bf16[192,2048]{1,0:T(8,128)(2,1)S(1)} %copy-done.4), channel_id=1, source_target_pairs={{0,1},{1,0},{2,3},{3,2},{4,5},{5,4},{6,7},{7,6},{8,9},{9,8},{10,11... | collective-permute-start | bytes 2359304 | tf_op jit(solution)/shard_map/ppermute | solution.py:70
  50.9 4.0 %collective-permute-done = bf16[128,128]{1,0:T(8,128)(2,1)S(1)} collective-permute-done((bf16[128,128]{1,0:T(8,128)(2,1)S(1)}, bf16[128,128]{1,0:T(8,128)(2,1)S(1)}, u32[]{:S(2)}, u32[]{:S(2)}) %collective-permute-start) | collective-permute-done | bytes 32800 | tf_op jit(solution)/shard_map/ppermute | solution.py:70
  55.0 4.5 %collective-permute-done.1 = bf16[128,128]{1,0:T(8,128)(2,1)S(1)} collective-permute-done((bf16[128,128]{1,0:T(8,128)(2,1)S(1)}, bf16[128,128]{1,0:T(8,128)(2,1)S(1)}, u32[]{:S(2)}, u32[]{:S(2)}) %collective-permute-start.1) | collective-permute-done | bytes 32800 | tf_op jit(solution)/shard_map/ppermute | solution.py:70
  59.6 5.4 %collective-permute-start.3 = (bf16[512,128]{1,0:T(8,128)(2,1)S(1)}, bf16[512,128]{1,0:T(8,128)(2,1)S(1)}, u32[]{:S(2)}, u32[]{:S(2)}) collective-permute-start(bf16[512,128]{1,0:T(8,128)(2,1)S(1)} %get-tuple-element.29), channel_id=1, source_target_pairs={{0,32},{1,33},{2,34},{3,35},{4,36},{5,37},{6,38},{7,39},{8,40},{9,... | collective-permute-start | bytes 393224 | tf_op jit(solution)/shard_map/ppermute | solution.py:70
  65.0 2.2 %collective-permute-start.4 = (bf16[512,128]{1,0:T(8,128)(2,1)S(1)}, bf16[512,128]{1,0:T(8,128)(2,1)S(1)}, u32[]{:S(2)}, u32[]{:S(2)}) collective-permute-start(bf16[512,128]{1,0:T(8,128)(2,1)S(1)} %get-tuple-element.29), channel_id=1, source_target_pairs={{0,64},{1,65},{2,66},{3,67},{4,68},{5,69},{6,70},{7,71},{8,72},{9,... | collective-permute-start | bytes 393224 | tf_op jit(solution)/shard_map/ppermute | solution.py:70
  67.2 2.0 %fusion = (bf16[2048,192]{1,0:T(8,128)(2,1)S(1)}, bf16[2048,192]{1,0:T(8,128)(2,1)S(1)}) fusion(bf16[2048,384]{1,0:T(8,128)(2,1)} %param.15), kind=kLoop, calls=%fused_computation.18 | loop fusion | bytes 3145728 | tf_op jit(solution)/shard_map/slice | solution.py:357
  69.2 1.9 %collective-permute-start.5 = (bf16[512,128]{1,0:T(8,128)(2,1)S(1)}, bf16[512,128]{1,0:T(8,128)(2,1)S(1)}, u32[]{:S(2)}, u32[]{:S(2)}) collective-permute-start(bf16[512,128]{1,0:T(8,128)(2,1)S(1)} %get-tuple-element.29), channel_id=1, source_target_pairs={{0,96},{1,97},{2,98},{3,99},{4,100},{5,101},{6,102},{7,103},{8,104... | collective-permute-start | bytes 393224 | tf_op jit(solution)/shard_map/ppermute | solution.py:70
  71.2 3.6 %collective-permute-done.4 = bf16[512,128]{1,0:T(8,128)(2,1)S(1)} collective-permute-done((bf16[512,128]{1,0:T(8,128)(2,1)S(1)}, bf16[512,128]{1,0:T(8,128)(2,1)S(1)}, u32[]{:S(2)}, u32[]{:S(2)}) %collective-permute-start.4) | collective-permute-done | bytes 131104 | tf_op jit(solution)/shard_map/ppermute | solution.py:70
  77.6 7.3 %partial_attention.1 = bf16[16,144,128]{2,1,0:T(8,128)(2,1)} custom-call(s32[16]{0:T(128)} %owner_ref.1, s32[16]{0:T(128)} %count_ref.1, bf16[2048,128]{1,0:T(8,128)(2,1)} %copy-done.5, bf16[16,64,1024]{2,1,0:T(8,128)(2,1)} %pool_ref.1), custom_call_target="tpu_custom_call" | custom-call | tf_op jit(solution)/shard_map/partial_attention/pallas_call | solution.py:266
  86.2 2.0 %fusion.1 = (bf16[2048,192]{1,0:T(8,128)(2,1)S(1)}, bf16[2048,192]{1,0:T(8,128)(2,1)S(1)}) fusion(bf16[2048,384]{1,0:T(8,128)(2,1)} %collective-permute-done.6), kind=kLoop, calls=%fused_computation.19 | loop fusion | bytes 3145728 | tf_op jit(solution)/shard_map/slice | solution.py:357
  88.2 2.8 %pad_maximum_fusion = (bf16[2048,384]{1,0:T(8,128)(2,1)}, bf16[2048,384]{1,0:T(8,128)(2,1)}) fusion(bf16[2048,192]{1,0:T(8,128)(2,1)S(1)} %get-tuple-element.9, bf16[2048,192]{1,0:T(8,128)(2,1)S(1)} %get-tuple-element.7, bf16[2048,192]{1,0:T(8,128)(2,1)S(1)} %get-tuple-element.8, bf16[2048,192]{1,0:T(8,128)(2,1)S(1)} %get-tuple-element.6), kind=kLoop, calls=%fused_computation | loop fusion | flops 6291456 | bytes 6291456 | tf_op jit(solution)/shard_map/concatenate | solution.py:356
  92.4 7.9 %expert.1 = bf16[512,2048]{1,0:T(8,128)(2,1)} custom-call(bf16[512,2048]{1,0:T(8,128)(2,1)} %bitcast.5, bf16[2048,384]{1,0:T(8,128)(2,1)} %get-tuple-element.37.gate_ref, bf16[2048,384]{1,0:T(8,128)(2,1)} %get-tuple-element.38.up_ref, bf16[384,2048]{1,0:T(8,128)(2,1)} %pad_maximum_fusion.2.down_ref), custom_call_target="tpu_custom_call" | custom-call | tf_op jit(solution)/shard_map/expert/pallas_call | solution.py:194
  100.3 10.4 %all-to-all-start.2 = ((bf16[32,16,2048]{2,1,0:T(8,128)(2,1)}), bf16[32,16,2048]{2,1,0:T(8,128)(2,1)S(1)}, u32[]{:S(2)}, u32[]{:S(2)}) async-start(bf16[32,16,2048]{2,1,0:T(8,128)(2,1)} %bitcast.6), calls=%async_computation.2 | async-start | bytes 4194304 | tf_op jit(solution)/shard_map/all_to_all | solution.py:60
  110.7 2.3 %mixing.1.mix_ref = bf16[256,512]{1,0:T(8,128)(2,1)} custom-call(bf16[8,16,2304]{2,1,0:T(8,128)(2,1)} %all_to_all.20.near_ref, s32[1,128]{1,0:T(1,128)} %bitcast.10), custom_call_target="tpu_custom_call" | custom-call | tf_op jit(solution)/shard_map/mixing/pallas_call | solution.py:364
  113.0 2.1 %collective-permute-start.8 = (bf16[4,144,128]{2,1,0:T(8,128)(2,1)S(1)}, bf16[4,144,128]{2,1,0:T(8,128)(2,1)S(1)}, u32[]{:S(2)}, u32[]{:S(2)}) collective-permute-start(bf16[4,144,128]{2,1,0:T(8,128)(2,1)S(1)} %get-tuple-element.14), channel_id=1, source_target_pairs={{0,32},{1,33},{2,34},{3,35},{4,36},{5,37},{6,38},{7,39},{8,40},{9,... | collective-permute-start | bytes 442376 | tf_op jit(solution)/shard_map/ppermute | solution.py:70
  115.1 3.1 %collective-permute-start.9 = (bf16[4,144,128]{2,1,0:T(8,128)(2,1)S(1)}, bf16[4,144,128]{2,1,0:T(8,128)(2,1)S(1)}, u32[]{:S(2)}, u32[]{:S(2)}) collective-permute-start(bf16[4,144,128]{2,1,0:T(8,128)(2,1)S(1)} %get-tuple-element.16), channel_id=1, source_target_pairs={{0,64},{1,65},{2,66},{3,67},{4,68},{5,69},{6,70},{7,71},{8,72},{9,... | collective-permute-start | bytes 442376 | tf_op jit(solution)/shard_map/ppermute | solution.py:70
  118.3 2.2 %collective-permute-start.10 = (bf16[4,144,128]{2,1,0:T(8,128)(2,1)S(1)}, bf16[4,144,128]{2,1,0:T(8,128)(2,1)S(1)}, u32[]{:S(2)}, u32[]{:S(2)}) collective-permute-start(bf16[4,144,128]{2,1,0:T(8,128)(2,1)S(1)} %get-tuple-element.15), channel_id=1, source_target_pairs={{0,96},{1,97},{2,98},{3,99},{4,100},{5,101},{6,102},{7,103},{8,104... | collective-permute-start | bytes 442376 | tf_op jit(solution)/shard_map/ppermute | solution.py:70
  120.5 19.8 %collective-permute-done.8 = bf16[4,144,128]{2,1,0:T(8,128)(2,1)S(1)} collective-permute-done((bf16[4,144,128]{2,1,0:T(8,128)(2,1)S(1)}, bf16[4,144,128]{2,1,0:T(8,128)(2,1)S(1)}, u32[]{:S(2)}, u32[]{:S(2)}) %collective-permute-start.8) | collective-permute-done | bytes 147488 | tf_op jit(solution)/shard_map/ppermute | solution.py:70
  140.3 9.8 %all-to-all-done.2.rows_ref = bf16[32,16,2048]{2,1,0:T(8,128)(2,1)S(1)} async-done(((bf16[32,16,2048]{2,1,0:T(8,128)(2,1)}), bf16[32,16,2048]{2,1,0:T(8,128)(2,1)S(1)}, u32[]{:S(2)}, u32[]{:S(2)}) %all-to-all-start.2) | async-done | bytes 2097184 | tf_op jit(solution)/shard_map/all_to_all | solution.py:60
  151.4 3.2 %combine.1 = bf16[8,16,2048]{2,1,0:T(8,128)(2,1)} custom-call(bf16[256,512]{1,0:T(8,128)(2,1)} %mixing.1.mix_ref, bf16[32,16,2048]{2,1,0:T(8,128)(2,1)} %copy-done.1), custom_call_target="tpu_custom_call" | custom-call | tf_op jit(solution)/shard_map/combine/pallas_call | solution.py:365
  154.6 5.7 %all-to-all-start.3 = ((bf16[8,16,2048]{2,1,0:T(8,128)(2,1)}), bf16[8,16,2048]{2,1,0:T(8,128)(2,1)S(1)}, u32[]{:S(2)}, u32[]{:S(2)}) async-start(bf16[8,16,2048]{2,1,0:T(8,128)(2,1)} %combine.1), calls=%async_computation.3 | async-start | bytes 1048576 | tf_op jit(solution)/shard_map/all_to_all | solution.py:60
  160.4 1.9 %collective-permute-start.13 = (bf16[4,144,128]{2,1,0:T(8,128)(2,1)S(1)}, bf16[4,144,128]{2,1,0:T(8,128)(2,1)S(1)}, u32[]{:S(2)}, u32[]{:S(2)}) collective-permute-start(bf16[4,144,128]{2,1,0:T(8,128)(2,1)S(1)} %pad_maximum_fusion.6), channel_id=1, source_target_pairs={{0,384},{1,385},{2,386},{3,387},{4,388},{5,389},{6,390},{7,391},{8... | collective-permute-start | bytes 442376 | tf_op jit(solution)/shard_map/ppermute | solution.py:70
  162.4 4.1 %collective-permute-start.12 = (bf16[4,144,128]{2,1,0:T(8,128)(2,1)S(1)}, bf16[4,144,128]{2,1,0:T(8,128)(2,1)S(1)}, u32[]{:S(2)}, u32[]{:S(2)}) collective-permute-start(bf16[4,144,128]{2,1,0:T(8,128)(2,1)S(1)} %pad_maximum_fusion.5), channel_id=1, source_target_pairs={{0,256},{1,257},{2,258},{3,259},{4,260},{5,261},{6,262},{7,263},{8... | collective-permute-start | bytes 442376 | tf_op jit(solution)/shard_map/ppermute | solution.py:70
  169.8 3.8 %collective-permute-done.11.got1_ref = bf16[4,144,128]{2,1,0:T(8,128)(2,1)S(1)} collective-permute-done((bf16[4,144,128]{2,1,0:T(8,128)(2,1)S(1)}, bf16[4,144,128]{2,1,0:T(8,128)(2,1)S(1)}, u32[]{:S(2)}, u32[]{:S(2)}) %collective-permute-start.11) | collective-permute-done | bytes 147488 | tf_op jit(solution)/shard_map/ppermute | solution.py:70
  174.2 2.6 %finish.1 = bf16[128,128]{1,0:T(8,128)(2,1)} custom-call(bf16[4,144,128]{2,1,0:T(8,128)(2,1)} %pad_maximum_fusion.3.got0_ref, bf16[4,144,128]{2,1,0:T(8,128)(2,1)} %copy-done.9, bf16[4,144,128]{2,1,0:T(8,128)(2,1)} %copy-done.8, bf16[4,144,128]{2,1,0:T(8,128)(2,1)} %copy-done.7, bf16[128,128]{1,0:T(8,128)(2,1)} %copy-done.6, bf16[2,1024]{1,0:T(2,128)(2,1)} %new_ref.1), custom_call_target="tpu_custom_call" | custom-call | tf_op jit(solution)/shard_map/finish/pallas_call | solution.py:329
  (55 shorter events, 16.7 us)
Async XLA Ops:
  24.7 10.3 %copy-start.10 = (bf16[2,8192]{1,0:T(2,128)(2,1)S(1)}, bf16[2,8192]{1,0:T(2,128)(2,1)}, u32[]{:S(2)}) copy-start(bf16[2,8192]{1,0:T(2,128)(2,1)} %param.17) | copy-start | bytes 98308
  24.7 24.3 %copy-start.4 = (bf16[192,2048]{1,0:T(8,128)(2,1)S(1)}, bf16[192,2048]{1,0:T(8,128)(2,1)}, u32[]{:S(2)}) copy-start(bf16[192,2048]{1,0:T(8,128)(2,1)} %param.16) | copy-start | bytes 2359300
  24.7 66.4 %all-to-all-start.1 = ((bf16[32,16,2048]{2,1,0:T(8,128)(2,1)}), bf16[32,16,2048]{2,1,0:T(8,128)(2,1)S(1)}, u32[]{:S(2)}, u32[]{:S(2)}) async-start(bf16[32,16,2048]{2,1,0:T(8,128)(2,1)} %dispatch.1), calls=%async_computation.1 | async-start | bytes 4194304 | tf_op jit(solution)/shard_map/all_to_all | solution.py:60
  35.0 34.2 %copy-start.6 = (bf16[128,128]{1,0:T(8,128)(2,1)}, bf16[128,128]{1,0:T(8,128)(2,1)S(1)}, u32[]{:S(2)}) copy-start(bf16[128,128]{1,0:T(8,128)(2,1)S(1)} %reshape.30.query_ref) | copy-start | bytes 98308
  35.0 20.0 %collective-permute-start = (bf16[128,128]{1,0:T(8,128)(2,1)S(1)}, bf16[128,128]{1,0:T(8,128)(2,1)S(1)}, u32[]{:S(2)}, u32[]{:S(2)}) collective-permute-start(bf16[128,128]{1,0:T(8,128)(2,1)S(1)} %reshape.30.query_ref), channel_id=1, source_target_pairs={{0,128},{1,129},{2,130},{3,131},{4,132},{5,133},{6,134},{7,135},{8... | collective-permute-start | bytes 98312 | tf_op jit(solution)/shard_map/ppermute | solution.py:70
  38.1 21.4 %collective-permute-start.1 = (bf16[128,128]{1,0:T(8,128)(2,1)S(1)}, bf16[128,128]{1,0:T(8,128)(2,1)S(1)}, u32[]{:S(2)}, u32[]{:S(2)}) collective-permute-start(bf16[128,128]{1,0:T(8,128)(2,1)S(1)} %reshape.30.query_ref), channel_id=1, source_target_pairs={{0,256},{1,257},{2,258},{3,259},{4,260},{5,261},{6,262},{7,263},{8... | collective-permute-start | bytes 98312 | tf_op jit(solution)/shard_map/ppermute | solution.py:70
  42.5 17.0 %collective-permute-start.2 = (bf16[128,128]{1,0:T(8,128)(2,1)S(1)}, bf16[128,128]{1,0:T(8,128)(2,1)S(1)}, u32[]{:S(2)}, u32[]{:S(2)}) collective-permute-start(bf16[128,128]{1,0:T(8,128)(2,1)S(1)} %reshape.30.query_ref), channel_id=1, source_target_pairs={{0,384},{1,385},{2,386},{3,387},{4,388},{5,389},{6,390},{7,391},{8... | collective-permute-start | bytes 98312 | tf_op jit(solution)/shard_map/ppermute | solution.py:70
  45.5 40.7 %collective-permute-start.6 = (bf16[2048,384]{1,0:T(8,128)(2,1)}, bf16[2048,384]{1,0:T(8,128)(2,1)}, u32[]{:S(2)}, u32[]{:S(2)}) collective-permute-start(bf16[2048,384]{1,0:T(8,128)(2,1)} %param.15), channel_id=1, source_target_pairs={{0,1},{1,0},{2,3},{3,2},{4,5},{5,4},{6,7},{7,6},{8,9},{9,8},{10,11... | collective-permute-start | bytes 4718600 | tf_op jit(solution)/shard_map/ppermute | solution.py:70
  49.0 35.9 %collective-permute-start.7 = (bf16[192,2048]{1,0:T(8,128)(2,1)S(1)}, bf16[192,2048]{1,0:T(8,128)(2,1)S(1)}, u32[]{:S(2)}, u32[]{:S(2)}) collective-permute-start(bf16[192,2048]{1,0:T(8,128)(2,1)S(1)} %copy-done.4), channel_id=1, source_target_pairs={{0,1},{1,0},{2,3},{3,2},{4,5},{5,4},{6,7},{7,6},{8,9},{9,8},{10,11... | collective-permute-start | bytes 2359304 | tf_op jit(solution)/shard_map/ppermute | solution.py:70
  59.6 11.6 %collective-permute-start.3 = (bf16[512,128]{1,0:T(8,128)(2,1)S(1)}, bf16[512,128]{1,0:T(8,128)(2,1)S(1)}, u32[]{:S(2)}, u32[]{:S(2)}) collective-permute-start(bf16[512,128]{1,0:T(8,128)(2,1)S(1)} %get-tuple-element.29), channel_id=1, source_target_pairs={{0,32},{1,33},{2,34},{3,35},{4,36},{5,37},{6,38},{7,39},{8,40},{9,... | collective-permute-start | bytes 393224 | tf_op jit(solution)/shard_map/ppermute | solution.py:70
  65.0 9.9 %collective-permute-start.4 = (bf16[512,128]{1,0:T(8,128)(2,1)S(1)}, bf16[512,128]{1,0:T(8,128)(2,1)S(1)}, u32[]{:S(2)}, u32[]{:S(2)}) collective-permute-start(bf16[512,128]{1,0:T(8,128)(2,1)S(1)} %get-tuple-element.29), channel_id=1, source_target_pairs={{0,64},{1,65},{2,66},{3,67},{4,68},{5,69},{6,70},{7,71},{8,72},{9,... | collective-permute-start | bytes 393224 | tf_op jit(solution)/shard_map/ppermute | solution.py:70
  69.2 7.5 %collective-permute-start.5 = (bf16[512,128]{1,0:T(8,128)(2,1)S(1)}, bf16[512,128]{1,0:T(8,128)(2,1)S(1)}, u32[]{:S(2)}, u32[]{:S(2)}) collective-permute-start(bf16[512,128]{1,0:T(8,128)(2,1)S(1)} %get-tuple-element.29), channel_id=1, source_target_pairs={{0,96},{1,97},{2,98},{3,99},{4,100},{5,101},{6,102},{7,103},{8,104... | collective-permute-start | bytes 393224 | tf_op jit(solution)/shard_map/ppermute | solution.py:70
  76.8 0.8 copy-start.5
  91.1 1.3 copy-start
  100.3 12.6 %copy-start.2 = (bf16[16,144,128]{2,1,0:T(8,128)(2,1)S(1)}, bf16[16,144,128]{2,1,0:T(8,128)(2,1)}, u32[]{:S(2)}) copy-start(bf16[16,144,128]{2,1,0:T(8,128)(2,1)} %partial_attention.1) | copy-start | bytes 1769476
  100.3 49.8 %all-to-all-start.2 = ((bf16[32,16,2048]{2,1,0:T(8,128)(2,1)}), bf16[32,16,2048]{2,1,0:T(8,128)(2,1)S(1)}, u32[]{:S(2)}, u32[]{:S(2)}) async-start(bf16[32,16,2048]{2,1,0:T(8,128)(2,1)} %bitcast.6), calls=%async_computation.2 | async-start | bytes 4194304 | tf_op jit(solution)/shard_map/all_to_all | solution.py:60
  113.0 27.3 %collective-permute-start.8 = (bf16[4,144,128]{2,1,0:T(8,128)(2,1)S(1)}, bf16[4,144,128]{2,1,0:T(8,128)(2,1)S(1)}, u32[]{:S(2)}, u32[]{:S(2)}) collective-permute-start(bf16[4,144,128]{2,1,0:T(8,128)(2,1)S(1)} %get-tuple-element.14), channel_id=1, source_target_pairs={{0,32},{1,33},{2,34},{3,35},{4,36},{5,37},{6,38},{7,39},{8,40},{9,... | collective-permute-start | bytes 442376 | tf_op jit(solution)/shard_map/ppermute | solution.py:70
  115.1 45.2 %collective-permute-start.9 = (bf16[4,144,128]{2,1,0:T(8,128)(2,1)S(1)}, bf16[4,144,128]{2,1,0:T(8,128)(2,1)S(1)}, u32[]{:S(2)}, u32[]{:S(2)}) collective-permute-start(bf16[4,144,128]{2,1,0:T(8,128)(2,1)S(1)} %get-tuple-element.16), channel_id=1, source_target_pairs={{0,64},{1,65},{2,66},{3,67},{4,68},{5,69},{6,70},{7,71},{8,72},{9,... | collective-permute-start | bytes 442376 | tf_op jit(solution)/shard_map/ppermute | solution.py:70
  118.3 42.1 %collective-permute-start.10 = (bf16[4,144,128]{2,1,0:T(8,128)(2,1)S(1)}, bf16[4,144,128]{2,1,0:T(8,128)(2,1)S(1)}, u32[]{:S(2)}, u32[]{:S(2)}) collective-permute-start(bf16[4,144,128]{2,1,0:T(8,128)(2,1)S(1)} %get-tuple-element.15), channel_id=1, source_target_pairs={{0,96},{1,97},{2,98},{3,99},{4,100},{5,101},{6,102},{7,103},{8,104... | collective-permute-start | bytes 442376 | tf_op jit(solution)/shard_map/ppermute | solution.py:70
  150.1 1.4 copy-start.1
  154.6 23.6 %all-to-all-start.3 = ((bf16[8,16,2048]{2,1,0:T(8,128)(2,1)}), bf16[8,16,2048]{2,1,0:T(8,128)(2,1)S(1)}, u32[]{:S(2)}, u32[]{:S(2)}) async-start(bf16[8,16,2048]{2,1,0:T(8,128)(2,1)} %combine.1), calls=%async_computation.3 | async-start | bytes 1048576 | tf_op jit(solution)/shard_map/all_to_all | solution.py:60
  160.4 8.7 %collective-permute-start.13 = (bf16[4,144,128]{2,1,0:T(8,128)(2,1)S(1)}, bf16[4,144,128]{2,1,0:T(8,128)(2,1)S(1)}, u32[]{:S(2)}, u32[]{:S(2)}) collective-permute-start(bf16[4,144,128]{2,1,0:T(8,128)(2,1)S(1)} %pad_maximum_fusion.6), channel_id=1, source_target_pairs={{0,384},{1,385},{2,386},{3,387},{4,388},{5,389},{6,390},{7,391},{8... | collective-permute-start | bytes 442376 | tf_op jit(solution)/shard_map/ppermute | solution.py:70
  162.4 7.4 %collective-permute-start.12 = (bf16[4,144,128]{2,1,0:T(8,128)(2,1)S(1)}, bf16[4,144,128]{2,1,0:T(8,128)(2,1)S(1)}, u32[]{:S(2)}, u32[]{:S(2)}) collective-permute-start(bf16[4,144,128]{2,1,0:T(8,128)(2,1)S(1)} %pad_maximum_fusion.5), channel_id=1, source_target_pairs={{0,256},{1,257},{2,258},{3,259},{4,260},{5,261},{6,262},{7,263},{8... | collective-permute-start | bytes 442376 | tf_op jit(solution)/shard_map/ppermute | solution.py:70
  166.5 7.1 %collective-permute-start.11 = (bf16[4,144,128]{2,1,0:T(8,128)(2,1)S(1)}, bf16[4,144,128]{2,1,0:T(8,128)(2,1)S(1)}, u32[]{:S(2)}, u32[]{:S(2)}) collective-permute-start(bf16[4,144,128]{2,1,0:T(8,128)(2,1)S(1)} %pad_maximum_fusion.4), channel_id=1, source_target_pairs={{0,128},{1,129},{2,130},{3,131},{4,132},{5,133},{6,134},{7,135},{8... | collective-permute-start | bytes 442376 | tf_op jit(solution)/shard_map/ppermute | solution.py:70
  169.1 4.5 %copy-start.7 = (bf16[4,144,128]{2,1,0:T(8,128)(2,1)}, bf16[4,144,128]{2,1,0:T(8,128)(2,1)S(1)}, u32[]{:S(2)}) copy-start(bf16[4,144,128]{2,1,0:T(8,128)(2,1)S(1)} %collective-permute-done.13.got3_ref) | copy-start | bytes 442372
  169.8 3.8 %copy-start.8 = (bf16[4,144,128]{2,1,0:T(8,128)(2,1)}, bf16[4,144,128]{2,1,0:T(8,128)(2,1)S(1)}, u32[]{:S(2)}) copy-start(bf16[4,144,128]{2,1,0:T(8,128)(2,1)S(1)} %collective-permute-done.12.got2_ref) | copy-start | bytes 442372
  173.6 0.7 copy-start.9
  178.2 0.8 copy-start.3

commit v3 on v2

--- a/solution.py
+++ b/solution.py
@@ -177,29 +177,32 @@
     out_ref[...] = jnp.sum(parts_ref[...].astype(F32), axis=0).astype(BF16)
 
 
-ROW_STEP = 128
-
-
-def expert_kernel(rows_ref, gate_ref, up_ref, down_ref, out_ref):
+ROW_STEP = 256
+
+
+def expert_kernel(rows_ref, gate_up_ref, other_gate_up_ref, down_ref, other_down_ref, out_ref):
     x = rows_ref[...]
-    gate = jnp.dot(x, gate_ref[...], preferred_element_type=F32)
-    up = jnp.dot(x, up_ref[...], preferred_element_type=F32)
-    act = (gate / (1.0 + jnp.exp(-gate)) * up).astype(BF16)
-    out_ref[...] = jnp.dot(act, down_ref[...], preferred_element_type=F32).astype(BF16)
-
-
-def expert(rows, gate, up, down):
+    total = jnp.zeros((ROW_STEP, D), F32)
+    for both_ref, back_ref in ((gate_up_ref, down_ref), (other_gate_up_ref, other_down_ref)):
+        both = jnp.dot(x, both_ref[...], preferred_element_type=F32)
+        gate, up = both[:, :HALF], both[:, HALF:]
+        act = (gate / (1.0 + jnp.exp(-gate)) * up).astype(BF16)
+        total = total + jnp.dot(act, back_ref[...], preferred_element_type=F32)
+    out_ref[...] = total.astype(BF16)
+
+
+def expert(rows, *weights):
     step = pl.BlockSpec((ROW_STEP, D), lambda i: (i, 0))
-    fixed = [pl.BlockSpec(w.shape, lambda i: (0, 0)) for w in (gate, up, down)]
+    fixed = [pl.BlockSpec(w.shape, lambda i: (0, 0)) for w in weights]
     return call(
         expert_kernel,
         "expert",
         shape(rows.shape),
-        4,
+        5,
         grid=(rows.shape[0] // ROW_STEP,),
         in_specs=[step] + fixed,
         out_specs=step,
-    )(rows, gate, up, down)
+    )(rows, *weights)
 
 
 def partial_kernel(owner_ref, count_ref, query_ref, pool_ref, send_ref, top_ref, sum_ref, acc_ref):
@@ -288,6 +291,7 @@
             axis=0,
         )
 
+    answers = []
     for i in range(REQUESTS):
         query = query_ref[i * HEADS : (i + 1) * HEADS, :].astype(F32)
         key = by_head(new_ref[i : i + 1, :KV].astype(F32))
@@ -309,25 +313,30 @@
             factor = jnp.exp(top - best)
             total = total + factor * part
             mixed = mixed + factor * ref[r, i * HEADS : (i + 1) * HEADS, :].astype(F32)
-        out_ref[i * HEADS : (i + 1) * HEADS, :] = (mixed / total).astype(BF16)
-
-
-def ask(queries, pool, owner, count):
+        answers.append(mixed / total)
+    for h in range(HEADS):
+        pair = jnp.concatenate([part[h : h + 1] for part in answers], axis=0)
+        out_ref[:, h * HEAD : (h + 1) * HEAD] = pair.astype(BF16)
+
+
+def queries_in_line(queries):
     own = queries.reshape(REQUESTS * HEADS, HEAD)
-    line = jnp.concatenate([own] + [moved(own, dx=k) for k in range(1, SIDE)], axis=0)
+    return jnp.concatenate([own] + [moved(own, dx=k) for k in range(1, SIDE)], axis=0)
+
+
+def partials_of(line, pool, owner, count):
     square = jnp.concatenate([line] + [moved(line, dz=k) for k in range(1, SIDE)], axis=0)
-    return own, partial_attention(owner, count, square, pool)
-
-
-def answer(own, partials, incoming):
-    partials = partials.reshape(SIDE, SIDE, MESSAGE, HEAD)
+    return partial_attention(owner, count, square, pool).reshape(SIDE, SIDE, MESSAGE, HEAD)
+
+
+def partials_by_column(partials):
     columns = [partials[0]] + [moved(partials[k], dz=k) for k in range(1, SIDE)]
-    got = []
-    for k in range(SIDE):
-        piece = jnp.stack([column[k] for column in columns])
-        got.append(moved(piece, dx=k) if k else piece)
-    out = call(finish_kernel, "finish", shape((REQUESTS * HEADS, HEAD)), 6)(*got, own, incoming)
-    return out.reshape(REQUESTS, HEADS * HEAD)
+    return [jnp.stack([column[k] for column in columns]) for k in range(SIDE)]
+
+
+def finish(pieces, own, incoming):
+    got = [moved(piece, dx=k) if k else piece for k, piece in enumerate(pieces)]
+    return call(finish_kernel, "finish", shape((REQUESTS, HEADS * HEAD)), 6)(*got, own, incoming)
 
 
 def shards(
@@ -348,22 +357,26 @@
         moe_input, expert_ids.T, route_weight.T
     )
     near = exchange(packed, RING_GROUPS)
+    line = queries_in_line(queries)
+    near, line = lax.optimization_barrier((near, line))
     send = call(dispatch_kernel, "dispatch", shape((REACH, ROWS, D)), 2)(near, slot_row)
     received = exchange(send, REACH_GROUPS)
 
-    own, partials = ask(queries, key_value_pool, block_owner, block_tokens)
+    partials = partials_of(line, key_value_pool, block_owner, block_tokens)
     other_gate_up, other_down = moved(w_gate_up, dc=1), moved(w_down, dc=1)
-    gate = jnp.concatenate([w_gate_up[:, :HALF], other_gate_up[:, :HALF]], axis=1)
-    up = jnp.concatenate([w_gate_up[:, HALF:], other_gate_up[:, HALF:]], axis=1)
-    down = jnp.concatenate([w_down, other_down], axis=0)
     received, partials = lax.optimization_barrier((received, partials))
 
-    rows = expert(received.reshape(REACH * ROWS, D), gate, up, down)
+    rows = expert(
+        received.reshape(REACH * ROWS, D), w_gate_up, other_gate_up, w_down, other_down
+    )
     returned = exchange(rows.reshape(REACH, ROWS, D), REACH_GROUPS)
-    attn_out = answer(own, partials, incoming_key_value)
     mix = call(mixing_kernel, "mixing", shape((2 * NEAR, REACH * ROWS)), 2)(near, slot_row)
+    pieces = partials_by_column(partials)
+    returned, pieces = lax.optimization_barrier((returned, pieces))
+
     parts = call(combine_kernel, "combine", shape((RING, TOK, D)), 2)(mix, returned)
     parts = exchange(parts, RING_GROUPS)
+    attn_out = finish(pieces, line[: REQUESTS * HEADS], incoming_key_value)
     moe_out = call(total_kernel, "total", shape((TOK, D)), 1)(parts)
     return (moe_out, attn_out)
 

time: 182 us -> 172 us (0.945)
  the two profiles are of different devices: /device:TPU:201 before, /device:TPU:1 now
where the time goes in v3:
time: 172 us; the launch traced here: 171 us
  starting transfers between devices  78.8 us (46%)
  waiting for transfers between devices  53.7 us (31%)
  Pallas kernels  29.9 us (17%)
  local copies, waits for them, and re-layouts  6.43 us (4%)
    ppermute x14, waiting for transfers between devices, moved(): return lax.ppermute(array, AXIS, pairs)  53.7 us
    ppermute x14, starting transfers between devices, moved(): return lax.ppermute(array, AXIS, pairs)  43.9 us
    all_to_all x4, starting transfers between devices, exchange(): lax.all_to_all(array, AXIS, split_axis=0, concat_axis=0, axis_index_group...  34.9 us
    pallas_call x1, Pallas kernels, expert(): call(expert_kernel, 'expert', shape(rows.shape), 5, grid=(rows.shape[0] /...  7.54 us
    pallas_call x1, Pallas kernels, partial_attention(): call(partial_kernel, 'partial_attention', shape((SIDE * SIDE, MESSAGE, HE...  7.33 us
    unnamed x18, local copies, waits for them, and re-layouts  4.95 us
  transfers between devices with their start and end apart: 18, of which 8 were waited for; matrix products, arithmetic and copies ran while one was open for 2% of the time, Pallas kernels for 7%

profile of v3, /device:TPU:1, one launch (start us, length us, event | category | flops | bytes accessed | tf_op | source)
XLA Modules:
  0.0 171.2 jit_solution(5544097315322572674)
XLA Ops:
  0.6 1.8 %pack.1 = bf16[8,16,2304]{2,1,0:T(8,128)(2,1)} custom-call(bf16[16,2048]{1,0:T(8,128)(2,1)} %token_ref.1, s32[8,16]{1,0:T(8,128)} %bitcast.24, f32[8,16]{1,0:T(8,128)} %bitcast.25), custom_call_target="tpu_custom_call" | custom-call | tf_op jit(solution)/shard_map/pack/pallas_call | solution.py:356
  2.4 7.7 %all-to-all-start = ((bf16[8,16,2304]{2,1,0:T(8,128)(2,1)}), bf16[8,16,2304]{2,1,0:T(8,128)(2,1)S(1)}, u32[]{:S(2)}, u32[]{:S(2)}) async-start(bf16[8,16,2304]{2,1,0:T(8,128)(2,1)} %pack.1), calls=%async_computation | async-start | bytes 1179648 | tf_op jit(solution)/shard_map/all_to_all | solution.py:60
  10.9 4.4 %collective-permute-start.2 = (bf16[128,128]{1,0:T(8,128)(2,1)S(1)}, bf16[128,128]{1,0:T(8,128)(2,1)S(1)}, u32[]{:S(2)}, u32[]{:S(2)}) collective-permute-start(bf16[128,128]{1,0:T(8,128)(2,1)S(1)} %reshape.23), channel_id=1, source_target_pairs={{0,384},{1,385},{2,386},{3,387},{4,388},{5,389},{6,390},{7,391},{8... | collective-permute-start | bytes 98312 | tf_op jit(solution)/shard_map/ppermute | solution.py:70
  15.3 2.4 %collective-permute-start.1 = (bf16[128,128]{1,0:T(8,128)(2,1)S(1)}, bf16[128,128]{1,0:T(8,128)(2,1)S(1)}, u32[]{:S(2)}, u32[]{:S(2)}) collective-permute-start(bf16[128,128]{1,0:T(8,128)(2,1)S(1)} %reshape.23), channel_id=1, source_target_pairs={{0,256},{1,257},{2,258},{3,259},{4,260},{5,261},{6,262},{7,263},{8... | collective-permute-start | bytes 98312 | tf_op jit(solution)/shard_map/ppermute | solution.py:70
  17.7 2.5 %collective-permute-start = (bf16[128,128]{1,0:T(8,128)(2,1)S(1)}, bf16[128,128]{1,0:T(8,128)(2,1)S(1)}, u32[]{:S(2)}, u32[]{:S(2)}) collective-permute-start(bf16[128,128]{1,0:T(8,128)(2,1)S(1)} %reshape.23), channel_id=1, source_target_pairs={{0,128},{1,129},{2,130},{3,131},{4,132},{5,133},{6,134},{7,135},{8... | collective-permute-start | bytes 98312 | tf_op jit(solution)/shard_map/ppermute | solution.py:70
  21.7 2.0 %collective-permute-done = bf16[128,128]{1,0:T(8,128)(2,1)S(1)} collective-permute-done((bf16[128,128]{1,0:T(8,128)(2,1)S(1)}, bf16[128,128]{1,0:T(8,128)(2,1)S(1)}, u32[]{:S(2)}, u32[]{:S(2)}) %collective-permute-start) | collective-permute-done | bytes 32800 | tf_op jit(solution)/shard_map/ppermute | solution.py:70
  24.6 3.4 %dispatch.1 = bf16[32,16,2048]{2,1,0:T(8,128)(2,1)} custom-call(bf16[8,16,2304]{2,1,0:T(8,128)(2,1)} %copy-done.2, s32[1,128]{1,0:T(1,128)} %bitcast.26), custom_call_target="tpu_custom_call" | custom-call | tf_op jit(solution)/shard_map/dispatch/pallas_call | solution.py:362
  28.0 12.2 %all-to-all-start.1 = ((bf16[32,16,2048]{2,1,0:T(8,128)(2,1)}), bf16[32,16,2048]{2,1,0:T(8,128)(2,1)S(1)}, u32[]{:S(2)}, u32[]{:S(2)}) async-start(bf16[32,16,2048]{2,1,0:T(8,128)(2,1)} %dispatch.1), calls=%async_computation.1 | async-start | bytes 4194304 | tf_op jit(solution)/shard_map/all_to_all | solution.py:60
  40.2 4.3 %collective-permute-start.6 = (bf16[2048,384]{1,0:T(8,128)(2,1)}, bf16[2048,384]{1,0:T(8,128)(2,1)}, u32[]{:S(2)}, u32[]{:S(2)}) collective-permute-start(bf16[2048,384]{1,0:T(8,128)(2,1)} %gate_up_ref.1), channel_id=1, source_target_pairs={{0,1},{1,0},{2,3},{3,2},{4,5},{5,4},{6,7},{7,6},{8,9},{9,8},{10,11... | collective-permute-start | bytes 4718600 | tf_op jit(solution)/shard_map/ppermute | solution.py:70
  44.5 1.9 %collective-permute-start.7 = (bf16[192,2048]{1,0:T(8,128)(2,1)S(1)}, bf16[192,2048]{1,0:T(8,128)(2,1)}, u32[]{:S(2)}, u32[]{:S(2)}) collective-permute-start(bf16[192,2048]{1,0:T(8,128)(2,1)S(1)} %copy-done.5), channel_id=1, source_target_pairs={{0,1},{1,0},{2,3},{3,2},{4,5},{5,4},{6,7},{7,6},{8,9},{9,8},{10,11... | collective-permute-start | bytes 2359304 | tf_op jit(solution)/shard_map/ppermute | solution.py:70
  46.4 5.2 %collective-permute-start.5 = (bf16[512,128]{1,0:T(8,128)(2,1)S(1)}, bf16[512,128]{1,0:T(8,128)(2,1)S(1)}, u32[]{:S(2)}, u32[]{:S(2)}) collective-permute-start(bf16[512,128]{1,0:T(8,128)(2,1)S(1)} %pad_maximum_fusion.5), channel_id=1, source_target_pairs={{0,96},{1,97},{2,98},{3,99},{4,100},{5,101},{6,102},{7,103},{8,104... | collective-permute-start | bytes 393224 | tf_op jit(solution)/shard_map/ppermute | solution.py:70
  51.6 1.9 %collective-permute-start.4 = (bf16[512,128]{1,0:T(8,128)(2,1)S(1)}, bf16[512,128]{1,0:T(8,128)(2,1)S(1)}, u32[]{:S(2)}, u32[]{:S(2)}) collective-permute-start(bf16[512,128]{1,0:T(8,128)(2,1)S(1)} %pad_maximum_fusion.5), channel_id=1, source_target_pairs={{0,64},{1,65},{2,66},{3,67},{4,68},{5,69},{6,70},{7,71},{8,72},{9,... | collective-permute-start | bytes 393224 | tf_op jit(solution)/shard_map/ppermute | solution.py:70
  53.5 2.5 %collective-permute-start.3 = (bf16[512,128]{1,0:T(8,128)(2,1)S(1)}, bf16[512,128]{1,0:T(8,128)(2,1)S(1)}, u32[]{:S(2)}, u32[]{:S(2)}) collective-permute-start(bf16[512,128]{1,0:T(8,128)(2,1)S(1)} %pad_maximum_fusion.5), channel_id=1, source_target_pairs={{0,32},{1,33},{2,34},{3,35},{4,36},{5,37},{6,38},{7,39},{8,40},{9,... | collective-permute-start | bytes 393224 | tf_op jit(solution)/shard_map/ppermute | solution.py:70
  56.0 12.3 %collective-permute-done.5 = bf16[512,128]{1,0:T(8,128)(2,1)S(1)} collective-permute-done((bf16[512,128]{1,0:T(8,128)(2,1)S(1)}, bf16[512,128]{1,0:T(8,128)(2,1)S(1)}, u32[]{:S(2)}, u32[]{:S(2)}) %collective-permute-start.5) | collective-permute-done | bytes 131104 | tf_op jit(solution)/shard_map/ppermute | solution.py:70
  68.3 8.9 %collective-permute-done.4 = bf16[512,128]{1,0:T(8,128)(2,1)S(1)} collective-permute-done((bf16[512,128]{1,0:T(8,128)(2,1)S(1)}, bf16[512,128]{1,0:T(8,128)(2,1)S(1)}, u32[]{:S(2)}, u32[]{:S(2)}) %collective-permute-start.4) | collective-permute-done | bytes 131104 | tf_op jit(solution)/shard_map/ppermute | solution.py:70
  78.0 7.3 %partial_attention.1 = bf16[16,144,128]{2,1,0:T(8,128)(2,1)} custom-call(s32[16]{0:T(128)} %owner_ref.1, s32[16]{0:T(128)} %count_ref.1, bf16[2048,128]{1,0:T(8,128)(2,1)} %pad_maximum_fusion.query_ref, bf16[16,64,1024]{2,1,0:T(8,128)(2,1)} %pool_ref.1), custom_call_target="tpu_custom_call" | custom-call | tf_op jit(solution)/shard_map/partial_attention/pallas_call | solution.py:269
  86.7 7.5 %expert.1 = bf16[512,2048]{1,0:T(8,128)(2,1)} custom-call(bf16[512,2048]{1,0:T(8,128)(2,1)} %bitcast.21, bf16[2048,384]{1,0:T(8,128)(2,1)} %gate_up_ref.1, bf16[2048,384]{1,0:T(8,128)(2,1)} %collective-permute-done.6.other_gate_up_ref, bf16[192,2048]{1,0:T(8,128)(2,1)} %down_ref.1, bf16[192,2048]{1,0:T(8,128)(2,1)} %collective-permute-done.7.other_down_ref), custom_call_target="tpu_custom_call" | custom-call | tf_op jit(solution)/shard_map/expert/pallas_call | solution.py:197
  94.2 8.2 %all-to-all-start.2 = ((bf16[32,16,2048]{2,1,0:T(8,128)(2,1)}), bf16[32,16,2048]{2,1,0:T(8,128)(2,1)S(1)}, u32[]{:S(2)}, u32[]{:S(2)}) async-start(bf16[32,16,2048]{2,1,0:T(8,128)(2,1)} %bitcast.20), calls=%async_computation.2 | async-start | bytes 4194304 | tf_op jit(solution)/shard_map/all_to_all | solution.py:60
  102.4 2.3 %mixing.1.mix_ref = bf16[256,512]{1,0:T(8,128)(2,1)} custom-call(bf16[8,16,2304]{2,1,0:T(8,128)(2,1)} %copy-done.2, s32[1,128]{1,0:T(1,128)} %bitcast.27), custom_call_target="tpu_custom_call" | custom-call | tf_op jit(solution)/shard_map/mixing/pallas_call | solution.py:373
  104.7 3.1 %collective-permute-start.8 = (bf16[4,144,128]{2,1,0:T(8,128)(2,1)S(1)}, bf16[4,144,128]{2,1,0:T(8,128)(2,1)S(1)}, u32[]{:S(2)}, u32[]{:S(2)}) collective-permute-start(bf16[4,144,128]{2,1,0:T(8,128)(2,1)S(1)} %get-tuple-element.24), channel_id=1, source_target_pairs={{0,32},{1,33},{2,34},{3,35},{4,36},{5,37},{6,38},{7,39},{8,40},{9,... | collective-permute-start | bytes 442376 | tf_op jit(solution)/shard_map/ppermute | solution.py:70
  107.9 3.9 %collective-permute-start.10 = (bf16[4,144,128]{2,1,0:T(8,128)(2,1)S(1)}, bf16[4,144,128]{2,1,0:T(8,128)(2,1)S(1)}, u32[]{:S(2)}, u32[]{:S(2)}) collective-permute-start(bf16[4,144,128]{2,1,0:T(8,128)(2,1)S(1)} %get-tuple-element.25), channel_id=1, source_target_pairs={{0,96},{1,97},{2,98},{3,99},{4,100},{5,101},{6,102},{7,103},{8,104... | collective-permute-start | bytes 442376 | tf_op jit(solution)/shard_map/ppermute | solution.py:70
  111.8 2.2 %collective-permute-start.9 = (bf16[4,144,128]{2,1,0:T(8,128)(2,1)S(1)}, bf16[4,144,128]{2,1,0:T(8,128)(2,1)S(1)}, u32[]{:S(2)}, u32[]{:S(2)}) collective-permute-start(bf16[4,144,128]{2,1,0:T(8,128)(2,1)S(1)} %get-tuple-element.26), channel_id=1, source_target_pairs={{0,64},{1,65},{2,66},{3,67},{4,68},{5,69},{6,70},{7,71},{8,72},{9,... | collective-permute-start | bytes 442376 | tf_op jit(solution)/shard_map/ppermute | solution.py:70
  114.1 20.0 %collective-permute-done.8 = bf16[4,144,128]{2,1,0:T(8,128)(2,1)S(1)} collective-permute-done((bf16[4,144,128]{2,1,0:T(8,128)(2,1)S(1)}, bf16[4,144,128]{2,1,0:T(8,128)(2,1)S(1)}, u32[]{:S(2)}, u32[]{:S(2)}) %collective-permute-start.8) | collective-permute-done | bytes 147488 | tf_op jit(solution)/shard_map/ppermute | solution.py:70
  134.1 6.1 %collective-permute-done.9 = bf16[4,144,128]{2,1,0:T(8,128)(2,1)S(1)} collective-permute-done((bf16[4,144,128]{2,1,0:T(8,128)(2,1)S(1)}, bf16[4,144,128]{2,1,0:T(8,128)(2,1)S(1)}, u32[]{:S(2)}, u32[]{:S(2)}) %collective-permute-start.9) | collective-permute-done | bytes 147488 | tf_op jit(solution)/shard_map/ppermute | solution.py:70
  142.4 3.2 %combine.1 = bf16[8,16,2048]{2,1,0:T(8,128)(2,1)} custom-call(bf16[256,512]{1,0:T(8,128)(2,1)} %mixing.1.mix_ref, bf16[32,16,2048]{2,1,0:T(8,128)(2,1)} %copy-done.1), custom_call_target="tpu_custom_call" | custom-call | tf_op jit(solution)/shard_map/combine/pallas_call | solution.py:377
  145.6 6.8 %all-to-all-start.3 = ((bf16[8,16,2048]{2,1,0:T(8,128)(2,1)}), bf16[8,16,2048]{2,1,0:T(8,128)(2,1)S(1)}, u32[]{:S(2)}, u32[]{:S(2)}) async-start(bf16[8,16,2048]{2,1,0:T(8,128)(2,1)} %combine.1), calls=%async_computation.3 | async-start | bytes 1048576 | tf_op jit(solution)/shard_map/all_to_all | solution.py:60
  152.4 2.8 %collective-permute-start.11 = (bf16[4,144,128]{2,1,0:T(8,128)(2,1)S(1)}, bf16[4,144,128]{2,1,0:T(8,128)(2,1)S(1)}, u32[]{:S(2)}, u32[]{:S(2)}) collective-permute-start(bf16[4,144,128]{2,1,0:T(8,128)(2,1)S(1)} %get-tuple-element.17), channel_id=1, source_target_pairs={{0,128},{1,129},{2,130},{3,131},{4,132},{5,133},{6,134},{7,135},{8... | collective-permute-start | bytes 442376 | tf_op jit(solution)/shard_map/ppermute | solution.py:70
  155.2 4.3 %collective-permute-start.12 = (bf16[4,144,128]{2,1,0:T(8,128)(2,1)S(1)}, bf16[4,144,128]{2,1,0:T(8,128)(2,1)S(1)}, u32[]{:S(2)}, u32[]{:S(2)}) collective-permute-start(bf16[4,144,128]{2,1,0:T(8,128)(2,1)S(1)} %get-tuple-element.18), channel_id=1, source_target_pairs={{0,256},{1,257},{2,258},{3,259},{4,260},{5,261},{6,262},{7,263},{8... | collective-permute-start | bytes 442376 | tf_op jit(solution)/shard_map/ppermute | solution.py:70
  159.5 2.4 %collective-permute-start.13 = (bf16[4,144,128]{2,1,0:T(8,128)(2,1)S(1)}, bf16[4,144,128]{2,1,0:T(8,128)(2,1)S(1)}, u32[]{:S(2)}, u32[]{:S(2)}) collective-permute-start(bf16[4,144,128]{2,1,0:T(8,128)(2,1)S(1)} %get-tuple-element.19), channel_id=1, source_target_pairs={{0,384},{1,385},{2,386},{3,387},{4,388},{5,389},{6,390},{7,391},{8... | collective-permute-start | bytes 442376 | tf_op jit(solution)/shard_map/ppermute | solution.py:70
  162.6 2.8 %collective-permute-done.13.got3_ref = bf16[4,144,128]{2,1,0:T(8,128)(2,1)S(1)} collective-permute-done((bf16[4,144,128]{2,1,0:T(8,128)(2,1)S(1)}, bf16[4,144,128]{2,1,0:T(8,128)(2,1)S(1)}, u32[]{:S(2)}, u32[]{:S(2)}) %collective-permute-start.13) | collective-permute-done | bytes 147488 | tf_op jit(solution)/shard_map/ppermute | solution.py:70
  166.1 2.6 %finish.1 = bf16[2,8192]{1,0:T(2,128)(2,1)} custom-call(bf16[4,144,128]{2,1,0:T(8,128)(2,1)} %get-tuple-element.16.got0_ref, bf16[4,144,128]{2,1,0:T(8,128)(2,1)} %copy-done.6, bf16[4,144,128]{2,1,0:T(8,128)(2,1)} %copy-done.7, bf16[4,144,128]{2,1,0:T(8,128)(2,1)} %copy-done.8, bf16[128,128]{1,0:T(8,128)(2,1)} %slice.100.query_ref, bf16[2,1024]{1,0:T(2,128)(2,1)} %new_ref.1), custom_call_target="tpu_custom_call" | custom-call | tf_op jit(solution)/shard_map/finish/pallas_call | solution.py:339
  169.5 1.7 %total.1 = bf16[16,2048]{1,0:T(8,128)(2,1)} custom-call(bf16[8,16,2048]{2,1,0:T(8,128)(2,1)} %copy-done.4), custom_call_target="tpu_custom_call" | custom-call | tf_op jit(solution)/shard_map/total/pallas_call | solution.py:380
  (41 shorter events, 9.6 us)
Async XLA Ops:
  2.4 21.3 %all-to-all-start = ((bf16[8,16,2304]{2,1,0:T(8,128)(2,1)}), bf16[8,16,2304]{2,1,0:T(8,128)(2,1)S(1)}, u32[]{:S(2)}, u32[]{:S(2)}) async-start(bf16[8,16,2304]{2,1,0:T(8,128)(2,1)} %pack.1), calls=%async_computation | async-start | bytes 1179648 | tf_op jit(solution)/shard_map/all_to_all | solution.py:60
  10.9 9.4 %collective-permute-start.2 = (bf16[128,128]{1,0:T(8,128)(2,1)S(1)}, bf16[128,128]{1,0:T(8,128)(2,1)S(1)}, u32[]{:S(2)}, u32[]{:S(2)}) collective-permute-start(bf16[128,128]{1,0:T(8,128)(2,1)S(1)} %reshape.23), channel_id=1, source_target_pairs={{0,384},{1,385},{2,386},{3,387},{4,388},{5,389},{6,390},{7,391},{8... | collective-permute-start | bytes 98312 | tf_op jit(solution)/shard_map/ppermute | solution.py:70
  15.3 6.5 %collective-permute-start.1 = (bf16[128,128]{1,0:T(8,128)(2,1)S(1)}, bf16[128,128]{1,0:T(8,128)(2,1)S(1)}, u32[]{:S(2)}, u32[]{:S(2)}) collective-permute-start(bf16[128,128]{1,0:T(8,128)(2,1)S(1)} %reshape.23), channel_id=1, source_target_pairs={{0,256},{1,257},{2,258},{3,259},{4,260},{5,261},{6,262},{7,263},{8... | collective-permute-start | bytes 98312 | tf_op jit(solution)/shard_map/ppermute | solution.py:70
  17.7 6.0 %collective-permute-start = (bf16[128,128]{1,0:T(8,128)(2,1)S(1)}, bf16[128,128]{1,0:T(8,128)(2,1)S(1)}, u32[]{:S(2)}, u32[]{:S(2)}) collective-permute-start(bf16[128,128]{1,0:T(8,128)(2,1)S(1)} %reshape.23), channel_id=1, source_target_pairs={{0,128},{1,129},{2,130},{3,131},{4,132},{5,133},{6,134},{7,135},{8... | collective-permute-start | bytes 98312 | tf_op jit(solution)/shard_map/ppermute | solution.py:70
  23.8 0.8 copy-start.2
  28.0 16.5 %copy-start.5 = (bf16[192,2048]{1,0:T(8,128)(2,1)S(1)}, bf16[192,2048]{1,0:T(8,128)(2,1)}, u32[]{:S(2)}) copy-start(bf16[192,2048]{1,0:T(8,128)(2,1)} %down_ref.1) | copy-start | bytes 2359300
  28.0 57.4 %all-to-all-start.1 = ((bf16[32,16,2048]{2,1,0:T(8,128)(2,1)}), bf16[32,16,2048]{2,1,0:T(8,128)(2,1)S(1)}, u32[]{:S(2)}, u32[]{:S(2)}) async-start(bf16[32,16,2048]{2,1,0:T(8,128)(2,1)} %dispatch.1), calls=%async_computation.1 | async-start | bytes 4194304 | tf_op jit(solution)/shard_map/all_to_all | solution.py:60
  40.2 45.2 %collective-permute-start.6 = (bf16[2048,384]{1,0:T(8,128)(2,1)}, bf16[2048,384]{1,0:T(8,128)(2,1)}, u32[]{:S(2)}, u32[]{:S(2)}) collective-permute-start(bf16[2048,384]{1,0:T(8,128)(2,1)} %gate_up_ref.1), channel_id=1, source_target_pairs={{0,1},{1,0},{2,3},{3,2},{4,5},{5,4},{6,7},{7,6},{8,9},{9,8},{10,11... | collective-permute-start | bytes 4718600 | tf_op jit(solution)/shard_map/ppermute | solution.py:70
  44.5 40.9 %collective-permute-start.7 = (bf16[192,2048]{1,0:T(8,128)(2,1)S(1)}, bf16[192,2048]{1,0:T(8,128)(2,1)}, u32[]{:S(2)}, u32[]{:S(2)}) collective-permute-start(bf16[192,2048]{1,0:T(8,128)(2,1)S(1)} %copy-done.5), channel_id=1, source_target_pairs={{0,1},{1,0},{2,3},{3,2},{4,5},{5,4},{6,7},{7,6},{8,9},{9,8},{10,11... | collective-permute-start | bytes 2359304 | tf_op jit(solution)/shard_map/ppermute | solution.py:70
  46.4 21.9 %collective-permute-start.5 = (bf16[512,128]{1,0:T(8,128)(2,1)S(1)}, bf16[512,128]{1,0:T(8,128)(2,1)S(1)}, u32[]{:S(2)}, u32[]{:S(2)}) collective-permute-start(bf16[512,128]{1,0:T(8,128)(2,1)S(1)} %pad_maximum_fusion.5), channel_id=1, source_target_pairs={{0,96},{1,97},{2,98},{3,99},{4,100},{5,101},{6,102},{7,103},{8,104... | collective-permute-start | bytes 393224 | tf_op jit(solution)/shard_map/ppermute | solution.py:70
  51.6 25.6 %collective-permute-start.4 = (bf16[512,128]{1,0:T(8,128)(2,1)S(1)}, bf16[512,128]{1,0:T(8,128)(2,1)S(1)}, u32[]{:S(2)}, u32[]{:S(2)}) collective-permute-start(bf16[512,128]{1,0:T(8,128)(2,1)S(1)} %pad_maximum_fusion.5), channel_id=1, source_target_pairs={{0,64},{1,65},{2,66},{3,67},{4,68},{5,69},{6,70},{7,71},{8,72},{9,... | collective-permute-start | bytes 393224 | tf_op jit(solution)/shard_map/ppermute | solution.py:70
  53.5 23.6 %collective-permute-start.3 = (bf16[512,128]{1,0:T(8,128)(2,1)S(1)}, bf16[512,128]{1,0:T(8,128)(2,1)S(1)}, u32[]{:S(2)}, u32[]{:S(2)}) collective-permute-start(bf16[512,128]{1,0:T(8,128)(2,1)S(1)} %pad_maximum_fusion.5), channel_id=1, source_target_pairs={{0,32},{1,33},{2,34},{3,35},{4,36},{5,37},{6,38},{7,39},{8,40},{9,... | collective-permute-start | bytes 393224 | tf_op jit(solution)/shard_map/ppermute | solution.py:70
  85.3 1.3 copy-start
  94.2 10.5 %copy-start.3 = (bf16[16,144,128]{2,1,0:T(8,128)(2,1)S(1)}, bf16[16,144,128]{2,1,0:T(8,128)(2,1)}, u32[]{:S(2)}) copy-start(bf16[16,144,128]{2,1,0:T(8,128)(2,1)} %partial_attention.1) | copy-start | bytes 1769476
  94.2 46.8 %all-to-all-start.2 = ((bf16[32,16,2048]{2,1,0:T(8,128)(2,1)}), bf16[32,16,2048]{2,1,0:T(8,128)(2,1)S(1)}, u32[]{:S(2)}, u32[]{:S(2)}) async-start(bf16[32,16,2048]{2,1,0:T(8,128)(2,1)} %bitcast.20), calls=%async_computation.2 | async-start | bytes 4194304 | tf_op jit(solution)/shard_map/all_to_all | solution.py:60
  104.7 29.4 %collective-permute-start.8 = (bf16[4,144,128]{2,1,0:T(8,128)(2,1)S(1)}, bf16[4,144,128]{2,1,0:T(8,128)(2,1)S(1)}, u32[]{:S(2)}, u32[]{:S(2)}) collective-permute-start(bf16[4,144,128]{2,1,0:T(8,128)(2,1)S(1)} %get-tuple-element.24), channel_id=1, source_target_pairs={{0,32},{1,33},{2,34},{3,35},{4,36},{5,37},{6,38},{7,39},{8,40},{9,... | collective-permute-start | bytes 442376 | tf_op jit(solution)/shard_map/ppermute | solution.py:70
  107.9 26.2 %collective-permute-start.10 = (bf16[4,144,128]{2,1,0:T(8,128)(2,1)S(1)}, bf16[4,144,128]{2,1,0:T(8,128)(2,1)S(1)}, u32[]{:S(2)}, u32[]{:S(2)}) collective-permute-start(bf16[4,144,128]{2,1,0:T(8,128)(2,1)S(1)} %get-tuple-element.25), channel_id=1, source_target_pairs={{0,96},{1,97},{2,98},{3,99},{4,100},{5,101},{6,102},{7,103},{8,104... | collective-permute-start | bytes 442376 | tf_op jit(solution)/shard_map/ppermute | solution.py:70
  111.8 28.4 %collective-permute-start.9 = (bf16[4,144,128]{2,1,0:T(8,128)(2,1)S(1)}, bf16[4,144,128]{2,1,0:T(8,128)(2,1)S(1)}, u32[]{:S(2)}, u32[]{:S(2)}) collective-permute-start(bf16[4,144,128]{2,1,0:T(8,128)(2,1)S(1)} %get-tuple-element.26), channel_id=1, source_target_pairs={{0,64},{1,65},{2,66},{3,67},{4,68},{5,69},{6,70},{7,71},{8,72},{9,... | collective-permute-start | bytes 442376 | tf_op jit(solution)/shard_map/ppermute | solution.py:70
  141.0 1.4 copy-start.1
  145.6 23.1 %all-to-all-start.3 = ((bf16[8,16,2048]{2,1,0:T(8,128)(2,1)}), bf16[8,16,2048]{2,1,0:T(8,128)(2,1)S(1)}, u32[]{:S(2)}, u32[]{:S(2)}) async-start(bf16[8,16,2048]{2,1,0:T(8,128)(2,1)} %combine.1), calls=%async_computation.3 | async-start | bytes 1048576 | tf_op jit(solution)/shard_map/all_to_all | solution.py:60
  152.4 10.1 %collective-permute-start.11 = (bf16[4,144,128]{2,1,0:T(8,128)(2,1)S(1)}, bf16[4,144,128]{2,1,0:T(8,128)(2,1)S(1)}, u32[]{:S(2)}, u32[]{:S(2)}) collective-permute-start(bf16[4,144,128]{2,1,0:T(8,128)(2,1)S(1)} %get-tuple-element.17), channel_id=1, source_target_pairs={{0,128},{1,129},{2,130},{3,131},{4,132},{5,133},{6,134},{7,135},{8... | collective-permute-start | bytes 442376 | tf_op jit(solution)/shard_map/ppermute | solution.py:70
  155.2 7.4 %collective-permute-start.12 = (bf16[4,144,128]{2,1,0:T(8,128)(2,1)S(1)}, bf16[4,144,128]{2,1,0:T(8,128)(2,1)S(1)}, u32[]{:S(2)}, u32[]{:S(2)}) collective-permute-start(bf16[4,144,128]{2,1,0:T(8,128)(2,1)S(1)} %get-tuple-element.18), channel_id=1, source_target_pairs={{0,256},{1,257},{2,258},{3,259},{4,260},{5,261},{6,262},{7,263},{8... | collective-permute-start | bytes 442376 | tf_op jit(solution)/shard_map/ppermute | solution.py:70
  159.5 5.9 %collective-permute-start.13 = (bf16[4,144,128]{2,1,0:T(8,128)(2,1)S(1)}, bf16[4,144,128]{2,1,0:T(8,128)(2,1)S(1)}, u32[]{:S(2)}, u32[]{:S(2)}) collective-permute-start(bf16[4,144,128]{2,1,0:T(8,128)(2,1)S(1)} %get-tuple-element.19), channel_id=1, source_target_pairs={{0,384},{1,385},{2,386},{3,387},{4,388},{5,389},{6,390},{7,391},{8... | collective-permute-start | bytes 442376 | tf_op jit(solution)/shard_map/ppermute | solution.py:70
  162.5 2.9 %copy-start.6 = (bf16[4,144,128]{2,1,0:T(8,128)(2,1)}, bf16[4,144,128]{2,1,0:T(8,128)(2,1)S(1)}, u32[]{:S(2)}) copy-start(bf16[4,144,128]{2,1,0:T(8,128)(2,1)S(1)} %collective-permute-done.11.got1_ref) | copy-start | bytes 442372
  162.6 2.8 %copy-start.7 = (bf16[4,144,128]{2,1,0:T(8,128)(2,1)}, bf16[4,144,128]{2,1,0:T(8,128)(2,1)S(1)}, u32[]{:S(2)}) copy-start(bf16[4,144,128]{2,1,0:T(8,128)(2,1)S(1)} %collective-permute-done.12.got2_ref) | copy-start | bytes 442372
  165.4 0.7 copy-start.8
  168.7 0.8 copy-start.4

commit v4 on v3

--- a/solution.py
+++ b/solution.py
@@ -319,24 +319,8 @@
         out_ref[:, h * HEAD : (h + 1) * HEAD] = pair.astype(BF16)
 
 
-def queries_in_line(queries):
-    own = queries.reshape(REQUESTS * HEADS, HEAD)
-    return jnp.concatenate([own] + [moved(own, dx=k) for k in range(1, SIDE)], axis=0)
-
-
-def partials_of(line, pool, owner, count):
-    square = jnp.concatenate([line] + [moved(line, dz=k) for k in range(1, SIDE)], axis=0)
-    return partial_attention(owner, count, square, pool).reshape(SIDE, SIDE, MESSAGE, HEAD)
-
-
-def partials_by_column(partials):
-    columns = [partials[0]] + [moved(partials[k], dz=k) for k in range(1, SIDE)]
-    return [jnp.stack([column[k] for column in columns]) for k in range(SIDE)]
-
-
-def finish(pieces, own, incoming):
-    got = [moved(piece, dx=k) if k else piece for k, piece in enumerate(pieces)]
-    return call(finish_kernel, "finish", shape((REQUESTS, HEADS * HEAD)), 6)(*got, own, incoming)
+def along(array, axis):
+    return [array] + [moved(array, **{axis: k}) for k in range(1, SIDE)]
 
 
 def shards(
@@ -356,27 +340,35 @@
     packed = call(pack_kernel, "pack", shape((RING, TOK, D + EXTRA)), 3)(
         moe_input, expert_ids.T, route_weight.T
     )
+    line = along(queries.reshape(REQUESTS * HEADS, HEAD), "dx")
+    packed, line[1] = lax.optimization_barrier((packed, line[1]))
     near = exchange(packed, RING_GROUPS)
-    line = queries_in_line(queries)
-    near, line = lax.optimization_barrier((near, line))
+    square = along(jnp.concatenate(line, axis=0), "dz")
+    near, square = lax.optimization_barrier((near, square))
     send = call(dispatch_kernel, "dispatch", shape((REACH, ROWS, D)), 2)(near, slot_row)
     received = exchange(send, REACH_GROUPS)
 
-    partials = partials_of(line, key_value_pool, block_owner, block_tokens)
     other_gate_up, other_down = moved(w_gate_up, dc=1), moved(w_down, dc=1)
-    received, partials = lax.optimization_barrier((received, partials))
+    partials = partial_attention(
+        block_owner, block_tokens, jnp.concatenate(square, axis=0), key_value_pool
+    ).reshape(SIDE, SIDE, MESSAGE, HEAD)
+    columns = [partials[0]] + [moved(partials[k], dz=k) for k in range(1, SIDE)]
 
     rows = expert(
         received.reshape(REACH * ROWS, D), w_gate_up, other_gate_up, w_down, other_down
     )
+    rows, columns = lax.optimization_barrier((rows, columns))
     returned = exchange(rows.reshape(REACH, ROWS, D), REACH_GROUPS)
     mix = call(mixing_kernel, "mixing", shape((2 * NEAR, REACH * ROWS)), 2)(near, slot_row)
-    pieces = partials_by_column(partials)
-    returned, pieces = lax.optimization_barrier((returned, pieces))
+    pieces = [jnp.stack([column[k] for column in columns]) for k in range(SIDE)]
+    got = [moved(piece, dx=k) if k else piece for k, piece in enumerate(pieces)]
+    returned, got = lax.optimization_barrier((returned, got))
 
     parts = call(combine_kernel, "combine", shape((RING, TOK, D)), 2)(mix, returned)
     parts = exchange(parts, RING_GROUPS)
-    attn_out = finish(pieces, line[: REQUESTS * HEADS], incoming_key_value)
+    attn_out = call(finish_kernel, "finish", shape((REQUESTS, HEADS * HEAD)), 6)(
+        *got, line[0], incoming_key_value
+    )
     moe_out = call(total_kernel, "total", shape((TOK, D)), 1)(parts)
     return (moe_out, attn_out)
 

time: 172 us -> 165 us (0.959)
  the two profiles are of different devices: /device:TPU:1 before, /device:TPU:2 now
where the time goes in v4:
time: 165 us; the launch traced here: 164 us
  starting transfers between devices  77.6 us (47%)
  waiting for transfers between devices  45.2 us (27%)
  Pallas kernels  29.9 us (18%)
  local copies, waits for them, and re-layouts  8.96 us (5%)
    ppermute x14, starting transfers between devices, moved(): return lax.ppermute(array, AXIS, pairs)  46.7 us
    all_to_all x4, starting transfers between devices, exchange(): lax.all_to_all(array, AXIS, split_axis=0, concat_axis=0, axis_index_group...  30.9 us
    ppermute x14, waiting for transfers between devices, moved(): return lax.ppermute(array, AXIS, pairs)  30.1 us
    all_to_all x4, waiting for transfers between devices, exchange(): lax.all_to_all(array, AXIS, split_axis=0, concat_axis=0, axis_index_group...  15.1 us
    pallas_call x1, Pallas kernels, expert(): call(expert_kernel, 'expert', shape(rows.shape), 5, grid=(rows.shape[0] /...  7.54 us
    pallas_call x1, Pallas kernels, partial_attention(): call(partial_kernel, 'partial_attention', shape((SIDE * SIDE, MESSAGE, HE...  7.35 us
    unnamed x23, local copies, waits for them, and re-layouts  5.23 us
    pallas_call x1, Pallas kernels, shards(): call(dispatch_kernel, 'dispatch', shape((REACH, ROWS, D)), 2)  3.4 us
  transfers between devices with their start and end apart: 18, of which 9 were waited for; matrix products, arithmetic and copies ran while one was open for 3% of the time, Pallas kernels for 13%

profile of v4, /device:TPU:2, one launch (start us, length us, event | category | flops | bytes accessed | tf_op | source)
XLA Modules:
  0.0 164.1 jit_solution(9001120397297619021)
XLA Ops:
  1.4 3.4 %collective-permute-start = (bf16[128,128]{1,0:T(8,128)(2,1)S(1)}, bf16[128,128]{1,0:T(8,128)(2,1)S(1)}, u32[]{:S(2)}, u32[]{:S(2)}) collective-permute-start(bf16[128,128]{1,0:T(8,128)(2,1)S(1)} %reshape.25.query_ref), channel_id=1, source_target_pairs={{0,128},{1,129},{2,130},{3,131},{4,132},{5,133},{6,134},{7,135},{8... | collective-permute-start | bytes 98312 | tf_op jit(solution)/shard_map/ppermute | solution.py:70
  6.7 4.5 %collective-permute-done = bf16[128,128]{1,0:T(8,128)(2,1)S(1)} collective-permute-done((bf16[128,128]{1,0:T(8,128)(2,1)S(1)}, bf16[128,128]{1,0:T(8,128)(2,1)S(1)}, u32[]{:S(2)}, u32[]{:S(2)}) %collective-permute-start) | collective-permute-done | bytes 32800 | tf_op jit(solution)/shard_map/ppermute | solution.py:70
  11.1 6.4 %all-to-all-start = ((bf16[8,16,2304]{2,1,0:T(8,128)(2,1)}), bf16[8,16,2304]{2,1,0:T(8,128)(2,1)S(1)}, u32[]{:S(2)}, u32[]{:S(2)}) async-start(bf16[8,16,2304]{2,1,0:T(8,128)(2,1)} %pack.1), calls=%async_computation | async-start | bytes 1179648 | tf_op jit(solution)/shard_map/all_to_all | solution.py:60
  17.6 4.0 %collective-permute-start.1 = (bf16[128,128]{1,0:T(8,128)(2,1)S(1)}, bf16[128,128]{1,0:T(8,128)(2,1)S(1)}, u32[]{:S(2)}, u32[]{:S(2)}) collective-permute-start(bf16[128,128]{1,0:T(8,128)(2,1)S(1)} %reshape.25.query_ref), channel_id=1, source_target_pairs={{0,256},{1,257},{2,258},{3,259},{4,260},{5,261},{6,262},{7,263},{8... | collective-permute-start | bytes 98312 | tf_op jit(solution)/shard_map/ppermute | solution.py:70
  21.6 3.3 %collective-permute-start.2 = (bf16[128,128]{1,0:T(8,128)(2,1)S(1)}, bf16[128,128]{1,0:T(8,128)(2,1)S(1)}, u32[]{:S(2)}, u32[]{:S(2)}) collective-permute-start(bf16[128,128]{1,0:T(8,128)(2,1)S(1)} %reshape.25.query_ref), channel_id=1, source_target_pairs={{0,384},{1,385},{2,386},{3,387},{4,388},{5,389},{6,390},{7,391},{8... | collective-permute-start | bytes 98312 | tf_op jit(solution)/shard_map/ppermute | solution.py:70
  25.0 2.4 %collective-permute-done.2 = bf16[128,128]{1,0:T(8,128)(2,1)S(1)} collective-permute-done((bf16[128,128]{1,0:T(8,128)(2,1)S(1)}, bf16[128,128]{1,0:T(8,128)(2,1)S(1)}, u32[]{:S(2)}, u32[]{:S(2)}) %collective-permute-start.2) | collective-permute-done | bytes 32800 | tf_op jit(solution)/shard_map/ppermute | solution.py:70
  27.4 3.9 %collective-permute-start.3 = (bf16[512,128]{1,0:T(8,128)(2,1)S(1)}, bf16[512,128]{1,0:T(8,128)(2,1)S(1)}, u32[]{:S(2)}, u32[]{:S(2)}) collective-permute-start(bf16[512,128]{1,0:T(8,128)(2,1)S(1)} %constant_dynamic-update-slice_fusion), channel_id=1, source_target_pairs={{0,32},{1,33},{2,34},{3,35},{4,36},{5,37},{6,38},{7,39},{8,40},{9,... | collective-permute-start | bytes 393224 | tf_op jit(solution)/shard_map/ppermute | solution.py:70
  31.3 4.3 %collective-permute-start.4 = (bf16[512,128]{1,0:T(8,128)(2,1)S(1)}, bf16[512,128]{1,0:T(8,128)(2,1)S(1)}, u32[]{:S(2)}, u32[]{:S(2)}) collective-permute-start(bf16[512,128]{1,0:T(8,128)(2,1)S(1)} %constant_dynamic-update-slice_fusion), channel_id=1, source_target_pairs={{0,64},{1,65},{2,66},{3,67},{4,68},{5,69},{6,70},{7,71},{8,72},{9,... | collective-permute-start | bytes 393224 | tf_op jit(solution)/shard_map/ppermute | solution.py:70
  35.6 3.4 %collective-permute-start.5 = (bf16[512,128]{1,0:T(8,128)(2,1)S(1)}, bf16[512,128]{1,0:T(8,128)(2,1)S(1)}, u32[]{:S(2)}, u32[]{:S(2)}) collective-permute-start(bf16[512,128]{1,0:T(8,128)(2,1)S(1)} %constant_dynamic-update-slice_fusion), channel_id=1, source_target_pairs={{0,96},{1,97},{2,98},{3,99},{4,100},{5,101},{6,102},{7,103},{8,104... | collective-permute-start | bytes 393224 | tf_op jit(solution)/shard_map/ppermute | solution.py:70
  39.0 1.8 %collective-permute-done.4 = bf16[512,128]{1,0:T(8,128)(2,1)S(1)} collective-permute-done((bf16[512,128]{1,0:T(8,128)(2,1)S(1)}, bf16[512,128]{1,0:T(8,128)(2,1)S(1)}, u32[]{:S(2)}, u32[]{:S(2)}) %collective-permute-start.4) | collective-permute-done | bytes 131104 | tf_op jit(solution)/shard_map/ppermute | solution.py:70
  43.3 3.4 %dispatch.1 = bf16[32,16,2048]{2,1,0:T(8,128)(2,1)} custom-call(bf16[8,16,2304]{2,1,0:T(8,128)(2,1)} %copy-done.2, s32[1,128]{1,0:T(1,128)} %bitcast.9), custom_call_target="tpu_custom_call" | custom-call | tf_op jit(solution)/shard_map/dispatch/pallas_call | solution.py:348
  46.7 10.6 %all-to-all-start.1 = ((bf16[32,16,2048]{2,1,0:T(8,128)(2,1)}), bf16[32,16,2048]{2,1,0:T(8,128)(2,1)S(1)}, u32[]{:S(2)}, u32[]{:S(2)}) async-start(bf16[32,16,2048]{2,1,0:T(8,128)(2,1)} %dispatch.1), calls=%async_computation.1 | async-start | bytes 4194304 | tf_op jit(solution)/shard_map/all_to_all | solution.py:60
  57.3 1.9 %collective-permute-start.6 = (bf16[2048,384]{1,0:T(8,128)(2,1)}, bf16[2048,384]{1,0:T(8,128)(2,1)}, u32[]{:S(2)}, u32[]{:S(2)}) collective-permute-start(bf16[2048,384]{1,0:T(8,128)(2,1)} %gate_up_ref.1), channel_id=1, source_target_pairs={{0,1},{1,0},{2,3},{3,2},{4,5},{5,4},{6,7},{7,6},{8,9},{9,8},{10,11... | collective-permute-start | bytes 4718600 | tf_op jit(solution)/shard_map/ppermute | solution.py:70
  59.2 2.4 %collective-permute-start.7 = (bf16[192,2048]{1,0:T(8,128)(2,1)S(1)}, bf16[192,2048]{1,0:T(8,128)(2,1)S(1)}, u32[]{:S(2)}, u32[]{:S(2)}) collective-permute-start(bf16[192,2048]{1,0:T(8,128)(2,1)S(1)} %copy-done.4), channel_id=1, source_target_pairs={{0,1},{1,0},{2,3},{3,2},{4,5},{5,4},{6,7},{7,6},{8,9},{9,8},{10,11... | collective-permute-start | bytes 2359304 | tf_op jit(solution)/shard_map/ppermute | solution.py:70
  62.5 7.3 %partial_attention.1 = bf16[16,144,128]{2,1,0:T(8,128)(2,1)} custom-call(s32[16]{0:T(128)} %owner_ref.1, s32[16]{0:T(128)} %count_ref.1, bf16[2048,128]{1,0:T(8,128)(2,1)} %pad_maximum_fusion.query_ref, bf16[16,64,1024]{2,1,0:T(8,128)(2,1)} %pool_ref.1), custom_call_target="tpu_custom_call" | custom-call | tf_op jit(solution)/shard_map/partial_attention/pallas_call | solution.py:269
  71.0 2.2 %collective-permute-start.8 = (bf16[4,144,128]{2,1,0:T(8,128)(2,1)S(1)}, bf16[4,144,128]{2,1,0:T(8,128)(2,1)}, u32[]{:S(2)}, u32[]{:S(2)}) collective-permute-start(bf16[4,144,128]{2,1,0:T(8,128)(2,1)S(1)} %get-tuple-element.38), channel_id=1, source_target_pairs={{0,32},{1,33},{2,34},{3,35},{4,36},{5,37},{6,38},{7,39},{8,40},{9,... | collective-permute-start | bytes 442376 | tf_op jit(solution)/shard_map/ppermute | solution.py:70
  73.3 5.4 %collective-permute-start.9 = (bf16[4,144,128]{2,1,0:T(8,128)(2,1)S(1)}, bf16[4,144,128]{2,1,0:T(8,128)(2,1)}, u32[]{:S(2)}, u32[]{:S(2)}) collective-permute-start(bf16[4,144,128]{2,1,0:T(8,128)(2,1)S(1)} %get-tuple-element.37), channel_id=1, source_target_pairs={{0,64},{1,65},{2,66},{3,67},{4,68},{5,69},{6,70},{7,71},{8,72},{9,... | collective-permute-start | bytes 442376 | tf_op jit(solution)/shard_map/ppermute | solution.py:70
  78.7 1.9 %collective-permute-start.10 = (bf16[4,144,128]{2,1,0:T(8,128)(2,1)S(1)}, bf16[4,144,128]{2,1,0:T(8,128)(2,1)}, u32[]{:S(2)}, u32[]{:S(2)}) collective-permute-start(bf16[4,144,128]{2,1,0:T(8,128)(2,1)S(1)} %get-tuple-element.36), channel_id=1, source_target_pairs={{0,96},{1,97},{2,98},{3,99},{4,100},{5,101},{6,102},{7,103},{8,104... | collective-permute-start | bytes 442376 | tf_op jit(solution)/shard_map/ppermute | solution.py:70
  81.5 4.4 %all-to-all-done.1 = bf16[32,16,2048]{2,1,0:T(8,128)(2,1)S(1)} async-done(((bf16[32,16,2048]{2,1,0:T(8,128)(2,1)}), bf16[32,16,2048]{2,1,0:T(8,128)(2,1)S(1)}, u32[]{:S(2)}, u32[]{:S(2)}) %all-to-all-start.1) | async-done | bytes 2097184 | tf_op jit(solution)/shard_map/all_to_all | solution.py:60
  87.2 7.5 %expert.1 = bf16[512,2048]{1,0:T(8,128)(2,1)} custom-call(bf16[512,2048]{1,0:T(8,128)(2,1)} %bitcast.6, bf16[2048,384]{1,0:T(8,128)(2,1)} %gate_up_ref.1, bf16[2048,384]{1,0:T(8,128)(2,1)} %collective-permute-done.6.other_gate_up_ref, bf16[192,2048]{1,0:T(8,128)(2,1)} %down_ref.1, bf16[192,2048]{1,0:T(8,128)(2,1)} %copy-done.5), custom_call_target="tpu_custom_call" | custom-call | tf_op jit(solution)/shard_map/expert/pallas_call | solution.py:197
  94.8 8.3 %all-to-all-start.2 = ((bf16[32,16,2048]{2,1,0:T(8,128)(2,1)}), bf16[32,16,2048]{2,1,0:T(8,128)(2,1)S(1)}, u32[]{:S(2)}, u32[]{:S(2)}) async-start(bf16[32,16,2048]{2,1,0:T(8,128)(2,1)} %bitcast.5), calls=%async_computation.2 | async-start | bytes 4194304 | tf_op jit(solution)/shard_map/all_to_all | solution.py:60
  104.9 3.4 %collective-permute-start.11 = (bf16[4,144,128]{2,1,0:T(8,128)(2,1)S(1)}, bf16[4,144,128]{2,1,0:T(8,128)(2,1)S(1)}, u32[]{:S(2)}, u32[]{:S(2)}) collective-permute-start(bf16[4,144,128]{2,1,0:T(8,128)(2,1)S(1)} %pad_maximum_fusion.2), channel_id=1, source_target_pairs={{0,128},{1,129},{2,130},{3,131},{4,132},{5,133},{6,134},{7,135},{8... | collective-permute-start | bytes 442376 | tf_op jit(solution)/shard_map/ppermute | solution.py:70
  108.3 2.7 %collective-permute-start.12 = (bf16[4,144,128]{2,1,0:T(8,128)(2,1)S(1)}, bf16[4,144,128]{2,1,0:T(8,128)(2,1)S(1)}, u32[]{:S(2)}, u32[]{:S(2)}) collective-permute-start(bf16[4,144,128]{2,1,0:T(8,128)(2,1)S(1)} %pad_maximum_fusion.3), channel_id=1, source_target_pairs={{0,256},{1,257},{2,258},{3,259},{4,260},{5,261},{6,262},{7,263},{8... | collective-permute-start | bytes 442376 | tf_op jit(solution)/shard_map/ppermute | solution.py:70
  111.1 4.3 %collective-permute-start.13 = (bf16[4,144,128]{2,1,0:T(8,128)(2,1)S(1)}, bf16[4,144,128]{2,1,0:T(8,128)(2,1)S(1)}, u32[]{:S(2)}, u32[]{:S(2)}) collective-permute-start(bf16[4,144,128]{2,1,0:T(8,128)(2,1)S(1)} %pad_maximum_fusion.4), channel_id=1, source_target_pairs={{0,384},{1,385},{2,386},{3,387},{4,388},{5,389},{6,390},{7,391},{8... | collective-permute-start | bytes 442376 | tf_op jit(solution)/shard_map/ppermute | solution.py:70
  115.5 2.3 %mixing.1.mix_ref = bf16[256,512]{1,0:T(8,128)(2,1)} custom-call(bf16[8,16,2304]{2,1,0:T(8,128)(2,1)} %copy-done.2, s32[1,128]{1,0:T(1,128)} %bitcast.10), custom_call_target="tpu_custom_call" | custom-call | tf_op jit(solution)/shard_map/mixing/pallas_call | solution.py:362
  118.4 11.4 %collective-permute-done.11.got1_ref = bf16[4,144,128]{2,1,0:T(8,128)(2,1)S(1)} collective-permute-done((bf16[4,144,128]{2,1,0:T(8,128)(2,1)S(1)}, bf16[4,144,128]{2,1,0:T(8,128)(2,1)S(1)}, u32[]{:S(2)}, u32[]{:S(2)}) %collective-permute-start.11) | collective-permute-done | bytes 147488 | tf_op jit(solution)/shard_map/ppermute | solution.py:70
  129.8 5.6 %collective-permute-done.12.got2_ref = bf16[4,144,128]{2,1,0:T(8,128)(2,1)S(1)} collective-permute-done((bf16[4,144,128]{2,1,0:T(8,128)(2,1)S(1)}, bf16[4,144,128]{2,1,0:T(8,128)(2,1)S(1)}, u32[]{:S(2)}, u32[]{:S(2)}) %collective-permute-start.12) | collective-permute-done | bytes 147488 | tf_op jit(solution)/shard_map/ppermute | solution.py:70
  135.4 2.8 %collective-permute-done.13.got3_ref = bf16[4,144,128]{2,1,0:T(8,128)(2,1)S(1)} collective-permute-done((bf16[4,144,128]{2,1,0:T(8,128)(2,1)S(1)}, bf16[4,144,128]{2,1,0:T(8,128)(2,1)S(1)}, u32[]{:S(2)}, u32[]{:S(2)}) %collective-permute-start.13) | collective-permute-done | bytes 147488 | tf_op jit(solution)/shard_map/ppermute | solution.py:70
  139.6 3.2 %combine.1 = bf16[8,16,2048]{2,1,0:T(8,128)(2,1)} custom-call(bf16[256,512]{1,0:T(8,128)(2,1)} %mixing.1.mix_ref, bf16[32,16,2048]{2,1,0:T(8,128)(2,1)} %copy-done.1), custom_call_target="tpu_custom_call" | custom-call | tf_op jit(solution)/shard_map/combine/pallas_call | solution.py:367
  142.8 5.5 %all-to-all-start.3 = ((bf16[8,16,2048]{2,1,0:T(8,128)(2,1)}), bf16[8,16,2048]{2,1,0:T(8,128)(2,1)S(1)}, u32[]{:S(2)}, u32[]{:S(2)}) async-start(bf16[8,16,2048]{2,1,0:T(8,128)(2,1)} %combine.1), calls=%async_computation.3 | async-start | bytes 1048576 | tf_op jit(solution)/shard_map/all_to_all | solution.py:60
  148.3 2.6 %finish.1 = bf16[2,8192]{1,0:T(2,128)(2,1)} custom-call(bf16[4,144,128]{2,1,0:T(8,128)(2,1)} %pad_maximum_fusion.1.got0_ref, bf16[4,144,128]{2,1,0:T(8,128)(2,1)} %copy-done.7, bf16[4,144,128]{2,1,0:T(8,128)(2,1)} %copy-done.8, bf16[4,144,128]{2,1,0:T(8,128)(2,1)} %copy-done.9, bf16[128,128]{1,0:T(8,128)(2,1)} %copy-done.6, bf16[2,1024]{1,0:T(2,128)(2,1)} %new_ref.1), custom_call_target="tpu_custom_call" | custom-call | tf_op jit(solution)/shard_map/finish/pallas_call | solution.py:369
  150.9 10.7 %all-to-all-done.3.parts_ref = bf16[8,16,2048]{2,1,0:T(8,128)(2,1)S(1)} async-done(((bf16[8,16,2048]{2,1,0:T(8,128)(2,1)}), bf16[8,16,2048]{2,1,0:T(8,128)(2,1)S(1)}, u32[]{:S(2)}, u32[]{:S(2)}) %all-to-all-start.3) | async-done | bytes 524320 | tf_op jit(solution)/shard_map/all_to_all | solution.py:60
  (45 shorter events, 15.8 us)
Async XLA Ops:
  1.4 45.3 %copy-start.6 = (bf16[128,128]{1,0:T(8,128)(2,1)}, bf16[128,128]{1,0:T(8,128)(2,1)S(1)}, u32[]{:S(2)}) copy-start(bf16[128,128]{1,0:T(8,128)(2,1)S(1)} %reshape.25.query_ref) | copy-start | bytes 98308
  1.4 9.7 %collective-permute-start = (bf16[128,128]{1,0:T(8,128)(2,1)S(1)}, bf16[128,128]{1,0:T(8,128)(2,1)S(1)}, u32[]{:S(2)}, u32[]{:S(2)}) collective-permute-start(bf16[128,128]{1,0:T(8,128)(2,1)S(1)} %reshape.25.query_ref), channel_id=1, source_target_pairs={{0,128},{1,129},{2,130},{3,131},{4,132},{5,133},{6,134},{7,135},{8... | collective-permute-start | bytes 98312 | tf_op jit(solution)/shard_map/ppermute | solution.py:70
  11.1 31.3 %all-to-all-start = ((bf16[8,16,2304]{2,1,0:T(8,128)(2,1)}), bf16[8,16,2304]{2,1,0:T(8,128)(2,1)S(1)}, u32[]{:S(2)}, u32[]{:S(2)}) async-start(bf16[8,16,2304]{2,1,0:T(8,128)(2,1)} %pack.1), calls=%async_computation | async-start | bytes 1179648 | tf_op jit(solution)/shard_map/all_to_all | solution.py:60
  17.6 7.4 %collective-permute-start.1 = (bf16[128,128]{1,0:T(8,128)(2,1)S(1)}, bf16[128,128]{1,0:T(8,128)(2,1)S(1)}, u32[]{:S(2)}, u32[]{:S(2)}) collective-permute-start(bf16[128,128]{1,0:T(8,128)(2,1)S(1)} %reshape.25.query_ref), channel_id=1, source_target_pairs={{0,256},{1,257},{2,258},{3,259},{4,260},{5,261},{6,262},{7,263},{8... | collective-permute-start | bytes 98312 | tf_op jit(solution)/shard_map/ppermute | solution.py:70
  21.6 5.8 %collective-permute-start.2 = (bf16[128,128]{1,0:T(8,128)(2,1)S(1)}, bf16[128,128]{1,0:T(8,128)(2,1)S(1)}, u32[]{:S(2)}, u32[]{:S(2)}) collective-permute-start(bf16[128,128]{1,0:T(8,128)(2,1)S(1)} %reshape.25.query_ref), channel_id=1, source_target_pairs={{0,384},{1,385},{2,386},{3,387},{4,388},{5,389},{6,390},{7,391},{8... | collective-permute-start | bytes 98312 | tf_op jit(solution)/shard_map/ppermute | solution.py:70
  27.4 11.6 %collective-permute-start.3 = (bf16[512,128]{1,0:T(8,128)(2,1)S(1)}, bf16[512,128]{1,0:T(8,128)(2,1)S(1)}, u32[]{:S(2)}, u32[]{:S(2)}) collective-permute-start(bf16[512,128]{1,0:T(8,128)(2,1)S(1)} %constant_dynamic-update-slice_fusion), channel_id=1, source_target_pairs={{0,32},{1,33},{2,34},{3,35},{4,36},{5,37},{6,38},{7,39},{8,40},{9,... | collective-permute-start | bytes 393224 | tf_op jit(solution)/shard_map/ppermute | solution.py:70
  31.3 9.5 %collective-permute-start.4 = (bf16[512,128]{1,0:T(8,128)(2,1)S(1)}, bf16[512,128]{1,0:T(8,128)(2,1)S(1)}, u32[]{:S(2)}, u32[]{:S(2)}) collective-permute-start(bf16[512,128]{1,0:T(8,128)(2,1)S(1)} %constant_dynamic-update-slice_fusion), channel_id=1, source_target_pairs={{0,64},{1,65},{2,66},{3,67},{4,68},{5,69},{6,70},{7,71},{8,72},{9,... | collective-permute-start | bytes 393224 | tf_op jit(solution)/shard_map/ppermute | solution.py:70
  35.6 6.9 %collective-permute-start.5 = (bf16[512,128]{1,0:T(8,128)(2,1)S(1)}, bf16[512,128]{1,0:T(8,128)(2,1)S(1)}, u32[]{:S(2)}, u32[]{:S(2)}) collective-permute-start(bf16[512,128]{1,0:T(8,128)(2,1)S(1)} %constant_dynamic-update-slice_fusion), channel_id=1, source_target_pairs={{0,96},{1,97},{2,98},{3,99},{4,100},{5,101},{6,102},{7,103},{8,104... | collective-permute-start | bytes 393224 | tf_op jit(solution)/shard_map/ppermute | solution.py:70
  42.5 0.8 copy-start.2
  46.7 12.5 %copy-start.4 = (bf16[192,2048]{1,0:T(8,128)(2,1)S(1)}, bf16[192,2048]{1,0:T(8,128)(2,1)}, u32[]{:S(2)}) copy-start(bf16[192,2048]{1,0:T(8,128)(2,1)} %down_ref.1) | copy-start | bytes 2359300
  46.7 39.2 %all-to-all-start.1 = ((bf16[32,16,2048]{2,1,0:T(8,128)(2,1)}), bf16[32,16,2048]{2,1,0:T(8,128)(2,1)S(1)}, u32[]{:S(2)}, u32[]{:S(2)}) async-start(bf16[32,16,2048]{2,1,0:T(8,128)(2,1)} %dispatch.1), calls=%async_computation.1 | async-start | bytes 4194304 | tf_op jit(solution)/shard_map/all_to_all | solution.py:60
  57.3 24.2 %collective-permute-start.6 = (bf16[2048,384]{1,0:T(8,128)(2,1)}, bf16[2048,384]{1,0:T(8,128)(2,1)}, u32[]{:S(2)}, u32[]{:S(2)}) collective-permute-start(bf16[2048,384]{1,0:T(8,128)(2,1)} %gate_up_ref.1), channel_id=1, source_target_pairs={{0,1},{1,0},{2,3},{3,2},{4,5},{5,4},{6,7},{7,6},{8,9},{9,8},{10,11... | collective-permute-start | bytes 4718600 | tf_op jit(solution)/shard_map/ppermute | solution.py:70
  59.2 21.4 %collective-permute-start.7 = (bf16[192,2048]{1,0:T(8,128)(2,1)S(1)}, bf16[192,2048]{1,0:T(8,128)(2,1)S(1)}, u32[]{:S(2)}, u32[]{:S(2)}) collective-permute-start(bf16[192,2048]{1,0:T(8,128)(2,1)S(1)} %copy-done.4), channel_id=1, source_target_pairs={{0,1},{1,0},{2,3},{3,2},{4,5},{5,4},{6,7},{7,6},{8,9},{9,8},{10,11... | collective-permute-start | bytes 2359304 | tf_op jit(solution)/shard_map/ppermute | solution.py:70
  71.0 23.8 %collective-permute-start.8 = (bf16[4,144,128]{2,1,0:T(8,128)(2,1)S(1)}, bf16[4,144,128]{2,1,0:T(8,128)(2,1)}, u32[]{:S(2)}, u32[]{:S(2)}) collective-permute-start(bf16[4,144,128]{2,1,0:T(8,128)(2,1)S(1)} %get-tuple-element.38), channel_id=1, source_target_pairs={{0,32},{1,33},{2,34},{3,35},{4,36},{5,37},{6,38},{7,39},{8,40},{9,... | collective-permute-start | bytes 442376 | tf_op jit(solution)/shard_map/ppermute | solution.py:70
  73.3 21.5 %collective-permute-start.9 = (bf16[4,144,128]{2,1,0:T(8,128)(2,1)S(1)}, bf16[4,144,128]{2,1,0:T(8,128)(2,1)}, u32[]{:S(2)}, u32[]{:S(2)}) collective-permute-start(bf16[4,144,128]{2,1,0:T(8,128)(2,1)S(1)} %get-tuple-element.37), channel_id=1, source_target_pairs={{0,64},{1,65},{2,66},{3,67},{4,68},{5,69},{6,70},{7,71},{8,72},{9,... | collective-permute-start | bytes 442376 | tf_op jit(solution)/shard_map/ppermute | solution.py:70
  78.7 16.1 %collective-permute-start.10 = (bf16[4,144,128]{2,1,0:T(8,128)(2,1)S(1)}, bf16[4,144,128]{2,1,0:T(8,128)(2,1)}, u32[]{:S(2)}, u32[]{:S(2)}) collective-permute-start(bf16[4,144,128]{2,1,0:T(8,128)(2,1)S(1)} %get-tuple-element.36), channel_id=1, source_target_pairs={{0,96},{1,97},{2,98},{3,99},{4,100},{5,101},{6,102},{7,103},{8,104... | collective-permute-start | bytes 442376 | tf_op jit(solution)/shard_map/ppermute | solution.py:70
  80.6 0.9 copy-start.5
  85.9 1.3 copy-start
  94.8 43.4 %all-to-all-start.2 = ((bf16[32,16,2048]{2,1,0:T(8,128)(2,1)}), bf16[32,16,2048]{2,1,0:T(8,128)(2,1)S(1)}, u32[]{:S(2)}, u32[]{:S(2)}) async-start(bf16[32,16,2048]{2,1,0:T(8,128)(2,1)} %bitcast.5), calls=%async_computation.2 | async-start | bytes 4194304 | tf_op jit(solution)/shard_map/all_to_all | solution.py:60
  104.9 24.9 %collective-permute-start.11 = (bf16[4,144,128]{2,1,0:T(8,128)(2,1)S(1)}, bf16[4,144,128]{2,1,0:T(8,128)(2,1)S(1)}, u32[]{:S(2)}, u32[]{:S(2)}) collective-permute-start(bf16[4,144,128]{2,1,0:T(8,128)(2,1)S(1)} %pad_maximum_fusion.2), channel_id=1, source_target_pairs={{0,128},{1,129},{2,130},{3,131},{4,132},{5,133},{6,134},{7,135},{8... | collective-permute-start | bytes 442376 | tf_op jit(solution)/shard_map/ppermute | solution.py:70
  108.3 27.1 %collective-permute-start.12 = (bf16[4,144,128]{2,1,0:T(8,128)(2,1)S(1)}, bf16[4,144,128]{2,1,0:T(8,128)(2,1)S(1)}, u32[]{:S(2)}, u32[]{:S(2)}) collective-permute-start(bf16[4,144,128]{2,1,0:T(8,128)(2,1)S(1)} %pad_maximum_fusion.3), channel_id=1, source_target_pairs={{0,256},{1,257},{2,258},{3,259},{4,260},{5,261},{6,262},{7,263},{8... | collective-permute-start | bytes 442376 | tf_op jit(solution)/shard_map/ppermute | solution.py:70
  111.1 27.1 %collective-permute-start.13 = (bf16[4,144,128]{2,1,0:T(8,128)(2,1)S(1)}, bf16[4,144,128]{2,1,0:T(8,128)(2,1)S(1)}, u32[]{:S(2)}, u32[]{:S(2)}) collective-permute-start(bf16[4,144,128]{2,1,0:T(8,128)(2,1)S(1)} %pad_maximum_fusion.4), channel_id=1, source_target_pairs={{0,384},{1,385},{2,386},{3,387},{4,388},{5,389},{6,390},{7,391},{8... | collective-permute-start | bytes 442376 | tf_op jit(solution)/shard_map/ppermute | solution.py:70
  129.8 18.5 %copy-start.7 = (bf16[4,144,128]{2,1,0:T(8,128)(2,1)}, bf16[4,144,128]{2,1,0:T(8,128)(2,1)S(1)}, u32[]{:S(2)}) copy-start(bf16[4,144,128]{2,1,0:T(8,128)(2,1)S(1)} %collective-permute-done.11.got1_ref) | copy-start | bytes 442372
  135.4 12.9 %copy-start.8 = (bf16[4,144,128]{2,1,0:T(8,128)(2,1)}, bf16[4,144,128]{2,1,0:T(8,128)(2,1)S(1)}, u32[]{:S(2)}) copy-start(bf16[4,144,128]{2,1,0:T(8,128)(2,1)S(1)} %collective-permute-done.12.got2_ref) | copy-start | bytes 442372
  138.2 10.1 %copy-start.9 = (bf16[4,144,128]{2,1,0:T(8,128)(2,1)}, bf16[4,144,128]{2,1,0:T(8,128)(2,1)S(1)}, u32[]{:S(2)}) copy-start(bf16[4,144,128]{2,1,0:T(8,128)(2,1)S(1)} %collective-permute-done.13.got3_ref) | copy-start | bytes 442372
  138.2 1.4 copy-start.1
  142.8 18.8 %all-to-all-start.3 = ((bf16[8,16,2048]{2,1,0:T(8,128)(2,1)}), bf16[8,16,2048]{2,1,0:T(8,128)(2,1)S(1)}, u32[]{:S(2)}, u32[]{:S(2)}) async-start(bf16[8,16,2048]{2,1,0:T(8,128)(2,1)} %combine.1), calls=%async_computation.3 | async-start | bytes 1048576 | tf_op jit(solution)/shard_map/all_to_all | solution.py:60
  161.6 0.8 copy-start.3

commit v5 on v4

--- a/solution.py
+++ b/solution.py
@@ -205,6 +205,50 @@
     )(rows, *weights)
 
 
+def write_states(ref, r, states):
+    lane, row = iota((HEADS, HEAD), 1), iota((HEADS, HEAD), 0)
+    line = iota((STAT, HEAD), 0)
+    stats = jnp.zeros((STAT, HEAD), F32)
+    for i, (top, total, mixed) in enumerate(states):
+        ref[r, i * HEADS : (i + 1) * HEADS, :] = mixed.astype(BF16)
+        flat = jnp.where(lane == row, top, 0.0) + jnp.where(lane == row + HEADS, total, 0.0)
+        flat = jnp.sum(flat, axis=0, keepdims=True)
+        for part, value in enumerate(split(flat)):
+            stats = jnp.where(line == i * 3 + part, value.astype(F32), stats)
+    ref[r, REQUESTS * HEADS :, :] = stats.astype(BF16)
+
+
+def read_state(ref, r, i):
+    lane, row = iota((HEADS, HEAD), 1), iota((HEADS, HEAD), 0)
+    stats = ref[r, REQUESTS * HEADS :, :].astype(F32)
+    flat = stats[i * 3 : i * 3 + 1] + stats[i * 3 + 1 : i * 3 + 2] + stats[i * 3 + 2 : i * 3 + 3]
+    top = jnp.sum(jnp.where(lane == row, flat, 0.0), axis=1, keepdims=True)
+    total = jnp.sum(jnp.where(lane == row + HEADS, flat, 0.0), axis=1, keepdims=True)
+    return top, total, ref[r, i * HEADS : (i + 1) * HEADS, :].astype(F32)
+
+
+def merged(states):
+    best = states[0][0]
+    for top, _, _ in states[1:]:
+        best = jnp.maximum(best, top)
+    sums, acc = 0.0, 0.0
+    for top, total, mixed in states:
+        factor = jnp.exp(top - best)
+        sums = sums + factor * total
+        acc = acc + factor * mixed
+    return best, sums, acc
+
+
+def merge_kernel(got0_ref, got1_ref, got2_ref, got3_ref, send_ref):
+    refs = (got0_ref, got1_ref, got2_ref, got3_ref)
+    for r in range(SIDE):
+        write_states(
+            send_ref,
+            r,
+            [merged([read_state(ref, r, i) for ref in refs]) for i in range(REQUESTS)],
+        )
+
+
 def partial_kernel(owner_ref, count_ref, query_ref, pool_ref, send_ref, top_ref, sum_ref, acc_ref):
     scale = 1.0 / math.sqrt(HEAD)
     top_ref[...] = jnp.full(top_ref.shape, NEG, F32)
@@ -217,8 +261,8 @@
     for b in range(BLOCKS):
         owner = owner_ref[b]
         ax, az, request = owner >> 3, (owner >> 1) & 3, owner & 1
-        asked = ((zl - az) & 3) * 8 + ((x - ax) & 3) * 2 + request
-        state = ((az - zl) & 3) * 8 + ((ax - x) & 3) * 2 + request
+        asked = ((x - ax) & 3) * 8 + ((zl - az) & 3) * 2 + request
+        state = ((ax - x) & 3) * 8 + ((az - zl) & 3) * 2 + request
         rows = pl.ds(pl.multiple_of(state * HEADS, HEADS), HEADS)
         query = query_ref[pl.ds(pl.multiple_of(asked * HEADS, HEADS), HEADS), :]
         wide = jnp.where(own, jnp.concatenate([query] * GROUPS, axis=1), jnp.zeros((), BF16))
@@ -248,20 +292,13 @@
         top_ref[rows, :] = best
         sum_ref[rows, :] = keep_old * sum_ref[rows, :] + add_new * total
         acc_ref[rows, :] = keep_old * acc_ref[rows, :] + add_new * mixed
-    lane, row = iota((HEADS, HEAD), 1), iota((HEADS, HEAD), 0)
-    line = iota((STAT, HEAD), 0)
     for r in range(SIDE * SIDE):
-        stats = jnp.zeros((STAT, HEAD), F32)
+        states = []
         for i in range(REQUESTS):
             at = (r * REQUESTS + i) * HEADS
-            send_ref[r, i * HEADS : (i + 1) * HEADS, :] = acc_ref[at : at + HEADS, :].astype(BF16)
-            flat = jnp.where(lane == row, top_ref[at : at + HEADS, :], 0.0) + jnp.where(
-                lane == row + HEADS, sum_ref[at : at + HEADS, :], 0.0
-            )
-            flat = jnp.sum(flat, axis=0, keepdims=True)
-            for part, value in enumerate(split(flat)):
-                stats = jnp.where(line == i * 3 + part, value.astype(F32), stats)
-        send_ref[r, REQUESTS * HEADS :, :] = stats.astype(BF16)
+            rows = slice(at, at + HEADS)
+            states.append((top_ref[rows, :], sum_ref[rows, :], acc_ref[rows, :]))
+        write_states(send_ref, r, states)
 
 
 def partial_attention(owner, count, queries, pool):
@@ -279,8 +316,6 @@
 def finish_kernel(got0_ref, got1_ref, got2_ref, got3_ref, query_ref, new_ref, out_ref):
     scale = 1.0 / math.sqrt(HEAD)
     per = HEADS // GROUPS
-    lane, row = iota((HEADS, HEAD), 1), iota((HEADS, HEAD), 0)
-    parts = [(ref, r) for ref in (got0_ref, got1_ref, got2_ref, got3_ref) for r in range(SIDE)]
 
     def by_head(line):
         return jnp.concatenate(
@@ -297,22 +332,9 @@
         key = by_head(new_ref[i : i + 1, :KV].astype(F32))
         value = by_head(new_ref[i : i + 1, KV:].astype(F32))
         own = jnp.sum(query * key, axis=1, keepdims=True) * scale
-        tops, sums = [], []
-        best = own
-        for ref, r in parts:
-            stats = ref[r, REQUESTS * HEADS :, :].astype(F32)
-            flat = stats[i * 3 : i * 3 + 1] + stats[i * 3 + 1 : i * 3 + 2]
-            flat = flat + stats[i * 3 + 2 : i * 3 + 3]
-            tops.append(jnp.sum(jnp.where(lane == row, flat, 0.0), axis=1, keepdims=True))
-            sums.append(jnp.sum(jnp.where(lane == row + HEADS, flat, 0.0), axis=1, keepdims=True))
-            best = jnp.maximum(best, tops[-1])
-        weight = jnp.exp(own - best)
-        total = weight
-        mixed = weight * value
-        for (ref, r), top, part in zip(parts, tops, sums):
-            factor = jnp.exp(top - best)
-            total = total + factor * part
-            mixed = mixed + factor * ref[r, i * HEADS : (i + 1) * HEADS, :].astype(F32)
+        states = [(own, jnp.ones((HEADS, 1), F32), value)]
+        states += [read_state(ref, 0, i) for ref in (got0_ref, got1_ref, got2_ref, got3_ref)]
+        _, total, mixed = merged(states)
         answers.append(mixed / total)
     for h in range(HEADS):
         pair = jnp.concatenate([part[h : h + 1] for part in answers], axis=0)
@@ -340,34 +362,33 @@
     packed = call(pack_kernel, "pack", shape((RING, TOK, D + EXTRA)), 3)(
         moe_input, expert_ids.T, route_weight.T
     )
-    line = along(queries.reshape(REQUESTS * HEADS, HEAD), "dx")
-    packed, line[1] = lax.optimization_barrier((packed, line[1]))
+    own_queries = queries.reshape(REQUESTS * HEADS, HEAD)
+    line = jnp.concatenate(along(own_queries, "dz"), axis=0)
     near = exchange(packed, RING_GROUPS)
-    square = along(jnp.concatenate(line, axis=0), "dz")
-    near, square = lax.optimization_barrier((near, square))
+    near, line = lax.optimization_barrier((near, line))
     send = call(dispatch_kernel, "dispatch", shape((REACH, ROWS, D)), 2)(near, slot_row)
     received = exchange(send, REACH_GROUPS)
 
     other_gate_up, other_down = moved(w_gate_up, dc=1), moved(w_down, dc=1)
-    partials = partial_attention(
-        block_owner, block_tokens, jnp.concatenate(square, axis=0), key_value_pool
-    ).reshape(SIDE, SIDE, MESSAGE, HEAD)
-    columns = [partials[0]] + [moved(partials[k], dz=k) for k in range(1, SIDE)]
-
+    all_queries = jnp.concatenate(along(line, "dx"), axis=0)
+    received, all_queries = lax.optimization_barrier((received, all_queries))
     rows = expert(
         received.reshape(REACH * ROWS, D), w_gate_up, other_gate_up, w_down, other_down
     )
-    rows, columns = lax.optimization_barrier((rows, columns))
+    rows, block_owner = lax.optimization_barrier((rows, block_owner))
     returned = exchange(rows.reshape(REACH, ROWS, D), REACH_GROUPS)
+    partials = partial_attention(block_owner, block_tokens, all_queries, key_value_pool)
+    partials = partials.reshape(SIDE, SIDE, MESSAGE, HEAD)
+    got = [partials[0]] + [moved(partials[k], dx=k) for k in range(1, SIDE)]
     mix = call(mixing_kernel, "mixing", shape((2 * NEAR, REACH * ROWS)), 2)(near, slot_row)
-    pieces = [jnp.stack([column[k] for column in columns]) for k in range(SIDE)]
-    got = [moved(piece, dx=k) if k else piece for k, piece in enumerate(pieces)]
     returned, got = lax.optimization_barrier((returned, got))
 
     parts = call(combine_kernel, "combine", shape((RING, TOK, D)), 2)(mix, returned)
     parts = exchange(parts, RING_GROUPS)
+    send = call(merge_kernel, "merge", shape((SIDE, MESSAGE, HEAD)), 4)(*got)
+    got = [send[:1]] + [moved(send[k : k + 1], dz=k) for k in range(1, SIDE)]
     attn_out = call(finish_kernel, "finish", shape((REQUESTS, HEADS * HEAD)), 6)(
-        *got, line[0], incoming_key_value
+        *got, own_queries, incoming_key_value
     )
     moe_out = call(total_kernel, "total", shape((TOK, D)), 1)(parts)
     return (moe_out, attn_out)

time: 165 us -> 161 us (0.976)
  the two profiles are of different devices: /device:TPU:2 before, /device:TPU:26 now
where the time goes in v5:
time: 161 us; the launch traced here: 160 us
  starting transfers between devices  82.3 us (51%)
  waiting for transfers between devices  35.3 us (22%)
  Pallas kernels  31.5 us (20%)
  local copies, waits for them, and re-layouts  8.94 us (6%)
    ppermute x14, starting transfers between devices, moved(): return lax.ppermute(array, AXIS, pairs)  46.6 us
    all_to_all x4, starting transfers between devices, exchange(): lax.all_to_all(array, AXIS, split_axis=0, concat_axis=0, axis_index_group...  35.7 us
    ppermute x14, waiting for transfers between devices, moved(): return lax.ppermute(array, AXIS, pairs)  35.3 us
    pallas_call x1, Pallas kernels, expert(): call(expert_kernel, 'expert', shape(rows.shape), 5, grid=(rows.shape[0] /...  7.54 us
    pallas_call x1, Pallas kernels, partial_attention(): call(partial_kernel, 'partial_attention', shape((SIDE * SIDE, MESSAGE, HE...  7.34 us
    unnamed x24, local copies, waits for them, and re-layouts  4.89 us
    pallas_call x1, Pallas kernels, shards(): call(dispatch_kernel, 'dispatch', shape((REACH, ROWS, D)), 2)  3.39 us
  transfers between devices with their start and end apart: 18, of which 8 were waited for; matrix products, arithmetic and copies ran while one was open for 3% of the time, Pallas kernels for 9%

profile of v5, /device:TPU:26, one launch (start us, length us, event | category | flops | bytes accessed | tf_op | source)
XLA Modules:
  0.0 159.7 jit_solution(17463729132395279438)
XLA Ops:
  2.4 10.3 %all-to-all-start = ((bf16[8,16,2304]{2,1,0:T(8,128)(2,1)}), bf16[8,16,2304]{2,1,0:T(8,128)(2,1)S(1)}, u32[]{:S(2)}, u32[]{:S(2)}) async-start(bf16[8,16,2304]{2,1,0:T(8,128)(2,1)} %pack.1), calls=%async_computation | async-start | bytes 1179648 | tf_op jit(solution)/shard_map/all_to_all | solution.py:60
  13.6 5.7 %collective-permute-start.2 = (bf16[128,128]{1,0:T(8,128)(2,1)S(1)}, bf16[128,128]{1,0:T(8,128)(2,1)S(1)}, u32[]{:S(2)}, u32[]{:S(2)}) collective-permute-start(bf16[128,128]{1,0:T(8,128)(2,1)S(1)} %reshape.25.query_ref), channel_id=1, source_target_pairs={{0,96},{1,97},{2,98},{3,99},{4,100},{5,101},{6,102},{7,103},{8,104... | collective-permute-start | bytes 98312 | tf_op jit(solution)/shard_map/ppermute | solution.py:70
  19.3 1.9 %collective-permute-start.1 = (bf16[128,128]{1,0:T(8,128)(2,1)S(1)}, bf16[128,128]{1,0:T(8,128)(2,1)S(1)}, u32[]{:S(2)}, u32[]{:S(2)}) collective-permute-start(bf16[128,128]{1,0:T(8,128)(2,1)S(1)} %reshape.25.query_ref), channel_id=1, source_target_pairs={{0,64},{1,65},{2,66},{3,67},{4,68},{5,69},{6,70},{7,71},{8,72},{9,... | collective-permute-start | bytes 98312 | tf_op jit(solution)/shard_map/ppermute | solution.py:70
  21.2 3.0 %collective-permute-start = (bf16[128,128]{1,0:T(8,128)(2,1)S(1)}, bf16[128,128]{1,0:T(8,128)(2,1)S(1)}, u32[]{:S(2)}, u32[]{:S(2)}) collective-permute-start(bf16[128,128]{1,0:T(8,128)(2,1)S(1)} %reshape.25.query_ref), channel_id=1, source_target_pairs={{0,32},{1,33},{2,34},{3,35},{4,36},{5,37},{6,38},{7,39},{8,40},{9,... | collective-permute-start | bytes 98312 | tf_op jit(solution)/shard_map/ppermute | solution.py:70
  24.3 2.6 %collective-permute-done.1 = bf16[128,128]{1,0:T(8,128)(2,1)S(1)} collective-permute-done((bf16[128,128]{1,0:T(8,128)(2,1)S(1)}, bf16[128,128]{1,0:T(8,128)(2,1)S(1)}, u32[]{:S(2)}, u32[]{:S(2)}) %collective-permute-start.1) | collective-permute-done | bytes 32800 | tf_op jit(solution)/shard_map/ppermute | solution.py:70
  26.8 2.0 %collective-permute-done = bf16[128,128]{1,0:T(8,128)(2,1)S(1)} collective-permute-done((bf16[128,128]{1,0:T(8,128)(2,1)S(1)}, bf16[128,128]{1,0:T(8,128)(2,1)S(1)}, u32[]{:S(2)}, u32[]{:S(2)}) %collective-permute-start) | collective-permute-done | bytes 32800 | tf_op jit(solution)/shard_map/ppermute | solution.py:70
  29.7 3.4 %dispatch.1 = bf16[32,16,2048]{2,1,0:T(8,128)(2,1)} custom-call(bf16[8,16,2304]{2,1,0:T(8,128)(2,1)} %copy-done.2, s32[1,128]{1,0:T(1,128)} %bitcast.9), custom_call_target="tpu_custom_call" | custom-call | tf_op jit(solution)/shard_map/dispatch/pallas_call | solution.py:369
  33.1 10.0 %all-to-all-start.1 = ((bf16[32,16,2048]{2,1,0:T(8,128)(2,1)}), bf16[32,16,2048]{2,1,0:T(8,128)(2,1)S(1)}, u32[]{:S(2)}, u32[]{:S(2)}) async-start(bf16[32,16,2048]{2,1,0:T(8,128)(2,1)} %dispatch.1), calls=%async_computation.1 | async-start | bytes 4194304 | tf_op jit(solution)/shard_map/all_to_all | solution.py:60
  43.1 1.9 %collective-permute-start.6 = (bf16[2048,384]{1,0:T(8,128)(2,1)}, bf16[2048,384]{1,0:T(8,128)(2,1)}, u32[]{:S(2)}, u32[]{:S(2)}) collective-permute-start(bf16[2048,384]{1,0:T(8,128)(2,1)} %gate_up_ref.1), channel_id=1, source_target_pairs={{0,1},{1,0},{2,3},{3,2},{4,5},{5,4},{6,7},{7,6},{8,9},{9,8},{10,11... | collective-permute-start | bytes 4718600 | tf_op jit(solution)/shard_map/ppermute | solution.py:70
  45.0 2.4 %collective-permute-start.7 = (bf16[192,2048]{1,0:T(8,128)(2,1)S(1)}, bf16[192,2048]{1,0:T(8,128)(2,1)}, u32[]{:S(2)}, u32[]{:S(2)}) collective-permute-start(bf16[192,2048]{1,0:T(8,128)(2,1)S(1)} %copy-done.4), channel_id=1, source_target_pairs={{0,1},{1,0},{2,3},{3,2},{4,5},{5,4},{6,7},{7,6},{8,9},{9,8},{10,11... | collective-permute-start | bytes 2359304 | tf_op jit(solution)/shard_map/ppermute | solution.py:70
  47.5 2.5 %collective-permute-start.5 = (bf16[512,128]{1,0:T(8,128)(2,1)S(1)}, bf16[512,128]{1,0:T(8,128)(2,1)S(1)}, u32[]{:S(2)}, u32[]{:S(2)}) collective-permute-start(bf16[512,128]{1,0:T(8,128)(2,1)S(1)} %pad_maximum_fusion.1), channel_id=1, source_target_pairs={{0,384},{1,385},{2,386},{3,387},{4,388},{5,389},{6,390},{7,391},{8... | collective-permute-start | bytes 393224 | tf_op jit(solution)/shard_map/ppermute | solution.py:70
  49.9 4.3 %collective-permute-start.4 = (bf16[512,128]{1,0:T(8,128)(2,1)S(1)}, bf16[512,128]{1,0:T(8,128)(2,1)S(1)}, u32[]{:S(2)}, u32[]{:S(2)}) collective-permute-start(bf16[512,128]{1,0:T(8,128)(2,1)S(1)} %pad_maximum_fusion.1), channel_id=1, source_target_pairs={{0,256},{1,257},{2,258},{3,259},{4,260},{5,261},{6,262},{7,263},{8... | collective-permute-start | bytes 393224 | tf_op jit(solution)/shard_map/ppermute | solution.py:70
  54.2 3.7 %collective-permute-start.3 = (bf16[512,128]{1,0:T(8,128)(2,1)S(1)}, bf16[512,128]{1,0:T(8,128)(2,1)S(1)}, u32[]{:S(2)}, u32[]{:S(2)}) collective-permute-start(bf16[512,128]{1,0:T(8,128)(2,1)S(1)} %pad_maximum_fusion.1), channel_id=1, source_target_pairs={{0,128},{1,129},{2,130},{3,131},{4,132},{5,133},{6,134},{7,135},{8... | collective-permute-start | bytes 393224 | tf_op jit(solution)/shard_map/ppermute | solution.py:70
  58.0 11.4 %collective-permute-done.5 = bf16[512,128]{1,0:T(8,128)(2,1)S(1)} collective-permute-done((bf16[512,128]{1,0:T(8,128)(2,1)S(1)}, bf16[512,128]{1,0:T(8,128)(2,1)S(1)}, u32[]{:S(2)}, u32[]{:S(2)}) %collective-permute-start.5) | collective-permute-done | bytes 131104 | tf_op jit(solution)/shard_map/ppermute | solution.py:70
  69.4 4.7 %collective-permute-done.4 = bf16[512,128]{1,0:T(8,128)(2,1)S(1)} collective-permute-done((bf16[512,128]{1,0:T(8,128)(2,1)S(1)}, bf16[512,128]{1,0:T(8,128)(2,1)S(1)}, u32[]{:S(2)}, u32[]{:S(2)}) %collective-permute-start.4) | collective-permute-done | bytes 131104 | tf_op jit(solution)/shard_map/ppermute | solution.py:70
  76.2 7.5 %expert.1 = bf16[512,2048]{1,0:T(8,128)(2,1)} custom-call(bf16[512,2048]{1,0:T(8,128)(2,1)} %bitcast.5, bf16[2048,384]{1,0:T(8,128)(2,1)} %gate_up_ref.1, bf16[2048,384]{1,0:T(8,128)(2,1)} %collective-permute-done.6.other_gate_up_ref, bf16[192,2048]{1,0:T(8,128)(2,1)} %down_ref.1, bf16[192,2048]{1,0:T(8,128)(2,1)} %collective-permute-done.7.other_down_ref), custom_call_target="tpu_custom_call" | custom-call | tf_op jit(solution)/shard_map/expert/pallas_call | solution.py:197
  83.7 9.2 %all-to-all-start.2 = ((bf16[32,16,2048]{2,1,0:T(8,128)(2,1)}), bf16[32,16,2048]{2,1,0:T(8,128)(2,1)S(1)}, u32[]{:S(2)}, u32[]{:S(2)}) async-start(bf16[32,16,2048]{2,1,0:T(8,128)(2,1)} %bitcast.6), calls=%async_computation.2 | async-start | bytes 4194304 | tf_op jit(solution)/shard_map/all_to_all | solution.py:60
  92.9 7.3 %partial_attention.1 = bf16[16,144,128]{2,1,0:T(8,128)(2,1)} custom-call(s32[16]{0:T(128)} %owner_ref, s32[16]{0:T(128)} %count_ref.1, bf16[2048,128]{1,0:T(8,128)(2,1)} %pad_maximum_fusion.query_ref, bf16[16,64,1024]{2,1,0:T(8,128)(2,1)} %pool_ref.1), custom_call_target="tpu_custom_call" | custom-call | tf_op jit(solution)/shard_map/partial_attention/pallas_call | solution.py:306
  100.2 1.8 %fusion = (bf16[4,144,128]{2,1,0:T(8,128)(2,1)S(1)}, bf16[4,144,128]{2,1,0:T(8,128)(2,1)S(1)}, bf16[4,144,128]{2,1,0:T(8,128)(2,1)S(1)}, bf16[4,144,128]{2,1,0:T(8,128)(2,1)}) fusion(bf16[16,144,128]{2,1,0:T(8,128)(2,1)} %partial_attention.1), kind=kLoop, calls=%fused_computation.2 | loop fusion | bytes 1179648 | tf_op jit(solution)/shard_map/slice | solution.py:382
  102.0 2.5 %collective-permute-start.10 = (bf16[4,144,128]{2,1,0:T(8,128)(2,1)S(1)}, bf16[4,144,128]{2,1,0:T(8,128)(2,1)S(1)}, u32[]{:S(2)}, u32[]{:S(2)}) collective-permute-start(bf16[4,144,128]{2,1,0:T(8,128)(2,1)S(1)} %get-tuple-element.24), channel_id=1, source_target_pairs={{0,384},{1,385},{2,386},{3,387},{4,388},{5,389},{6,390},{7,391},{8... | collective-permute-start | bytes 442376 | tf_op jit(solution)/shard_map/ppermute | solution.py:70
  104.5 4.3 %collective-permute-start.9 = (bf16[4,144,128]{2,1,0:T(8,128)(2,1)S(1)}, bf16[4,144,128]{2,1,0:T(8,128)(2,1)S(1)}, u32[]{:S(2)}, u32[]{:S(2)}) collective-permute-start(bf16[4,144,128]{2,1,0:T(8,128)(2,1)S(1)} %get-tuple-element.25), channel_id=1, source_target_pairs={{0,256},{1,257},{2,258},{3,259},{4,260},{5,261},{6,262},{7,263},{8... | collective-permute-start | bytes 442376 | tf_op jit(solution)/shard_map/ppermute | solution.py:70
  108.8 3.7 %collective-permute-start.8 = (bf16[4,144,128]{2,1,0:T(8,128)(2,1)S(1)}, bf16[4,144,128]{2,1,0:T(8,128)(2,1)S(1)}, u32[]{:S(2)}, u32[]{:S(2)}) collective-permute-start(bf16[4,144,128]{2,1,0:T(8,128)(2,1)S(1)} %get-tuple-element.26), channel_id=1, source_target_pairs={{0,128},{1,129},{2,130},{3,131},{4,132},{5,133},{6,134},{7,135},{8... | collective-permute-start | bytes 442376 | tf_op jit(solution)/shard_map/ppermute | solution.py:70
  112.5 2.3 %mixing.1.mix_ref = bf16[256,512]{1,0:T(8,128)(2,1)} custom-call(bf16[8,16,2304]{2,1,0:T(8,128)(2,1)} %copy-done.2, s32[1,128]{1,0:T(1,128)} %bitcast.10), custom_call_target="tpu_custom_call" | custom-call | tf_op jit(solution)/shard_map/mixing/pallas_call | solution.py:383
  114.8 8.0 %collective-permute-done.10.got3_ref = bf16[4,144,128]{2,1,0:T(8,128)(2,1)S(1)} collective-permute-done((bf16[4,144,128]{2,1,0:T(8,128)(2,1)S(1)}, bf16[4,144,128]{2,1,0:T(8,128)(2,1)S(1)}, u32[]{:S(2)}, u32[]{:S(2)}) %collective-permute-start.10) | collective-permute-done | bytes 147488 | tf_op jit(solution)/shard_map/ppermute | solution.py:70
  122.8 2.0 %collective-permute-done.9.got2_ref = bf16[4,144,128]{2,1,0:T(8,128)(2,1)S(1)} collective-permute-done((bf16[4,144,128]{2,1,0:T(8,128)(2,1)S(1)}, bf16[4,144,128]{2,1,0:T(8,128)(2,1)S(1)}, u32[]{:S(2)}, u32[]{:S(2)}) %collective-permute-start.9) | collective-permute-done | bytes 147488 | tf_op jit(solution)/shard_map/ppermute | solution.py:70
  126.2 3.2 %combine.1 = bf16[8,16,2048]{2,1,0:T(8,128)(2,1)} custom-call(bf16[256,512]{1,0:T(8,128)(2,1)} %mixing.1.mix_ref, bf16[32,16,2048]{2,1,0:T(8,128)(2,1)} %copy-done.1), custom_call_target="tpu_custom_call" | custom-call | tf_op jit(solution)/shard_map/combine/pallas_call | solution.py:386
  129.5 6.2 %all-to-all-start.3 = ((bf16[8,16,2048]{2,1,0:T(8,128)(2,1)}), bf16[8,16,2048]{2,1,0:T(8,128)(2,1)S(1)}, u32[]{:S(2)}, u32[]{:S(2)}) async-start(bf16[8,16,2048]{2,1,0:T(8,128)(2,1)} %combine.1), calls=%async_computation.3 | async-start | bytes 1048576 | tf_op jit(solution)/shard_map/all_to_all | solution.py:60
  135.7 2.5 %merge.1 = bf16[4,144,128]{2,1,0:T(8,128)(2,1)} custom-call(bf16[4,144,128]{2,1,0:T(8,128)(2,1)} %get-tuple-element.20.got0_ref, bf16[4,144,128]{2,1,0:T(8,128)(2,1)} %copy-done.8, bf16[4,144,128]{2,1,0:T(8,128)(2,1)} %copy-done.7, bf16[4,144,128]{2,1,0:T(8,128)(2,1)} %copy-done.6), custom_call_target="tpu_custom_call" | custom-call | tf_op jit(solution)/shard_map/merge/pallas_call | solution.py:388
  139.6 5.7 %collective-permute-start.13 = (bf16[1,144,128]{2,1,0:T(8,128)(2,1)S(1)}, bf16[1,144,128]{2,1,0:T(8,128)(2,1)S(1)}, u32[]{:S(2)}, u32[]{:S(2)}) collective-permute-start(bf16[1,144,128]{2,1,0:T(8,128)(2,1)S(1)} %get-tuple-element.28), channel_id=1, source_target_pairs={{0,96},{1,97},{2,98},{3,99},{4,100},{5,101},{6,102},{7,103},{8,104... | collective-permute-start | bytes 110600 | tf_op jit(solution)/shard_map/ppermute | solution.py:70
  145.3 1.9 %collective-permute-start.12 = (bf16[1,144,128]{2,1,0:T(8,128)(2,1)S(1)}, bf16[1,144,128]{2,1,0:T(8,128)(2,1)S(1)}, u32[]{:S(2)}, u32[]{:S(2)}) collective-permute-start(bf16[1,144,128]{2,1,0:T(8,128)(2,1)S(1)} %get-tuple-element.29), channel_id=1, source_target_pairs={{0,64},{1,65},{2,66},{3,67},{4,68},{5,69},{6,70},{7,71},{8,72},{9,... | collective-permute-start | bytes 110600 | tf_op jit(solution)/shard_map/ppermute | solution.py:70
  147.2 3.0 %collective-permute-start.11 = (bf16[1,144,128]{2,1,0:T(8,128)(2,1)S(1)}, bf16[1,144,128]{2,1,0:T(8,128)(2,1)S(1)}, u32[]{:S(2)}, u32[]{:S(2)}) collective-permute-start(bf16[1,144,128]{2,1,0:T(8,128)(2,1)S(1)} %get-tuple-element.30), channel_id=1, source_target_pairs={{0,32},{1,33},{2,34},{3,35},{4,36},{5,37},{6,38},{7,39},{8,40},{9,... | collective-permute-start | bytes 110600 | tf_op jit(solution)/shard_map/ppermute | solution.py:70
  152.1 2.8 %collective-permute-done.11.got1_ref = bf16[1,144,128]{2,1,0:T(8,128)(2,1)S(1)} collective-permute-done((bf16[1,144,128]{2,1,0:T(8,128)(2,1)S(1)}, bf16[1,144,128]{2,1,0:T(8,128)(2,1)S(1)}, u32[]{:S(2)}, u32[]{:S(2)}) %collective-permute-start.11) | collective-permute-done | bytes 36896 | tf_op jit(solution)/shard_map/ppermute | solution.py:70
  (42 shorter events, 15.0 us)
Async XLA Ops:
  2.4 26.4 %all-to-all-start = ((bf16[8,16,2304]{2,1,0:T(8,128)(2,1)}), bf16[8,16,2304]{2,1,0:T(8,128)(2,1)S(1)}, u32[]{:S(2)}, u32[]{:S(2)}) async-start(bf16[8,16,2304]{2,1,0:T(8,128)(2,1)} %pack.1), calls=%async_computation | async-start | bytes 1179648 | tf_op jit(solution)/shard_map/all_to_all | solution.py:60
  13.5 19.5 %copy-start.5 = (bf16[128,128]{1,0:T(8,128)(2,1)}, bf16[128,128]{1,0:T(8,128)(2,1)S(1)}, u32[]{:S(2)}) copy-start(bf16[128,128]{1,0:T(8,128)(2,1)S(1)} %reshape.25.query_ref) | copy-start | bytes 98308
  13.6 10.7 %collective-permute-start.2 = (bf16[128,128]{1,0:T(8,128)(2,1)S(1)}, bf16[128,128]{1,0:T(8,128)(2,1)S(1)}, u32[]{:S(2)}, u32[]{:S(2)}) collective-permute-start(bf16[128,128]{1,0:T(8,128)(2,1)S(1)} %reshape.25.query_ref), channel_id=1, source_target_pairs={{0,96},{1,97},{2,98},{3,99},{4,100},{5,101},{6,102},{7,103},{8,104... | collective-permute-start | bytes 98312 | tf_op jit(solution)/shard_map/ppermute | solution.py:70
  19.3 7.5 %collective-permute-start.1 = (bf16[128,128]{1,0:T(8,128)(2,1)S(1)}, bf16[128,128]{1,0:T(8,128)(2,1)S(1)}, u32[]{:S(2)}, u32[]{:S(2)}) collective-permute-start(bf16[128,128]{1,0:T(8,128)(2,1)S(1)} %reshape.25.query_ref), channel_id=1, source_target_pairs={{0,64},{1,65},{2,66},{3,67},{4,68},{5,69},{6,70},{7,71},{8,72},{9,... | collective-permute-start | bytes 98312 | tf_op jit(solution)/shard_map/ppermute | solution.py:70
  21.2 7.6 %collective-permute-start = (bf16[128,128]{1,0:T(8,128)(2,1)S(1)}, bf16[128,128]{1,0:T(8,128)(2,1)S(1)}, u32[]{:S(2)}, u32[]{:S(2)}) collective-permute-start(bf16[128,128]{1,0:T(8,128)(2,1)S(1)} %reshape.25.query_ref), channel_id=1, source_target_pairs={{0,32},{1,33},{2,34},{3,35},{4,36},{5,37},{6,38},{7,39},{8,40},{9,... | collective-permute-start | bytes 98312 | tf_op jit(solution)/shard_map/ppermute | solution.py:70
  28.8 0.8 copy-start.2
  33.0 12.0 %copy-start.4 = (bf16[192,2048]{1,0:T(8,128)(2,1)S(1)}, bf16[192,2048]{1,0:T(8,128)(2,1)}, u32[]{:S(2)}) copy-start(bf16[192,2048]{1,0:T(8,128)(2,1)} %down_ref.1) | copy-start | bytes 2359300
  33.1 41.8 %all-to-all-start.1 = ((bf16[32,16,2048]{2,1,0:T(8,128)(2,1)}), bf16[32,16,2048]{2,1,0:T(8,128)(2,1)S(1)}, u32[]{:S(2)}, u32[]{:S(2)}) async-start(bf16[32,16,2048]{2,1,0:T(8,128)(2,1)} %dispatch.1), calls=%async_computation.1 | async-start | bytes 4194304 | tf_op jit(solution)/shard_map/all_to_all | solution.py:60
  43.1 31.7 %collective-permute-start.6 = (bf16[2048,384]{1,0:T(8,128)(2,1)}, bf16[2048,384]{1,0:T(8,128)(2,1)}, u32[]{:S(2)}, u32[]{:S(2)}) collective-permute-start(bf16[2048,384]{1,0:T(8,128)(2,1)} %gate_up_ref.1), channel_id=1, source_target_pairs={{0,1},{1,0},{2,3},{3,2},{4,5},{5,4},{6,7},{7,6},{8,9},{9,8},{10,11... | collective-permute-start | bytes 4718600 | tf_op jit(solution)/shard_map/ppermute | solution.py:70
  45.0 29.8 %collective-permute-start.7 = (bf16[192,2048]{1,0:T(8,128)(2,1)S(1)}, bf16[192,2048]{1,0:T(8,128)(2,1)}, u32[]{:S(2)}, u32[]{:S(2)}) collective-permute-start(bf16[192,2048]{1,0:T(8,128)(2,1)S(1)} %copy-done.4), channel_id=1, source_target_pairs={{0,1},{1,0},{2,3},{3,2},{4,5},{5,4},{6,7},{7,6},{8,9},{9,8},{10,11... | collective-permute-start | bytes 2359304 | tf_op jit(solution)/shard_map/ppermute | solution.py:70
  47.5 21.9 %collective-permute-start.5 = (bf16[512,128]{1,0:T(8,128)(2,1)S(1)}, bf16[512,128]{1,0:T(8,128)(2,1)S(1)}, u32[]{:S(2)}, u32[]{:S(2)}) collective-permute-start(bf16[512,128]{1,0:T(8,128)(2,1)S(1)} %pad_maximum_fusion.1), channel_id=1, source_target_pairs={{0,384},{1,385},{2,386},{3,387},{4,388},{5,389},{6,390},{7,391},{8... | collective-permute-start | bytes 393224 | tf_op jit(solution)/shard_map/ppermute | solution.py:70
  49.9 24.1 %collective-permute-start.4 = (bf16[512,128]{1,0:T(8,128)(2,1)S(1)}, bf16[512,128]{1,0:T(8,128)(2,1)S(1)}, u32[]{:S(2)}, u32[]{:S(2)}) collective-permute-start(bf16[512,128]{1,0:T(8,128)(2,1)S(1)} %pad_maximum_fusion.1), channel_id=1, source_target_pairs={{0,256},{1,257},{2,258},{3,259},{4,260},{5,261},{6,262},{7,263},{8... | collective-permute-start | bytes 393224 | tf_op jit(solution)/shard_map/ppermute | solution.py:70
  54.2 19.8 %collective-permute-start.3 = (bf16[512,128]{1,0:T(8,128)(2,1)S(1)}, bf16[512,128]{1,0:T(8,128)(2,1)S(1)}, u32[]{:S(2)}, u32[]{:S(2)}) collective-permute-start(bf16[512,128]{1,0:T(8,128)(2,1)S(1)} %pad_maximum_fusion.1), channel_id=1, source_target_pairs={{0,128},{1,129},{2,130},{3,131},{4,132},{5,133},{6,134},{7,135},{8... | collective-permute-start | bytes 393224 | tf_op jit(solution)/shard_map/ppermute | solution.py:70
  74.8 1.3 copy-start
  83.7 41.2 %all-to-all-start.2 = ((bf16[32,16,2048]{2,1,0:T(8,128)(2,1)}), bf16[32,16,2048]{2,1,0:T(8,128)(2,1)S(1)}, u32[]{:S(2)}, u32[]{:S(2)}) async-start(bf16[32,16,2048]{2,1,0:T(8,128)(2,1)} %bitcast.6), calls=%async_computation.2 | async-start | bytes 4194304 | tf_op jit(solution)/shard_map/all_to_all | solution.py:60
  102.0 20.8 %collective-permute-start.10 = (bf16[4,144,128]{2,1,0:T(8,128)(2,1)S(1)}, bf16[4,144,128]{2,1,0:T(8,128)(2,1)S(1)}, u32[]{:S(2)}, u32[]{:S(2)}) collective-permute-start(bf16[4,144,128]{2,1,0:T(8,128)(2,1)S(1)} %get-tuple-element.24), channel_id=1, source_target_pairs={{0,384},{1,385},{2,386},{3,387},{4,388},{5,389},{6,390},{7,391},{8... | collective-permute-start | bytes 442376 | tf_op jit(solution)/shard_map/ppermute | solution.py:70
  104.5 20.4 %collective-permute-start.9 = (bf16[4,144,128]{2,1,0:T(8,128)(2,1)S(1)}, bf16[4,144,128]{2,1,0:T(8,128)(2,1)S(1)}, u32[]{:S(2)}, u32[]{:S(2)}) collective-permute-start(bf16[4,144,128]{2,1,0:T(8,128)(2,1)S(1)} %get-tuple-element.25), channel_id=1, source_target_pairs={{0,256},{1,257},{2,258},{3,259},{4,260},{5,261},{6,262},{7,263},{8... | collective-permute-start | bytes 442376 | tf_op jit(solution)/shard_map/ppermute | solution.py:70
  108.8 16.1 %collective-permute-start.8 = (bf16[4,144,128]{2,1,0:T(8,128)(2,1)S(1)}, bf16[4,144,128]{2,1,0:T(8,128)(2,1)S(1)}, u32[]{:S(2)}, u32[]{:S(2)}) collective-permute-start(bf16[4,144,128]{2,1,0:T(8,128)(2,1)S(1)} %get-tuple-element.26), channel_id=1, source_target_pairs={{0,128},{1,129},{2,130},{3,131},{4,132},{5,133},{6,134},{7,135},{8... | collective-permute-start | bytes 442376 | tf_op jit(solution)/shard_map/ppermute | solution.py:70
  122.8 12.8 %copy-start.6 = (bf16[4,144,128]{2,1,0:T(8,128)(2,1)}, bf16[4,144,128]{2,1,0:T(8,128)(2,1)S(1)}, u32[]{:S(2)}) copy-start(bf16[4,144,128]{2,1,0:T(8,128)(2,1)S(1)} %collective-permute-done.10.got3_ref) | copy-start | bytes 442372
  124.8 10.8 %copy-start.7 = (bf16[4,144,128]{2,1,0:T(8,128)(2,1)}, bf16[4,144,128]{2,1,0:T(8,128)(2,1)S(1)}, u32[]{:S(2)}) copy-start(bf16[4,144,128]{2,1,0:T(8,128)(2,1)S(1)} %collective-permute-done.9.got2_ref) | copy-start | bytes 442372
  124.9 10.8 %copy-start.8 = (bf16[4,144,128]{2,1,0:T(8,128)(2,1)}, bf16[4,144,128]{2,1,0:T(8,128)(2,1)S(1)}, u32[]{:S(2)}) copy-start(bf16[4,144,128]{2,1,0:T(8,128)(2,1)S(1)} %collective-permute-done.8.got1_ref) | copy-start | bytes 442372
  124.9 1.4 copy-start.1
  129.5 27.7 %all-to-all-start.3 = ((bf16[8,16,2048]{2,1,0:T(8,128)(2,1)}), bf16[8,16,2048]{2,1,0:T(8,128)(2,1)S(1)}, u32[]{:S(2)}, u32[]{:S(2)}) async-start(bf16[8,16,2048]{2,1,0:T(8,128)(2,1)} %combine.1), calls=%async_computation.3 | async-start | bytes 1048576 | tf_op jit(solution)/shard_map/all_to_all | solution.py:60
  139.6 10.7 %collective-permute-start.13 = (bf16[1,144,128]{2,1,0:T(8,128)(2,1)S(1)}, bf16[1,144,128]{2,1,0:T(8,128)(2,1)S(1)}, u32[]{:S(2)}, u32[]{:S(2)}) collective-permute-start(bf16[1,144,128]{2,1,0:T(8,128)(2,1)S(1)} %get-tuple-element.28), channel_id=1, source_target_pairs={{0,96},{1,97},{2,98},{3,99},{4,100},{5,101},{6,102},{7,103},{8,104... | collective-permute-start | bytes 110600 | tf_op jit(solution)/shard_map/ppermute | solution.py:70
  145.3 6.8 %collective-permute-start.12 = (bf16[1,144,128]{2,1,0:T(8,128)(2,1)S(1)}, bf16[1,144,128]{2,1,0:T(8,128)(2,1)S(1)}, u32[]{:S(2)}, u32[]{:S(2)}) collective-permute-start(bf16[1,144,128]{2,1,0:T(8,128)(2,1)S(1)} %get-tuple-element.29), channel_id=1, source_target_pairs={{0,64},{1,65},{2,66},{3,67},{4,68},{5,69},{6,70},{7,71},{8,72},{9,... | collective-permute-start | bytes 110600 | tf_op jit(solution)/shard_map/ppermute | solution.py:70
  147.2 7.7 %collective-permute-start.11 = (bf16[1,144,128]{2,1,0:T(8,128)(2,1)S(1)}, bf16[1,144,128]{2,1,0:T(8,128)(2,1)S(1)}, u32[]{:S(2)}, u32[]{:S(2)}) collective-permute-start(bf16[1,144,128]{2,1,0:T(8,128)(2,1)S(1)} %get-tuple-element.30), channel_id=1, source_target_pairs={{0,32},{1,33},{2,34},{3,35},{4,36},{5,37},{6,38},{7,39},{8,40},{9,... | collective-permute-start | bytes 110600 | tf_op jit(solution)/shard_map/ppermute | solution.py:70
  150.3 4.6 %copy-start.9 = (bf16[1,144,128]{2,1,0:T(8,128)(2,1)}, bf16[1,144,128]{2,1,0:T(8,128)(2,1)S(1)}, u32[]{:S(2)}) copy-start(bf16[1,144,128]{2,1,0:T(8,128)(2,1)S(1)} %collective-permute-done.13.got3_ref) | copy-start | bytes 110596
  152.1 2.8 %copy-start.10 = (bf16[1,144,128]{2,1,0:T(8,128)(2,1)}, bf16[1,144,128]{2,1,0:T(8,128)(2,1)S(1)}, u32[]{:S(2)}) copy-start(bf16[1,144,128]{2,1,0:T(8,128)(2,1)S(1)} %collective-permute-done.12.got2_ref) | copy-start | bytes 110596
  154.9 0.6 copy-start.11
  157.2 0.8 copy-start.3

commit v6 on v5

--- a/solution.py
+++ b/solution.py
@@ -70,6 +70,14 @@
     return lax.ppermute(array, AXIS, pairs)
 
 
+def doubled(array, fx=0, fz=0):
+    pairs = []
+    for device in range(512):
+        x, zl, y, zh, c = position(device)
+        pairs.append((device, number(x ^ fx, zl ^ fz, y, zh, c)))
+    return jnp.concatenate([array, lax.ppermute(array, AXIS, pairs)], axis=0)
+
+
 def iota(shape, dim):
     return lax.broadcasted_iota(jnp.int32, shape, dim)
 
@@ -239,17 +247,18 @@
     return best, sums, acc
 
 
-def merge_kernel(got0_ref, got1_ref, got2_ref, got3_ref, send_ref):
+def merge_kernel(got0_ref, got1_ref, got2_ref, got3_ref, *sends):
     refs = (got0_ref, got1_ref, got2_ref, got3_ref)
     for r in range(SIDE):
         write_states(
-            send_ref,
-            r,
+            sends[r],
+            0,
             [merged([read_state(ref, r, i) for ref in refs]) for i in range(REQUESTS)],
         )
 
 
-def partial_kernel(owner_ref, count_ref, query_ref, pool_ref, send_ref, top_ref, sum_ref, acc_ref):
+def partial_kernel(owner_ref, count_ref, query_ref, pool_ref, *refs):
+    sends, (top_ref, sum_ref, acc_ref) = refs[:SIDE], refs[SIDE:]
     scale = 1.0 / math.sqrt(HEAD)
     top_ref[...] = jnp.full(top_ref.shape, NEG, F32)
     sum_ref[...] = jnp.zeros(sum_ref.shape, F32)
@@ -261,7 +270,8 @@
     for b in range(BLOCKS):
         owner = owner_ref[b]
         ax, az, request = owner >> 3, (owner >> 1) & 3, owner & 1
-        asked = ((x - ax) & 3) * 8 + ((zl - az) & 3) * 2 + request
+        fx, fz = ax ^ x, az ^ zl
+        asked = (fz & 1) * 16 + (fz >> 1) * 8 + (fx & 1) * 4 + (fx >> 1) * 2 + request
         state = ((ax - x) & 3) * 8 + ((az - zl) & 3) * 2 + request
         rows = pl.ds(pl.multiple_of(state * HEADS, HEADS), HEADS)
         query = query_ref[pl.ds(pl.multiple_of(asked * HEADS, HEADS), HEADS), :]
@@ -298,7 +308,7 @@
             at = (r * REQUESTS + i) * HEADS
             rows = slice(at, at + HEADS)
             states.append((top_ref[rows, :], sum_ref[rows, :], acc_ref[rows, :]))
-        write_states(send_ref, r, states)
+        write_states(sends[r // SIDE], r % SIDE, states)
 
 
 def partial_attention(owner, count, queries, pool):
@@ -306,9 +316,10 @@
     return call(
         partial_kernel,
         "partial_attention",
-        shape((SIDE * SIDE, MESSAGE, HEAD)),
+        [shape((SIDE, MESSAGE, HEAD))] * SIDE,
         4,
         in_specs=[smem, smem] + whole(2),
+        out_specs=whole(SIDE),
         scratch_shapes=[pltpu.VMEM((SIDE * SIDE * REQUESTS * HEADS, HEAD), F32)] * 3,
     )(owner, count, queries, pool)
 
@@ -341,8 +352,8 @@
         out_ref[:, h * HEAD : (h + 1) * HEAD] = pair.astype(BF16)
 
 
-def along(array, axis):
-    return [array] + [moved(array, **{axis: k}) for k in range(1, SIDE)]
+def spread(arrays, axis):
+    return [moved(array, **{axis: k}) if k else array for k, array in enumerate(arrays)]
 
 
 def shards(
@@ -363,32 +374,36 @@
         moe_input, expert_ids.T, route_weight.T
     )
     own_queries = queries.reshape(REQUESTS * HEADS, HEAD)
-    line = jnp.concatenate(along(own_queries, "dz"), axis=0)
     near = exchange(packed, RING_GROUPS)
-    near, line = lax.optimization_barrier((near, line))
+    all_queries = doubled(doubled(own_queries, fx=2), fx=1)
+    all_queries = doubled(doubled(all_queries, fz=2), fz=1)
+    near, all_queries = lax.optimization_barrier((near, all_queries))
     send = call(dispatch_kernel, "dispatch", shape((REACH, ROWS, D)), 2)(near, slot_row)
     received = exchange(send, REACH_GROUPS)
 
     other_gate_up, other_down = moved(w_gate_up, dc=1), moved(w_down, dc=1)
-    all_queries = jnp.concatenate(along(line, "dx"), axis=0)
-    received, all_queries = lax.optimization_barrier((received, all_queries))
+    partials = partial_attention(block_owner, block_tokens, all_queries, key_value_pool)
+    across = spread(partials, "dx")
     rows = expert(
         received.reshape(REACH * ROWS, D), w_gate_up, other_gate_up, w_down, other_down
     )
-    rows, block_owner = lax.optimization_barrier((rows, block_owner))
+    rows, across = lax.optimization_barrier((rows, across))
     returned = exchange(rows.reshape(REACH, ROWS, D), REACH_GROUPS)
-    partials = partial_attention(block_owner, block_tokens, all_queries, key_value_pool)
-    partials = partials.reshape(SIDE, SIDE, MESSAGE, HEAD)
-    got = [partials[0]] + [moved(partials[k], dx=k) for k in range(1, SIDE)]
+
     mix = call(mixing_kernel, "mixing", shape((2 * NEAR, REACH * ROWS)), 2)(near, slot_row)
-    returned, got = lax.optimization_barrier((returned, got))
-
+    met = call(
+        merge_kernel,
+        "merge",
+        [shape((1, MESSAGE, HEAD))] * SIDE,
+        4,
+        out_specs=whole(SIDE),
+    )(*across)
+    met = spread(met, "dz")
     parts = call(combine_kernel, "combine", shape((RING, TOK, D)), 2)(mix, returned)
+    parts, met = lax.optimization_barrier((parts, met))
     parts = exchange(parts, RING_GROUPS)
-    send = call(merge_kernel, "merge", shape((SIDE, MESSAGE, HEAD)), 4)(*got)
-    got = [send[:1]] + [moved(send[k : k + 1], dz=k) for k in range(1, SIDE)]
     attn_out = call(finish_kernel, "finish", shape((REQUESTS, HEADS * HEAD)), 6)(
-        *got, own_queries, incoming_key_value
+        *met, own_queries, incoming_key_value
     )
     moe_out = call(total_kernel, "total", shape((TOK, D)), 1)(parts)
     return (moe_out, attn_out)

time: 161 us -> 161 us (level)
  the two profiles are of different devices: /device:TPU:26 before, /device:TPU:8 now
where the time goes in v6:
time: 161 us; the launch traced here: 160 us
  starting transfers between devices  72.6 us (45%)
  waiting for transfers between devices  48.5 us (30%)
  Pallas kernels  31.1 us (19%)
  local copies, waits for them, and re-layouts  6.81 us (4%)
    all_to_all x4, starting transfers between devices, exchange(): lax.all_to_all(array, AXIS, split_axis=0, concat_axis=0, axis_index_group...  33.1 us
    all_to_all x4, waiting for transfers between devices, exchange(): lax.all_to_all(array, AXIS, split_axis=0, concat_axis=0, axis_index_group...  33 us
    ppermute x8, starting transfers between devices, moved(): return lax.ppermute(array, AXIS, pairs)  25.4 us
    ppermute x4, waiting for transfers between devices, doubled(): return jnp.concatenate([array, lax.ppermute(array, AXIS, pairs)], axis=0)  15.5 us
    ppermute x4, starting transfers between devices, doubled(): return jnp.concatenate([array, lax.ppermute(array, AXIS, pairs)], axis=0)  14.2 us
    pallas_call x1, Pallas kernels, expert(): call(expert_kernel, 'expert', shape(rows.shape), 5, grid=(rows.shape[0] /...  7.54 us
    pallas_call x1, Pallas kernels, partial_attention(): call(partial_kernel, 'partial_attention', [shape((SIDE, MESSAGE, HEAD))]...  6.98 us
    unnamed x32, local copies, waits for them, and re-layouts  5.98 us
  transfers between devices with their start and end apart: 16, of which 6 were waited for; matrix products, arithmetic and copies ran while one was open for 0% of the time, Pallas kernels for 16%

profile of v6, /device:TPU:8, one launch (start us, length us, event | category | flops | bytes accessed | tf_op | source)
XLA Modules:
  0.0 160.1 jit_solution(966542783332513374)
XLA Ops:
  1.4 4.9 %collective-permute-start = (bf16[128,128]{1,0:T(8,128)(2,1)S(1)}, bf16[128,128]{1,0:T(8,128)(2,1)S(1)}, u32[]{:S(2)}, u32[]{:S(2)}) collective-permute-start(bf16[128,128]{1,0:T(8,128)(2,1)S(1)} %reshape.16.query_ref), channel_id=1, source_target_pairs={{0,256},{1,257},{2,258},{3,259},{4,260},{5,261},{6,262},{7,263},{8... | collective-permute-start | bytes 98312 | tf_op jit(solution)/shard_map/ppermute | solution.py:78
  6.4 1.8 %pack.1 = bf16[8,16,2304]{2,1,0:T(8,128)(2,1)} custom-call(bf16[16,2048]{1,0:T(8,128)(2,1)} %token_ref.1, s32[8,16]{1,0:T(8,128)} %bitcast.7, f32[8,16]{1,0:T(8,128)} %bitcast.8), custom_call_target="tpu_custom_call" | custom-call | tf_op jit(solution)/shard_map/pack/pallas_call | solution.py:373
  8.2 10.3 %all-to-all-start = ((bf16[8,16,2304]{2,1,0:T(8,128)(2,1)}), bf16[8,16,2304]{2,1,0:T(8,128)(2,1)S(1)}, u32[]{:S(2)}, u32[]{:S(2)}) async-start(bf16[8,16,2304]{2,1,0:T(8,128)(2,1)} %pack.1), calls=%async_computation | async-start | bytes 1179648 | tf_op jit(solution)/shard_map/all_to_all | solution.py:60
  18.5 2.5 %collective-permute-start.1 = (bf16[256,128]{1,0:T(8,128)(2,1)S(1)}, bf16[256,128]{1,0:T(8,128)(2,1)S(1)}, u32[]{:S(2)}, u32[]{:S(2)}) collective-permute-start(bf16[256,128]{1,0:T(8,128)(2,1)S(1)} %pad_maximum_fusion.2), channel_id=1, source_target_pairs={{0,128},{1,129},{2,130},{3,131},{4,132},{5,133},{6,134},{7,135},{8... | collective-permute-start | bytes 196616 | tf_op jit(solution)/shard_map/ppermute | solution.py:78
  21.0 3.7 %collective-permute-done.1 = bf16[256,128]{1,0:T(8,128)(2,1)S(1)} collective-permute-done((bf16[256,128]{1,0:T(8,128)(2,1)S(1)}, bf16[256,128]{1,0:T(8,128)(2,1)S(1)}, u32[]{:S(2)}, u32[]{:S(2)}) %collective-permute-start.1) | collective-permute-done | bytes 65568 | tf_op jit(solution)/shard_map/ppermute | solution.py:78
  24.7 4.8 %collective-permute-start.2 = (bf16[512,128]{1,0:T(8,128)(2,1)S(1)}, bf16[512,128]{1,0:T(8,128)(2,1)S(1)}, u32[]{:S(2)}, u32[]{:S(2)}) collective-permute-start(bf16[512,128]{1,0:T(8,128)(2,1)S(1)} %pad_maximum_fusion.1), channel_id=1, source_target_pairs={{0,64},{1,65},{2,66},{3,67},{4,68},{5,69},{6,70},{7,71},{8,72},{9,... | collective-permute-start | bytes 393224 | tf_op jit(solution)/shard_map/ppermute | solution.py:78
  29.5 5.6 %collective-permute-done.2 = bf16[512,128]{1,0:T(8,128)(2,1)S(1)} collective-permute-done((bf16[512,128]{1,0:T(8,128)(2,1)S(1)}, bf16[512,128]{1,0:T(8,128)(2,1)S(1)}, u32[]{:S(2)}, u32[]{:S(2)}) %collective-permute-start.2) | collective-permute-done | bytes 131104 | tf_op jit(solution)/shard_map/ppermute | solution.py:78
  35.2 1.9 %collective-permute-start.3 = (bf16[1024,128]{1,0:T(8,128)(2,1)S(1)}, bf16[1024,128]{1,0:T(8,128)(2,1)S(1)}, u32[]{:S(2)}, u32[]{:S(2)}) collective-permute-start(bf16[1024,128]{1,0:T(8,128)(2,1)S(1)} %pad_maximum_fusion), channel_id=1, source_target_pairs={{0,32},{1,33},{2,34},{3,35},{4,36},{5,37},{6,38},{7,39},{8,40},{9,... | collective-permute-start | bytes 786440 | tf_op jit(solution)/shard_map/ppermute | solution.py:78
  37.2 6.3 %collective-permute-done.3 = bf16[1024,128]{1,0:T(8,128)(2,1)S(1)} collective-permute-done((bf16[1024,128]{1,0:T(8,128)(2,1)S(1)}, bf16[1024,128]{1,0:T(8,128)(2,1)S(1)}, u32[]{:S(2)}, u32[]{:S(2)}) %collective-permute-start.3) | collective-permute-done | bytes 262176 | tf_op jit(solution)/shard_map/ppermute | solution.py:78
  44.3 3.4 %dispatch.1 = bf16[32,16,2048]{2,1,0:T(8,128)(2,1)} custom-call(bf16[8,16,2304]{2,1,0:T(8,128)(2,1)} %copy-done.2, s32[1,128]{1,0:T(1,128)} %bitcast.9), custom_call_target="tpu_custom_call" | custom-call | tf_op jit(solution)/shard_map/dispatch/pallas_call | solution.py:381
  47.7 8.4 %all-to-all-start.1 = ((bf16[32,16,2048]{2,1,0:T(8,128)(2,1)}), bf16[32,16,2048]{2,1,0:T(8,128)(2,1)S(1)}, u32[]{:S(2)}, u32[]{:S(2)}) async-start(bf16[32,16,2048]{2,1,0:T(8,128)(2,1)} %dispatch.1), calls=%async_computation.1 | async-start | bytes 4194304 | tf_op jit(solution)/shard_map/all_to_all | solution.py:60
  56.2 1.9 %collective-permute-start.4 = (bf16[2048,384]{1,0:T(8,128)(2,1)}, bf16[2048,384]{1,0:T(8,128)(2,1)}, u32[]{:S(2)}, u32[]{:S(2)}) collective-permute-start(bf16[2048,384]{1,0:T(8,128)(2,1)} %gate_up_ref.1), channel_id=1, source_target_pairs={{0,1},{1,0},{2,3},{3,2},{4,5},{5,4},{6,7},{7,6},{8,9},{9,8},{10,11... | collective-permute-start | bytes 4718600 | tf_op jit(solution)/shard_map/ppermute | solution.py:70
  58.1 2.4 %collective-permute-start.5 = (bf16[192,2048]{1,0:T(8,128)(2,1)S(1)}, bf16[192,2048]{1,0:T(8,128)(2,1)S(1)}, u32[]{:S(2)}, u32[]{:S(2)}) collective-permute-start(bf16[192,2048]{1,0:T(8,128)(2,1)S(1)} %copy-done.5), channel_id=1, source_target_pairs={{0,1},{1,0},{2,3},{3,2},{4,5},{5,4},{6,7},{7,6},{8,9},{9,8},{10,11... | collective-permute-start | bytes 2359304 | tf_op jit(solution)/shard_map/ppermute | solution.py:70
  60.5 7.0 %partial_attention.1 = (bf16[4,144,128]{2,1,0:T(8,128)(2,1)}, bf16[4,144,128]{2,1,0:T(8,128)(2,1)}, bf16[4,144,128]{2,1,0:T(8,128)(2,1)}, bf16[4,144,128]{2,1,0:T(8,128)(2,1)}) custom-call(s32[16]{0:T(128)} %owner_ref.1, s32[16]{0:T(128)} %count_ref.1, bf16[2048,128]{1,0:T(8,128)(2,1)} %copy-done.7, bf16[16,64,1024]{2,1,0:T(8,128)(2,1)} %pool_ref.1), custom_call_target="tpu_custom_call" | custom-call | tf_op jit(solution)/shard_map/partial_attention/pallas_call | solution.py:316
  67.5 3.4 %collective-permute-start.6 = (bf16[4,144,128]{2,1,0:T(8,128)(2,1)}, bf16[4,144,128]{2,1,0:T(8,128)(2,1)S(1)}, u32[]{:S(2)}, u32[]{:S(2)}) collective-permute-start(bf16[4,144,128]{2,1,0:T(8,128)(2,1)} %get-tuple-element.25), channel_id=1, source_target_pairs={{0,128},{1,129},{2,130},{3,131},{4,132},{5,133},{6,134},{7,135},{8... | collective-permute-start | bytes 442376 | tf_op jit(solution)/shard_map/ppermute | solution.py:70
  70.9 4.6 %collective-permute-start.7 = (bf16[4,144,128]{2,1,0:T(8,128)(2,1)}, bf16[4,144,128]{2,1,0:T(8,128)(2,1)S(1)}, u32[]{:S(2)}, u32[]{:S(2)}) collective-permute-start(bf16[4,144,128]{2,1,0:T(8,128)(2,1)} %get-tuple-element.26), channel_id=1, source_target_pairs={{0,256},{1,257},{2,258},{3,259},{4,260},{5,261},{6,262},{7,263},{8... | collective-permute-start | bytes 442376 | tf_op jit(solution)/shard_map/ppermute | solution.py:70
  75.5 3.3 %collective-permute-start.8 = (bf16[4,144,128]{2,1,0:T(8,128)(2,1)}, bf16[4,144,128]{2,1,0:T(8,128)(2,1)S(1)}, u32[]{:S(2)}, u32[]{:S(2)}) collective-permute-start(bf16[4,144,128]{2,1,0:T(8,128)(2,1)} %get-tuple-element.27), channel_id=1, source_target_pairs={{0,384},{1,385},{2,386},{3,387},{4,388},{5,389},{6,390},{7,391},{8... | collective-permute-start | bytes 442376 | tf_op jit(solution)/shard_map/ppermute | solution.py:70
  79.7 6.2 %all-to-all-done.1 = bf16[32,16,2048]{2,1,0:T(8,128)(2,1)S(1)} async-done(((bf16[32,16,2048]{2,1,0:T(8,128)(2,1)}), bf16[32,16,2048]{2,1,0:T(8,128)(2,1)S(1)}, u32[]{:S(2)}, u32[]{:S(2)}) %all-to-all-start.1) | async-done | bytes 2097184 | tf_op jit(solution)/shard_map/all_to_all | solution.py:60
  87.2 7.5 %expert.1 = bf16[512,2048]{1,0:T(8,128)(2,1)} custom-call(bf16[512,2048]{1,0:T(8,128)(2,1)} %bitcast.6, bf16[2048,384]{1,0:T(8,128)(2,1)} %gate_up_ref.1, bf16[2048,384]{1,0:T(8,128)(2,1)} %collective-permute-done.4.other_gate_up_ref, bf16[192,2048]{1,0:T(8,128)(2,1)} %down_ref.1, bf16[192,2048]{1,0:T(8,128)(2,1)} %copy-done.6), custom_call_target="tpu_custom_call" | custom-call | tf_op jit(solution)/shard_map/expert/pallas_call | solution.py:205
  95.5 6.9 %all-to-all-start.2 = ((bf16[32,16,2048]{2,1,0:T(8,128)(2,1)}), bf16[32,16,2048]{2,1,0:T(8,128)(2,1)S(1)}, u32[]{:S(2)}, u32[]{:S(2)}) async-start(bf16[32,16,2048]{2,1,0:T(8,128)(2,1)} %bitcast.5), calls=%async_computation.2 | async-start | bytes 4194304 | tf_op jit(solution)/shard_map/all_to_all | solution.py:60
  102.4 2.4 %merge.1 = (bf16[1,144,128]{2,1,0:T(8,128)(2,1)}, bf16[1,144,128]{2,1,0:T(8,128)(2,1)}, bf16[1,144,128]{2,1,0:T(8,128)(2,1)}, bf16[1,144,128]{2,1,0:T(8,128)(2,1)}) custom-call(bf16[4,144,128]{2,1,0:T(8,128)(2,1)} %get-tuple-element.29.got0_ref, bf16[4,144,128]{2,1,0:T(8,128)(2,1)} %copy-done.8, bf16[4,144,128]{2,1,0:T(8,128)(2,1)} %copy-done.9, ...), custom_call_target="tpu_custom_call" | custom-call | tf_op jit(solution)/shard_map/merge/pallas_call | solution.py:394
  104.8 1.9 %collective-permute-start.9 = (bf16[1,144,128]{2,1,0:T(8,128)(2,1)}, bf16[1,144,128]{2,1,0:T(8,128)(2,1)S(1)}, u32[]{:S(2)}, u32[]{:S(2)}) collective-permute-start(bf16[1,144,128]{2,1,0:T(8,128)(2,1)} %get-tuple-element.34), channel_id=1, source_target_pairs={{0,32},{1,33},{2,34},{3,35},{4,36},{5,37},{6,38},{7,39},{8,40},{9,... | collective-permute-start | bytes 110600 | tf_op jit(solution)/shard_map/ppermute | solution.py:70
  106.8 5.9 %collective-permute-start.10 = (bf16[1,144,128]{2,1,0:T(8,128)(2,1)}, bf16[1,144,128]{2,1,0:T(8,128)(2,1)S(1)}, u32[]{:S(2)}, u32[]{:S(2)}) collective-permute-start(bf16[1,144,128]{2,1,0:T(8,128)(2,1)} %get-tuple-element.35), channel_id=1, source_target_pairs={{0,64},{1,65},{2,66},{3,67},{4,68},{5,69},{6,70},{7,71},{8,72},{9,... | collective-permute-start | bytes 110600 | tf_op jit(solution)/shard_map/ppermute | solution.py:70
  112.7 1.9 %collective-permute-start.11 = (bf16[1,144,128]{2,1,0:T(8,128)(2,1)}, bf16[1,144,128]{2,1,0:T(8,128)(2,1)S(1)}, u32[]{:S(2)}, u32[]{:S(2)}) collective-permute-start(bf16[1,144,128]{2,1,0:T(8,128)(2,1)} %get-tuple-element.36), channel_id=1, source_target_pairs={{0,96},{1,97},{2,98},{3,99},{4,100},{5,101},{6,102},{7,103},{8,104... | collective-permute-start | bytes 110600 | tf_op jit(solution)/shard_map/ppermute | solution.py:70
  114.6 2.3 %mixing.1.mix_ref = bf16[256,512]{1,0:T(8,128)(2,1)} custom-call(bf16[8,16,2304]{2,1,0:T(8,128)(2,1)} %copy-done.2, s32[1,128]{1,0:T(1,128)} %bitcast.10), custom_call_target="tpu_custom_call" | custom-call | tf_op jit(solution)/shard_map/mixing/pallas_call | solution.py:393
  116.9 15.3 %all-to-all-done.2.rows_ref = bf16[32,16,2048]{2,1,0:T(8,128)(2,1)S(1)} async-done(((bf16[32,16,2048]{2,1,0:T(8,128)(2,1)}), bf16[32,16,2048]{2,1,0:T(8,128)(2,1)S(1)}, u32[]{:S(2)}, u32[]{:S(2)}) %all-to-all-start.2) | async-done | bytes 2097184 | tf_op jit(solution)/shard_map/all_to_all | solution.py:60
  132.2 1.3 copy-done.1
  133.5 3.2 %combine.1 = bf16[8,16,2048]{2,1,0:T(8,128)(2,1)} custom-call(bf16[256,512]{1,0:T(8,128)(2,1)} %mixing.1.mix_ref, bf16[32,16,2048]{2,1,0:T(8,128)(2,1)} %copy-done.1), custom_call_target="tpu_custom_call" | custom-call | tf_op jit(solution)/shard_map/combine/pallas_call | solution.py:402
  136.8 7.5 %all-to-all-start.3 = ((bf16[8,16,2048]{2,1,0:T(8,128)(2,1)}), bf16[8,16,2048]{2,1,0:T(8,128)(2,1)S(1)}, u32[]{:S(2)}, u32[]{:S(2)}) async-start(bf16[8,16,2048]{2,1,0:T(8,128)(2,1)} %combine.1), calls=%async_computation.3 | async-start | bytes 1048576 | tf_op jit(solution)/shard_map/all_to_all | solution.py:60
  144.3 1.7 %finish.1 = bf16[2,8192]{1,0:T(2,128)(2,1)} custom-call(bf16[1,144,128]{2,1,0:T(8,128)(2,1)} %get-tuple-element.38.got0_ref, bf16[1,144,128]{2,1,0:T(8,128)(2,1)} %copy-done.11, bf16[1,144,128]{2,1,0:T(8,128)(2,1)} %copy-done.12, bf16[1,144,128]{2,1,0:T(8,128)(2,1)} %copy-done.13, bf16[128,128]{1,0:T(8,128)(2,1)} %copy-done.4, bf16[2,1024]{1,0:T(2,128)(2,1)} %new_ref.1), custom_call_target="tpu_custom_call" | custom-call | tf_op jit(solution)/shard_map/finish/pallas_call | solution.py:405
  146.0 11.5 %all-to-all-done.3.parts_ref = bf16[8,16,2048]{2,1,0:T(8,128)(2,1)S(1)} async-done(((bf16[8,16,2048]{2,1,0:T(8,128)(2,1)}), bf16[8,16,2048]{2,1,0:T(8,128)(2,1)S(1)}, u32[]{:S(2)}, u32[]{:S(2)}) %all-to-all-start.3) | async-done | bytes 524320 | tf_op jit(solution)/shard_map/all_to_all | solution.py:60
  158.3 1.7 %total.1 = bf16[16,2048]{1,0:T(8,128)(2,1)} custom-call(bf16[8,16,2048]{2,1,0:T(8,128)(2,1)} %copy-done.3), custom_call_target="tpu_custom_call" | custom-call | tf_op jit(solution)/shard_map/total/pallas_call | solution.py:408
  (46 shorter events, 5.5 us)
Async XLA Ops:
  1.4 46.3 %copy-start.4 = (bf16[128,128]{1,0:T(8,128)(2,1)}, bf16[128,128]{1,0:T(8,128)(2,1)S(1)}, u32[]{:S(2)}) copy-start(bf16[128,128]{1,0:T(8,128)(2,1)S(1)} %reshape.16.query_ref) | copy-start | bytes 98308
  1.4 17.1 %collective-permute-start = (bf16[128,128]{1,0:T(8,128)(2,1)S(1)}, bf16[128,128]{1,0:T(8,128)(2,1)S(1)}, u32[]{:S(2)}, u32[]{:S(2)}) collective-permute-start(bf16[128,128]{1,0:T(8,128)(2,1)S(1)} %reshape.16.query_ref), channel_id=1, source_target_pairs={{0,256},{1,257},{2,258},{3,259},{4,260},{5,261},{6,262},{7,263},{8... | collective-permute-start | bytes 98312 | tf_op jit(solution)/shard_map/ppermute | solution.py:78
  8.2 35.3 %all-to-all-start = ((bf16[8,16,2304]{2,1,0:T(8,128)(2,1)}), bf16[8,16,2304]{2,1,0:T(8,128)(2,1)S(1)}, u32[]{:S(2)}, u32[]{:S(2)}) async-start(bf16[8,16,2304]{2,1,0:T(8,128)(2,1)} %pack.1), calls=%async_computation | async-start | bytes 1179648 | tf_op jit(solution)/shard_map/all_to_all | solution.py:60
  18.5 6.2 %collective-permute-start.1 = (bf16[256,128]{1,0:T(8,128)(2,1)S(1)}, bf16[256,128]{1,0:T(8,128)(2,1)S(1)}, u32[]{:S(2)}, u32[]{:S(2)}) collective-permute-start(bf16[256,128]{1,0:T(8,128)(2,1)S(1)} %pad_maximum_fusion.2), channel_id=1, source_target_pairs={{0,128},{1,129},{2,130},{3,131},{4,132},{5,133},{6,134},{7,135},{8... | collective-permute-start | bytes 196616 | tf_op jit(solution)/shard_map/ppermute | solution.py:78
  24.7 10.5 %collective-permute-start.2 = (bf16[512,128]{1,0:T(8,128)(2,1)S(1)}, bf16[512,128]{1,0:T(8,128)(2,1)S(1)}, u32[]{:S(2)}, u32[]{:S(2)}) collective-permute-start(bf16[512,128]{1,0:T(8,128)(2,1)S(1)} %pad_maximum_fusion.1), channel_id=1, source_target_pairs={{0,64},{1,65},{2,66},{3,67},{4,68},{5,69},{6,70},{7,71},{8,72},{9,... | collective-permute-start | bytes 393224 | tf_op jit(solution)/shard_map/ppermute | solution.py:78
  35.2 8.3 %collective-permute-start.3 = (bf16[1024,128]{1,0:T(8,128)(2,1)S(1)}, bf16[1024,128]{1,0:T(8,128)(2,1)S(1)}, u32[]{:S(2)}, u32[]{:S(2)}) collective-permute-start(bf16[1024,128]{1,0:T(8,128)(2,1)S(1)} %pad_maximum_fusion), channel_id=1, source_target_pairs={{0,32},{1,33},{2,34},{3,35},{4,36},{5,37},{6,38},{7,39},{8,40},{9,... | collective-permute-start | bytes 786440 | tf_op jit(solution)/shard_map/ppermute | solution.py:78
  43.5 17.0 %copy-start.7 = (bf16[2048,128]{1,0:T(8,128)(2,1)}, bf16[2048,128]{1,0:T(8,128)(2,1)S(1)}, u32[]{:S(2)}) copy-start(bf16[2048,128]{1,0:T(8,128)(2,1)S(1)} %constant_dynamic-update-slice_fusion.query_ref) | copy-start | bytes 1572868
  43.5 0.9 copy-start.2
  47.7 10.4 %copy-start.5 = (bf16[192,2048]{1,0:T(8,128)(2,1)S(1)}, bf16[192,2048]{1,0:T(8,128)(2,1)}, u32[]{:S(2)}) copy-start(bf16[192,2048]{1,0:T(8,128)(2,1)} %down_ref.1) | copy-start | bytes 2359300
  47.7 38.2 %all-to-all-start.1 = ((bf16[32,16,2048]{2,1,0:T(8,128)(2,1)}), bf16[32,16,2048]{2,1,0:T(8,128)(2,1)S(1)}, u32[]{:S(2)}, u32[]{:S(2)}) async-start(bf16[32,16,2048]{2,1,0:T(8,128)(2,1)} %dispatch.1), calls=%async_computation.1 | async-start | bytes 4194304 | tf_op jit(solution)/shard_map/all_to_all | solution.py:60
  56.2 23.6 %collective-permute-start.4 = (bf16[2048,384]{1,0:T(8,128)(2,1)}, bf16[2048,384]{1,0:T(8,128)(2,1)}, u32[]{:S(2)}, u32[]{:S(2)}) collective-permute-start(bf16[2048,384]{1,0:T(8,128)(2,1)} %gate_up_ref.1), channel_id=1, source_target_pairs={{0,1},{1,0},{2,3},{3,2},{4,5},{5,4},{6,7},{7,6},{8,9},{9,8},{10,11... | collective-permute-start | bytes 4718600 | tf_op jit(solution)/shard_map/ppermute | solution.py:70
  58.1 20.8 %collective-permute-start.5 = (bf16[192,2048]{1,0:T(8,128)(2,1)S(1)}, bf16[192,2048]{1,0:T(8,128)(2,1)S(1)}, u32[]{:S(2)}, u32[]{:S(2)}) collective-permute-start(bf16[192,2048]{1,0:T(8,128)(2,1)S(1)} %copy-done.5), channel_id=1, source_target_pairs={{0,1},{1,0},{2,3},{3,2},{4,5},{5,4},{6,7},{7,6},{8,9},{9,8},{10,11... | collective-permute-start | bytes 2359304 | tf_op jit(solution)/shard_map/ppermute | solution.py:70
  67.5 27.3 %collective-permute-start.6 = (bf16[4,144,128]{2,1,0:T(8,128)(2,1)}, bf16[4,144,128]{2,1,0:T(8,128)(2,1)S(1)}, u32[]{:S(2)}, u32[]{:S(2)}) collective-permute-start(bf16[4,144,128]{2,1,0:T(8,128)(2,1)} %get-tuple-element.25), channel_id=1, source_target_pairs={{0,128},{1,129},{2,130},{3,131},{4,132},{5,133},{6,134},{7,135},{8... | collective-permute-start | bytes 442376 | tf_op jit(solution)/shard_map/ppermute | solution.py:70
  70.9 23.9 %collective-permute-start.7 = (bf16[4,144,128]{2,1,0:T(8,128)(2,1)}, bf16[4,144,128]{2,1,0:T(8,128)(2,1)S(1)}, u32[]{:S(2)}, u32[]{:S(2)}) collective-permute-start(bf16[4,144,128]{2,1,0:T(8,128)(2,1)} %get-tuple-element.26), channel_id=1, source_target_pairs={{0,256},{1,257},{2,258},{3,259},{4,260},{5,261},{6,262},{7,263},{8... | collective-permute-start | bytes 442376 | tf_op jit(solution)/shard_map/ppermute | solution.py:70
  75.5 19.3 %collective-permute-start.8 = (bf16[4,144,128]{2,1,0:T(8,128)(2,1)}, bf16[4,144,128]{2,1,0:T(8,128)(2,1)S(1)}, u32[]{:S(2)}, u32[]{:S(2)}) collective-permute-start(bf16[4,144,128]{2,1,0:T(8,128)(2,1)} %get-tuple-element.27), channel_id=1, source_target_pairs={{0,384},{1,385},{2,386},{3,387},{4,388},{5,389},{6,390},{7,391},{8... | collective-permute-start | bytes 442376 | tf_op jit(solution)/shard_map/ppermute | solution.py:70
  78.9 0.9 copy-start.6
  85.9 1.3 copy-start
  94.8 0.7 copy-start.8
  94.8 0.7 copy-start.9
  94.8 0.7 copy-start.10
  95.5 36.6 %all-to-all-start.2 = ((bf16[32,16,2048]{2,1,0:T(8,128)(2,1)}), bf16[32,16,2048]{2,1,0:T(8,128)(2,1)S(1)}, u32[]{:S(2)}, u32[]{:S(2)}) async-start(bf16[32,16,2048]{2,1,0:T(8,128)(2,1)} %bitcast.5), calls=%async_computation.2 | async-start | bytes 4194304 | tf_op jit(solution)/shard_map/all_to_all | solution.py:60
  104.8 31.9 %collective-permute-start.9 = (bf16[1,144,128]{2,1,0:T(8,128)(2,1)}, bf16[1,144,128]{2,1,0:T(8,128)(2,1)S(1)}, u32[]{:S(2)}, u32[]{:S(2)}) collective-permute-start(bf16[1,144,128]{2,1,0:T(8,128)(2,1)} %get-tuple-element.34), channel_id=1, source_target_pairs={{0,32},{1,33},{2,34},{3,35},{4,36},{5,37},{6,38},{7,39},{8,40},{9,... | collective-permute-start | bytes 110600 | tf_op jit(solution)/shard_map/ppermute | solution.py:70
  106.8 30.0 %collective-permute-start.10 = (bf16[1,144,128]{2,1,0:T(8,128)(2,1)}, bf16[1,144,128]{2,1,0:T(8,128)(2,1)S(1)}, u32[]{:S(2)}, u32[]{:S(2)}) collective-permute-start(bf16[1,144,128]{2,1,0:T(8,128)(2,1)} %get-tuple-element.35), channel_id=1, source_target_pairs={{0,64},{1,65},{2,66},{3,67},{4,68},{5,69},{6,70},{7,71},{8,72},{9,... | collective-permute-start | bytes 110600 | tf_op jit(solution)/shard_map/ppermute | solution.py:70
  112.7 24.1 %collective-permute-start.11 = (bf16[1,144,128]{2,1,0:T(8,128)(2,1)}, bf16[1,144,128]{2,1,0:T(8,128)(2,1)S(1)}, u32[]{:S(2)}, u32[]{:S(2)}) collective-permute-start(bf16[1,144,128]{2,1,0:T(8,128)(2,1)} %get-tuple-element.36), channel_id=1, source_target_pairs={{0,96},{1,97},{2,98},{3,99},{4,100},{5,101},{6,102},{7,103},{8,104... | collective-permute-start | bytes 110600 | tf_op jit(solution)/shard_map/ppermute | solution.py:70
  132.2 1.3 copy-start.1
  136.7 7.5 %copy-start.11 = (bf16[1,144,128]{2,1,0:T(8,128)(2,1)}, bf16[1,144,128]{2,1,0:T(8,128)(2,1)S(1)}, u32[]{:S(2)}) copy-start(bf16[1,144,128]{2,1,0:T(8,128)(2,1)S(1)} %collective-permute-done.9.got1_ref) | copy-start | bytes 110596
  136.7 7.5 %copy-start.12 = (bf16[1,144,128]{2,1,0:T(8,128)(2,1)}, bf16[1,144,128]{2,1,0:T(8,128)(2,1)S(1)}, u32[]{:S(2)}) copy-start(bf16[1,144,128]{2,1,0:T(8,128)(2,1)S(1)} %collective-permute-done.10.got2_ref) | copy-start | bytes 110596
  136.8 7.5 %copy-start.13 = (bf16[1,144,128]{2,1,0:T(8,128)(2,1)}, bf16[1,144,128]{2,1,0:T(8,128)(2,1)S(1)}, u32[]{:S(2)}) copy-start(bf16[1,144,128]{2,1,0:T(8,128)(2,1)S(1)} %collective-permute-done.11.got3_ref) | copy-start | bytes 110596
  136.8 20.8 %all-to-all-start.3 = ((bf16[8,16,2048]{2,1,0:T(8,128)(2,1)}), bf16[8,16,2048]{2,1,0:T(8,128)(2,1)S(1)}, u32[]{:S(2)}, u32[]{:S(2)}) async-start(bf16[8,16,2048]{2,1,0:T(8,128)(2,1)} %combine.1), calls=%async_computation.3 | async-start | bytes 1048576 | tf_op jit(solution)/shard_map/all_to_all | solution.py:60
  157.5 0.8 copy-start.3

commit v7 on v6

--- a/solution.py
+++ b/solution.py
@@ -32,7 +32,7 @@
 
 F32 = jnp.float32
 BF16 = jnp.bfloat16
-VMEM_LIMIT = 56 * 1024 * 1024
+VMEM_LIMIT = 62 * 1024 * 1024
 AXIS = "d"
 
 
@@ -68,14 +68,6 @@
         x, zl, y, zh, c = position(device)
         pairs.append((device, number((x + dx) % 4, (zl + dz) % 4, y, zh, (c + dc) % 2)))
     return lax.ppermute(array, AXIS, pairs)
-
-
-def doubled(array, fx=0, fz=0):
-    pairs = []
-    for device in range(512):
-        x, zl, y, zh, c = position(device)
-        pairs.append((device, number(x ^ fx, zl ^ fz, y, zh, c)))
-    return jnp.concatenate([array, lax.ppermute(array, AXIS, pairs)], axis=0)
 
 
 def iota(shape, dim):
@@ -270,8 +262,7 @@
     for b in range(BLOCKS):
         owner = owner_ref[b]
         ax, az, request = owner >> 3, (owner >> 1) & 3, owner & 1
-        fx, fz = ax ^ x, az ^ zl
-        asked = (fz & 1) * 16 + (fz >> 1) * 8 + (fx & 1) * 4 + (fx >> 1) * 2 + request
+        asked = ((x - ax) & 3) * 8 + ((zl - az) & 3) * 2 + request
         state = ((ax - x) & 3) * 8 + ((az - zl) & 3) * 2 + request
         rows = pl.ds(pl.multiple_of(state * HEADS, HEADS), HEADS)
         query = query_ref[pl.ds(pl.multiple_of(asked * HEADS, HEADS), HEADS), :]
@@ -352,6 +343,10 @@
         out_ref[:, h * HEAD : (h + 1) * HEAD] = pair.astype(BF16)
 
 
+def along(array, axis):
+    return [array] + [moved(array, **{axis: k}) for k in range(1, SIDE)]
+
+
 def spread(arrays, axis):
     return [moved(array, **{axis: k}) if k else array for k, array in enumerate(arrays)]
 
@@ -375,22 +370,28 @@
     )
     own_queries = queries.reshape(REQUESTS * HEADS, HEAD)
     near = exchange(packed, RING_GROUPS)
-    all_queries = doubled(doubled(own_queries, fx=2), fx=1)
-    all_queries = doubled(doubled(all_queries, fz=2), fz=1)
-    near, all_queries = lax.optimization_barrier((near, all_queries))
+    line = jnp.concatenate(along(own_queries, "dz"), axis=0)
+    near, line = lax.optimization_barrier((near, line))
     send = call(dispatch_kernel, "dispatch", shape((REACH, ROWS, D)), 2)(near, slot_row)
     received = exchange(send, REACH_GROUPS)
 
     other_gate_up, other_down = moved(w_gate_up, dc=1), moved(w_down, dc=1)
-    partials = partial_attention(block_owner, block_tokens, all_queries, key_value_pool)
-    across = spread(partials, "dx")
+    square = along(line, "dx")
     rows = expert(
         received.reshape(REACH * ROWS, D), w_gate_up, other_gate_up, w_down, other_down
     )
-    rows, across = lax.optimization_barrier((rows, across))
+    rows, square = lax.optimization_barrier((rows, square))
     returned = exchange(rows.reshape(REACH, ROWS, D), REACH_GROUPS)
 
+    partials = partial_attention(
+        block_owner, block_tokens, jnp.concatenate(square, axis=0), key_value_pool
+    )
+    across = spread(partials, "dx")
     mix = call(mixing_kernel, "mixing", shape((2 * NEAR, REACH * ROWS)), 2)(near, slot_row)
+    parts = call(combine_kernel, "combine", shape((RING, TOK, D)), 2)(mix, returned)
+    parts, across = lax.optimization_barrier((parts, across))
+    parts = exchange(parts, RING_GROUPS)
+
     met = call(
         merge_kernel,
         "merge",
@@ -398,12 +399,8 @@
         4,
         out_specs=whole(SIDE),
     )(*across)
-    met = spread(met, "dz")
-    parts = call(combine_kernel, "combine", shape((RING, TOK, D)), 2)(mix, returned)
-    parts, met = lax.optimization_barrier((parts, met))
-    parts = exchange(parts, RING_GROUPS)
     attn_out = call(finish_kernel, "finish", shape((REQUESTS, HEADS * HEAD)), 6)(
-        *met, own_queries, incoming_key_value
+        *spread(met, "dz"), own_queries, incoming_key_value
     )
     moe_out = call(total_kernel, "total", shape((TOK, D)), 1)(parts)
     return (moe_out, attn_out)

time: 161 us -> 149 us (0.925)
  waiting for transfers between devices: 48.5 us -> 28 us
  starting transfers between devices: 72.6 us -> 82.2 us
  local copies, waits for them, and re-layouts: 6.81 us -> 3.89 us
  other arithmetic: 0.03 us -> 1.77 us
    ppermute x8 -> x14, starting transfers between devices: 25.4 us -> 49.2 us  [moved(): return lax.ppermute(array, AXIS, pairs)]
    ppermute x4 -> x0, waiting for transfers between devices: 15.5 us -> none  [doubled(): return jnp.concatenate([array, lax.ppermute(array, AXIS, pairs)], axis=0)]
    ppermute x4 -> x0, starting transfers between devices: 14.2 us -> none  [doubled(): return jnp.concatenate([array, lax.ppermute(array, AXIS, pairs)], axis=0)]
    all_to_all x4, waiting for transfers between devices: 33 us -> 20.8 us  [exchange(): lax.all_to_all(array, AXIS, split_axis=0, concat_axis=0, axis_index_group...]
    ppermute x8 -> x14, waiting for transfers between devices: 0.02 us -> 7.24 us  [moved(): return lax.ppermute(array, AXIS, pairs)]
    unnamed x32 -> x24, local copies, waits for them, and re-layouts: 5.98 us -> 3.1 us
    concatenate x3 -> x2, other arithmetic: 0.03 us -> 1.77 us  [the longest x1 1.76 us: shards(): jnp.concatenate(square, axis=0)]
  transfers between devices with their start and end apart: 16 -> 18, of which waited for: 6 -> 5; matrix products, arithmetic and copies ran while one was open for 0% -> 2% of each run, Pallas kernels for 16% -> 16%
where the time goes in v7:
time: 149 us; the launch traced here: 148 us
  starting transfers between devices  82.2 us (55%)
  Pallas kernels  31.1 us (21%)
  waiting for transfers between devices  28 us (19%)
  local copies, waits for them, and re-layouts  3.89 us (3%)
  other arithmetic  1.77 us (1%)
    ppermute x14, starting transfers between devices, moved(): return lax.ppermute(array, AXIS, pairs)  49.2 us
    all_to_all x4, starting transfers between devices, exchange(): lax.all_to_all(array, AXIS, split_axis=0, concat_axis=0, axis_index_group...  33 us
    all_to_all x4, waiting for transfers between devices, exchange(): lax.all_to_all(array, AXIS, split_axis=0, concat_axis=0, axis_index_group...  20.8 us
    pallas_call x1, Pallas kernels, expert(): call(expert_kernel, 'expert', shape(rows.shape), 5, grid=(rows.shape[0] /...  7.54 us
    ppermute x14, waiting for transfers between devices, moved(): return lax.ppermute(array, AXIS, pairs)  7.24 us
    pallas_call x1, Pallas kernels, partial_attention(): call(partial_kernel, 'partial_attention', [shape((SIDE, MESSAGE, HEAD))]...  6.99 us
    pallas_call x1, Pallas kernels, shards(): call(dispatch_kernel, 'dispatch', shape((REACH, ROWS, D)), 2)  3.39 us
    pallas_call x1, Pallas kernels, shards(): call(combine_kernel, 'combine', shape((RING, TOK, D)), 2)(mix, returned)  3.19 us
  transfers between devices with their start and end apart: 18, of which 5 were waited for; matrix products, arithmetic and copies ran while one was open for 2% of the time, Pallas kernels for 16%

profile of v7, /device:TPU:8, one launch (start us, length us, event | category | flops | bytes accessed | tf_op | source)
XLA Modules:
  0.0 147.9 jit_solution(13774536234704514028)
XLA Ops:
  0.6 1.8 %pack.1 = bf16[8,16,2304]{2,1,0:T(8,128)(2,1)} custom-call(bf16[16,2048]{1,0:T(8,128)(2,1)} %token_ref.1, s32[8,16]{1,0:T(8,128)} %bitcast.6, f32[8,16]{1,0:T(8,128)} %bitcast.7), custom_call_target="tpu_custom_call" | custom-call | tf_op jit(solution)/shard_map/pack/pallas_call | solution.py:368
  2.4 10.3 %all-to-all-start = ((bf16[8,16,2304]{2,1,0:T(8,128)(2,1)}), bf16[8,16,2304]{2,1,0:T(8,128)(2,1)S(1)}, u32[]{:S(2)}, u32[]{:S(2)}) async-start(bf16[8,16,2304]{2,1,0:T(8,128)(2,1)} %pack.1), calls=%async_computation | async-start | bytes 1179648 | tf_op jit(solution)/shard_map/all_to_all | solution.py:60
  13.6 5.7 %collective-permute-start.2 = (bf16[128,128]{1,0:T(8,128)(2,1)S(1)}, bf16[128,128]{1,0:T(8,128)(2,1)S(1)}, u32[]{:S(2)}, u32[]{:S(2)}) collective-permute-start(bf16[128,128]{1,0:T(8,128)(2,1)S(1)} %reshape.16.query_ref), channel_id=1, source_target_pairs={{0,96},{1,97},{2,98},{3,99},{4,100},{5,101},{6,102},{7,103},{8,104... | collective-permute-start | bytes 98312 | tf_op jit(solution)/shard_map/ppermute | solution.py:70
  19.3 1.9 %collective-permute-start.1 = (bf16[128,128]{1,0:T(8,128)(2,1)S(1)}, bf16[128,128]{1,0:T(8,128)(2,1)S(1)}, u32[]{:S(2)}, u32[]{:S(2)}) collective-permute-start(bf16[128,128]{1,0:T(8,128)(2,1)S(1)} %reshape.16.query_ref), channel_id=1, source_target_pairs={{0,64},{1,65},{2,66},{3,67},{4,68},{5,69},{6,70},{7,71},{8,72},{9,... | collective-permute-start | bytes 98312 | tf_op jit(solution)/shard_map/ppermute | solution.py:70
  21.2 3.0 %collective-permute-start = (bf16[128,128]{1,0:T(8,128)(2,1)S(1)}, bf16[128,128]{1,0:T(8,128)(2,1)S(1)}, u32[]{:S(2)}, u32[]{:S(2)}) collective-permute-start(bf16[128,128]{1,0:T(8,128)(2,1)S(1)} %reshape.16.query_ref), channel_id=1, source_target_pairs={{0,32},{1,33},{2,34},{3,35},{4,36},{5,37},{6,38},{7,39},{8,40},{9,... | collective-permute-start | bytes 98312 | tf_op jit(solution)/shard_map/ppermute | solution.py:70
  24.3 2.3 %collective-permute-done.1 = bf16[128,128]{1,0:T(8,128)(2,1)S(1)} collective-permute-done((bf16[128,128]{1,0:T(8,128)(2,1)S(1)}, bf16[128,128]{1,0:T(8,128)(2,1)S(1)}, u32[]{:S(2)}, u32[]{:S(2)}) %collective-permute-start.1) | collective-permute-done | bytes 32800 | tf_op jit(solution)/shard_map/ppermute | solution.py:70
  26.6 2.2 %collective-permute-done = bf16[128,128]{1,0:T(8,128)(2,1)S(1)} collective-permute-done((bf16[128,128]{1,0:T(8,128)(2,1)S(1)}, bf16[128,128]{1,0:T(8,128)(2,1)S(1)}, u32[]{:S(2)}, u32[]{:S(2)}) %collective-permute-start) | collective-permute-done | bytes 32800 | tf_op jit(solution)/shard_map/ppermute | solution.py:70
  29.7 3.4 %dispatch.1 = bf16[32,16,2048]{2,1,0:T(8,128)(2,1)} custom-call(bf16[8,16,2304]{2,1,0:T(8,128)(2,1)} %copy-done, s32[1,128]{1,0:T(1,128)} %bitcast.8), custom_call_target="tpu_custom_call" | custom-call | tf_op jit(solution)/shard_map/dispatch/pallas_call | solution.py:375
  33.1 10.4 %all-to-all-start.1 = ((bf16[32,16,2048]{2,1,0:T(8,128)(2,1)}), bf16[32,16,2048]{2,1,0:T(8,128)(2,1)}, u32[]{:S(2)}, u32[]{:S(2)}) async-start(bf16[32,16,2048]{2,1,0:T(8,128)(2,1)} %dispatch.1), calls=%async_computation.1 | async-start | bytes 4194304 | tf_op jit(solution)/shard_map/all_to_all | solution.py:60
  43.4 1.9 %collective-permute-start.3 = (bf16[2048,384]{1,0:T(8,128)(2,1)S(1)}, bf16[2048,384]{1,0:T(8,128)(2,1)}, u32[]{:S(2)}, u32[]{:S(2)}) collective-permute-start(bf16[2048,384]{1,0:T(8,128)(2,1)S(1)} %copy-done.2), channel_id=1, source_target_pairs={{0,1},{1,0},{2,3},{3,2},{4,5},{5,4},{6,7},{7,6},{8,9},{9,8},{10,11... | collective-permute-start | bytes 4718600 | tf_op jit(solution)/shard_map/ppermute | solution.py:70
  45.4 2.4 %collective-permute-start.4 = (bf16[192,2048]{1,0:T(8,128)(2,1)S(1)}, bf16[192,2048]{1,0:T(8,128)(2,1)S(1)}, u32[]{:S(2)}, u32[]{:S(2)}) collective-permute-start(bf16[192,2048]{1,0:T(8,128)(2,1)S(1)} %copy-done.3), channel_id=1, source_target_pairs={{0,1},{1,0},{2,3},{3,2},{4,5},{5,4},{6,7},{7,6},{8,9},{9,8},{10,11... | collective-permute-start | bytes 2359304 | tf_op jit(solution)/shard_map/ppermute | solution.py:70
  47.8 3.4 %collective-permute-start.5 = (bf16[512,128]{1,0:T(8,128)(2,1)S(1)}, bf16[512,128]{1,0:T(8,128)(2,1)S(1)}, u32[]{:S(2)}, u32[]{:S(2)}) collective-permute-start(bf16[512,128]{1,0:T(8,128)(2,1)S(1)} %pad_maximum_fusion.1), channel_id=1, source_target_pairs={{0,128},{1,129},{2,130},{3,131},{4,132},{5,133},{6,134},{7,135},{8... | collective-permute-start | bytes 393224 | tf_op jit(solution)/shard_map/ppermute | solution.py:70
  51.2 4.6 %collective-permute-start.6 = (bf16[512,128]{1,0:T(8,128)(2,1)S(1)}, bf16[512,128]{1,0:T(8,128)(2,1)S(1)}, u32[]{:S(2)}, u32[]{:S(2)}) collective-permute-start(bf16[512,128]{1,0:T(8,128)(2,1)S(1)} %pad_maximum_fusion.1), channel_id=1, source_target_pairs={{0,256},{1,257},{2,258},{3,259},{4,260},{5,261},{6,262},{7,263},{8... | collective-permute-start | bytes 393224 | tf_op jit(solution)/shard_map/ppermute | solution.py:70
  55.8 3.3 %collective-permute-start.7 = (bf16[512,128]{1,0:T(8,128)(2,1)S(1)}, bf16[512,128]{1,0:T(8,128)(2,1)}, u32[]{:S(2)}, u32[]{:S(2)}) collective-permute-start(bf16[512,128]{1,0:T(8,128)(2,1)S(1)} %pad_maximum_fusion.1), channel_id=1, source_target_pairs={{0,384},{1,385},{2,386},{3,387},{4,388},{5,389},{6,390},{7,391},{8... | collective-permute-start | bytes 393224 | tf_op jit(solution)/shard_map/ppermute | solution.py:70
  60.0 13.1 %all-to-all-done.1 = bf16[32,16,2048]{2,1,0:T(8,128)(2,1)} async-done(((bf16[32,16,2048]{2,1,0:T(8,128)(2,1)}), bf16[32,16,2048]{2,1,0:T(8,128)(2,1)}, u32[]{:S(2)}, u32[]{:S(2)}) %all-to-all-start.1) | async-done | bytes 2097184 | tf_op jit(solution)/shard_map/all_to_all | solution.py:60
  73.2 7.5 %expert.1 = bf16[512,2048]{1,0:T(8,128)(2,1)} custom-call(bf16[512,2048]{1,0:T(8,128)(2,1)} %bitcast.3.rows_ref, bf16[2048,384]{1,0:T(8,128)(2,1)} %gate_up_ref.1, bf16[2048,384]{1,0:T(8,128)(2,1)} %collective-permute-done.3.other_gate_up_ref, bf16[192,2048]{1,0:T(8,128)(2,1)} %down_ref.1, bf16[192,2048]{1,0:T(8,128)(2,1)} %copy-done.4), custom_call_target="tpu_custom_call" | custom-call | tf_op jit(solution)/shard_map/expert/pallas_call | solution.py:197
  80.7 7.5 %all-to-all-start.2 = ((bf16[32,16,2048]{2,1,0:T(8,128)(2,1)}), bf16[32,16,2048]{2,1,0:T(8,128)(2,1)}, u32[]{:S(2)}, u32[]{:S(2)}) async-start(bf16[32,16,2048]{2,1,0:T(8,128)(2,1)} %bitcast.5), calls=%async_computation.2 | async-start | bytes 4194304 | tf_op jit(solution)/shard_map/all_to_all | solution.py:60
  88.2 1.8 %pad_maximum_fusion.query_ref = bf16[2048,128]{1,0:T(8,128)(2,1)} fusion(bf16[512,128]{1,0:T(8,128)(2,1)} %collective-permute-done.7, bf16[512,128]{1,0:T(8,128)(2,1)S(1)} %collective-permute-done.6, bf16[512,128]{1,0:T(8,128)(2,1)S(1)} %collective-permute-done.5, bf16[512,128]{1,0:T(8,128)(2,1)S(1)} %pad_maximum_fusion.1), kind=kLoop, calls=%fused_computation | loop fusion | flops 2097152 | bytes 1048576 | tf_op jit(solution)/shard_map/concatenate | solution.py:387
  90.0 7.0 %partial_attention.1 = (bf16[4,144,128]{2,1,0:T(8,128)(2,1)}, bf16[4,144,128]{2,1,0:T(8,128)(2,1)}, bf16[4,144,128]{2,1,0:T(8,128)(2,1)}, bf16[4,144,128]{2,1,0:T(8,128)(2,1)}) custom-call(s32[16]{0:T(128)} %owner_ref.1, s32[16]{0:T(128)} %count_ref.1, bf16[2048,128]{1,0:T(8,128)(2,1)} %pad_maximum_fusion.query_ref, bf16[16,64,1024]{2,1,0:T(8,128)(2,1)} %pool_ref.1), custom_call_target="tpu_custom_call" | custom-call | tf_op jit(solution)/shard_map/partial_attention/pallas_call | solution.py:307
  97.0 3.4 %collective-permute-start.8 = (bf16[4,144,128]{2,1,0:T(8,128)(2,1)}, bf16[4,144,128]{2,1,0:T(8,128)(2,1)S(1)}, u32[]{:S(2)}, u32[]{:S(2)}) collective-permute-start(bf16[4,144,128]{2,1,0:T(8,128)(2,1)} %get-tuple-element.30), channel_id=1, source_target_pairs={{0,128},{1,129},{2,130},{3,131},{4,132},{5,133},{6,134},{7,135},{8... | collective-permute-start | bytes 442376 | tf_op jit(solution)/shard_map/ppermute | solution.py:70
  100.3 4.6 %collective-permute-start.9 = (bf16[4,144,128]{2,1,0:T(8,128)(2,1)}, bf16[4,144,128]{2,1,0:T(8,128)(2,1)S(1)}, u32[]{:S(2)}, u32[]{:S(2)}) collective-permute-start(bf16[4,144,128]{2,1,0:T(8,128)(2,1)} %get-tuple-element.31), channel_id=1, source_target_pairs={{0,256},{1,257},{2,258},{3,259},{4,260},{5,261},{6,262},{7,263},{8... | collective-permute-start | bytes 442376 | tf_op jit(solution)/shard_map/ppermute | solution.py:70
  105.0 3.3 %collective-permute-start.10 = (bf16[4,144,128]{2,1,0:T(8,128)(2,1)}, bf16[4,144,128]{2,1,0:T(8,128)(2,1)S(1)}, u32[]{:S(2)}, u32[]{:S(2)}) collective-permute-start(bf16[4,144,128]{2,1,0:T(8,128)(2,1)} %get-tuple-element.32), channel_id=1, source_target_pairs={{0,384},{1,385},{2,386},{3,387},{4,388},{5,389},{6,390},{7,391},{8... | collective-permute-start | bytes 442376 | tf_op jit(solution)/shard_map/ppermute | solution.py:70
  108.3 2.3 %mixing.1.mix_ref = bf16[256,512]{1,0:T(8,128)(2,1)} custom-call(bf16[8,16,2304]{2,1,0:T(8,128)(2,1)} %copy-done, s32[1,128]{1,0:T(1,128)} %bitcast.9), custom_call_target="tpu_custom_call" | custom-call | tf_op jit(solution)/shard_map/mixing/pallas_call | solution.py:390
  110.6 7.6 %all-to-all-done.2.rows_ref = bf16[32,16,2048]{2,1,0:T(8,128)(2,1)} async-done(((bf16[32,16,2048]{2,1,0:T(8,128)(2,1)}), bf16[32,16,2048]{2,1,0:T(8,128)(2,1)}, u32[]{:S(2)}, u32[]{:S(2)}) %all-to-all-start.2) | async-done | bytes 2097184 | tf_op jit(solution)/shard_map/all_to_all | solution.py:60
  118.2 3.2 %combine.1 = bf16[8,16,2048]{2,1,0:T(8,128)(2,1)} custom-call(bf16[256,512]{1,0:T(8,128)(2,1)} %mixing.1.mix_ref, bf16[32,16,2048]{2,1,0:T(8,128)(2,1)} %all-to-all-done.2.rows_ref), custom_call_target="tpu_custom_call" | custom-call | tf_op jit(solution)/shard_map/combine/pallas_call | solution.py:391
  121.4 4.9 %all-to-all-start.3 = ((bf16[8,16,2048]{2,1,0:T(8,128)(2,1)}), bf16[8,16,2048]{2,1,0:T(8,128)(2,1)S(1)}, u32[]{:S(2)}, u32[]{:S(2)}) async-start(bf16[8,16,2048]{2,1,0:T(8,128)(2,1)} %combine.1), calls=%async_computation.3 | async-start | bytes 1048576 | tf_op jit(solution)/shard_map/all_to_all | solution.py:60
  126.3 2.4 %merge.1 = (bf16[1,144,128]{2,1,0:T(8,128)(2,1)}, bf16[1,144,128]{2,1,0:T(8,128)(2,1)}, bf16[1,144,128]{2,1,0:T(8,128)(2,1)}, bf16[1,144,128]{2,1,0:T(8,128)(2,1)}) custom-call(bf16[4,144,128]{2,1,0:T(8,128)(2,1)} %get-tuple-element.34.got0_ref, bf16[4,144,128]{2,1,0:T(8,128)(2,1)} %copy-done.6, bf16[4,144,128]{2,1,0:T(8,128)(2,1)} %copy-done.7, ...), custom_call_target="tpu_custom_call" | custom-call | tf_op jit(solution)/shard_map/merge/pallas_call | solution.py:395
  128.8 3.9 %collective-permute-start.11 = (bf16[1,144,128]{2,1,0:T(8,128)(2,1)}, bf16[1,144,128]{2,1,0:T(8,128)(2,1)S(1)}, u32[]{:S(2)}, u32[]{:S(2)}) collective-permute-start(bf16[1,144,128]{2,1,0:T(8,128)(2,1)} %get-tuple-element.39), channel_id=1, source_target_pairs={{0,32},{1,33},{2,34},{3,35},{4,36},{5,37},{6,38},{7,39},{8,40},{9,... | collective-permute-start | bytes 110600 | tf_op jit(solution)/shard_map/ppermute | solution.py:70
  132.7 4.3 %collective-permute-start.12 = (bf16[1,144,128]{2,1,0:T(8,128)(2,1)}, bf16[1,144,128]{2,1,0:T(8,128)(2,1)S(1)}, u32[]{:S(2)}, u32[]{:S(2)}) collective-permute-start(bf16[1,144,128]{2,1,0:T(8,128)(2,1)} %get-tuple-element.40), channel_id=1, source_target_pairs={{0,64},{1,65},{2,66},{3,67},{4,68},{5,69},{6,70},{7,71},{8,72},{9,... | collective-permute-start | bytes 110600 | tf_op jit(solution)/shard_map/ppermute | solution.py:70
  137.0 3.4 %collective-permute-start.13 = (bf16[1,144,128]{2,1,0:T(8,128)(2,1)}, bf16[1,144,128]{2,1,0:T(8,128)(2,1)S(1)}, u32[]{:S(2)}, u32[]{:S(2)}) collective-permute-start(bf16[1,144,128]{2,1,0:T(8,128)(2,1)} %get-tuple-element.41), channel_id=1, source_target_pairs={{0,96},{1,97},{2,98},{3,99},{4,100},{5,101},{6,102},{7,103},{8,104... | collective-permute-start | bytes 110600 | tf_op jit(solution)/shard_map/ppermute | solution.py:70
  140.4 2.6 %collective-permute-done.13.got3_ref = bf16[1,144,128]{2,1,0:T(8,128)(2,1)S(1)} collective-permute-done((bf16[1,144,128]{2,1,0:T(8,128)(2,1)}, bf16[1,144,128]{2,1,0:T(8,128)(2,1)S(1)}, u32[]{:S(2)}, u32[]{:S(2)}) %collective-permute-start.13) | collective-permute-done | bytes 36896 | tf_op jit(solution)/shard_map/ppermute | solution.py:70
  146.1 1.7 %total.1 = bf16[16,2048]{1,0:T(8,128)(2,1)} custom-call(bf16[8,16,2048]{2,1,0:T(8,128)(2,1)} %copy-done.1), custom_call_target="tpu_custom_call" | custom-call | tf_op jit(solution)/shard_map/total/pallas_call | solution.py:405
  (40 shorter events, 5.6 us)
Async XLA Ops:
  2.4 26.4 %all-to-all-start = ((bf16[8,16,2304]{2,1,0:T(8,128)(2,1)}), bf16[8,16,2304]{2,1,0:T(8,128)(2,1)S(1)}, u32[]{:S(2)}, u32[]{:S(2)}) async-start(bf16[8,16,2304]{2,1,0:T(8,128)(2,1)} %pack.1), calls=%async_computation | async-start | bytes 1179648 | tf_op jit(solution)/shard_map/all_to_all | solution.py:60
  13.5 19.5 %copy-start.5 = (bf16[128,128]{1,0:T(8,128)(2,1)}, bf16[128,128]{1,0:T(8,128)(2,1)S(1)}, u32[]{:S(2)}) copy-start(bf16[128,128]{1,0:T(8,128)(2,1)S(1)} %reshape.16.query_ref) | copy-start | bytes 98308
  13.6 10.7 %collective-permute-start.2 = (bf16[128,128]{1,0:T(8,128)(2,1)S(1)}, bf16[128,128]{1,0:T(8,128)(2,1)S(1)}, u32[]{:S(2)}, u32[]{:S(2)}) collective-permute-start(bf16[128,128]{1,0:T(8,128)(2,1)S(1)} %reshape.16.query_ref), channel_id=1, source_target_pairs={{0,96},{1,97},{2,98},{3,99},{4,100},{5,101},{6,102},{7,103},{8,104... | collective-permute-start | bytes 98312 | tf_op jit(solution)/shard_map/ppermute | solution.py:70
  19.3 7.3 %collective-permute-start.1 = (bf16[128,128]{1,0:T(8,128)(2,1)S(1)}, bf16[128,128]{1,0:T(8,128)(2,1)S(1)}, u32[]{:S(2)}, u32[]{:S(2)}) collective-permute-start(bf16[128,128]{1,0:T(8,128)(2,1)S(1)} %reshape.16.query_ref), channel_id=1, source_target_pairs={{0,64},{1,65},{2,66},{3,67},{4,68},{5,69},{6,70},{7,71},{8,72},{9,... | collective-permute-start | bytes 98312 | tf_op jit(solution)/shard_map/ppermute | solution.py:70
  21.2 7.6 %collective-permute-start = (bf16[128,128]{1,0:T(8,128)(2,1)S(1)}, bf16[128,128]{1,0:T(8,128)(2,1)S(1)}, u32[]{:S(2)}, u32[]{:S(2)}) collective-permute-start(bf16[128,128]{1,0:T(8,128)(2,1)S(1)} %reshape.16.query_ref), channel_id=1, source_target_pairs={{0,32},{1,33},{2,34},{3,35},{4,36},{5,37},{6,38},{7,39},{8,40},{9,... | collective-permute-start | bytes 98312 | tf_op jit(solution)/shard_map/ppermute | solution.py:70
  28.8 0.8 copy-start
  33.0 10.4 %copy-start.2 = (bf16[2048,384]{1,0:T(8,128)(2,1)S(1)}, bf16[2048,384]{1,0:T(8,128)(2,1)}, u32[]{:S(2)}) copy-start(bf16[2048,384]{1,0:T(8,128)(2,1)} %gate_up_ref.1) | copy-start | bytes 4718596
  33.0 12.3 %copy-start.3 = (bf16[192,2048]{1,0:T(8,128)(2,1)S(1)}, bf16[192,2048]{1,0:T(8,128)(2,1)}, u32[]{:S(2)}) copy-start(bf16[192,2048]{1,0:T(8,128)(2,1)} %down_ref.1) | copy-start | bytes 2359300
  33.1 40.1 %all-to-all-start.1 = ((bf16[32,16,2048]{2,1,0:T(8,128)(2,1)}), bf16[32,16,2048]{2,1,0:T(8,128)(2,1)}, u32[]{:S(2)}, u32[]{:S(2)}) async-start(bf16[32,16,2048]{2,1,0:T(8,128)(2,1)} %dispatch.1), calls=%async_computation.1 | async-start | bytes 4194304 | tf_op jit(solution)/shard_map/all_to_all | solution.py:60
  43.4 16.6 %collective-permute-start.3 = (bf16[2048,384]{1,0:T(8,128)(2,1)S(1)}, bf16[2048,384]{1,0:T(8,128)(2,1)}, u32[]{:S(2)}, u32[]{:S(2)}) collective-permute-start(bf16[2048,384]{1,0:T(8,128)(2,1)S(1)} %copy-done.2), channel_id=1, source_target_pairs={{0,1},{1,0},{2,3},{3,2},{4,5},{5,4},{6,7},{7,6},{8,9},{9,8},{10,11... | collective-permute-start | bytes 4718600 | tf_op jit(solution)/shard_map/ppermute | solution.py:70
  45.4 13.8 %collective-permute-start.4 = (bf16[192,2048]{1,0:T(8,128)(2,1)S(1)}, bf16[192,2048]{1,0:T(8,128)(2,1)S(1)}, u32[]{:S(2)}, u32[]{:S(2)}) collective-permute-start(bf16[192,2048]{1,0:T(8,128)(2,1)S(1)} %copy-done.3), channel_id=1, source_target_pairs={{0,1},{1,0},{2,3},{3,2},{4,5},{5,4},{6,7},{7,6},{8,9},{9,8},{10,11... | collective-permute-start | bytes 2359304 | tf_op jit(solution)/shard_map/ppermute | solution.py:70
  47.8 32.9 %collective-permute-start.5 = (bf16[512,128]{1,0:T(8,128)(2,1)S(1)}, bf16[512,128]{1,0:T(8,128)(2,1)S(1)}, u32[]{:S(2)}, u32[]{:S(2)}) collective-permute-start(bf16[512,128]{1,0:T(8,128)(2,1)S(1)} %pad_maximum_fusion.1), channel_id=1, source_target_pairs={{0,128},{1,129},{2,130},{3,131},{4,132},{5,133},{6,134},{7,135},{8... | collective-permute-start | bytes 393224 | tf_op jit(solution)/shard_map/ppermute | solution.py:70
  51.2 29.6 %collective-permute-start.6 = (bf16[512,128]{1,0:T(8,128)(2,1)S(1)}, bf16[512,128]{1,0:T(8,128)(2,1)S(1)}, u32[]{:S(2)}, u32[]{:S(2)}) collective-permute-start(bf16[512,128]{1,0:T(8,128)(2,1)S(1)} %pad_maximum_fusion.1), channel_id=1, source_target_pairs={{0,256},{1,257},{2,258},{3,259},{4,260},{5,261},{6,262},{7,263},{8... | collective-permute-start | bytes 393224 | tf_op jit(solution)/shard_map/ppermute | solution.py:70
  55.8 24.9 %collective-permute-start.7 = (bf16[512,128]{1,0:T(8,128)(2,1)S(1)}, bf16[512,128]{1,0:T(8,128)(2,1)}, u32[]{:S(2)}, u32[]{:S(2)}) collective-permute-start(bf16[512,128]{1,0:T(8,128)(2,1)S(1)} %pad_maximum_fusion.1), channel_id=1, source_target_pairs={{0,384},{1,385},{2,386},{3,387},{4,388},{5,389},{6,390},{7,391},{8... | collective-permute-start | bytes 393224 | tf_op jit(solution)/shard_map/ppermute | solution.py:70
  59.1 0.9 copy-start.4
  80.7 37.4 %all-to-all-start.2 = ((bf16[32,16,2048]{2,1,0:T(8,128)(2,1)}), bf16[32,16,2048]{2,1,0:T(8,128)(2,1)}, u32[]{:S(2)}, u32[]{:S(2)}) async-start(bf16[32,16,2048]{2,1,0:T(8,128)(2,1)} %bitcast.5), calls=%async_computation.2 | async-start | bytes 4194304 | tf_op jit(solution)/shard_map/all_to_all | solution.py:60
  97.0 24.4 %collective-permute-start.8 = (bf16[4,144,128]{2,1,0:T(8,128)(2,1)}, bf16[4,144,128]{2,1,0:T(8,128)(2,1)S(1)}, u32[]{:S(2)}, u32[]{:S(2)}) collective-permute-start(bf16[4,144,128]{2,1,0:T(8,128)(2,1)} %get-tuple-element.30), channel_id=1, source_target_pairs={{0,128},{1,129},{2,130},{3,131},{4,132},{5,133},{6,134},{7,135},{8... | collective-permute-start | bytes 442376 | tf_op jit(solution)/shard_map/ppermute | solution.py:70
  100.3 21.1 %collective-permute-start.9 = (bf16[4,144,128]{2,1,0:T(8,128)(2,1)}, bf16[4,144,128]{2,1,0:T(8,128)(2,1)S(1)}, u32[]{:S(2)}, u32[]{:S(2)}) collective-permute-start(bf16[4,144,128]{2,1,0:T(8,128)(2,1)} %get-tuple-element.31), channel_id=1, source_target_pairs={{0,256},{1,257},{2,258},{3,259},{4,260},{5,261},{6,262},{7,263},{8... | collective-permute-start | bytes 442376 | tf_op jit(solution)/shard_map/ppermute | solution.py:70
  105.0 16.4 %collective-permute-start.10 = (bf16[4,144,128]{2,1,0:T(8,128)(2,1)}, bf16[4,144,128]{2,1,0:T(8,128)(2,1)S(1)}, u32[]{:S(2)}, u32[]{:S(2)}) collective-permute-start(bf16[4,144,128]{2,1,0:T(8,128)(2,1)} %get-tuple-element.32), channel_id=1, source_target_pairs={{0,384},{1,385},{2,386},{3,387},{4,388},{5,389},{6,390},{7,391},{8... | collective-permute-start | bytes 442376 | tf_op jit(solution)/shard_map/ppermute | solution.py:70
  121.4 4.9 %copy-start.6 = (bf16[4,144,128]{2,1,0:T(8,128)(2,1)}, bf16[4,144,128]{2,1,0:T(8,128)(2,1)S(1)}, u32[]{:S(2)}) copy-start(bf16[4,144,128]{2,1,0:T(8,128)(2,1)S(1)} %collective-permute-done.8.got1_ref) | copy-start | bytes 442372
  121.4 4.9 %copy-start.7 = (bf16[4,144,128]{2,1,0:T(8,128)(2,1)}, bf16[4,144,128]{2,1,0:T(8,128)(2,1)S(1)}, u32[]{:S(2)}) copy-start(bf16[4,144,128]{2,1,0:T(8,128)(2,1)S(1)} %collective-permute-done.9.got2_ref) | copy-start | bytes 442372
  121.4 4.9 %copy-start.8 = (bf16[4,144,128]{2,1,0:T(8,128)(2,1)}, bf16[4,144,128]{2,1,0:T(8,128)(2,1)S(1)}, u32[]{:S(2)}) copy-start(bf16[4,144,128]{2,1,0:T(8,128)(2,1)S(1)} %collective-permute-done.10.got3_ref) | copy-start | bytes 442372
  121.4 23.9 %all-to-all-start.3 = ((bf16[8,16,2048]{2,1,0:T(8,128)(2,1)}), bf16[8,16,2048]{2,1,0:T(8,128)(2,1)S(1)}, u32[]{:S(2)}, u32[]{:S(2)}) async-start(bf16[8,16,2048]{2,1,0:T(8,128)(2,1)} %combine.1), calls=%async_computation.3 | async-start | bytes 1048576 | tf_op jit(solution)/shard_map/all_to_all | solution.py:60
  128.8 11.6 %collective-permute-start.11 = (bf16[1,144,128]{2,1,0:T(8,128)(2,1)}, bf16[1,144,128]{2,1,0:T(8,128)(2,1)S(1)}, u32[]{:S(2)}, u32[]{:S(2)}) collective-permute-start(bf16[1,144,128]{2,1,0:T(8,128)(2,1)} %get-tuple-element.39), channel_id=1, source_target_pairs={{0,32},{1,33},{2,34},{3,35},{4,36},{5,37},{6,38},{7,39},{8,40},{9,... | collective-permute-start | bytes 110600 | tf_op jit(solution)/shard_map/ppermute | solution.py:70
  132.7 7.7 %collective-permute-start.12 = (bf16[1,144,128]{2,1,0:T(8,128)(2,1)}, bf16[1,144,128]{2,1,0:T(8,128)(2,1)S(1)}, u32[]{:S(2)}, u32[]{:S(2)}) collective-permute-start(bf16[1,144,128]{2,1,0:T(8,128)(2,1)} %get-tuple-element.40), channel_id=1, source_target_pairs={{0,64},{1,65},{2,66},{3,67},{4,68},{5,69},{6,70},{7,71},{8,72},{9,... | collective-permute-start | bytes 110600 | tf_op jit(solution)/shard_map/ppermute | solution.py:70
  137.0 6.1 %collective-permute-start.13 = (bf16[1,144,128]{2,1,0:T(8,128)(2,1)}, bf16[1,144,128]{2,1,0:T(8,128)(2,1)S(1)}, u32[]{:S(2)}, u32[]{:S(2)}) collective-permute-start(bf16[1,144,128]{2,1,0:T(8,128)(2,1)} %get-tuple-element.41), channel_id=1, source_target_pairs={{0,96},{1,97},{2,98},{3,99},{4,100},{5,101},{6,102},{7,103},{8,104... | collective-permute-start | bytes 110600 | tf_op jit(solution)/shard_map/ppermute | solution.py:70
  140.3 2.7 %copy-start.9 = (bf16[1,144,128]{2,1,0:T(8,128)(2,1)}, bf16[1,144,128]{2,1,0:T(8,128)(2,1)S(1)}, u32[]{:S(2)}) copy-start(bf16[1,144,128]{2,1,0:T(8,128)(2,1)S(1)} %collective-permute-done.11.got1_ref) | copy-start | bytes 110596
  140.4 2.7 %copy-start.10 = (bf16[1,144,128]{2,1,0:T(8,128)(2,1)}, bf16[1,144,128]{2,1,0:T(8,128)(2,1)S(1)}, u32[]{:S(2)}) copy-start(bf16[1,144,128]{2,1,0:T(8,128)(2,1)S(1)} %collective-permute-done.12.got2_ref) | copy-start | bytes 110596
  143.0 0.6 copy-start.11
  145.4 0.8 copy-start.1

commit v8 on v7

--- a/solution.py
+++ b/solution.py
@@ -32,7 +32,9 @@
 
 F32 = jnp.float32
 BF16 = jnp.bfloat16
-VMEM_LIMIT = 62 * 1024 * 1024
+VMEM_LIMIT = 32 * 1024 * 1024
+VMEM_MOST = 60 * 1024 * 1024
+VMEM_ALL = 62 * 1024 * 1024
 AXIS = "d"
 
 
@@ -96,7 +98,7 @@
         out_shape=shapes,
         in_specs=more.pop("in_specs", whole(inputs)),
         out_specs=more.pop("out_specs", whole(1)[0]),
-        compiler_params=pltpu.CompilerParams(vmem_limit_bytes=VMEM_LIMIT),
+        compiler_params=pltpu.CompilerParams(vmem_limit_bytes=more.pop("limit", VMEM_LIMIT)),
         **more,
     )
 
@@ -177,32 +179,63 @@
     out_ref[...] = jnp.sum(parts_ref[...].astype(F32), axis=0).astype(BF16)
 
 
-ROW_STEP = 256
-
-
-def expert_kernel(rows_ref, gate_up_ref, other_gate_up_ref, down_ref, other_down_ref, out_ref):
-    x = rows_ref[...]
-    total = jnp.zeros((ROW_STEP, D), F32)
-    for both_ref, back_ref in ((gate_up_ref, down_ref), (other_gate_up_ref, other_down_ref)):
-        both = jnp.dot(x, both_ref[...], preferred_element_type=F32)
-        gate, up = both[:, :HALF], both[:, HALF:]
-        act = (gate / (1.0 + jnp.exp(-gate)) * up).astype(BF16)
-        total = total + jnp.dot(act, back_ref[...], preferred_element_type=F32)
-    out_ref[...] = total.astype(BF16)
+EXPERT_STEPS = 2
+
+
+def expert_kernel(rows_ref, *refs):
+    sources, out_ref, held, made_ref, came_sem, left_sem = refs[:4], refs[4], refs[5:9], *refs[9:]
+    come = [
+        pltpu.make_async_copy(source, kept, came_sem.at[i])
+        for i, (source, kept) in enumerate(zip(sources, held))
+    ]
+    for copy in come:
+        copy.start()
+    step = REACH // EXPERT_STEPS
+    leave = []
+    for s in range(EXPERT_STEPS):
+        x = rows_ref[s * step : (s + 1) * step].reshape(step * ROWS, D)
+        total = jnp.zeros((step * ROWS, D), F32)
+        for pair in range(2):
+            if s == 0:
+                come[2 * pair].wait()
+            both = jnp.dot(x, held[2 * pair][...], preferred_element_type=F32)
+            gate, up = both[:, :HALF], both[:, HALF:]
+            act = (gate / (1.0 + jnp.exp(-gate)) * up).astype(BF16)
+            if s == 0:
+                come[2 * pair + 1].wait()
+            total = total + jnp.dot(act, held[2 * pair + 1][...], preferred_element_type=F32)
+        made_ref[s] = total.astype(BF16).reshape(step, ROWS, D)
+        leave.append(
+            pltpu.make_async_copy(
+                made_ref.at[s], out_ref.at[s * step : (s + 1) * step], left_sem.at[s]
+            )
+        )
+        leave[-1].start()
+    for copy in leave:
+        copy.wait()
+
+
+def on_core(array):
+    return pltpu.with_memory_space_constraint(array, pltpu.VMEM)
 
 
 def expert(rows, *weights):
-    step = pl.BlockSpec((ROW_STEP, D), lambda i: (i, 0))
-    fixed = [pl.BlockSpec(w.shape, lambda i: (0, 0)) for w in weights]
+    apart = pl.BlockSpec(memory_space=pltpu.HBM)
     return call(
         expert_kernel,
         "expert",
         shape(rows.shape),
         5,
-        grid=(rows.shape[0] // ROW_STEP,),
-        in_specs=[step] + fixed,
-        out_specs=step,
-    )(rows, *weights)
+        in_specs=whole(1) + [apart] * 4,
+        out_specs=apart,
+        limit=VMEM_MOST,
+        scratch_shapes=[pltpu.VMEM(w.shape, BF16) for w in weights]
+        + [
+            pltpu.VMEM((EXPERT_STEPS, REACH // EXPERT_STEPS, ROWS, D), BF16),
+            pltpu.SemaphoreType.DMA((4,)),
+            pltpu.SemaphoreType.DMA((EXPERT_STEPS,)),
+        ],
+    )(on_core(rows), *weights)
 
 
 def write_states(ref, r, states):
@@ -365,30 +398,33 @@
     block_tokens,
 ):
     slot_row = expert_slot.reshape(1, SLOTS)
-    packed = call(pack_kernel, "pack", shape((RING, TOK, D + EXTRA)), 3)(
+    packed = call(pack_kernel, "pack", shape((RING, TOK, D + EXTRA)), 3, limit=VMEM_ALL)(
         moe_input, expert_ids.T, route_weight.T
     )
     own_queries = queries.reshape(REQUESTS * HEADS, HEAD)
     near = exchange(packed, RING_GROUPS)
-    line = jnp.concatenate(along(own_queries, "dz"), axis=0)
-    near, line = lax.optimization_barrier((near, line))
-    send = call(dispatch_kernel, "dispatch", shape((REACH, ROWS, D)), 2)(near, slot_row)
+    line = along(own_queries, "dz")
+    send = call(dispatch_kernel, "dispatch", shape((REACH, ROWS, D)), 2, limit=VMEM_ALL)(
+        near, slot_row
+    )
+    send, line = lax.optimization_barrier((send, line))
+    line = jnp.concatenate(line, axis=0)
     received = exchange(send, REACH_GROUPS)
 
     other_gate_up, other_down = moved(w_gate_up, dc=1), moved(w_down, dc=1)
     square = along(line, "dx")
     rows = expert(
-        received.reshape(REACH * ROWS, D), w_gate_up, other_gate_up, w_down, other_down
+        received, w_gate_up, w_down, other_gate_up, other_down
     )
     rows, square = lax.optimization_barrier((rows, square))
-    returned = exchange(rows.reshape(REACH, ROWS, D), REACH_GROUPS)
+    returned = exchange(rows, REACH_GROUPS)
 
     partials = partial_attention(
         block_owner, block_tokens, jnp.concatenate(square, axis=0), key_value_pool
     )
     across = spread(partials, "dx")
     mix = call(mixing_kernel, "mixing", shape((2 * NEAR, REACH * ROWS)), 2)(near, slot_row)
-    parts = call(combine_kernel, "combine", shape((RING, TOK, D)), 2)(mix, returned)
+    parts = call(combine_kernel, "combine", shape((RING, TOK, D)), 2)(mix, on_core(returned))
     parts, across = lax.optimization_barrier((parts, across))
     parts = exchange(parts, RING_GROUPS)
 

time: 149 us -> 139 us (0.933)
  the two profiles are of different devices: /device:TPU:8 before, /device:TPU:2 now
where the time goes in v8:
time: 139 us; the launch traced here: 138 us
  starting transfers between devices  82.6 us (59%)
  waiting for transfers between devices  28 us (20%)
  Pallas kernels  21.2 us (15%)
  local copies, waits for them, and re-layouts  4.77 us (3%)
    ppermute x14, starting transfers between devices, moved(): return lax.ppermute(array, AXIS, pairs)  48.4 us
    all_to_all x4, starting transfers between devices, exchange(): lax.all_to_all(array, AXIS, split_axis=0, concat_axis=0, axis_index_group...  34.2 us
    all_to_all x4, waiting for transfers between devices, exchange(): lax.all_to_all(array, AXIS, split_axis=0, concat_axis=0, axis_index_group...  22.2 us
    pallas_call x1, Pallas kernels, expert(): call(expert_kernel, 'expert', shape(rows.shape), 5, in_specs=whole(1) + [...  6.54 us
    ppermute x14, waiting for transfers between devices, moved(): return lax.ppermute(array, AXIS, pairs)  5.8 us
    pallas_call x1, Pallas kernels, partial_attention(): call(partial_kernel, 'partial_attention', [shape((SIDE, MESSAGE, HEAD))]...  5.11 us
    unnamed x23, local copies, waits for them, and re-layouts  3.97 us
    pallas_call x1, Pallas kernels, shards(): call(dispatch_kernel, 'dispatch', shape((REACH, ROWS, D)), 2, limit=VMEM_...  3.4 us
  transfers between devices with their start and end apart: 18, of which 7 were waited for; matrix products, arithmetic and copies ran while one was open for 1% of the time, Pallas kernels for 13%

profile of v8, /device:TPU:2, one launch (start us, length us, event | category | flops | bytes accessed | tf_op | source)
XLA Modules:
  0.0 138.5 jit_solution(2207045708960419521)
XLA Ops:
  0.6 1.8 %pack.1 = bf16[8,16,2304]{2,1,0:T(8,128)(2,1)} custom-call(bf16[16,2048]{1,0:T(8,128)(2,1)} %token_ref.1, s32[8,16]{1,0:T(8,128)} %bitcast.5, f32[8,16]{1,0:T(8,128)} %bitcast.6), custom_call_target="tpu_custom_call" | custom-call | tf_op jit(solution)/shard_map/pack/pallas_call | solution.py:401
  2.4 10.3 %all-to-all-start = ((bf16[8,16,2304]{2,1,0:T(8,128)(2,1)}), bf16[8,16,2304]{2,1,0:T(8,128)(2,1)S(1)}, u32[]{:S(2)}, u32[]{:S(2)}) async-start(bf16[8,16,2304]{2,1,0:T(8,128)(2,1)} %pack.1), calls=%async_computation | async-start | bytes 1179648 | tf_op jit(solution)/shard_map/all_to_all | solution.py:62
  13.5 3.9 %collective-permute-start = (bf16[128,128]{1,0:T(8,128)(2,1)S(1)}, bf16[128,128]{1,0:T(8,128)(2,1)S(1)}, u32[]{:S(2)}, u32[]{:S(2)}) collective-permute-start(bf16[128,128]{1,0:T(8,128)(2,1)S(1)} %reshape.11.query_ref), channel_id=1, source_target_pairs={{0,32},{1,33},{2,34},{3,35},{4,36},{5,37},{6,38},{7,39},{8,40},{9,... | collective-permute-start | bytes 98312 | tf_op jit(solution)/shard_map/ppermute | solution.py:72
  17.5 4.3 %collective-permute-start.1 = (bf16[128,128]{1,0:T(8,128)(2,1)S(1)}, bf16[128,128]{1,0:T(8,128)(2,1)S(1)}, u32[]{:S(2)}, u32[]{:S(2)}) collective-permute-start(bf16[128,128]{1,0:T(8,128)(2,1)S(1)} %reshape.11.query_ref), channel_id=1, source_target_pairs={{0,64},{1,65},{2,66},{3,67},{4,68},{5,69},{6,70},{7,71},{8,72},{9,... | collective-permute-start | bytes 98312 | tf_op jit(solution)/shard_map/ppermute | solution.py:72
  21.8 3.4 %collective-permute-start.2 = (bf16[128,128]{1,0:T(8,128)(2,1)S(1)}, bf16[128,128]{1,0:T(8,128)(2,1)S(1)}, u32[]{:S(2)}, u32[]{:S(2)}) collective-permute-start(bf16[128,128]{1,0:T(8,128)(2,1)S(1)} %reshape.11.query_ref), channel_id=1, source_target_pairs={{0,96},{1,97},{2,98},{3,99},{4,100},{5,101},{6,102},{7,103},{8,104... | collective-permute-start | bytes 98312 | tf_op jit(solution)/shard_map/ppermute | solution.py:72
  25.1 1.2 all-to-all-done.near_ref
  27.2 3.4 %dispatch.1 = bf16[32,16,2048]{2,1,0:T(8,128)(2,1)} custom-call(bf16[8,16,2304]{2,1,0:T(8,128)(2,1)} %copy-done, s32[1,128]{1,0:T(1,128)} %bitcast.3), custom_call_target="tpu_custom_call" | custom-call | tf_op jit(solution)/shard_map/dispatch/pallas_call | solution.py:407
  30.6 10.4 %all-to-all-start.1 = ((bf16[32,16,2048]{2,1,0:T(8,128)(2,1)}), bf16[32,16,2048]{2,1,0:T(8,128)(2,1)S(1)}, u32[]{:S(2)}, u32[]{:S(2)}) async-start(bf16[32,16,2048]{2,1,0:T(8,128)(2,1)} %dispatch.1), calls=%async_computation.1 | async-start | bytes 4194304 | tf_op jit(solution)/shard_map/all_to_all | solution.py:62
  41.0 1.9 %collective-permute-start.3 = (bf16[2048,384]{1,0:T(8,128)(2,1)}, bf16[2048,384]{1,0:T(8,128)(2,1)}, u32[]{:S(2)}, u32[]{:S(2)}) collective-permute-start(bf16[2048,384]{1,0:T(8,128)(2,1)} %refs_0_.1), channel_id=1, source_target_pairs={{0,1},{1,0},{2,3},{3,2},{4,5},{5,4},{6,7},{7,6},{8,9},{9,8},{10,11... | collective-permute-start | bytes 4718600 | tf_op jit(solution)/shard_map/ppermute | solution.py:72
  43.0 2.4 %collective-permute-start.4 = (bf16[192,2048]{1,0:T(8,128)(2,1)S(1)}, bf16[192,2048]{1,0:T(8,128)(2,1)S(1)}, u32[]{:S(2)}, u32[]{:S(2)}) collective-permute-start(bf16[192,2048]{1,0:T(8,128)(2,1)S(1)} %copy-done.7), channel_id=1, source_target_pairs={{0,1},{1,0},{2,3},{3,2},{4,5},{5,4},{6,7},{7,6},{8,9},{9,8},{10,11... | collective-permute-start | bytes 2359304 | tf_op jit(solution)/shard_map/ppermute | solution.py:72
  45.4 3.4 %collective-permute-start.5 = (bf16[512,128]{1,0:T(8,128)(2,1)S(1)}, bf16[512,128]{1,0:T(8,128)(2,1)S(1)}, u32[]{:S(2)}, u32[]{:S(2)}) collective-permute-start(bf16[512,128]{1,0:T(8,128)(2,1)S(1)} %constant_dynamic-update-slice_fusion), channel_id=1, source_target_pairs={{0,128},{1,129},{2,130},{3,131},{4,132},{5,133},{6,134},{7,135},{8... | collective-permute-start | bytes 393224 | tf_op jit(solution)/shard_map/ppermute | solution.py:72
  48.8 2.7 %collective-permute-start.6 = (bf16[512,128]{1,0:T(8,128)(2,1)S(1)}, bf16[512,128]{1,0:T(8,128)(2,1)S(1)}, u32[]{:S(2)}, u32[]{:S(2)}) collective-permute-start(bf16[512,128]{1,0:T(8,128)(2,1)S(1)} %constant_dynamic-update-slice_fusion), channel_id=1, source_target_pairs={{0,256},{1,257},{2,258},{3,259},{4,260},{5,261},{6,262},{7,263},{8... | collective-permute-start | bytes 393224 | tf_op jit(solution)/shard_map/ppermute | solution.py:72
  51.6 4.3 %collective-permute-start.7 = (bf16[512,128]{1,0:T(8,128)(2,1)S(1)}, bf16[512,128]{1,0:T(8,128)(2,1)S(1)}, u32[]{:S(2)}, u32[]{:S(2)}) collective-permute-start(bf16[512,128]{1,0:T(8,128)(2,1)S(1)} %constant_dynamic-update-slice_fusion), channel_id=1, source_target_pairs={{0,384},{1,385},{2,386},{3,387},{4,388},{5,389},{6,390},{7,391},{8... | collective-permute-start | bytes 393224 | tf_op jit(solution)/shard_map/ppermute | solution.py:72
  56.8 12.0 %all-to-all-done.1.rows_ref = bf16[32,16,2048]{2,1,0:T(8,128)(2,1)S(1)} async-done(((bf16[32,16,2048]{2,1,0:T(8,128)(2,1)}), bf16[32,16,2048]{2,1,0:T(8,128)(2,1)S(1)}, u32[]{:S(2)}, u32[]{:S(2)}) %all-to-all-start.1) | async-done | bytes 2097184 | tf_op jit(solution)/shard_map/all_to_all | solution.py:62
  68.8 6.5 %expert.1 = bf16[32,16,2048]{2,1,0:T(8,128)(2,1)} custom-call(bf16[32,16,2048]{2,1,0:T(8,128)(2,1)S(1)} %all-to-all-done.1.rows_ref, bf16[2048,384]{1,0:T(8,128)(2,1)} %refs_0_.1, bf16[192,2048]{1,0:T(8,128)(2,1)} %refs_1_.1, bf16[2048,384]{1,0:T(8,128)(2,1)} %collective-permute-done.3.refs_2_, bf16[192,2048]{1,0:T(8,128)(2,1)} %copy-done.8), custom_call_target="tpu_custom_call" | custom-call | tf_op jit(solution)/shard_map/expert/pallas_call | solution.py:224
  76.1 8.0 %all-to-all-start.2 = ((bf16[32,16,2048]{2,1,0:T(8,128)(2,1)}), bf16[32,16,2048]{2,1,0:T(8,128)(2,1)S(1)}, u32[]{:S(2)}, u32[]{:S(2)}) async-start(bf16[32,16,2048]{2,1,0:T(8,128)(2,1)} %expert.1), calls=%async_computation.2 | async-start | bytes 4194304 | tf_op jit(solution)/shard_map/all_to_all | solution.py:62
  84.1 1.0 pad_maximum_fusion.query_ref
  85.1 1.6 %copy-done.2 = bf16[16,64,1024]{2,1,0:T(8,128)(2,1)S(1)} copy-done((bf16[16,64,1024]{2,1,0:T(8,128)(2,1)S(1)}, bf16[16,64,1024]{2,1,0:T(8,128)(2,1)}, u32[]{:S(2)}) %copy-start.2) | copy-done | bytes 2097176
  86.7 5.1 %partial_attention.1 = (bf16[4,144,128]{2,1,0:T(8,128)(2,1)S(1)}, bf16[4,144,128]{2,1,0:T(8,128)(2,1)S(1)}, bf16[4,144,128]{2,1,0:T(8,128)(2,1)S(1)}, bf16[4,144,128]{2,1,0:T(8,128)(2,1)S(1)}) custom-call(s32[16]{0:T(128)S(1)} %copy-done.5, s32[16]{0:T(128)S(1)} %copy-done.6, bf16[2048,128]{1,0:T(8,128)(2,1)S(1)} %pad_maximum_fusion.query_ref, ...), custom_call_target="tpu_custom_call" | custom-call | tf_op jit(solution)/shard_map/partial_attention/pallas_call | solution.py:340
  91.8 3.4 %collective-permute-start.8 = (bf16[4,144,128]{2,1,0:T(8,128)(2,1)S(1)}, bf16[4,144,128]{2,1,0:T(8,128)(2,1)S(1)}, u32[]{:S(2)}, u32[]{:S(2)}) collective-permute-start(bf16[4,144,128]{2,1,0:T(8,128)(2,1)S(1)} %get-tuple-element.36), channel_id=1, source_target_pairs={{0,128},{1,129},{2,130},{3,131},{4,132},{5,133},{6,134},{7,135},{8... | collective-permute-start | bytes 442376 | tf_op jit(solution)/shard_map/ppermute | solution.py:72
  95.2 2.7 %collective-permute-start.9 = (bf16[4,144,128]{2,1,0:T(8,128)(2,1)S(1)}, bf16[4,144,128]{2,1,0:T(8,128)(2,1)S(1)}, u32[]{:S(2)}, u32[]{:S(2)}) collective-permute-start(bf16[4,144,128]{2,1,0:T(8,128)(2,1)S(1)} %get-tuple-element.37), channel_id=1, source_target_pairs={{0,256},{1,257},{2,258},{3,259},{4,260},{5,261},{6,262},{7,263},{8... | collective-permute-start | bytes 442376 | tf_op jit(solution)/shard_map/ppermute | solution.py:72
  97.9 4.3 %collective-permute-start.10 = (bf16[4,144,128]{2,1,0:T(8,128)(2,1)S(1)}, bf16[4,144,128]{2,1,0:T(8,128)(2,1)S(1)}, u32[]{:S(2)}, u32[]{:S(2)}) collective-permute-start(bf16[4,144,128]{2,1,0:T(8,128)(2,1)S(1)} %get-tuple-element.38), channel_id=1, source_target_pairs={{0,384},{1,385},{2,386},{3,387},{4,388},{5,389},{6,390},{7,391},{8... | collective-permute-start | bytes 442376 | tf_op jit(solution)/shard_map/ppermute | solution.py:72
  102.8 9.0 %all-to-all-done.2.rows_ref = bf16[32,16,2048]{2,1,0:T(8,128)(2,1)S(1)} async-done(((bf16[32,16,2048]{2,1,0:T(8,128)(2,1)}), bf16[32,16,2048]{2,1,0:T(8,128)(2,1)S(1)}, u32[]{:S(2)}, u32[]{:S(2)}) %all-to-all-start.2) | async-done | bytes 2097184 | tf_op jit(solution)/shard_map/all_to_all | solution.py:62
  111.8 1.5 %combine.1 = bf16[8,16,2048]{2,1,0:T(8,128)(2,1)} custom-call(bf16[256,512]{1,0:T(8,128)(2,1)S(1)} %mixing.1.mix_ref, bf16[32,16,2048]{2,1,0:T(8,128)(2,1)S(1)} %all-to-all-done.2.rows_ref), custom_call_target="tpu_custom_call" | custom-call | tf_op jit(solution)/shard_map/combine/pallas_call | solution.py:427
  113.3 0.9 collective-permute-done.9.got2_ref
  114.2 2.4 %collective-permute-done.10.got3_ref = bf16[4,144,128]{2,1,0:T(8,128)(2,1)S(1)} collective-permute-done((bf16[4,144,128]{2,1,0:T(8,128)(2,1)S(1)}, bf16[4,144,128]{2,1,0:T(8,128)(2,1)S(1)}, u32[]{:S(2)}, u32[]{:S(2)}) %collective-permute-start.10) | collective-permute-done | bytes 147488 | tf_op jit(solution)/shard_map/ppermute | solution.py:72
  116.6 5.5 %all-to-all-start.3 = ((bf16[8,16,2048]{2,1,0:T(8,128)(2,1)}), bf16[8,16,2048]{2,1,0:T(8,128)(2,1)S(1)}, u32[]{:S(2)}, u32[]{:S(2)}) async-start(bf16[8,16,2048]{2,1,0:T(8,128)(2,1)} %combine.1), calls=%async_computation.3 | async-start | bytes 1048576 | tf_op jit(solution)/shard_map/all_to_all | solution.py:62
  122.8 3.9 %collective-permute-start.11 = (bf16[1,144,128]{2,1,0:T(8,128)(2,1)S(1)}, bf16[1,144,128]{2,1,0:T(8,128)(2,1)S(1)}, u32[]{:S(2)}, u32[]{:S(2)}) collective-permute-start(bf16[1,144,128]{2,1,0:T(8,128)(2,1)S(1)} %get-tuple-element.45), channel_id=1, source_target_pairs={{0,32},{1,33},{2,34},{3,35},{4,36},{5,37},{6,38},{7,39},{8,40},{9,... | collective-permute-start | bytes 110600 | tf_op jit(solution)/shard_map/ppermute | solution.py:72
  126.7 4.3 %collective-permute-start.12 = (bf16[1,144,128]{2,1,0:T(8,128)(2,1)S(1)}, bf16[1,144,128]{2,1,0:T(8,128)(2,1)S(1)}, u32[]{:S(2)}, u32[]{:S(2)}) collective-permute-start(bf16[1,144,128]{2,1,0:T(8,128)(2,1)S(1)} %get-tuple-element.46), channel_id=1, source_target_pairs={{0,64},{1,65},{2,66},{3,67},{4,68},{5,69},{6,70},{7,71},{8,72},{9,... | collective-permute-start | bytes 110600 | tf_op jit(solution)/shard_map/ppermute | solution.py:72
  131.0 3.4 %collective-permute-start.13 = (bf16[1,144,128]{2,1,0:T(8,128)(2,1)S(1)}, bf16[1,144,128]{2,1,0:T(8,128)(2,1)S(1)}, u32[]{:S(2)}, u32[]{:S(2)}) collective-permute-start(bf16[1,144,128]{2,1,0:T(8,128)(2,1)S(1)} %get-tuple-element.47), channel_id=1, source_target_pairs={{0,96},{1,97},{2,98},{3,99},{4,100},{5,101},{6,102},{7,103},{8,104... | collective-permute-start | bytes 110600 | tf_op jit(solution)/shard_map/ppermute | solution.py:72
  134.4 1.1 collective-permute-done.12.got2_ref
  135.5 1.4 %collective-permute-done.13.got3_ref = bf16[1,144,128]{2,1,0:T(8,128)(2,1)S(1)} collective-permute-done((bf16[1,144,128]{2,1,0:T(8,128)(2,1)S(1)}, bf16[1,144,128]{2,1,0:T(8,128)(2,1)S(1)}, u32[]{:S(2)}, u32[]{:S(2)}) %collective-permute-start.13) | collective-permute-done | bytes 36896 | tf_op jit(solution)/shard_map/ppermute | solution.py:72
  (39 shorter events, 6.0 us)
Async XLA Ops:
  2.4 23.9 %all-to-all-start = ((bf16[8,16,2304]{2,1,0:T(8,128)(2,1)}), bf16[8,16,2304]{2,1,0:T(8,128)(2,1)S(1)}, u32[]{:S(2)}, u32[]{:S(2)}) async-start(bf16[8,16,2304]{2,1,0:T(8,128)(2,1)} %pack.1), calls=%async_computation | async-start | bytes 1179648 | tf_op jit(solution)/shard_map/all_to_all | solution.py:62
  13.5 17.0 %collective-permute-start = (bf16[128,128]{1,0:T(8,128)(2,1)S(1)}, bf16[128,128]{1,0:T(8,128)(2,1)S(1)}, u32[]{:S(2)}, u32[]{:S(2)}) collective-permute-start(bf16[128,128]{1,0:T(8,128)(2,1)S(1)} %reshape.11.query_ref), channel_id=1, source_target_pairs={{0,32},{1,33},{2,34},{3,35},{4,36},{5,37},{6,38},{7,39},{8,40},{9,... | collective-permute-start | bytes 98312 | tf_op jit(solution)/shard_map/ppermute | solution.py:72
  17.5 13.1 %collective-permute-start.1 = (bf16[128,128]{1,0:T(8,128)(2,1)S(1)}, bf16[128,128]{1,0:T(8,128)(2,1)S(1)}, u32[]{:S(2)}, u32[]{:S(2)}) collective-permute-start(bf16[128,128]{1,0:T(8,128)(2,1)S(1)} %reshape.11.query_ref), channel_id=1, source_target_pairs={{0,64},{1,65},{2,66},{3,67},{4,68},{5,69},{6,70},{7,71},{8,72},{9,... | collective-permute-start | bytes 98312 | tf_op jit(solution)/shard_map/ppermute | solution.py:72
  21.8 8.8 %collective-permute-start.2 = (bf16[128,128]{1,0:T(8,128)(2,1)S(1)}, bf16[128,128]{1,0:T(8,128)(2,1)S(1)}, u32[]{:S(2)}, u32[]{:S(2)}) collective-permute-start(bf16[128,128]{1,0:T(8,128)(2,1)S(1)} %reshape.11.query_ref), channel_id=1, source_target_pairs={{0,96},{1,97},{2,98},{3,99},{4,100},{5,101},{6,102},{7,103},{8,104... | collective-permute-start | bytes 98312 | tf_op jit(solution)/shard_map/ppermute | solution.py:72
  26.4 0.8 copy-start
  30.6 12.4 %copy-start.7 = (bf16[192,2048]{1,0:T(8,128)(2,1)S(1)}, bf16[192,2048]{1,0:T(8,128)(2,1)}, u32[]{:S(2)}) copy-start(bf16[192,2048]{1,0:T(8,128)(2,1)} %refs_1_.1) | copy-start | bytes 2359300
  30.6 38.2 %all-to-all-start.1 = ((bf16[32,16,2048]{2,1,0:T(8,128)(2,1)}), bf16[32,16,2048]{2,1,0:T(8,128)(2,1)S(1)}, u32[]{:S(2)}, u32[]{:S(2)}) async-start(bf16[32,16,2048]{2,1,0:T(8,128)(2,1)} %dispatch.1), calls=%async_computation.1 | async-start | bytes 4194304 | tf_op jit(solution)/shard_map/all_to_all | solution.py:62
  41.0 15.8 %collective-permute-start.3 = (bf16[2048,384]{1,0:T(8,128)(2,1)}, bf16[2048,384]{1,0:T(8,128)(2,1)}, u32[]{:S(2)}, u32[]{:S(2)}) collective-permute-start(bf16[2048,384]{1,0:T(8,128)(2,1)} %refs_0_.1), channel_id=1, source_target_pairs={{0,1},{1,0},{2,3},{3,2},{4,5},{5,4},{6,7},{7,6},{8,9},{9,8},{10,11... | collective-permute-start | bytes 4718600 | tf_op jit(solution)/shard_map/ppermute | solution.py:72
  43.0 13.0 %collective-permute-start.4 = (bf16[192,2048]{1,0:T(8,128)(2,1)S(1)}, bf16[192,2048]{1,0:T(8,128)(2,1)S(1)}, u32[]{:S(2)}, u32[]{:S(2)}) collective-permute-start(bf16[192,2048]{1,0:T(8,128)(2,1)S(1)} %copy-done.7), channel_id=1, source_target_pairs={{0,1},{1,0},{2,3},{3,2},{4,5},{5,4},{6,7},{7,6},{8,9},{9,8},{10,11... | collective-permute-start | bytes 2359304 | tf_op jit(solution)/shard_map/ppermute | solution.py:72
  45.4 30.0 %collective-permute-start.5 = (bf16[512,128]{1,0:T(8,128)(2,1)S(1)}, bf16[512,128]{1,0:T(8,128)(2,1)S(1)}, u32[]{:S(2)}, u32[]{:S(2)}) collective-permute-start(bf16[512,128]{1,0:T(8,128)(2,1)S(1)} %constant_dynamic-update-slice_fusion), channel_id=1, source_target_pairs={{0,128},{1,129},{2,130},{3,131},{4,132},{5,133},{6,134},{7,135},{8... | collective-permute-start | bytes 393224 | tf_op jit(solution)/shard_map/ppermute | solution.py:72
  48.8 26.6 %collective-permute-start.6 = (bf16[512,128]{1,0:T(8,128)(2,1)S(1)}, bf16[512,128]{1,0:T(8,128)(2,1)S(1)}, u32[]{:S(2)}, u32[]{:S(2)}) collective-permute-start(bf16[512,128]{1,0:T(8,128)(2,1)S(1)} %constant_dynamic-update-slice_fusion), channel_id=1, source_target_pairs={{0,256},{1,257},{2,258},{3,259},{4,260},{5,261},{6,262},{7,263},{8... | collective-permute-start | bytes 393224 | tf_op jit(solution)/shard_map/ppermute | solution.py:72
  51.6 23.9 %collective-permute-start.7 = (bf16[512,128]{1,0:T(8,128)(2,1)S(1)}, bf16[512,128]{1,0:T(8,128)(2,1)S(1)}, u32[]{:S(2)}, u32[]{:S(2)}) collective-permute-start(bf16[512,128]{1,0:T(8,128)(2,1)S(1)} %constant_dynamic-update-slice_fusion), channel_id=1, source_target_pairs={{0,384},{1,385},{2,386},{3,387},{4,388},{5,389},{6,390},{7,391},{8... | collective-permute-start | bytes 393224 | tf_op jit(solution)/shard_map/ppermute | solution.py:72
  55.9 0.9 copy-start.8
  75.4 9.7 %copy-start.5 = (s32[16]{0:T(128)S(1)}, s32[16]{0:T(128)}, u32[]{:S(2)}) copy-start(s32[16]{0:T(128)} %owner_ref.1) | copy-start | bytes 196
  75.4 9.7 %copy-start.6 = (s32[16]{0:T(128)S(1)}, s32[16]{0:T(128)}, u32[]{:S(2)}) copy-start(s32[16]{0:T(128)} %count_ref.1) | copy-start | bytes 196
  75.4 0.6 copy-start.9
  76.1 35.7 %all-to-all-start.2 = ((bf16[32,16,2048]{2,1,0:T(8,128)(2,1)}), bf16[32,16,2048]{2,1,0:T(8,128)(2,1)S(1)}, u32[]{:S(2)}, u32[]{:S(2)}) async-start(bf16[32,16,2048]{2,1,0:T(8,128)(2,1)} %expert.1), calls=%async_computation.2 | async-start | bytes 4194304 | tf_op jit(solution)/shard_map/all_to_all | solution.py:62
  84.1 18.2 %copy-start.1 = (bf16[8,16,2304]{2,1,0:T(8,128)(2,1)S(1)}, bf16[8,16,2304]{2,1,0:T(8,128)(2,1)}, u32[]{:S(2)}) copy-start(bf16[8,16,2304]{2,1,0:T(8,128)(2,1)} %copy-done) | copy-start | bytes 1769476
  84.1 18.2 %copy-start.4 = (s32[128]{0:T(128)S(1)}, s32[128]{0:T(128)}, u32[]{:S(2)}) copy-start(s32[128]{0:T(128)} %param.14) | copy-start | bytes 1540
  85.1 1.6 %copy-start.2 = (bf16[16,64,1024]{2,1,0:T(8,128)(2,1)S(1)}, bf16[16,64,1024]{2,1,0:T(8,128)(2,1)}, u32[]{:S(2)}) copy-start(bf16[16,64,1024]{2,1,0:T(8,128)(2,1)} %pool_ref.1) | copy-start | bytes 6291460
  91.8 21.5 %collective-permute-start.8 = (bf16[4,144,128]{2,1,0:T(8,128)(2,1)S(1)}, bf16[4,144,128]{2,1,0:T(8,128)(2,1)S(1)}, u32[]{:S(2)}, u32[]{:S(2)}) collective-permute-start(bf16[4,144,128]{2,1,0:T(8,128)(2,1)S(1)} %get-tuple-element.36), channel_id=1, source_target_pairs={{0,128},{1,129},{2,130},{3,131},{4,132},{5,133},{6,134},{7,135},{8... | collective-permute-start | bytes 442376 | tf_op jit(solution)/shard_map/ppermute | solution.py:72
  95.2 19.0 %collective-permute-start.9 = (bf16[4,144,128]{2,1,0:T(8,128)(2,1)S(1)}, bf16[4,144,128]{2,1,0:T(8,128)(2,1)S(1)}, u32[]{:S(2)}, u32[]{:S(2)}) collective-permute-start(bf16[4,144,128]{2,1,0:T(8,128)(2,1)S(1)} %get-tuple-element.37), channel_id=1, source_target_pairs={{0,256},{1,257},{2,258},{3,259},{4,260},{5,261},{6,262},{7,263},{8... | collective-permute-start | bytes 442376 | tf_op jit(solution)/shard_map/ppermute | solution.py:72
  97.9 18.7 %collective-permute-start.10 = (bf16[4,144,128]{2,1,0:T(8,128)(2,1)S(1)}, bf16[4,144,128]{2,1,0:T(8,128)(2,1)S(1)}, u32[]{:S(2)}, u32[]{:S(2)}) collective-permute-start(bf16[4,144,128]{2,1,0:T(8,128)(2,1)S(1)} %get-tuple-element.38), channel_id=1, source_target_pairs={{0,384},{1,385},{2,386},{3,387},{4,388},{5,389},{6,390},{7,391},{8... | collective-permute-start | bytes 442376 | tf_op jit(solution)/shard_map/ppermute | solution.py:72
  102.8 34.1 %copy-start.3 = (bf16[2,1024]{1,0:T(2,128)(2,1)S(1)}, bf16[2,1024]{1,0:T(2,128)(2,1)}, u32[]{:S(2)}) copy-start(bf16[2,1024]{1,0:T(2,128)(2,1)} %new_ref.1) | copy-start | bytes 12292
  116.6 21.2 %all-to-all-start.3 = ((bf16[8,16,2048]{2,1,0:T(8,128)(2,1)}), bf16[8,16,2048]{2,1,0:T(8,128)(2,1)S(1)}, u32[]{:S(2)}, u32[]{:S(2)}) async-start(bf16[8,16,2048]{2,1,0:T(8,128)(2,1)} %combine.1), calls=%async_computation.3 | async-start | bytes 1048576 | tf_op jit(solution)/shard_map/all_to_all | solution.py:62
  122.8 11.6 %collective-permute-start.11 = (bf16[1,144,128]{2,1,0:T(8,128)(2,1)S(1)}, bf16[1,144,128]{2,1,0:T(8,128)(2,1)S(1)}, u32[]{:S(2)}, u32[]{:S(2)}) collective-permute-start(bf16[1,144,128]{2,1,0:T(8,128)(2,1)S(1)} %get-tuple-element.45), channel_id=1, source_target_pairs={{0,32},{1,33},{2,34},{3,35},{4,36},{5,37},{6,38},{7,39},{8,40},{9,... | collective-permute-start | bytes 110600 | tf_op jit(solution)/shard_map/ppermute | solution.py:72
  126.7 8.7 %collective-permute-start.12 = (bf16[1,144,128]{2,1,0:T(8,128)(2,1)S(1)}, bf16[1,144,128]{2,1,0:T(8,128)(2,1)S(1)}, u32[]{:S(2)}, u32[]{:S(2)}) collective-permute-start(bf16[1,144,128]{2,1,0:T(8,128)(2,1)S(1)} %get-tuple-element.46), channel_id=1, source_target_pairs={{0,64},{1,65},{2,66},{3,67},{4,68},{5,69},{6,70},{7,71},{8,72},{9,... | collective-permute-start | bytes 110600 | tf_op jit(solution)/shard_map/ppermute | solution.py:72
  131.0 5.9 %collective-permute-start.13 = (bf16[1,144,128]{2,1,0:T(8,128)(2,1)S(1)}, bf16[1,144,128]{2,1,0:T(8,128)(2,1)S(1)}, u32[]{:S(2)}, u32[]{:S(2)}) collective-permute-start(bf16[1,144,128]{2,1,0:T(8,128)(2,1)S(1)} %get-tuple-element.47), channel_id=1, source_target_pairs={{0,96},{1,97},{2,98},{3,99},{4,100},{5,101},{6,102},{7,103},{8,104... | collective-permute-start | bytes 110600 | tf_op jit(solution)/shard_map/ppermute | solution.py:72

commit v9 on v8

--- a/solution.py
+++ b/solution.py
@@ -64,11 +64,12 @@
     )
 
 
-def moved(array, dx=0, dz=0, dc=0):
+def moved(array, first=0, second=0, core=0):
     pairs = []
     for device in range(512):
         x, zl, y, zh, c = position(device)
-        pairs.append((device, number((x + dx) % 4, (zl + dz) % 4, y, zh, (c + dc) % 2)))
+        dx, dz = (first, second) if c else (second, first)
+        pairs.append((device, number((x + dx) % 4, (zl + dz) % 4, y, zh, (c + core) % 2)))
     return lax.ppermute(array, AXIS, pairs)
 
 
@@ -183,10 +184,17 @@
 
 
 def expert_kernel(rows_ref, *refs):
-    sources, out_ref, held, made_ref, came_sem, left_sem = refs[:4], refs[4], refs[5:9], *refs[9:]
+    sources, out_ref, wide_ref, tall_ref, made_ref, came_sem, left_sem = refs[:4], *refs[4:]
+    both, quarter = 2 * HALF, HALF
+    places = (
+        wide_ref.at[:, :both],
+        wide_ref.at[:, both:],
+        tall_ref.at[:quarter],
+        tall_ref.at[quarter:],
+    )
     come = [
-        pltpu.make_async_copy(source, kept, came_sem.at[i])
-        for i, (source, kept) in enumerate(zip(sources, held))
+        pltpu.make_async_copy(source, place, came_sem.at[i])
+        for i, (source, place) in enumerate(zip(sources, places))
     ]
     for copy in come:
         copy.start()
@@ -194,16 +202,19 @@
     leave = []
     for s in range(EXPERT_STEPS):
         x = rows_ref[s * step : (s + 1) * step].reshape(step * ROWS, D)
-        total = jnp.zeros((step * ROWS, D), F32)
-        for pair in range(2):
-            if s == 0:
-                come[2 * pair].wait()
-            both = jnp.dot(x, held[2 * pair][...], preferred_element_type=F32)
-            gate, up = both[:, :HALF], both[:, HALF:]
-            act = (gate / (1.0 + jnp.exp(-gate)) * up).astype(BF16)
-            if s == 0:
-                come[2 * pair + 1].wait()
-            total = total + jnp.dot(act, held[2 * pair + 1][...], preferred_element_type=F32)
+        if s == 0:
+            come[0].wait()
+            come[1].wait()
+        wide = jnp.dot(x, wide_ref[...], preferred_element_type=F32)
+        acts = []
+        for at in (0, both):
+            gate, up = wide[:, at : at + HALF], wide[:, at + HALF : at + both]
+            acts.append((gate / (1.0 + jnp.exp(-gate)) * up).astype(BF16))
+        act = jnp.concatenate(acts, axis=1)
+        if s == 0:
+            come[2].wait()
+            come[3].wait()
+        total = jnp.dot(act, tall_ref[...], preferred_element_type=F32)
         made_ref[s] = total.astype(BF16).reshape(step, ROWS, D)
         leave.append(
             pltpu.make_async_copy(
@@ -229,8 +240,9 @@
         in_specs=whole(1) + [apart] * 4,
         out_specs=apart,
         limit=VMEM_MOST,
-        scratch_shapes=[pltpu.VMEM(w.shape, BF16) for w in weights]
-        + [
+        scratch_shapes=[
+            pltpu.VMEM((D, 4 * HALF), BF16),
+            pltpu.VMEM((2 * HALF, D), BF16),
             pltpu.VMEM((EXPERT_STEPS, REACH // EXPERT_STEPS, ROWS, D), BF16),
             pltpu.SemaphoreType.DMA((4,)),
             pltpu.SemaphoreType.DMA((EXPERT_STEPS,)),
@@ -282,21 +294,26 @@
         )
 
 
+def pair(x_first, dz, dx):
+    return jnp.where(x_first, dz * 4 + dx, dx * 4 + dz)
+
+
 def partial_kernel(owner_ref, count_ref, query_ref, pool_ref, *refs):
     sends, (top_ref, sum_ref, acc_ref) = refs[:SIDE], refs[SIDE:]
     scale = 1.0 / math.sqrt(HEAD)
     top_ref[...] = jnp.full(top_ref.shape, NEG, F32)
     sum_ref[...] = jnp.zeros(sum_ref.shape, F32)
     acc_ref[...] = jnp.zeros(acc_ref.shape, F32)
-    x, zl, _, _, _ = position(lax.axis_index(AXIS))
+    x, zl, _, _, c = position(lax.axis_index(AXIS))
+    x_first = c == 1
     per = HEADS // GROUPS
     own = iota((HEADS, KV), 1) // HEAD == iota((HEADS, KV), 0) // per
     slot = iota((HEADS, LEN), 1)
     for b in range(BLOCKS):
         owner = owner_ref[b]
         ax, az, request = owner >> 3, (owner >> 1) & 3, owner & 1
-        asked = ((x - ax) & 3) * 8 + ((zl - az) & 3) * 2 + request
-        state = ((ax - x) & 3) * 8 + ((az - zl) & 3) * 2 + request
+        asked = pair(x_first, (zl - az) & 3, (x - ax) & 3) * 2 + request
+        state = pair(x_first, (az - zl) & 3, (ax - x) & 3) * 2 + request
         rows = pl.ds(pl.multiple_of(state * HEADS, HEADS), HEADS)
         query = query_ref[pl.ds(pl.multiple_of(asked * HEADS, HEADS), HEADS), :]
         wide = jnp.where(own, jnp.concatenate([query] * GROUPS, axis=1), jnp.zeros((), BF16))
@@ -403,7 +420,7 @@
     )
     own_queries = queries.reshape(REQUESTS * HEADS, HEAD)
     near = exchange(packed, RING_GROUPS)
-    line = along(own_queries, "dz")
+    line = along(own_queries, "first")
     send = call(dispatch_kernel, "dispatch", shape((REACH, ROWS, D)), 2, limit=VMEM_ALL)(
         near, slot_row
     )
@@ -411,10 +428,10 @@
     line = jnp.concatenate(line, axis=0)
     received = exchange(send, REACH_GROUPS)
 
-    other_gate_up, other_down = moved(w_gate_up, dc=1), moved(w_down, dc=1)
-    square = along(line, "dx")
+    other_gate_up, other_down = moved(w_gate_up, core=1), moved(w_down, core=1)
+    square = along(line, "second")
     rows = expert(
-        received, w_gate_up, w_down, other_gate_up, other_down
+        received, w_gate_up, other_gate_up, w_down, other_down
     )
     rows, square = lax.optimization_barrier((rows, square))
     returned = exchange(rows, REACH_GROUPS)
@@ -422,7 +439,7 @@
     partials = partial_attention(
         block_owner, block_tokens, jnp.concatenate(square, axis=0), key_value_pool
     )
-    across = spread(partials, "dx")
+    across = spread(partials, "second")
     mix = call(mixing_kernel, "mixing", shape((2 * NEAR, REACH * ROWS)), 2)(near, slot_row)
     parts = call(combine_kernel, "combine", shape((RING, TOK, D)), 2)(mix, on_core(returned))
     parts, across = lax.optimization_barrier((parts, across))
@@ -436,7 +453,7 @@
         out_specs=whole(SIDE),
     )(*across)
     attn_out = call(finish_kernel, "finish", shape((REQUESTS, HEADS * HEAD)), 6)(
-        *spread(met, "dz"), own_queries, incoming_key_value
+        *spread(met, "first"), own_queries, incoming_key_value
     )
     moe_out = call(total_kernel, "total", shape((TOK, D)), 1)(parts)
     return (moe_out, attn_out)

time: 139 us -> 137 us (0.986)
  waiting for transfers between devices: 28 us -> 25.9 us
    ppermute x14, waiting for transfers between devices: 5.8 us -> 2.83 us  [moved(): return lax.ppermute(array, AXIS, pairs)]
  transfers between devices with their start and end apart: 18 -> 18, of which waited for: 7 -> 5; matrix products, arithmetic and copies ran while one was open for 1% -> 1% of each run, Pallas kernels for 13% -> 14%
where the time goes in v9:
time: 137 us; the launch traced here: 136 us
  starting transfers between devices  81.8 us (60%)
  waiting for transfers between devices  25.9 us (19%)
  Pallas kernels  21.5 us (16%)
  local copies, waits for them, and re-layouts  4.77 us (3%)
    ppermute x14, starting transfers between devices, moved(): return lax.ppermute(array, AXIS, pairs)  48.4 us
    all_to_all x4, starting transfers between devices, exchange(): lax.all_to_all(array, AXIS, split_axis=0, concat_axis=0, axis_index_group...  33.4 us
    all_to_all x4, waiting for transfers between devices, exchange(): lax.all_to_all(array, AXIS, split_axis=0, concat_axis=0, axis_index_group...  23.1 us
    pallas_call x1, Pallas kernels, expert(): call(expert_kernel, 'expert', shape(rows.shape), 5, in_specs=whole(1) + [...  6.87 us
    pallas_call x1, Pallas kernels, partial_attention(): call(partial_kernel, 'partial_attention', [shape((SIDE, MESSAGE, HEAD))]...  5.12 us
    unnamed x23, local copies, waits for them, and re-layouts  3.97 us
    pallas_call x1, Pallas kernels, shards(): call(dispatch_kernel, 'dispatch', shape((REACH, ROWS, D)), 2, limit=VMEM_...  3.4 us
    ppermute x14, waiting for transfers between devices, moved(): return lax.ppermute(array, AXIS, pairs)  2.83 us
  transfers between devices with their start and end apart: 18, of which 5 were waited for; matrix products, arithmetic and copies ran while one was open for 1% of the time, Pallas kernels for 14%

profile of v9, /device:TPU:2, one launch (start us, length us, event | category | flops | bytes accessed | tf_op | source)
XLA Modules:
  0.0 136.0 jit_solution(3639289617032173289)
XLA Ops:
  0.6 1.8 %pack.1 = bf16[8,16,2304]{2,1,0:T(8,128)(2,1)} custom-call(bf16[16,2048]{1,0:T(8,128)(2,1)} %token_ref.1, s32[8,16]{1,0:T(8,128)} %bitcast.5, f32[8,16]{1,0:T(8,128)} %bitcast.6), custom_call_target="tpu_custom_call" | custom-call | tf_op jit(solution)/shard_map/pack/pallas_call | solution.py:418
  2.4 10.3 %all-to-all-start = ((bf16[8,16,2304]{2,1,0:T(8,128)(2,1)}), bf16[8,16,2304]{2,1,0:T(8,128)(2,1)S(1)}, u32[]{:S(2)}, u32[]{:S(2)}) async-start(bf16[8,16,2304]{2,1,0:T(8,128)(2,1)} %pack.1), calls=%async_computation | async-start | bytes 1179648 | tf_op jit(solution)/shard_map/all_to_all | solution.py:62
  13.5 3.9 %collective-permute-start = (bf16[128,128]{1,0:T(8,128)(2,1)S(1)}, bf16[128,128]{1,0:T(8,128)(2,1)S(1)}, u32[]{:S(2)}, u32[]{:S(2)}) collective-permute-start(bf16[128,128]{1,0:T(8,128)(2,1)S(1)} %reshape.11.query_ref), channel_id=1, source_target_pairs={{0,32},{1,129},{2,34},{3,131},{4,36},{5,133},{6,38},{7,135},{8,40}... | collective-permute-start | bytes 98312 | tf_op jit(solution)/shard_map/ppermute | solution.py:73
  17.5 4.3 %collective-permute-start.1 = (bf16[128,128]{1,0:T(8,128)(2,1)S(1)}, bf16[128,128]{1,0:T(8,128)(2,1)S(1)}, u32[]{:S(2)}, u32[]{:S(2)}) collective-permute-start(bf16[128,128]{1,0:T(8,128)(2,1)S(1)} %reshape.11.query_ref), channel_id=1, source_target_pairs={{0,64},{1,257},{2,66},{3,259},{4,68},{5,261},{6,70},{7,263},{8,72}... | collective-permute-start | bytes 98312 | tf_op jit(solution)/shard_map/ppermute | solution.py:73
  21.8 3.4 %collective-permute-start.2 = (bf16[128,128]{1,0:T(8,128)(2,1)S(1)}, bf16[128,128]{1,0:T(8,128)(2,1)S(1)}, u32[]{:S(2)}, u32[]{:S(2)}) collective-permute-start(bf16[128,128]{1,0:T(8,128)(2,1)S(1)} %reshape.11.query_ref), channel_id=1, source_target_pairs={{0,96},{1,385},{2,98},{3,387},{4,100},{5,389},{6,102},{7,391},{8,1... | collective-permute-start | bytes 98312 | tf_op jit(solution)/shard_map/ppermute | solution.py:73
  25.1 1.6 %all-to-all-done.near_ref = bf16[8,16,2304]{2,1,0:T(8,128)(2,1)S(1)} async-done(((bf16[8,16,2304]{2,1,0:T(8,128)(2,1)}), bf16[8,16,2304]{2,1,0:T(8,128)(2,1)S(1)}, u32[]{:S(2)}, u32[]{:S(2)}) %all-to-all-start) | async-done | bytes 589856 | tf_op jit(solution)/shard_map/all_to_all | solution.py:62
  26.8 0.8 copy-done
  27.6 3.4 %dispatch.1 = bf16[32,16,2048]{2,1,0:T(8,128)(2,1)} custom-call(bf16[8,16,2304]{2,1,0:T(8,128)(2,1)} %copy-done, s32[1,128]{1,0:T(1,128)} %bitcast.3), custom_call_target="tpu_custom_call" | custom-call | tf_op jit(solution)/shard_map/dispatch/pallas_call | solution.py:424
  31.0 10.4 %all-to-all-start.1 = ((bf16[32,16,2048]{2,1,0:T(8,128)(2,1)}), bf16[32,16,2048]{2,1,0:T(8,128)(2,1)S(1)}, u32[]{:S(2)}, u32[]{:S(2)}) async-start(bf16[32,16,2048]{2,1,0:T(8,128)(2,1)} %dispatch.1), calls=%async_computation.1 | async-start | bytes 4194304 | tf_op jit(solution)/shard_map/all_to_all | solution.py:62
  41.4 1.9 %collective-permute-start.3 = (bf16[2048,384]{1,0:T(8,128)(2,1)}, bf16[2048,384]{1,0:T(8,128)(2,1)}, u32[]{:S(2)}, u32[]{:S(2)}) collective-permute-start(bf16[2048,384]{1,0:T(8,128)(2,1)} %refs_0_.1), channel_id=1, source_target_pairs={{0,1},{1,0},{2,3},{3,2},{4,5},{5,4},{6,7},{7,6},{8,9},{9,8},{10,11... | collective-permute-start | bytes 4718600 | tf_op jit(solution)/shard_map/ppermute | solution.py:73
  43.3 2.4 %collective-permute-start.4 = (bf16[192,2048]{1,0:T(8,128)(2,1)S(1)}, bf16[192,2048]{1,0:T(8,128)(2,1)S(1)}, u32[]{:S(2)}, u32[]{:S(2)}) collective-permute-start(bf16[192,2048]{1,0:T(8,128)(2,1)S(1)} %copy-done.7), channel_id=1, source_target_pairs={{0,1},{1,0},{2,3},{3,2},{4,5},{5,4},{6,7},{7,6},{8,9},{9,8},{10,11... | collective-permute-start | bytes 2359304 | tf_op jit(solution)/shard_map/ppermute | solution.py:73
  45.8 3.4 %collective-permute-start.5 = (bf16[512,128]{1,0:T(8,128)(2,1)S(1)}, bf16[512,128]{1,0:T(8,128)(2,1)S(1)}, u32[]{:S(2)}, u32[]{:S(2)}) collective-permute-start(bf16[512,128]{1,0:T(8,128)(2,1)S(1)} %constant_dynamic-update-slice_fusion), channel_id=1, source_target_pairs={{0,128},{1,33},{2,130},{3,35},{4,132},{5,37},{6,134},{7,39},{8,136... | collective-permute-start | bytes 393224 | tf_op jit(solution)/shard_map/ppermute | solution.py:73
  49.2 2.7 %collective-permute-start.6 = (bf16[512,128]{1,0:T(8,128)(2,1)S(1)}, bf16[512,128]{1,0:T(8,128)(2,1)S(1)}, u32[]{:S(2)}, u32[]{:S(2)}) collective-permute-start(bf16[512,128]{1,0:T(8,128)(2,1)S(1)} %constant_dynamic-update-slice_fusion), channel_id=1, source_target_pairs={{0,256},{1,65},{2,258},{3,67},{4,260},{5,69},{6,262},{7,71},{8,264... | collective-permute-start | bytes 393224 | tf_op jit(solution)/shard_map/ppermute | solution.py:73
  51.9 4.3 %collective-permute-start.7 = (bf16[512,128]{1,0:T(8,128)(2,1)S(1)}, bf16[512,128]{1,0:T(8,128)(2,1)S(1)}, u32[]{:S(2)}, u32[]{:S(2)}) collective-permute-start(bf16[512,128]{1,0:T(8,128)(2,1)S(1)} %constant_dynamic-update-slice_fusion), channel_id=1, source_target_pairs={{0,384},{1,97},{2,386},{3,99},{4,388},{5,101},{6,390},{7,103},{8,3... | collective-permute-start | bytes 393224 | tf_op jit(solution)/shard_map/ppermute | solution.py:73
  56.3 0.9 copy-done.8
  57.2 11.8 %all-to-all-done.1.rows_ref = bf16[32,16,2048]{2,1,0:T(8,128)(2,1)S(1)} async-done(((bf16[32,16,2048]{2,1,0:T(8,128)(2,1)}), bf16[32,16,2048]{2,1,0:T(8,128)(2,1)S(1)}, u32[]{:S(2)}, u32[]{:S(2)}) %all-to-all-start.1) | async-done | bytes 2097184 | tf_op jit(solution)/shard_map/all_to_all | solution.py:62
  69.0 6.9 %expert.1 = bf16[32,16,2048]{2,1,0:T(8,128)(2,1)} custom-call(bf16[32,16,2048]{2,1,0:T(8,128)(2,1)S(1)} %all-to-all-done.1.rows_ref, bf16[2048,384]{1,0:T(8,128)(2,1)} %refs_0_.1, bf16[2048,384]{1,0:T(8,128)(2,1)} %collective-permute-done.3.refs_1_, bf16[192,2048]{1,0:T(8,128)(2,1)} %refs_2_.1, bf16[192,2048]{1,0:T(8,128)(2,1)} %copy-done.8), custom_call_target="tpu_custom_call" | custom-call | tf_op jit(solution)/shard_map/expert/pallas_call | solution.py:235
  76.6 8.0 %all-to-all-start.2 = ((bf16[32,16,2048]{2,1,0:T(8,128)(2,1)}), bf16[32,16,2048]{2,1,0:T(8,128)(2,1)S(1)}, u32[]{:S(2)}, u32[]{:S(2)}) async-start(bf16[32,16,2048]{2,1,0:T(8,128)(2,1)} %expert.1), calls=%async_computation.2 | async-start | bytes 4194304 | tf_op jit(solution)/shard_map/all_to_all | solution.py:62
  84.7 1.0 pad_maximum_fusion.query_ref
  85.7 1.6 %copy-done.2 = bf16[16,64,1024]{2,1,0:T(8,128)(2,1)S(1)} copy-done((bf16[16,64,1024]{2,1,0:T(8,128)(2,1)S(1)}, bf16[16,64,1024]{2,1,0:T(8,128)(2,1)}, u32[]{:S(2)}) %copy-start.2) | copy-done | bytes 2097176
  87.3 5.1 %partial_attention.1 = (bf16[4,144,128]{2,1,0:T(8,128)(2,1)S(1)}, bf16[4,144,128]{2,1,0:T(8,128)(2,1)S(1)}, bf16[4,144,128]{2,1,0:T(8,128)(2,1)S(1)}, bf16[4,144,128]{2,1,0:T(8,128)(2,1)S(1)}) custom-call(s32[16]{0:T(128)S(1)} %copy-done.5, s32[16]{0:T(128)S(1)} %copy-done.6, bf16[2048,128]{1,0:T(8,128)(2,1)S(1)} %pad_maximum_fusion.query_ref, ...), custom_call_target="tpu_custom_call" | custom-call | tf_op jit(solution)/shard_map/partial_attention/pallas_call | solution.py:357
  92.4 3.4 %collective-permute-start.8 = (bf16[4,144,128]{2,1,0:T(8,128)(2,1)S(1)}, bf16[4,144,128]{2,1,0:T(8,128)(2,1)S(1)}, u32[]{:S(2)}, u32[]{:S(2)}) collective-permute-start(bf16[4,144,128]{2,1,0:T(8,128)(2,1)S(1)} %get-tuple-element.36), channel_id=1, source_target_pairs={{0,128},{1,33},{2,130},{3,35},{4,132},{5,37},{6,134},{7,39},{8,136... | collective-permute-start | bytes 442376 | tf_op jit(solution)/shard_map/ppermute | solution.py:73
  95.8 2.7 %collective-permute-start.9 = (bf16[4,144,128]{2,1,0:T(8,128)(2,1)S(1)}, bf16[4,144,128]{2,1,0:T(8,128)(2,1)S(1)}, u32[]{:S(2)}, u32[]{:S(2)}) collective-permute-start(bf16[4,144,128]{2,1,0:T(8,128)(2,1)S(1)} %get-tuple-element.37), channel_id=1, source_target_pairs={{0,256},{1,65},{2,258},{3,67},{4,260},{5,69},{6,262},{7,71},{8,264... | collective-permute-start | bytes 442376 | tf_op jit(solution)/shard_map/ppermute | solution.py:73
  98.5 4.3 %collective-permute-start.10 = (bf16[4,144,128]{2,1,0:T(8,128)(2,1)S(1)}, bf16[4,144,128]{2,1,0:T(8,128)(2,1)S(1)}, u32[]{:S(2)}, u32[]{:S(2)}) collective-permute-start(bf16[4,144,128]{2,1,0:T(8,128)(2,1)S(1)} %get-tuple-element.38), channel_id=1, source_target_pairs={{0,384},{1,97},{2,386},{3,99},{4,388},{5,101},{6,390},{7,103},{8,3... | collective-permute-start | bytes 442376 | tf_op jit(solution)/shard_map/ppermute | solution.py:73
  103.4 9.7 %all-to-all-done.2.rows_ref = bf16[32,16,2048]{2,1,0:T(8,128)(2,1)S(1)} async-done(((bf16[32,16,2048]{2,1,0:T(8,128)(2,1)}), bf16[32,16,2048]{2,1,0:T(8,128)(2,1)S(1)}, u32[]{:S(2)}, u32[]{:S(2)}) %all-to-all-start.2) | async-done | bytes 2097184 | tf_op jit(solution)/shard_map/all_to_all | solution.py:62
  113.1 1.5 %combine.1 = bf16[8,16,2048]{2,1,0:T(8,128)(2,1)} custom-call(bf16[256,512]{1,0:T(8,128)(2,1)S(1)} %mixing.1.mix_ref, bf16[32,16,2048]{2,1,0:T(8,128)(2,1)S(1)} %all-to-all-done.2.rows_ref), custom_call_target="tpu_custom_call" | custom-call | tf_op jit(solution)/shard_map/combine/pallas_call | solution.py:444
  115.0 4.6 %all-to-all-start.3 = ((bf16[8,16,2048]{2,1,0:T(8,128)(2,1)}), bf16[8,16,2048]{2,1,0:T(8,128)(2,1)S(1)}, u32[]{:S(2)}, u32[]{:S(2)}) async-start(bf16[8,16,2048]{2,1,0:T(8,128)(2,1)} %combine.1), calls=%async_computation.3 | async-start | bytes 1048576 | tf_op jit(solution)/shard_map/all_to_all | solution.py:62
  120.3 3.9 %collective-permute-start.11 = (bf16[1,144,128]{2,1,0:T(8,128)(2,1)S(1)}, bf16[1,144,128]{2,1,0:T(8,128)(2,1)S(1)}, u32[]{:S(2)}, u32[]{:S(2)}) collective-permute-start(bf16[1,144,128]{2,1,0:T(8,128)(2,1)S(1)} %get-tuple-element.45), channel_id=1, source_target_pairs={{0,32},{1,129},{2,34},{3,131},{4,36},{5,133},{6,38},{7,135},{8,40}... | collective-permute-start | bytes 110600 | tf_op jit(solution)/shard_map/ppermute | solution.py:73
  124.2 4.3 %collective-permute-start.12 = (bf16[1,144,128]{2,1,0:T(8,128)(2,1)S(1)}, bf16[1,144,128]{2,1,0:T(8,128)(2,1)S(1)}, u32[]{:S(2)}, u32[]{:S(2)}) collective-permute-start(bf16[1,144,128]{2,1,0:T(8,128)(2,1)S(1)} %get-tuple-element.46), channel_id=1, source_target_pairs={{0,64},{1,257},{2,66},{3,259},{4,68},{5,261},{6,70},{7,263},{8,72}... | collective-permute-start | bytes 110600 | tf_op jit(solution)/shard_map/ppermute | solution.py:73
  128.5 3.4 %collective-permute-start.13 = (bf16[1,144,128]{2,1,0:T(8,128)(2,1)S(1)}, bf16[1,144,128]{2,1,0:T(8,128)(2,1)S(1)}, u32[]{:S(2)}, u32[]{:S(2)}) collective-permute-start(bf16[1,144,128]{2,1,0:T(8,128)(2,1)S(1)} %get-tuple-element.47), channel_id=1, source_target_pairs={{0,96},{1,385},{2,98},{3,387},{4,100},{5,389},{6,102},{7,391},{8,1... | collective-permute-start | bytes 110600 | tf_op jit(solution)/shard_map/ppermute | solution.py:73
  131.9 2.5 %collective-permute-done.13.got3_ref = bf16[1,144,128]{2,1,0:T(8,128)(2,1)S(1)} collective-permute-done((bf16[1,144,128]{2,1,0:T(8,128)(2,1)S(1)}, bf16[1,144,128]{2,1,0:T(8,128)(2,1)S(1)}, u32[]{:S(2)}, u32[]{:S(2)}) %collective-permute-start.13) | collective-permute-done | bytes 36896 | tf_op jit(solution)/shard_map/ppermute | solution.py:73
  134.4 0.9 finish.1
  (39 shorter events, 3.8 us)
Async XLA Ops:
  2.4 24.3 %all-to-all-start = ((bf16[8,16,2304]{2,1,0:T(8,128)(2,1)}), bf16[8,16,2304]{2,1,0:T(8,128)(2,1)S(1)}, u32[]{:S(2)}, u32[]{:S(2)}) async-start(bf16[8,16,2304]{2,1,0:T(8,128)(2,1)} %pack.1), calls=%async_computation | async-start | bytes 1179648 | tf_op jit(solution)/shard_map/all_to_all | solution.py:62
  13.5 17.4 %collective-permute-start = (bf16[128,128]{1,0:T(8,128)(2,1)S(1)}, bf16[128,128]{1,0:T(8,128)(2,1)S(1)}, u32[]{:S(2)}, u32[]{:S(2)}) collective-permute-start(bf16[128,128]{1,0:T(8,128)(2,1)S(1)} %reshape.11.query_ref), channel_id=1, source_target_pairs={{0,32},{1,129},{2,34},{3,131},{4,36},{5,133},{6,38},{7,135},{8,40}... | collective-permute-start | bytes 98312 | tf_op jit(solution)/shard_map/ppermute | solution.py:73
  17.5 13.5 %collective-permute-start.1 = (bf16[128,128]{1,0:T(8,128)(2,1)S(1)}, bf16[128,128]{1,0:T(8,128)(2,1)S(1)}, u32[]{:S(2)}, u32[]{:S(2)}) collective-permute-start(bf16[128,128]{1,0:T(8,128)(2,1)S(1)} %reshape.11.query_ref), channel_id=1, source_target_pairs={{0,64},{1,257},{2,66},{3,259},{4,68},{5,261},{6,70},{7,263},{8,72}... | collective-permute-start | bytes 98312 | tf_op jit(solution)/shard_map/ppermute | solution.py:73
  21.8 9.2 %collective-permute-start.2 = (bf16[128,128]{1,0:T(8,128)(2,1)S(1)}, bf16[128,128]{1,0:T(8,128)(2,1)S(1)}, u32[]{:S(2)}, u32[]{:S(2)}) collective-permute-start(bf16[128,128]{1,0:T(8,128)(2,1)S(1)} %reshape.11.query_ref), channel_id=1, source_target_pairs={{0,96},{1,385},{2,98},{3,387},{4,100},{5,389},{6,102},{7,391},{8,1... | collective-permute-start | bytes 98312 | tf_op jit(solution)/shard_map/ppermute | solution.py:73
  26.8 0.8 copy-start
  31.0 12.4 %copy-start.7 = (bf16[192,2048]{1,0:T(8,128)(2,1)S(1)}, bf16[192,2048]{1,0:T(8,128)(2,1)}, u32[]{:S(2)}) copy-start(bf16[192,2048]{1,0:T(8,128)(2,1)} %refs_2_.1) | copy-start | bytes 2359300
  31.0 38.0 %all-to-all-start.1 = ((bf16[32,16,2048]{2,1,0:T(8,128)(2,1)}), bf16[32,16,2048]{2,1,0:T(8,128)(2,1)S(1)}, u32[]{:S(2)}, u32[]{:S(2)}) async-start(bf16[32,16,2048]{2,1,0:T(8,128)(2,1)} %dispatch.1), calls=%async_computation.1 | async-start | bytes 4194304 | tf_op jit(solution)/shard_map/all_to_all | solution.py:62
  41.4 15.8 %collective-permute-start.3 = (bf16[2048,384]{1,0:T(8,128)(2,1)}, bf16[2048,384]{1,0:T(8,128)(2,1)}, u32[]{:S(2)}, u32[]{:S(2)}) collective-permute-start(bf16[2048,384]{1,0:T(8,128)(2,1)} %refs_0_.1), channel_id=1, source_target_pairs={{0,1},{1,0},{2,3},{3,2},{4,5},{5,4},{6,7},{7,6},{8,9},{9,8},{10,11... | collective-permute-start | bytes 4718600 | tf_op jit(solution)/shard_map/ppermute | solution.py:73
  43.3 13.0 %collective-permute-start.4 = (bf16[192,2048]{1,0:T(8,128)(2,1)S(1)}, bf16[192,2048]{1,0:T(8,128)(2,1)S(1)}, u32[]{:S(2)}, u32[]{:S(2)}) collective-permute-start(bf16[192,2048]{1,0:T(8,128)(2,1)S(1)} %copy-done.7), channel_id=1, source_target_pairs={{0,1},{1,0},{2,3},{3,2},{4,5},{5,4},{6,7},{7,6},{8,9},{9,8},{10,11... | collective-permute-start | bytes 2359304 | tf_op jit(solution)/shard_map/ppermute | solution.py:73
  45.8 30.1 %collective-permute-start.5 = (bf16[512,128]{1,0:T(8,128)(2,1)S(1)}, bf16[512,128]{1,0:T(8,128)(2,1)S(1)}, u32[]{:S(2)}, u32[]{:S(2)}) collective-permute-start(bf16[512,128]{1,0:T(8,128)(2,1)S(1)} %constant_dynamic-update-slice_fusion), channel_id=1, source_target_pairs={{0,128},{1,33},{2,130},{3,35},{4,132},{5,37},{6,134},{7,39},{8,136... | collective-permute-start | bytes 393224 | tf_op jit(solution)/shard_map/ppermute | solution.py:73
  49.2 26.7 %collective-permute-start.6 = (bf16[512,128]{1,0:T(8,128)(2,1)S(1)}, bf16[512,128]{1,0:T(8,128)(2,1)S(1)}, u32[]{:S(2)}, u32[]{:S(2)}) collective-permute-start(bf16[512,128]{1,0:T(8,128)(2,1)S(1)} %constant_dynamic-update-slice_fusion), channel_id=1, source_target_pairs={{0,256},{1,65},{2,258},{3,67},{4,260},{5,69},{6,262},{7,71},{8,264... | collective-permute-start | bytes 393224 | tf_op jit(solution)/shard_map/ppermute | solution.py:73
  51.9 24.0 %collective-permute-start.7 = (bf16[512,128]{1,0:T(8,128)(2,1)S(1)}, bf16[512,128]{1,0:T(8,128)(2,1)S(1)}, u32[]{:S(2)}, u32[]{:S(2)}) collective-permute-start(bf16[512,128]{1,0:T(8,128)(2,1)S(1)} %constant_dynamic-update-slice_fusion), channel_id=1, source_target_pairs={{0,384},{1,97},{2,386},{3,99},{4,388},{5,101},{6,390},{7,103},{8,3... | collective-permute-start | bytes 393224 | tf_op jit(solution)/shard_map/ppermute | solution.py:73
  56.3 0.9 copy-start.8
  75.9 9.8 %copy-start.5 = (s32[16]{0:T(128)S(1)}, s32[16]{0:T(128)}, u32[]{:S(2)}) copy-start(s32[16]{0:T(128)} %owner_ref.1) | copy-start | bytes 196
  75.9 9.8 %copy-start.6 = (s32[16]{0:T(128)S(1)}, s32[16]{0:T(128)}, u32[]{:S(2)}) copy-start(s32[16]{0:T(128)} %count_ref.1) | copy-start | bytes 196
  76.0 0.6 copy-start.9
  76.6 36.5 %all-to-all-start.2 = ((bf16[32,16,2048]{2,1,0:T(8,128)(2,1)}), bf16[32,16,2048]{2,1,0:T(8,128)(2,1)S(1)}, u32[]{:S(2)}, u32[]{:S(2)}) async-start(bf16[32,16,2048]{2,1,0:T(8,128)(2,1)} %expert.1), calls=%async_computation.2 | async-start | bytes 4194304 | tf_op jit(solution)/shard_map/all_to_all | solution.py:62
  84.6 18.2 %copy-start.1 = (bf16[8,16,2304]{2,1,0:T(8,128)(2,1)S(1)}, bf16[8,16,2304]{2,1,0:T(8,128)(2,1)}, u32[]{:S(2)}) copy-start(bf16[8,16,2304]{2,1,0:T(8,128)(2,1)} %copy-done) | copy-start | bytes 1769476
  84.7 18.2 %copy-start.4 = (s32[128]{0:T(128)S(1)}, s32[128]{0:T(128)}, u32[]{:S(2)}) copy-start(s32[128]{0:T(128)} %param.14) | copy-start | bytes 1540
  85.7 1.6 %copy-start.2 = (bf16[16,64,1024]{2,1,0:T(8,128)(2,1)S(1)}, bf16[16,64,1024]{2,1,0:T(8,128)(2,1)}, u32[]{:S(2)}) copy-start(bf16[16,64,1024]{2,1,0:T(8,128)(2,1)} %pool_ref.1) | copy-start | bytes 6291460
  92.4 22.2 %collective-permute-start.8 = (bf16[4,144,128]{2,1,0:T(8,128)(2,1)S(1)}, bf16[4,144,128]{2,1,0:T(8,128)(2,1)S(1)}, u32[]{:S(2)}, u32[]{:S(2)}) collective-permute-start(bf16[4,144,128]{2,1,0:T(8,128)(2,1)S(1)} %get-tuple-element.36), channel_id=1, source_target_pairs={{0,128},{1,33},{2,130},{3,35},{4,132},{5,37},{6,134},{7,39},{8,136... | collective-permute-start | bytes 442376 | tf_op jit(solution)/shard_map/ppermute | solution.py:73
  95.8 18.8 %collective-permute-start.9 = (bf16[4,144,128]{2,1,0:T(8,128)(2,1)S(1)}, bf16[4,144,128]{2,1,0:T(8,128)(2,1)S(1)}, u32[]{:S(2)}, u32[]{:S(2)}) collective-permute-start(bf16[4,144,128]{2,1,0:T(8,128)(2,1)S(1)} %get-tuple-element.37), channel_id=1, source_target_pairs={{0,256},{1,65},{2,258},{3,67},{4,260},{5,69},{6,262},{7,71},{8,264... | collective-permute-start | bytes 442376 | tf_op jit(solution)/shard_map/ppermute | solution.py:73
  98.5 16.4 %collective-permute-start.10 = (bf16[4,144,128]{2,1,0:T(8,128)(2,1)S(1)}, bf16[4,144,128]{2,1,0:T(8,128)(2,1)S(1)}, u32[]{:S(2)}, u32[]{:S(2)}) collective-permute-start(bf16[4,144,128]{2,1,0:T(8,128)(2,1)S(1)} %get-tuple-element.38), channel_id=1, source_target_pairs={{0,384},{1,97},{2,386},{3,99},{4,388},{5,101},{6,390},{7,103},{8,3... | collective-permute-start | bytes 442376 | tf_op jit(solution)/shard_map/ppermute | solution.py:73
  103.4 31.0 %copy-start.3 = (bf16[2,1024]{1,0:T(2,128)(2,1)S(1)}, bf16[2,1024]{1,0:T(2,128)(2,1)}, u32[]{:S(2)}) copy-start(bf16[2,1024]{1,0:T(2,128)(2,1)} %new_ref.1) | copy-start | bytes 12292
  115.0 20.3 %all-to-all-start.3 = ((bf16[8,16,2048]{2,1,0:T(8,128)(2,1)}), bf16[8,16,2048]{2,1,0:T(8,128)(2,1)S(1)}, u32[]{:S(2)}, u32[]{:S(2)}) async-start(bf16[8,16,2048]{2,1,0:T(8,128)(2,1)} %combine.1), calls=%async_computation.3 | async-start | bytes 1048576 | tf_op jit(solution)/shard_map/all_to_all | solution.py:62
  120.3 11.6 %collective-permute-start.11 = (bf16[1,144,128]{2,1,0:T(8,128)(2,1)S(1)}, bf16[1,144,128]{2,1,0:T(8,128)(2,1)S(1)}, u32[]{:S(2)}, u32[]{:S(2)}) collective-permute-start(bf16[1,144,128]{2,1,0:T(8,128)(2,1)S(1)} %get-tuple-element.45), channel_id=1, source_target_pairs={{0,32},{1,129},{2,34},{3,131},{4,36},{5,133},{6,38},{7,135},{8,40}... | collective-permute-start | bytes 110600 | tf_op jit(solution)/shard_map/ppermute | solution.py:73
  124.2 7.7 %collective-permute-start.12 = (bf16[1,144,128]{2,1,0:T(8,128)(2,1)S(1)}, bf16[1,144,128]{2,1,0:T(8,128)(2,1)S(1)}, u32[]{:S(2)}, u32[]{:S(2)}) collective-permute-start(bf16[1,144,128]{2,1,0:T(8,128)(2,1)S(1)} %get-tuple-element.46), channel_id=1, source_target_pairs={{0,64},{1,257},{2,66},{3,259},{4,68},{5,261},{6,70},{7,263},{8,72}... | collective-permute-start | bytes 110600 | tf_op jit(solution)/shard_map/ppermute | solution.py:73
  128.5 5.9 %collective-permute-start.13 = (bf16[1,144,128]{2,1,0:T(8,128)(2,1)S(1)}, bf16[1,144,128]{2,1,0:T(8,128)(2,1)S(1)}, u32[]{:S(2)}, u32[]{:S(2)}) collective-permute-start(bf16[1,144,128]{2,1,0:T(8,128)(2,1)S(1)} %get-tuple-element.47), channel_id=1, source_target_pairs={{0,96},{1,385},{2,98},{3,387},{4,100},{5,389},{6,102},{7,391},{8,1... | collective-permute-start | bytes 110600 | tf_op jit(solution)/shard_map/ppermute | solution.py:73

commit v10 on v9

--- a/solution.py
+++ b/solution.py
@@ -148,12 +148,40 @@
     return hits, weights, here, taken
 
 
-def dispatch_kernel(near_ref, slot_ref, out_ref):
+CHUNKS = 4
+
+
+def dispatch_kernel(near_ref, slot_ref, out_ref, made_ref, left_sem):
     _, _, _, taken = routing(near_ref, slot_ref)
     pick = jnp.where(taken, 1.0, 0.0).reshape(REACH * ROWS, NEAR).astype(BF16)
-    tokens = near_ref[:, :, :D].reshape(NEAR, D)
-    rows = jnp.dot(pick, tokens, preferred_element_type=F32)
-    out_ref[...] = rows.astype(BF16).reshape(REACH, ROWS, D)
+    width = D // CHUNKS
+    leave = []
+    for s in range(CHUNKS):
+        columns = slice(s * width, (s + 1) * width)
+        tokens = near_ref[:, :, columns].reshape(NEAR, width)
+        rows = jnp.dot(pick, tokens, preferred_element_type=F32)
+        made_ref[s] = rows.astype(BF16).reshape(REACH, ROWS, width)
+        leave.append(
+            pltpu.make_async_copy(made_ref.at[s], out_ref.at[:, :, columns], left_sem.at[s])
+        )
+        leave[-1].start()
+    for copy in leave:
+        copy.wait()
+
+
+def dispatch(near, slot_row):
+    return call(
+        dispatch_kernel,
+        "dispatch",
+        shape((REACH, ROWS, D)),
+        2,
+        out_specs=pl.BlockSpec(memory_space=pltpu.HBM),
+        scratch_shapes=[
+            pltpu.VMEM((CHUNKS, REACH, ROWS, D // CHUNKS), BF16),
+            pltpu.SemaphoreType.DMA((CHUNKS,)),
+        ],
+        limit=VMEM_ALL,
+    )(on_core(near), slot_row)
 
 
 def mixing_kernel(near_ref, slot_ref, out_ref):
@@ -204,8 +232,12 @@
         x = rows_ref[s * step : (s + 1) * step].reshape(step * ROWS, D)
         if s == 0:
             come[0].wait()
+            left = jnp.dot(x, wide_ref[:, :both], preferred_element_type=F32)
             come[1].wait()
-        wide = jnp.dot(x, wide_ref[...], preferred_element_type=F32)
+            right = jnp.dot(x, wide_ref[:, both:], preferred_element_type=F32)
+            wide = jnp.concatenate([left, right], axis=1)
+        else:
+            wide = jnp.dot(x, wide_ref[...], preferred_element_type=F32)
         acts = []
         for at in (0, both):
             gate, up = wide[:, at : at + HALF], wide[:, at + HALF : at + both]
@@ -421,9 +453,7 @@
     own_queries = queries.reshape(REQUESTS * HEADS, HEAD)
     near = exchange(packed, RING_GROUPS)
     line = along(own_queries, "first")
-    send = call(dispatch_kernel, "dispatch", shape((REACH, ROWS, D)), 2, limit=VMEM_ALL)(
-        near, slot_row
-    )
+    send = dispatch(near, slot_row)
     send, line = lax.optimization_barrier((send, line))
     line = jnp.concatenate(line, axis=0)
     received = exchange(send, REACH_GROUPS)

time: 137 us -> 138 us (level)
  the two profiles are of different devices: /device:TPU:2 before, /device:TPU:8 now
where the time goes in v10:
time: 138 us; the launch traced here: 137 us
  starting transfers between devices  82.1 us (59%)
  Pallas kernels  22.5 us (16%)
  waiting for transfers between devices  22.3 us (16%)
  local copies, waits for them, and re-layouts  7.88 us (6%)
    ppermute x14, starting transfers between devices, moved(): return lax.ppermute(array, AXIS, pairs)  50.1 us
    all_to_all x4, starting transfers between devices, exchange(): lax.all_to_all(array, AXIS, split_axis=0, concat_axis=0, axis_index_group...  32 us
    all_to_all x4, waiting for transfers between devices, exchange(): lax.all_to_all(array, AXIS, split_axis=0, concat_axis=0, axis_index_group...  19.8 us
    pallas_call x1, Pallas kernels, expert(): call(expert_kernel, 'expert', shape(rows.shape), 5, in_specs=whole(1) + [...  6.85 us
    pallas_call x1, Pallas kernels, partial_attention(): call(partial_kernel, 'partial_attention', [shape((SIDE, MESSAGE, HEAD))]...  6.01 us
    unnamed x21, local copies, waits for them, and re-layouts  5.72 us
  transfers between devices with their start and end apart: 18, of which 4 were waited for; matrix products, arithmetic and copies ran while one was open for 4% of the time, Pallas kernels for 15%

profile of v10, /device:TPU:8, one launch (start us, length us, event | category | flops | bytes accessed | tf_op | source)
XLA Modules:
  0.0 136.8 jit_solution(18047284222349244162)
XLA Ops:
  0.6 1.8 %pack.1 = bf16[8,16,2304]{2,1,0:T(8,128)(2,1)} custom-call(bf16[16,2048]{1,0:T(8,128)(2,1)} %token_ref.1, s32[8,16]{1,0:T(8,128)} %bitcast.5, f32[8,16]{1,0:T(8,128)} %bitcast.6), custom_call_target="tpu_custom_call" | custom-call | tf_op jit(solution)/shard_map/pack/pallas_call | solution.py:450
  2.5 10.3 %all-to-all-start = ((bf16[8,16,2304]{2,1,0:T(8,128)(2,1)}), bf16[8,16,2304]{2,1,0:T(8,128)(2,1)S(1)}, u32[]{:S(2)}, u32[]{:S(2)}) async-start(bf16[8,16,2304]{2,1,0:T(8,128)(2,1)} %pack.1), calls=%async_computation | async-start | bytes 1179648 | tf_op jit(solution)/shard_map/all_to_all | solution.py:62
  13.6 3.9 %collective-permute-start = (bf16[128,128]{1,0:T(8,128)(2,1)S(1)}, bf16[128,128]{1,0:T(8,128)(2,1)S(1)}, u32[]{:S(2)}, u32[]{:S(2)}) collective-permute-start(bf16[128,128]{1,0:T(8,128)(2,1)S(1)} %reshape.11.query_ref), channel_id=1, source_target_pairs={{0,32},{1,129},{2,34},{3,131},{4,36},{5,133},{6,38},{7,135},{8,40}... | collective-permute-start | bytes 98312 | tf_op jit(solution)/shard_map/ppermute | solution.py:73
  17.5 4.3 %collective-permute-start.1 = (bf16[128,128]{1,0:T(8,128)(2,1)S(1)}, bf16[128,128]{1,0:T(8,128)(2,1)S(1)}, u32[]{:S(2)}, u32[]{:S(2)}) collective-permute-start(bf16[128,128]{1,0:T(8,128)(2,1)S(1)} %reshape.11.query_ref), channel_id=1, source_target_pairs={{0,64},{1,257},{2,66},{3,259},{4,68},{5,261},{6,70},{7,263},{8,72}... | collective-permute-start | bytes 98312 | tf_op jit(solution)/shard_map/ppermute | solution.py:73
  21.8 3.4 %collective-permute-start.2 = (bf16[128,128]{1,0:T(8,128)(2,1)S(1)}, bf16[128,128]{1,0:T(8,128)(2,1)S(1)}, u32[]{:S(2)}, u32[]{:S(2)}) collective-permute-start(bf16[128,128]{1,0:T(8,128)(2,1)S(1)} %reshape.11.query_ref), channel_id=1, source_target_pairs={{0,96},{1,385},{2,98},{3,387},{4,100},{5,389},{6,102},{7,391},{8,1... | collective-permute-start | bytes 98312 | tf_op jit(solution)/shard_map/ppermute | solution.py:73
  25.2 1.6 %all-to-all-done.near_ref = bf16[8,16,2304]{2,1,0:T(8,128)(2,1)S(1)} async-done(((bf16[8,16,2304]{2,1,0:T(8,128)(2,1)}), bf16[8,16,2304]{2,1,0:T(8,128)(2,1)S(1)}, u32[]{:S(2)}, u32[]{:S(2)}) %all-to-all-start) | async-done | bytes 589856 | tf_op jit(solution)/shard_map/all_to_all | solution.py:62
  26.8 2.6 %dispatch.1 = bf16[32,16,2048]{2,1,0:T(8,128)(2,1)} custom-call(bf16[8,16,2304]{2,1,0:T(8,128)(2,1)S(1)} %all-to-all-done.near_ref, s32[1,128]{1,0:T(1,128)} %bitcast.3), custom_call_target="tpu_custom_call" | custom-call | tf_op jit(solution)/shard_map/dispatch/pallas_call | solution.py:173
  30.1 10.2 %all-to-all-start.1 = ((bf16[32,16,2048]{2,1,0:T(8,128)(2,1)}), bf16[32,16,2048]{2,1,0:T(8,128)(2,1)S(1)}, u32[]{:S(2)}, u32[]{:S(2)}) async-start(bf16[32,16,2048]{2,1,0:T(8,128)(2,1)} %dispatch.1), calls=%async_computation.1 | async-start | bytes 4194304 | tf_op jit(solution)/shard_map/all_to_all | solution.py:62
  40.2 1.9 %collective-permute-start.3 = (bf16[2048,384]{1,0:T(8,128)(2,1)}, bf16[2048,384]{1,0:T(8,128)(2,1)}, u32[]{:S(2)}, u32[]{:S(2)}) collective-permute-start(bf16[2048,384]{1,0:T(8,128)(2,1)} %refs_0_.1), channel_id=1, source_target_pairs={{0,1},{1,0},{2,3},{3,2},{4,5},{5,4},{6,7},{7,6},{8,9},{9,8},{10,11... | collective-permute-start | bytes 4718600 | tf_op jit(solution)/shard_map/ppermute | solution.py:73
  42.2 2.4 %collective-permute-start.4 = (bf16[192,2048]{1,0:T(8,128)(2,1)S(1)}, bf16[192,2048]{1,0:T(8,128)(2,1)S(1)}, u32[]{:S(2)}, u32[]{:S(2)}) collective-permute-start(bf16[192,2048]{1,0:T(8,128)(2,1)S(1)} %copy-done.5), channel_id=1, source_target_pairs={{0,1},{1,0},{2,3},{3,2},{4,5},{5,4},{6,7},{7,6},{8,9},{9,8},{10,11... | collective-permute-start | bytes 2359304 | tf_op jit(solution)/shard_map/ppermute | solution.py:73
  45.8 1.4 %constant_dynamic-update-slice_fusion.1 = bf16[512,128]{1,0:T(8,128)(2,1)} fusion(bf16[512,128]{1,0:T(8,128)(2,1)} %constant_dynamic-update-slice_fusion.2, bf16[128,128]{1,0:T(8,128)(2,1)} %copy-done.7), kind=kLoop, calls=%fused_computation.2 | loop fusion | bytes 65536
  47.2 1.4 %constant_dynamic-update-slice_fusion = bf16[512,128]{1,0:T(8,128)(2,1)} fusion(bf16[512,128]{1,0:T(8,128)(2,1)} %constant_dynamic-update-slice_fusion.1, bf16[128,128]{1,0:T(8,128)(2,1)} %copy-done.8), kind=kLoop, calls=%fused_computation.1 | loop fusion | bytes 65536 | tf_op jit(solution)/shard_map/concatenate | solution.py:458
  48.6 3.4 %collective-permute-start.5 = (bf16[512,128]{1,0:T(8,128)(2,1)}, bf16[512,128]{1,0:T(8,128)(2,1)}, u32[]{:S(2)}, u32[]{:S(2)}) collective-permute-start(bf16[512,128]{1,0:T(8,128)(2,1)} %constant_dynamic-update-slice_fusion), channel_id=1, source_target_pairs={{0,128},{1,33},{2,130},{3,35},{4,132},{5,37},{6,134},{7,39},{8,136... | collective-permute-start | bytes 393224 | tf_op jit(solution)/shard_map/ppermute | solution.py:73
  51.9 4.6 %collective-permute-start.6 = (bf16[512,128]{1,0:T(8,128)(2,1)}, bf16[512,128]{1,0:T(8,128)(2,1)}, u32[]{:S(2)}, u32[]{:S(2)}) collective-permute-start(bf16[512,128]{1,0:T(8,128)(2,1)} %constant_dynamic-update-slice_fusion), channel_id=1, source_target_pairs={{0,256},{1,65},{2,258},{3,67},{4,260},{5,69},{6,262},{7,71},{8,264... | collective-permute-start | bytes 393224 | tf_op jit(solution)/shard_map/ppermute | solution.py:73
  56.6 3.3 %collective-permute-start.7 = (bf16[512,128]{1,0:T(8,128)(2,1)}, bf16[512,128]{1,0:T(8,128)(2,1)}, u32[]{:S(2)}, u32[]{:S(2)}) collective-permute-start(bf16[512,128]{1,0:T(8,128)(2,1)} %constant_dynamic-update-slice_fusion), channel_id=1, source_target_pairs={{0,384},{1,97},{2,386},{3,99},{4,388},{5,101},{6,390},{7,103},{8,3... | collective-permute-start | bytes 393224 | tf_op jit(solution)/shard_map/ppermute | solution.py:73
  60.8 9.1 %all-to-all-done.1.rows_ref = bf16[32,16,2048]{2,1,0:T(8,128)(2,1)S(1)} async-done(((bf16[32,16,2048]{2,1,0:T(8,128)(2,1)}), bf16[32,16,2048]{2,1,0:T(8,128)(2,1)S(1)}, u32[]{:S(2)}, u32[]{:S(2)}) %all-to-all-start.1) | async-done | bytes 2097184 | tf_op jit(solution)/shard_map/all_to_all | solution.py:62
  69.9 6.8 %expert.1 = bf16[32,16,2048]{2,1,0:T(8,128)(2,1)} custom-call(bf16[32,16,2048]{2,1,0:T(8,128)(2,1)S(1)} %all-to-all-done.1.rows_ref, bf16[2048,384]{1,0:T(8,128)(2,1)} %refs_0_.1, bf16[2048,384]{1,0:T(8,128)(2,1)} %collective-permute-done.3.refs_1_, bf16[192,2048]{1,0:T(8,128)(2,1)} %refs_2_.1, bf16[192,2048]{1,0:T(8,128)(2,1)} %copy-done.6), custom_call_target="tpu_custom_call" | custom-call | tf_op jit(solution)/shard_map/expert/pallas_call | solution.py:267
  76.8 6.0 %all-to-all-start.2 = ((bf16[32,16,2048]{2,1,0:T(8,128)(2,1)}), bf16[32,16,2048]{2,1,0:T(8,128)(2,1)S(1)}, u32[]{:S(2)}, u32[]{:S(2)}) async-start(bf16[32,16,2048]{2,1,0:T(8,128)(2,1)} %expert.1), calls=%async_computation.2 | async-start | bytes 4194304 | tf_op jit(solution)/shard_map/all_to_all | solution.py:62
  82.8 1.1 pad_maximum_fusion.query_ref
  84.0 1.6 %copy-done = bf16[16,64,1024]{2,1,0:T(8,128)(2,1)S(1)} copy-done((bf16[16,64,1024]{2,1,0:T(8,128)(2,1)S(1)}, bf16[16,64,1024]{2,1,0:T(8,128)(2,1)}, u32[]{:S(2)}) %copy-start) | copy-done | bytes 2097176
  85.6 6.0 %partial_attention.1 = (bf16[4,144,128]{2,1,0:T(8,128)(2,1)S(1)}, bf16[4,144,128]{2,1,0:T(8,128)(2,1)}, bf16[4,144,128]{2,1,0:T(8,128)(2,1)}, bf16[4,144,128]{2,1,0:T(8,128)(2,1)}) custom-call(s32[16]{0:T(128)S(1)} %copy-done.3, s32[16]{0:T(128)S(1)} %copy-done.4, bf16[2048,128]{1,0:T(8,128)(2,1)S(1)} %pad_maximum_fusion.query_ref, ...), custom_call_target="tpu_custom_call" | custom-call | tf_op jit(solution)/shard_map/partial_attention/pallas_call | solution.py:389
  91.6 3.4 %collective-permute-start.8 = (bf16[4,144,128]{2,1,0:T(8,128)(2,1)}, bf16[4,144,128]{2,1,0:T(8,128)(2,1)S(1)}, u32[]{:S(2)}, u32[]{:S(2)}) collective-permute-start(bf16[4,144,128]{2,1,0:T(8,128)(2,1)} %get-tuple-element.36), channel_id=1, source_target_pairs={{0,128},{1,33},{2,130},{3,35},{4,132},{5,37},{6,134},{7,39},{8,136... | collective-permute-start | bytes 442376 | tf_op jit(solution)/shard_map/ppermute | solution.py:73
  94.9 4.6 %collective-permute-start.9 = (bf16[4,144,128]{2,1,0:T(8,128)(2,1)}, bf16[4,144,128]{2,1,0:T(8,128)(2,1)S(1)}, u32[]{:S(2)}, u32[]{:S(2)}) collective-permute-start(bf16[4,144,128]{2,1,0:T(8,128)(2,1)} %get-tuple-element.37), channel_id=1, source_target_pairs={{0,256},{1,65},{2,258},{3,67},{4,260},{5,69},{6,262},{7,71},{8,264... | collective-permute-start | bytes 442376 | tf_op jit(solution)/shard_map/ppermute | solution.py:73
  99.6 3.3 %collective-permute-start.10 = (bf16[4,144,128]{2,1,0:T(8,128)(2,1)}, bf16[4,144,128]{2,1,0:T(8,128)(2,1)}, u32[]{:S(2)}, u32[]{:S(2)}) collective-permute-start(bf16[4,144,128]{2,1,0:T(8,128)(2,1)} %get-tuple-element.38), channel_id=1, source_target_pairs={{0,384},{1,97},{2,386},{3,99},{4,388},{5,101},{6,390},{7,103},{8,3... | collective-permute-start | bytes 442376 | tf_op jit(solution)/shard_map/ppermute | solution.py:73
  103.4 9.1 %all-to-all-done.2.rows_ref = bf16[32,16,2048]{2,1,0:T(8,128)(2,1)S(1)} async-done(((bf16[32,16,2048]{2,1,0:T(8,128)(2,1)}), bf16[32,16,2048]{2,1,0:T(8,128)(2,1)S(1)}, u32[]{:S(2)}, u32[]{:S(2)}) %all-to-all-start.2) | async-done | bytes 2097184 | tf_op jit(solution)/shard_map/all_to_all | solution.py:62
  112.5 1.5 %combine.1 = bf16[8,16,2048]{2,1,0:T(8,128)(2,1)} custom-call(bf16[256,512]{1,0:T(8,128)(2,1)S(1)} %mixing.1.mix_ref, bf16[32,16,2048]{2,1,0:T(8,128)(2,1)S(1)} %all-to-all-done.2.rows_ref), custom_call_target="tpu_custom_call" | custom-call | tf_op jit(solution)/shard_map/combine/pallas_call | solution.py:474
  114.0 5.5 %all-to-all-start.3 = ((bf16[8,16,2048]{2,1,0:T(8,128)(2,1)}), bf16[8,16,2048]{2,1,0:T(8,128)(2,1)S(1)}, u32[]{:S(2)}, u32[]{:S(2)}) async-start(bf16[8,16,2048]{2,1,0:T(8,128)(2,1)} %combine.1), calls=%async_computation.3 | async-start | bytes 1048576 | tf_op jit(solution)/shard_map/all_to_all | solution.py:62
  119.6 1.6 %merge.1 = (bf16[1,144,128]{2,1,0:T(8,128)(2,1)S(1)}, bf16[1,144,128]{2,1,0:T(8,128)(2,1)S(1)}, bf16[1,144,128]{2,1,0:T(8,128)(2,1)S(1)}, bf16[1,144,128]{2,1,0:T(8,128)(2,1)S(1)}) custom-call(bf16[4,144,128]{2,1,0:T(8,128)(2,1)S(1)} %get-tuple-element.40.got0_ref, bf16[4,144,128]{2,1,0:T(8,128)(2,1)S(1)} %collective-permute-done.8.got1_ref, ...), custom_call_target="tpu_custom_call" | custom-call | tf_op jit(solution)/shard_map/merge/pallas_call | solution.py:478
  121.2 3.9 %collective-permute-start.11 = (bf16[1,144,128]{2,1,0:T(8,128)(2,1)S(1)}, bf16[1,144,128]{2,1,0:T(8,128)(2,1)S(1)}, u32[]{:S(2)}, u32[]{:S(2)}) collective-permute-start(bf16[1,144,128]{2,1,0:T(8,128)(2,1)S(1)} %get-tuple-element.45), channel_id=1, source_target_pairs={{0,32},{1,129},{2,34},{3,131},{4,36},{5,133},{6,38},{7,135},{8,40}... | collective-permute-start | bytes 110600 | tf_op jit(solution)/shard_map/ppermute | solution.py:73
  125.1 4.3 %collective-permute-start.12 = (bf16[1,144,128]{2,1,0:T(8,128)(2,1)S(1)}, bf16[1,144,128]{2,1,0:T(8,128)(2,1)S(1)}, u32[]{:S(2)}, u32[]{:S(2)}) collective-permute-start(bf16[1,144,128]{2,1,0:T(8,128)(2,1)S(1)} %get-tuple-element.46), channel_id=1, source_target_pairs={{0,64},{1,257},{2,66},{3,259},{4,68},{5,261},{6,70},{7,263},{8,72}... | collective-permute-start | bytes 110600 | tf_op jit(solution)/shard_map/ppermute | solution.py:73
  129.4 3.4 %collective-permute-start.13 = (bf16[1,144,128]{2,1,0:T(8,128)(2,1)S(1)}, bf16[1,144,128]{2,1,0:T(8,128)(2,1)S(1)}, u32[]{:S(2)}, u32[]{:S(2)}) collective-permute-start(bf16[1,144,128]{2,1,0:T(8,128)(2,1)S(1)} %get-tuple-element.47), channel_id=1, source_target_pairs={{0,96},{1,385},{2,98},{3,387},{4,100},{5,389},{6,102},{7,391},{8,1... | collective-permute-start | bytes 110600 | tf_op jit(solution)/shard_map/ppermute | solution.py:73
  132.8 2.5 %collective-permute-done.13.got3_ref = bf16[1,144,128]{2,1,0:T(8,128)(2,1)S(1)} collective-permute-done((bf16[1,144,128]{2,1,0:T(8,128)(2,1)S(1)}, bf16[1,144,128]{2,1,0:T(8,128)(2,1)S(1)}, u32[]{:S(2)}, u32[]{:S(2)}) %collective-permute-start.13) | collective-permute-done | bytes 36896 | tf_op jit(solution)/shard_map/ppermute | solution.py:73
  (37 shorter events, 5.7 us)
Async XLA Ops:
  2.5 24.3 %all-to-all-start = ((bf16[8,16,2304]{2,1,0:T(8,128)(2,1)}), bf16[8,16,2304]{2,1,0:T(8,128)(2,1)S(1)}, u32[]{:S(2)}, u32[]{:S(2)}) async-start(bf16[8,16,2304]{2,1,0:T(8,128)(2,1)} %pack.1), calls=%async_computation | async-start | bytes 1179648 | tf_op jit(solution)/shard_map/all_to_all | solution.py:62
  13.6 15.8 %collective-permute-start = (bf16[128,128]{1,0:T(8,128)(2,1)S(1)}, bf16[128,128]{1,0:T(8,128)(2,1)S(1)}, u32[]{:S(2)}, u32[]{:S(2)}) collective-permute-start(bf16[128,128]{1,0:T(8,128)(2,1)S(1)} %reshape.11.query_ref), channel_id=1, source_target_pairs={{0,32},{1,129},{2,34},{3,131},{4,36},{5,133},{6,38},{7,135},{8,40}... | collective-permute-start | bytes 98312 | tf_op jit(solution)/shard_map/ppermute | solution.py:73
  17.5 11.9 %collective-permute-start.1 = (bf16[128,128]{1,0:T(8,128)(2,1)S(1)}, bf16[128,128]{1,0:T(8,128)(2,1)S(1)}, u32[]{:S(2)}, u32[]{:S(2)}) collective-permute-start(bf16[128,128]{1,0:T(8,128)(2,1)S(1)} %reshape.11.query_ref), channel_id=1, source_target_pairs={{0,64},{1,257},{2,66},{3,259},{4,68},{5,261},{6,70},{7,263},{8,72}... | collective-permute-start | bytes 98312 | tf_op jit(solution)/shard_map/ppermute | solution.py:73
  21.8 7.7 %collective-permute-start.2 = (bf16[128,128]{1,0:T(8,128)(2,1)S(1)}, bf16[128,128]{1,0:T(8,128)(2,1)S(1)}, u32[]{:S(2)}, u32[]{:S(2)}) collective-permute-start(bf16[128,128]{1,0:T(8,128)(2,1)S(1)} %reshape.11.query_ref), channel_id=1, source_target_pairs={{0,96},{1,385},{2,98},{3,387},{4,100},{5,389},{6,102},{7,391},{8,1... | collective-permute-start | bytes 98312 | tf_op jit(solution)/shard_map/ppermute | solution.py:73
  29.4 12.8 %copy-start.5 = (bf16[192,2048]{1,0:T(8,128)(2,1)S(1)}, bf16[192,2048]{1,0:T(8,128)(2,1)}, u32[]{:S(2)}) copy-start(bf16[192,2048]{1,0:T(8,128)(2,1)} %refs_2_.1) | copy-start | bytes 2359300
  29.4 0.6 copy-start.7
  29.4 0.6 copy-start.8
  30.1 39.8 %all-to-all-start.1 = ((bf16[32,16,2048]{2,1,0:T(8,128)(2,1)}), bf16[32,16,2048]{2,1,0:T(8,128)(2,1)S(1)}, u32[]{:S(2)}, u32[]{:S(2)}) async-start(bf16[32,16,2048]{2,1,0:T(8,128)(2,1)} %dispatch.1), calls=%async_computation.1 | async-start | bytes 4194304 | tf_op jit(solution)/shard_map/all_to_all | solution.py:62
  40.2 20.6 %collective-permute-start.3 = (bf16[2048,384]{1,0:T(8,128)(2,1)}, bf16[2048,384]{1,0:T(8,128)(2,1)}, u32[]{:S(2)}, u32[]{:S(2)}) collective-permute-start(bf16[2048,384]{1,0:T(8,128)(2,1)} %refs_0_.1), channel_id=1, source_target_pairs={{0,1},{1,0},{2,3},{3,2},{4,5},{5,4},{6,7},{7,6},{8,9},{9,8},{10,11... | collective-permute-start | bytes 4718600 | tf_op jit(solution)/shard_map/ppermute | solution.py:73
  42.2 17.7 %collective-permute-start.4 = (bf16[192,2048]{1,0:T(8,128)(2,1)S(1)}, bf16[192,2048]{1,0:T(8,128)(2,1)S(1)}, u32[]{:S(2)}, u32[]{:S(2)}) collective-permute-start(bf16[192,2048]{1,0:T(8,128)(2,1)S(1)} %copy-done.5), channel_id=1, source_target_pairs={{0,1},{1,0},{2,3},{3,2},{4,5},{5,4},{6,7},{7,6},{8,9},{9,8},{10,11... | collective-permute-start | bytes 2359304 | tf_op jit(solution)/shard_map/ppermute | solution.py:73
  48.6 28.2 %collective-permute-start.5 = (bf16[512,128]{1,0:T(8,128)(2,1)}, bf16[512,128]{1,0:T(8,128)(2,1)}, u32[]{:S(2)}, u32[]{:S(2)}) collective-permute-start(bf16[512,128]{1,0:T(8,128)(2,1)} %constant_dynamic-update-slice_fusion), channel_id=1, source_target_pairs={{0,128},{1,33},{2,130},{3,35},{4,132},{5,37},{6,134},{7,39},{8,136... | collective-permute-start | bytes 393224 | tf_op jit(solution)/shard_map/ppermute | solution.py:73
  51.9 24.8 %collective-permute-start.6 = (bf16[512,128]{1,0:T(8,128)(2,1)}, bf16[512,128]{1,0:T(8,128)(2,1)}, u32[]{:S(2)}, u32[]{:S(2)}) collective-permute-start(bf16[512,128]{1,0:T(8,128)(2,1)} %constant_dynamic-update-slice_fusion), channel_id=1, source_target_pairs={{0,256},{1,65},{2,258},{3,67},{4,260},{5,69},{6,262},{7,71},{8,264... | collective-permute-start | bytes 393224 | tf_op jit(solution)/shard_map/ppermute | solution.py:73
  56.6 20.2 %collective-permute-start.7 = (bf16[512,128]{1,0:T(8,128)(2,1)}, bf16[512,128]{1,0:T(8,128)(2,1)}, u32[]{:S(2)}, u32[]{:S(2)}) collective-permute-start(bf16[512,128]{1,0:T(8,128)(2,1)} %constant_dynamic-update-slice_fusion), channel_id=1, source_target_pairs={{0,384},{1,97},{2,386},{3,99},{4,388},{5,101},{6,390},{7,103},{8,3... | collective-permute-start | bytes 393224 | tf_op jit(solution)/shard_map/ppermute | solution.py:73
  59.9 0.9 copy-start.6
  76.7 7.2 %copy-start.3 = (s32[16]{0:T(128)S(1)}, s32[16]{0:T(128)}, u32[]{:S(2)}) copy-start(s32[16]{0:T(128)} %owner_ref.1) | copy-start | bytes 196
  76.8 7.2 %copy-start.4 = (s32[16]{0:T(128)S(1)}, s32[16]{0:T(128)}, u32[]{:S(2)}) copy-start(s32[16]{0:T(128)} %count_ref.1) | copy-start | bytes 196
  76.8 35.7 %all-to-all-start.2 = ((bf16[32,16,2048]{2,1,0:T(8,128)(2,1)}), bf16[32,16,2048]{2,1,0:T(8,128)(2,1)S(1)}, u32[]{:S(2)}, u32[]{:S(2)}) async-start(bf16[32,16,2048]{2,1,0:T(8,128)(2,1)} %expert.1), calls=%async_computation.2 | async-start | bytes 4194304 | tf_op jit(solution)/shard_map/all_to_all | solution.py:62
  82.8 20.1 %copy-start.2 = (s32[128]{0:T(128)S(1)}, s32[128]{0:T(128)}, u32[]{:S(2)}) copy-start(s32[128]{0:T(128)} %param.14) | copy-start | bytes 1540
  84.0 1.6 %copy-start = (bf16[16,64,1024]{2,1,0:T(8,128)(2,1)S(1)}, bf16[16,64,1024]{2,1,0:T(8,128)(2,1)}, u32[]{:S(2)}) copy-start(bf16[16,64,1024]{2,1,0:T(8,128)(2,1)} %pool_ref.1) | copy-start | bytes 6291460
  91.6 22.5 %collective-permute-start.8 = (bf16[4,144,128]{2,1,0:T(8,128)(2,1)}, bf16[4,144,128]{2,1,0:T(8,128)(2,1)S(1)}, u32[]{:S(2)}, u32[]{:S(2)}) collective-permute-start(bf16[4,144,128]{2,1,0:T(8,128)(2,1)} %get-tuple-element.36), channel_id=1, source_target_pairs={{0,128},{1,33},{2,130},{3,35},{4,132},{5,37},{6,134},{7,39},{8,136... | collective-permute-start | bytes 442376 | tf_op jit(solution)/shard_map/ppermute | solution.py:73
  94.9 19.1 %collective-permute-start.9 = (bf16[4,144,128]{2,1,0:T(8,128)(2,1)}, bf16[4,144,128]{2,1,0:T(8,128)(2,1)S(1)}, u32[]{:S(2)}, u32[]{:S(2)}) collective-permute-start(bf16[4,144,128]{2,1,0:T(8,128)(2,1)} %get-tuple-element.37), channel_id=1, source_target_pairs={{0,256},{1,65},{2,258},{3,67},{4,260},{5,69},{6,262},{7,71},{8,264... | collective-permute-start | bytes 442376 | tf_op jit(solution)/shard_map/ppermute | solution.py:73
  99.6 14.5 %collective-permute-start.10 = (bf16[4,144,128]{2,1,0:T(8,128)(2,1)}, bf16[4,144,128]{2,1,0:T(8,128)(2,1)}, u32[]{:S(2)}, u32[]{:S(2)}) collective-permute-start(bf16[4,144,128]{2,1,0:T(8,128)(2,1)} %get-tuple-element.38), channel_id=1, source_target_pairs={{0,384},{1,97},{2,386},{3,99},{4,388},{5,101},{6,390},{7,103},{8,3... | collective-permute-start | bytes 442376 | tf_op jit(solution)/shard_map/ppermute | solution.py:73
  103.4 31.8 %copy-start.1 = (bf16[2,1024]{1,0:T(2,128)(2,1)S(1)}, bf16[2,1024]{1,0:T(2,128)(2,1)}, u32[]{:S(2)}) copy-start(bf16[2,1024]{1,0:T(2,128)(2,1)} %new_ref.1) | copy-start | bytes 12292
  114.0 22.1 %all-to-all-start.3 = ((bf16[8,16,2048]{2,1,0:T(8,128)(2,1)}), bf16[8,16,2048]{2,1,0:T(8,128)(2,1)S(1)}, u32[]{:S(2)}, u32[]{:S(2)}) async-start(bf16[8,16,2048]{2,1,0:T(8,128)(2,1)} %combine.1), calls=%async_computation.3 | async-start | bytes 1048576 | tf_op jit(solution)/shard_map/all_to_all | solution.py:62
  121.2 11.6 %collective-permute-start.11 = (bf16[1,144,128]{2,1,0:T(8,128)(2,1)S(1)}, bf16[1,144,128]{2,1,0:T(8,128)(2,1)S(1)}, u32[]{:S(2)}, u32[]{:S(2)}) collective-permute-start(bf16[1,144,128]{2,1,0:T(8,128)(2,1)S(1)} %get-tuple-element.45), channel_id=1, source_target_pairs={{0,32},{1,129},{2,34},{3,131},{4,36},{5,133},{6,38},{7,135},{8,40}... | collective-permute-start | bytes 110600 | tf_op jit(solution)/shard_map/ppermute | solution.py:73
  125.1 7.7 %collective-permute-start.12 = (bf16[1,144,128]{2,1,0:T(8,128)(2,1)S(1)}, bf16[1,144,128]{2,1,0:T(8,128)(2,1)S(1)}, u32[]{:S(2)}, u32[]{:S(2)}) collective-permute-start(bf16[1,144,128]{2,1,0:T(8,128)(2,1)S(1)} %get-tuple-element.46), channel_id=1, source_target_pairs={{0,64},{1,257},{2,66},{3,259},{4,68},{5,261},{6,70},{7,263},{8,72}... | collective-permute-start | bytes 110600 | tf_op jit(solution)/shard_map/ppermute | solution.py:73
  129.4 5.9 %collective-permute-start.13 = (bf16[1,144,128]{2,1,0:T(8,128)(2,1)S(1)}, bf16[1,144,128]{2,1,0:T(8,128)(2,1)S(1)}, u32[]{:S(2)}, u32[]{:S(2)}) collective-permute-start(bf16[1,144,128]{2,1,0:T(8,128)(2,1)S(1)} %get-tuple-element.47), channel_id=1, source_target_pairs={{0,96},{1,385},{2,98},{3,387},{4,100},{5,389},{6,102},{7,391},{8,1... | collective-permute-start | bytes 110600 | tf_op jit(solution)/shard_map/ppermute | solution.py:73

commit v11 on v10

--- a/solution.py
+++ b/solution.py
@@ -70,6 +70,14 @@
         x, zl, y, zh, c = position(device)
         dx, dz = (first, second) if c else (second, first)
         pairs.append((device, number((x + dx) % 4, (zl + dz) % 4, y, zh, (c + core) % 2)))
+    return lax.ppermute(array, AXIS, pairs)
+
+
+def swapped(array, flip):
+    pairs = []
+    for device in range(512):
+        x, zl, y, zh, c = position(device)
+        pairs.append((device, number(x ^ (flip * c), zl ^ (flip * (1 - c)), y, zh, c)))
     return lax.ppermute(array, AXIS, pairs)
 
 
@@ -344,7 +352,9 @@
     for b in range(BLOCKS):
         owner = owner_ref[b]
         ax, az, request = owner >> 3, (owner >> 1) & 3, owner & 1
-        asked = pair(x_first, (zl - az) & 3, (x - ax) & 3) * 2 + request
+        first = jnp.where(x_first, ax ^ x, az ^ zl)
+        second = jnp.where(x_first, (zl - az) & 3, (x - ax) & 3)
+        asked = (second * 4 + (first & 1) * 2 + (first >> 1)) * 2 + request
         state = pair(x_first, (az - zl) & 3, (ax - x) & 3) * 2 + request
         rows = pl.ds(pl.multiple_of(state * HEADS, HEADS), HEADS)
         query = query_ref[pl.ds(pl.multiple_of(asked * HEADS, HEADS), HEADS), :]
@@ -452,10 +462,11 @@
     )
     own_queries = queries.reshape(REQUESTS * HEADS, HEAD)
     near = exchange(packed, RING_GROUPS)
-    line = along(own_queries, "first")
+    half = jnp.concatenate([own_queries, swapped(own_queries, 2)], axis=0)
+    rest = swapped(half, 1)
     send = dispatch(near, slot_row)
-    send, line = lax.optimization_barrier((send, line))
-    line = jnp.concatenate(line, axis=0)
+    send, rest = lax.optimization_barrier((send, rest))
+    line = jnp.concatenate([half, rest], axis=0)
     received = exchange(send, REACH_GROUPS)
 
     other_gate_up, other_down = moved(w_gate_up, core=1), moved(w_down, core=1)

time: 138 us -> 138 us (level)
  waiting for transfers between devices: 22.3 us -> 28.5 us
  starting transfers between devices: 82.1 us -> 77.2 us
    ppermute x14 -> x11, starting transfers between devices: 50.1 us -> 38.5 us  [moved(): return lax.ppermute(array, AXIS, pairs)]
    ppermute x0 -> x2, starting transfers between devices: none -> 6.74 us  [swapped(): return lax.ppermute(array, AXIS, pairs)]
    ppermute x0 -> x2, waiting for transfers between devices: none -> 4.53 us  [swapped(): return lax.ppermute(array, AXIS, pairs)]
    all_to_all x4, waiting for transfers between devices: 19.8 us -> 21.5 us  [exchange(): lax.all_to_all(array, AXIS, split_axis=0, concat_axis=0, axis_index_group...]
    unnamed x21 -> x18, local copies, waits for them, and re-layouts: 5.72 us -> 4.35 us
  transfers between devices with their start and end apart: 18 -> 17, of which waited for: 4 -> 5; matrix products, arithmetic and copies ran while one was open for 4% -> 3% of each run, Pallas kernels for 15% -> 15%
where the time goes in v11:
time: 138 us; the launch traced here: 137 us
  starting transfers between devices  77.2 us (56%)
  waiting for transfers between devices  28.5 us (21%)
  Pallas kernels  22.5 us (16%)
  local copies, waits for them, and re-layouts  6.61 us (5%)
    ppermute x11, starting transfers between devices, moved(): return lax.ppermute(array, AXIS, pairs)  38.5 us
    all_to_all x4, starting transfers between devices, exchange(): lax.all_to_all(array, AXIS, split_axis=0, concat_axis=0, axis_index_group...  31.9 us
    all_to_all x4, waiting for transfers between devices, exchange(): lax.all_to_all(array, AXIS, split_axis=0, concat_axis=0, axis_index_group...  21.5 us
    pallas_call x1, Pallas kernels, expert(): call(expert_kernel, 'expert', shape(rows.shape), 5, in_specs=whole(1) + [...  6.84 us
    ppermute x2, starting transfers between devices, swapped(): return lax.ppermute(array, AXIS, pairs)  6.74 us
    pallas_call x1, Pallas kernels, partial_attention(): call(partial_kernel, 'partial_attention', [shape((SIDE, MESSAGE, HEAD))]...  6 us
    ppermute x2, waiting for transfers between devices, swapped(): return lax.ppermute(array, AXIS, pairs)  4.53 us
    unnamed x18, local copies, waits for them, and re-layouts  4.35 us
  transfers between devices with their start and end apart: 17, of which 5 were waited for; matrix products, arithmetic and copies ran while one was open for 3% of the time, Pallas kernels for 15%

profile of v11, /device:TPU:8, one launch (start us, length us, event | category | flops | bytes accessed | tf_op | source)
XLA Modules:
  0.0 136.9 jit_solution(3154505187627261315)
XLA Ops:
  0.6 1.8 %pack.1 = bf16[8,16,2304]{2,1,0:T(8,128)(2,1)} custom-call(bf16[16,2048]{1,0:T(8,128)(2,1)} %token_ref.1, s32[8,16]{1,0:T(8,128)} %bitcast.5, f32[8,16]{1,0:T(8,128)} %bitcast.6), custom_call_target="tpu_custom_call" | custom-call | tf_op jit(solution)/shard_map/pack/pallas_call | solution.py:460
  2.5 10.3 %all-to-all-start = ((bf16[8,16,2304]{2,1,0:T(8,128)(2,1)}), bf16[8,16,2304]{2,1,0:T(8,128)(2,1)S(1)}, u32[]{:S(2)}, u32[]{:S(2)}) async-start(bf16[8,16,2304]{2,1,0:T(8,128)(2,1)} %pack.1), calls=%async_computation | async-start | bytes 1179648 | tf_op jit(solution)/shard_map/all_to_all | solution.py:62
  13.6 4.8 %collective-permute-start = (bf16[128,128]{1,0:T(8,128)(2,1)S(1)}, bf16[128,128]{1,0:T(8,128)(2,1)S(1)}, u32[]{:S(2)}, u32[]{:S(2)}) collective-permute-start(bf16[128,128]{1,0:T(8,128)(2,1)S(1)} %reshape.11.query_ref), channel_id=1, source_target_pairs={{0,64},{1,257},{2,66},{3,259},{4,68},{5,261},{6,70},{7,263},{8,72}... | collective-permute-start | bytes 98312 | tf_op jit(solution)/shard_map/ppermute | solution.py:81
  18.4 4.5 %collective-permute-done = bf16[128,128]{1,0:T(8,128)(2,1)S(1)} collective-permute-done((bf16[128,128]{1,0:T(8,128)(2,1)S(1)}, bf16[128,128]{1,0:T(8,128)(2,1)S(1)}, u32[]{:S(2)}, u32[]{:S(2)}) %collective-permute-start) | collective-permute-done | bytes 32800 | tf_op jit(solution)/shard_map/ppermute | solution.py:81
  22.9 1.9 %collective-permute-start.1 = (bf16[256,128]{1,0:T(8,128)(2,1)S(1)}, bf16[256,128]{1,0:T(8,128)(2,1)S(1)}, u32[]{:S(2)}, u32[]{:S(2)}) collective-permute-start(bf16[256,128]{1,0:T(8,128)(2,1)S(1)} %pad_maximum_fusion.1), channel_id=1, source_target_pairs={{0,32},{1,129},{2,34},{3,131},{4,36},{5,133},{6,38},{7,135},{8,40}... | collective-permute-start | bytes 196616 | tf_op jit(solution)/shard_map/ppermute | solution.py:81
  24.8 1.9 %all-to-all-done.near_ref = bf16[8,16,2304]{2,1,0:T(8,128)(2,1)S(1)} async-done(((bf16[8,16,2304]{2,1,0:T(8,128)(2,1)}), bf16[8,16,2304]{2,1,0:T(8,128)(2,1)S(1)}, u32[]{:S(2)}, u32[]{:S(2)}) %all-to-all-start) | async-done | bytes 589856 | tf_op jit(solution)/shard_map/all_to_all | solution.py:62
  26.8 2.6 %dispatch.1 = bf16[32,16,2048]{2,1,0:T(8,128)(2,1)} custom-call(bf16[8,16,2304]{2,1,0:T(8,128)(2,1)S(1)} %all-to-all-done.near_ref, s32[1,128]{1,0:T(1,128)} %bitcast.3), custom_call_target="tpu_custom_call" | custom-call | tf_op jit(solution)/shard_map/dispatch/pallas_call | solution.py:181
  30.0 10.2 %all-to-all-start.1 = ((bf16[32,16,2048]{2,1,0:T(8,128)(2,1)}), bf16[32,16,2048]{2,1,0:T(8,128)(2,1)S(1)}, u32[]{:S(2)}, u32[]{:S(2)}) async-start(bf16[32,16,2048]{2,1,0:T(8,128)(2,1)} %dispatch.1), calls=%async_computation.1 | async-start | bytes 4194304 | tf_op jit(solution)/shard_map/all_to_all | solution.py:62
  40.2 1.9 %collective-permute-start.2 = (bf16[2048,384]{1,0:T(8,128)(2,1)}, bf16[2048,384]{1,0:T(8,128)(2,1)}, u32[]{:S(2)}, u32[]{:S(2)}) collective-permute-start(bf16[2048,384]{1,0:T(8,128)(2,1)} %refs_0_.1), channel_id=1, source_target_pairs={{0,1},{1,0},{2,3},{3,2},{4,5},{5,4},{6,7},{7,6},{8,9},{9,8},{10,11... | collective-permute-start | bytes 4718600 | tf_op jit(solution)/shard_map/ppermute | solution.py:73
  42.1 2.4 %collective-permute-start.3 = (bf16[192,2048]{1,0:T(8,128)(2,1)S(1)}, bf16[192,2048]{1,0:T(8,128)(2,1)S(1)}, u32[]{:S(2)}, u32[]{:S(2)}) collective-permute-start(bf16[192,2048]{1,0:T(8,128)(2,1)S(1)} %copy-done.5), channel_id=1, source_target_pairs={{0,1},{1,0},{2,3},{3,2},{4,5},{5,4},{6,7},{7,6},{8,9},{9,8},{10,11... | collective-permute-start | bytes 2359304 | tf_op jit(solution)/shard_map/ppermute | solution.py:73
  45.8 1.5 %constant_dynamic-update-slice_fusion = bf16[512,128]{1,0:T(8,128)(2,1)} fusion(bf16[512,128]{1,0:T(8,128)(2,1)} %constant_dynamic-update-slice_fusion.1, bf16[256,128]{1,0:T(8,128)(2,1)} %copy-done.7), kind=kLoop, calls=%fused_computation.2 | loop fusion | bytes 131072 | tf_op jit(solution)/shard_map/concatenate | solution.py:469
  47.3 3.4 %collective-permute-start.4 = (bf16[512,128]{1,0:T(8,128)(2,1)}, bf16[512,128]{1,0:T(8,128)(2,1)}, u32[]{:S(2)}, u32[]{:S(2)}) collective-permute-start(bf16[512,128]{1,0:T(8,128)(2,1)} %constant_dynamic-update-slice_fusion), channel_id=1, source_target_pairs={{0,128},{1,33},{2,130},{3,35},{4,132},{5,37},{6,134},{7,39},{8,136... | collective-permute-start | bytes 393224 | tf_op jit(solution)/shard_map/ppermute | solution.py:73
  50.6 4.6 %collective-permute-start.5 = (bf16[512,128]{1,0:T(8,128)(2,1)}, bf16[512,128]{1,0:T(8,128)(2,1)}, u32[]{:S(2)}, u32[]{:S(2)}) collective-permute-start(bf16[512,128]{1,0:T(8,128)(2,1)} %constant_dynamic-update-slice_fusion), channel_id=1, source_target_pairs={{0,256},{1,65},{2,258},{3,67},{4,260},{5,69},{6,262},{7,71},{8,264... | collective-permute-start | bytes 393224 | tf_op jit(solution)/shard_map/ppermute | solution.py:73
  55.3 3.3 %collective-permute-start.6 = (bf16[512,128]{1,0:T(8,128)(2,1)}, bf16[512,128]{1,0:T(8,128)(2,1)}, u32[]{:S(2)}, u32[]{:S(2)}) collective-permute-start(bf16[512,128]{1,0:T(8,128)(2,1)} %constant_dynamic-update-slice_fusion), channel_id=1, source_target_pairs={{0,384},{1,97},{2,386},{3,99},{4,388},{5,101},{6,390},{7,103},{8,3... | collective-permute-start | bytes 393224 | tf_op jit(solution)/shard_map/ppermute | solution.py:73
  59.5 10.4 %all-to-all-done.1.rows_ref = bf16[32,16,2048]{2,1,0:T(8,128)(2,1)S(1)} async-done(((bf16[32,16,2048]{2,1,0:T(8,128)(2,1)}), bf16[32,16,2048]{2,1,0:T(8,128)(2,1)S(1)}, u32[]{:S(2)}, u32[]{:S(2)}) %all-to-all-start.1) | async-done | bytes 2097184 | tf_op jit(solution)/shard_map/all_to_all | solution.py:62
  69.9 6.8 %expert.1 = bf16[32,16,2048]{2,1,0:T(8,128)(2,1)} custom-call(bf16[32,16,2048]{2,1,0:T(8,128)(2,1)S(1)} %all-to-all-done.1.rows_ref, bf16[2048,384]{1,0:T(8,128)(2,1)} %refs_0_.1, bf16[2048,384]{1,0:T(8,128)(2,1)} %collective-permute-done.2.refs_1_, bf16[192,2048]{1,0:T(8,128)(2,1)} %refs_2_.1, bf16[192,2048]{1,0:T(8,128)(2,1)} %copy-done.6), custom_call_target="tpu_custom_call" | custom-call | tf_op jit(solution)/shard_map/expert/pallas_call | solution.py:275
  76.8 5.8 %all-to-all-start.2 = ((bf16[32,16,2048]{2,1,0:T(8,128)(2,1)}), bf16[32,16,2048]{2,1,0:T(8,128)(2,1)S(1)}, u32[]{:S(2)}, u32[]{:S(2)}) async-start(bf16[32,16,2048]{2,1,0:T(8,128)(2,1)} %expert.1), calls=%async_computation.2 | async-start | bytes 4194304 | tf_op jit(solution)/shard_map/all_to_all | solution.py:62
  82.6 1.1 pad_maximum_fusion.query_ref
  83.8 1.6 %copy-done = bf16[16,64,1024]{2,1,0:T(8,128)(2,1)S(1)} copy-done((bf16[16,64,1024]{2,1,0:T(8,128)(2,1)S(1)}, bf16[16,64,1024]{2,1,0:T(8,128)(2,1)}, u32[]{:S(2)}) %copy-start) | copy-done | bytes 2097176
  85.4 6.0 %partial_attention.1 = (bf16[4,144,128]{2,1,0:T(8,128)(2,1)S(1)}, bf16[4,144,128]{2,1,0:T(8,128)(2,1)}, bf16[4,144,128]{2,1,0:T(8,128)(2,1)}, bf16[4,144,128]{2,1,0:T(8,128)(2,1)}) custom-call(s32[16]{0:T(128)S(1)} %copy-done.3, s32[16]{0:T(128)S(1)} %copy-done.4, bf16[2048,128]{1,0:T(8,128)(2,1)S(1)} %pad_maximum_fusion.query_ref, ...), custom_call_target="tpu_custom_call" | custom-call | tf_op jit(solution)/shard_map/partial_attention/pallas_call | solution.py:399
  91.4 3.4 %collective-permute-start.7 = (bf16[4,144,128]{2,1,0:T(8,128)(2,1)}, bf16[4,144,128]{2,1,0:T(8,128)(2,1)S(1)}, u32[]{:S(2)}, u32[]{:S(2)}) collective-permute-start(bf16[4,144,128]{2,1,0:T(8,128)(2,1)} %get-tuple-element.30), channel_id=1, source_target_pairs={{0,128},{1,33},{2,130},{3,35},{4,132},{5,37},{6,134},{7,39},{8,136... | collective-permute-start | bytes 442376 | tf_op jit(solution)/shard_map/ppermute | solution.py:73
  94.8 4.6 %collective-permute-start.8 = (bf16[4,144,128]{2,1,0:T(8,128)(2,1)}, bf16[4,144,128]{2,1,0:T(8,128)(2,1)S(1)}, u32[]{:S(2)}, u32[]{:S(2)}) collective-permute-start(bf16[4,144,128]{2,1,0:T(8,128)(2,1)} %get-tuple-element.31), channel_id=1, source_target_pairs={{0,256},{1,65},{2,258},{3,67},{4,260},{5,69},{6,262},{7,71},{8,264... | collective-permute-start | bytes 442376 | tf_op jit(solution)/shard_map/ppermute | solution.py:73
  99.4 3.3 %collective-permute-start.9 = (bf16[4,144,128]{2,1,0:T(8,128)(2,1)}, bf16[4,144,128]{2,1,0:T(8,128)(2,1)}, u32[]{:S(2)}, u32[]{:S(2)}) collective-permute-start(bf16[4,144,128]{2,1,0:T(8,128)(2,1)} %get-tuple-element.32), channel_id=1, source_target_pairs={{0,384},{1,97},{2,386},{3,99},{4,388},{5,101},{6,390},{7,103},{8,3... | collective-permute-start | bytes 442376 | tf_op jit(solution)/shard_map/ppermute | solution.py:73
  103.3 9.2 %all-to-all-done.2.rows_ref = bf16[32,16,2048]{2,1,0:T(8,128)(2,1)S(1)} async-done(((bf16[32,16,2048]{2,1,0:T(8,128)(2,1)}), bf16[32,16,2048]{2,1,0:T(8,128)(2,1)S(1)}, u32[]{:S(2)}, u32[]{:S(2)}) %all-to-all-start.2) | async-done | bytes 2097184 | tf_op jit(solution)/shard_map/all_to_all | solution.py:62
  112.5 1.5 %combine.1 = bf16[8,16,2048]{2,1,0:T(8,128)(2,1)} custom-call(bf16[256,512]{1,0:T(8,128)(2,1)S(1)} %mixing.1.mix_ref, bf16[32,16,2048]{2,1,0:T(8,128)(2,1)S(1)} %all-to-all-done.2.rows_ref), custom_call_target="tpu_custom_call" | custom-call | tf_op jit(solution)/shard_map/combine/pallas_call | solution.py:485
  114.0 5.6 %all-to-all-start.3 = ((bf16[8,16,2048]{2,1,0:T(8,128)(2,1)}), bf16[8,16,2048]{2,1,0:T(8,128)(2,1)S(1)}, u32[]{:S(2)}, u32[]{:S(2)}) async-start(bf16[8,16,2048]{2,1,0:T(8,128)(2,1)} %combine.1), calls=%async_computation.3 | async-start | bytes 1048576 | tf_op jit(solution)/shard_map/all_to_all | solution.py:62
  119.7 1.6 %merge.1 = (bf16[1,144,128]{2,1,0:T(8,128)(2,1)S(1)}, bf16[1,144,128]{2,1,0:T(8,128)(2,1)S(1)}, bf16[1,144,128]{2,1,0:T(8,128)(2,1)S(1)}, bf16[1,144,128]{2,1,0:T(8,128)(2,1)S(1)}) custom-call(bf16[4,144,128]{2,1,0:T(8,128)(2,1)S(1)} %get-tuple-element.34.got0_ref, bf16[4,144,128]{2,1,0:T(8,128)(2,1)S(1)} %collective-permute-done.7.got1_ref, ...), custom_call_target="tpu_custom_call" | custom-call | tf_op jit(solution)/shard_map/merge/pallas_call | solution.py:489
  121.3 3.9 %collective-permute-start.10 = (bf16[1,144,128]{2,1,0:T(8,128)(2,1)S(1)}, bf16[1,144,128]{2,1,0:T(8,128)(2,1)S(1)}, u32[]{:S(2)}, u32[]{:S(2)}) collective-permute-start(bf16[1,144,128]{2,1,0:T(8,128)(2,1)S(1)} %get-tuple-element.39), channel_id=1, source_target_pairs={{0,32},{1,129},{2,34},{3,131},{4,36},{5,133},{6,38},{7,135},{8,40}... | collective-permute-start | bytes 110600 | tf_op jit(solution)/shard_map/ppermute | solution.py:73
  125.2 4.3 %collective-permute-start.11 = (bf16[1,144,128]{2,1,0:T(8,128)(2,1)S(1)}, bf16[1,144,128]{2,1,0:T(8,128)(2,1)S(1)}, u32[]{:S(2)}, u32[]{:S(2)}) collective-permute-start(bf16[1,144,128]{2,1,0:T(8,128)(2,1)S(1)} %get-tuple-element.40), channel_id=1, source_target_pairs={{0,64},{1,257},{2,66},{3,259},{4,68},{5,261},{6,70},{7,263},{8,72}... | collective-permute-start | bytes 110600 | tf_op jit(solution)/shard_map/ppermute | solution.py:73
  129.5 3.4 %collective-permute-start.12 = (bf16[1,144,128]{2,1,0:T(8,128)(2,1)S(1)}, bf16[1,144,128]{2,1,0:T(8,128)(2,1)S(1)}, u32[]{:S(2)}, u32[]{:S(2)}) collective-permute-start(bf16[1,144,128]{2,1,0:T(8,128)(2,1)S(1)} %get-tuple-element.41), channel_id=1, source_target_pairs={{0,96},{1,385},{2,98},{3,387},{4,100},{5,389},{6,102},{7,391},{8,1... | collective-permute-start | bytes 110600 | tf_op jit(solution)/shard_map/ppermute | solution.py:73
  132.9 2.5 %collective-permute-done.12.got3_ref = bf16[1,144,128]{2,1,0:T(8,128)(2,1)S(1)} collective-permute-done((bf16[1,144,128]{2,1,0:T(8,128)(2,1)S(1)}, bf16[1,144,128]{2,1,0:T(8,128)(2,1)S(1)}, u32[]{:S(2)}, u32[]{:S(2)}) %collective-permute-start.12) | collective-permute-done | bytes 36896 | tf_op jit(solution)/shard_map/ppermute | solution.py:73
  135.3 0.9 finish.1
  (33 shorter events, 4.8 us)
Async XLA Ops:
  2.5 24.3 %all-to-all-start = ((bf16[8,16,2304]{2,1,0:T(8,128)(2,1)}), bf16[8,16,2304]{2,1,0:T(8,128)(2,1)S(1)}, u32[]{:S(2)}, u32[]{:S(2)}) async-start(bf16[8,16,2304]{2,1,0:T(8,128)(2,1)} %pack.1), calls=%async_computation | async-start | bytes 1179648 | tf_op jit(solution)/shard_map/all_to_all | solution.py:62
  13.6 9.4 %collective-permute-start = (bf16[128,128]{1,0:T(8,128)(2,1)S(1)}, bf16[128,128]{1,0:T(8,128)(2,1)S(1)}, u32[]{:S(2)}, u32[]{:S(2)}) collective-permute-start(bf16[128,128]{1,0:T(8,128)(2,1)S(1)} %reshape.11.query_ref), channel_id=1, source_target_pairs={{0,64},{1,257},{2,66},{3,259},{4,68},{5,261},{6,70},{7,263},{8,72}... | collective-permute-start | bytes 98312 | tf_op jit(solution)/shard_map/ppermute | solution.py:81
  22.9 6.5 %collective-permute-start.1 = (bf16[256,128]{1,0:T(8,128)(2,1)S(1)}, bf16[256,128]{1,0:T(8,128)(2,1)S(1)}, u32[]{:S(2)}, u32[]{:S(2)}) collective-permute-start(bf16[256,128]{1,0:T(8,128)(2,1)S(1)} %pad_maximum_fusion.1), channel_id=1, source_target_pairs={{0,32},{1,129},{2,34},{3,131},{4,36},{5,133},{6,38},{7,135},{8,40}... | collective-permute-start | bytes 196616 | tf_op jit(solution)/shard_map/ppermute | solution.py:81
  29.4 12.8 %copy-start.5 = (bf16[192,2048]{1,0:T(8,128)(2,1)S(1)}, bf16[192,2048]{1,0:T(8,128)(2,1)}, u32[]{:S(2)}) copy-start(bf16[192,2048]{1,0:T(8,128)(2,1)} %refs_2_.1) | copy-start | bytes 2359300
  29.4 0.6 copy-start.7
  30.0 39.9 %all-to-all-start.1 = ((bf16[32,16,2048]{2,1,0:T(8,128)(2,1)}), bf16[32,16,2048]{2,1,0:T(8,128)(2,1)S(1)}, u32[]{:S(2)}, u32[]{:S(2)}) async-start(bf16[32,16,2048]{2,1,0:T(8,128)(2,1)} %dispatch.1), calls=%async_computation.1 | async-start | bytes 4194304 | tf_op jit(solution)/shard_map/all_to_all | solution.py:62
  40.2 19.3 %collective-permute-start.2 = (bf16[2048,384]{1,0:T(8,128)(2,1)}, bf16[2048,384]{1,0:T(8,128)(2,1)}, u32[]{:S(2)}, u32[]{:S(2)}) collective-permute-start(bf16[2048,384]{1,0:T(8,128)(2,1)} %refs_0_.1), channel_id=1, source_target_pairs={{0,1},{1,0},{2,3},{3,2},{4,5},{5,4},{6,7},{7,6},{8,9},{9,8},{10,11... | collective-permute-start | bytes 4718600 | tf_op jit(solution)/shard_map/ppermute | solution.py:73
  42.1 16.5 %collective-permute-start.3 = (bf16[192,2048]{1,0:T(8,128)(2,1)S(1)}, bf16[192,2048]{1,0:T(8,128)(2,1)S(1)}, u32[]{:S(2)}, u32[]{:S(2)}) collective-permute-start(bf16[192,2048]{1,0:T(8,128)(2,1)S(1)} %copy-done.5), channel_id=1, source_target_pairs={{0,1},{1,0},{2,3},{3,2},{4,5},{5,4},{6,7},{7,6},{8,9},{9,8},{10,11... | collective-permute-start | bytes 2359304 | tf_op jit(solution)/shard_map/ppermute | solution.py:73
  47.3 29.5 %collective-permute-start.4 = (bf16[512,128]{1,0:T(8,128)(2,1)}, bf16[512,128]{1,0:T(8,128)(2,1)}, u32[]{:S(2)}, u32[]{:S(2)}) collective-permute-start(bf16[512,128]{1,0:T(8,128)(2,1)} %constant_dynamic-update-slice_fusion), channel_id=1, source_target_pairs={{0,128},{1,33},{2,130},{3,35},{4,132},{5,37},{6,134},{7,39},{8,136... | collective-permute-start | bytes 393224 | tf_op jit(solution)/shard_map/ppermute | solution.py:73
  50.6 26.2 %collective-permute-start.5 = (bf16[512,128]{1,0:T(8,128)(2,1)}, bf16[512,128]{1,0:T(8,128)(2,1)}, u32[]{:S(2)}, u32[]{:S(2)}) collective-permute-start(bf16[512,128]{1,0:T(8,128)(2,1)} %constant_dynamic-update-slice_fusion), channel_id=1, source_target_pairs={{0,256},{1,65},{2,258},{3,67},{4,260},{5,69},{6,262},{7,71},{8,264... | collective-permute-start | bytes 393224 | tf_op jit(solution)/shard_map/ppermute | solution.py:73
  55.3 21.5 %collective-permute-start.6 = (bf16[512,128]{1,0:T(8,128)(2,1)}, bf16[512,128]{1,0:T(8,128)(2,1)}, u32[]{:S(2)}, u32[]{:S(2)}) collective-permute-start(bf16[512,128]{1,0:T(8,128)(2,1)} %constant_dynamic-update-slice_fusion), channel_id=1, source_target_pairs={{0,384},{1,97},{2,386},{3,99},{4,388},{5,101},{6,390},{7,103},{8,3... | collective-permute-start | bytes 393224 | tf_op jit(solution)/shard_map/ppermute | solution.py:73
  58.6 0.9 copy-start.6
  76.7 7.0 %copy-start.3 = (s32[16]{0:T(128)S(1)}, s32[16]{0:T(128)}, u32[]{:S(2)}) copy-start(s32[16]{0:T(128)} %owner_ref.1) | copy-start | bytes 196
  76.8 7.0 %copy-start.4 = (s32[16]{0:T(128)S(1)}, s32[16]{0:T(128)}, u32[]{:S(2)}) copy-start(s32[16]{0:T(128)} %count_ref.1) | copy-start | bytes 196
  76.8 35.7 %all-to-all-start.2 = ((bf16[32,16,2048]{2,1,0:T(8,128)(2,1)}), bf16[32,16,2048]{2,1,0:T(8,128)(2,1)S(1)}, u32[]{:S(2)}, u32[]{:S(2)}) async-start(bf16[32,16,2048]{2,1,0:T(8,128)(2,1)} %expert.1), calls=%async_computation.2 | async-start | bytes 4194304 | tf_op jit(solution)/shard_map/all_to_all | solution.py:62
  82.6 20.1 %copy-start.2 = (s32[128]{0:T(128)S(1)}, s32[128]{0:T(128)}, u32[]{:S(2)}) copy-start(s32[128]{0:T(128)} %param.14) | copy-start | bytes 1540
  83.8 1.6 %copy-start = (bf16[16,64,1024]{2,1,0:T(8,128)(2,1)S(1)}, bf16[16,64,1024]{2,1,0:T(8,128)(2,1)}, u32[]{:S(2)}) copy-start(bf16[16,64,1024]{2,1,0:T(8,128)(2,1)} %pool_ref.1) | copy-start | bytes 6291460
  91.4 22.6 %collective-permute-start.7 = (bf16[4,144,128]{2,1,0:T(8,128)(2,1)}, bf16[4,144,128]{2,1,0:T(8,128)(2,1)S(1)}, u32[]{:S(2)}, u32[]{:S(2)}) collective-permute-start(bf16[4,144,128]{2,1,0:T(8,128)(2,1)} %get-tuple-element.30), channel_id=1, source_target_pairs={{0,128},{1,33},{2,130},{3,35},{4,132},{5,37},{6,134},{7,39},{8,136... | collective-permute-start | bytes 442376 | tf_op jit(solution)/shard_map/ppermute | solution.py:73
  94.8 19.2 %collective-permute-start.8 = (bf16[4,144,128]{2,1,0:T(8,128)(2,1)}, bf16[4,144,128]{2,1,0:T(8,128)(2,1)S(1)}, u32[]{:S(2)}, u32[]{:S(2)}) collective-permute-start(bf16[4,144,128]{2,1,0:T(8,128)(2,1)} %get-tuple-element.31), channel_id=1, source_target_pairs={{0,256},{1,65},{2,258},{3,67},{4,260},{5,69},{6,262},{7,71},{8,264... | collective-permute-start | bytes 442376 | tf_op jit(solution)/shard_map/ppermute | solution.py:73
  99.4 14.6 %collective-permute-start.9 = (bf16[4,144,128]{2,1,0:T(8,128)(2,1)}, bf16[4,144,128]{2,1,0:T(8,128)(2,1)}, u32[]{:S(2)}, u32[]{:S(2)}) collective-permute-start(bf16[4,144,128]{2,1,0:T(8,128)(2,1)} %get-tuple-element.32), channel_id=1, source_target_pairs={{0,384},{1,97},{2,386},{3,99},{4,388},{5,101},{6,390},{7,103},{8,3... | collective-permute-start | bytes 442376 | tf_op jit(solution)/shard_map/ppermute | solution.py:73
  103.3 32.1 %copy-start.1 = (bf16[2,1024]{1,0:T(2,128)(2,1)S(1)}, bf16[2,1024]{1,0:T(2,128)(2,1)}, u32[]{:S(2)}) copy-start(bf16[2,1024]{1,0:T(2,128)(2,1)} %new_ref.1) | copy-start | bytes 12292
  114.0 22.2 %all-to-all-start.3 = ((bf16[8,16,2048]{2,1,0:T(8,128)(2,1)}), bf16[8,16,2048]{2,1,0:T(8,128)(2,1)S(1)}, u32[]{:S(2)}, u32[]{:S(2)}) async-start(bf16[8,16,2048]{2,1,0:T(8,128)(2,1)} %combine.1), calls=%async_computation.3 | async-start | bytes 1048576 | tf_op jit(solution)/shard_map/all_to_all | solution.py:62
  121.3 11.6 %collective-permute-start.10 = (bf16[1,144,128]{2,1,0:T(8,128)(2,1)S(1)}, bf16[1,144,128]{2,1,0:T(8,128)(2,1)S(1)}, u32[]{:S(2)}, u32[]{:S(2)}) collective-permute-start(bf16[1,144,128]{2,1,0:T(8,128)(2,1)S(1)} %get-tuple-element.39), channel_id=1, source_target_pairs={{0,32},{1,129},{2,34},{3,131},{4,36},{5,133},{6,38},{7,135},{8,40}... | collective-permute-start | bytes 110600 | tf_op jit(solution)/shard_map/ppermute | solution.py:73
  125.2 7.7 %collective-permute-start.11 = (bf16[1,144,128]{2,1,0:T(8,128)(2,1)S(1)}, bf16[1,144,128]{2,1,0:T(8,128)(2,1)S(1)}, u32[]{:S(2)}, u32[]{:S(2)}) collective-permute-start(bf16[1,144,128]{2,1,0:T(8,128)(2,1)S(1)} %get-tuple-element.40), channel_id=1, source_target_pairs={{0,64},{1,257},{2,66},{3,259},{4,68},{5,261},{6,70},{7,263},{8,72}... | collective-permute-start | bytes 110600 | tf_op jit(solution)/shard_map/ppermute | solution.py:73
  129.5 5.9 %collective-permute-start.12 = (bf16[1,144,128]{2,1,0:T(8,128)(2,1)S(1)}, bf16[1,144,128]{2,1,0:T(8,128)(2,1)S(1)}, u32[]{:S(2)}, u32[]{:S(2)}) collective-permute-start(bf16[1,144,128]{2,1,0:T(8,128)(2,1)S(1)} %get-tuple-element.41), channel_id=1, source_target_pairs={{0,96},{1,385},{2,98},{3,387},{4,100},{5,389},{6,102},{7,391},{8,1... | collective-permute-start | bytes 110600 | tf_op jit(solution)/shard_map/ppermute | solution.py:73

commit v12 on v11

--- a/solution.py
+++ b/solution.py
@@ -189,7 +189,7 @@
             pltpu.SemaphoreType.DMA((CHUNKS,)),
         ],
         limit=VMEM_ALL,
-    )(on_core(near), slot_row)
+    )(near, slot_row)
 
 
 def mixing_kernel(near_ref, slot_ref, out_ref):

time: 138 us -> 138 us (level)
  waiting for transfers between devices: 28.5 us -> 31.9 us
  local copies, waits for them, and re-layouts: 6.61 us -> 4.78 us
  Pallas kernels: 22.5 us -> 21.1 us
    all_to_all x4, waiting for transfers between devices: 21.5 us -> 24.9 us  [exchange(): lax.all_to_all(array, AXIS, split_axis=0, concat_axis=0, axis_index_group...]
    concatenate x1, local copies, waits for them, and re-layouts: 1.47 us -> 0.01 us  [shards(): line = jnp.concatenate([half, rest], axis=0)]
    unnamed x18 -> x22, local copies, waits for them, and re-layouts: 4.35 us -> 3.98 us
  transfers between devices with their start and end apart: 17 -> 17, of which waited for: 5 -> 5; matrix products, arithmetic and copies ran while one was open for 3% -> 1% of each run, Pallas kernels for 15% -> 14%
where the time goes in v12:
time: 138 us; the launch traced here: 137 us
  starting transfers between devices  77.1 us (56%)
  waiting for transfers between devices  31.9 us (23%)
  Pallas kernels  21.1 us (15%)
  local copies, waits for them, and re-layouts  4.78 us (3%)
    ppermute x11, starting transfers between devices, moved(): return lax.ppermute(array, AXIS, pairs)  38.6 us
    all_to_all x4, starting transfers between devices, exchange(): lax.all_to_all(array, AXIS, split_axis=0, concat_axis=0, axis_index_group...  31.8 us
    all_to_all x4, waiting for transfers between devices, exchange(): lax.all_to_all(array, AXIS, split_axis=0, concat_axis=0, axis_index_group...  24.9 us
    pallas_call x1, Pallas kernels, expert(): call(expert_kernel, 'expert', shape(rows.shape), 5, in_specs=whole(1) + [...  6.85 us
    ppermute x2, starting transfers between devices, swapped(): return lax.ppermute(array, AXIS, pairs)  6.74 us
    pallas_call x1, Pallas kernels, partial_attention(): call(partial_kernel, 'partial_attention', [shape((SIDE, MESSAGE, HEAD))]...  5.11 us
    ppermute x2, waiting for transfers between devices, swapped(): return lax.ppermute(array, AXIS, pairs)  4.53 us
    unnamed x22, local copies, waits for them, and re-layouts  3.98 us
  transfers between devices with their start and end apart: 17, of which 5 were waited for; matrix products, arithmetic and copies ran while one was open for 1% of the time, Pallas kernels for 14%

profile of v12, /device:TPU:8, one launch (start us, length us, event | category | flops | bytes accessed | tf_op | source)
XLA Modules:
  0.0 136.9 jit_solution(14157791982361062532)
XLA Ops:
  0.6 1.8 %pack.1 = bf16[8,16,2304]{2,1,0:T(8,128)(2,1)} custom-call(bf16[16,2048]{1,0:T(8,128)(2,1)} %token_ref.1, s32[8,16]{1,0:T(8,128)} %bitcast.5, f32[8,16]{1,0:T(8,128)} %bitcast.6), custom_call_target="tpu_custom_call" | custom-call | tf_op jit(solution)/shard_map/pack/pallas_call | solution.py:460
  2.5 10.3 %all-to-all-start = ((bf16[8,16,2304]{2,1,0:T(8,128)(2,1)}), bf16[8,16,2304]{2,1,0:T(8,128)(2,1)S(1)}, u32[]{:S(2)}, u32[]{:S(2)}) async-start(bf16[8,16,2304]{2,1,0:T(8,128)(2,1)} %pack.1), calls=%async_computation | async-start | bytes 1179648 | tf_op jit(solution)/shard_map/all_to_all | solution.py:62
  13.6 4.8 %collective-permute-start = (bf16[128,128]{1,0:T(8,128)(2,1)S(1)}, bf16[128,128]{1,0:T(8,128)(2,1)S(1)}, u32[]{:S(2)}, u32[]{:S(2)}) collective-permute-start(bf16[128,128]{1,0:T(8,128)(2,1)S(1)} %reshape.11.query_ref), channel_id=1, source_target_pairs={{0,64},{1,257},{2,66},{3,259},{4,68},{5,261},{6,70},{7,263},{8,72}... | collective-permute-start | bytes 98312 | tf_op jit(solution)/shard_map/ppermute | solution.py:81
  18.4 4.5 %collective-permute-done = bf16[128,128]{1,0:T(8,128)(2,1)S(1)} collective-permute-done((bf16[128,128]{1,0:T(8,128)(2,1)S(1)}, bf16[128,128]{1,0:T(8,128)(2,1)S(1)}, u32[]{:S(2)}, u32[]{:S(2)}) %collective-permute-start) | collective-permute-done | bytes 32800 | tf_op jit(solution)/shard_map/ppermute | solution.py:81
  22.9 1.9 %collective-permute-start.1 = (bf16[256,128]{1,0:T(8,128)(2,1)S(1)}, bf16[256,128]{1,0:T(8,128)(2,1)S(1)}, u32[]{:S(2)}, u32[]{:S(2)}) collective-permute-start(bf16[256,128]{1,0:T(8,128)(2,1)S(1)} %pad_maximum_fusion.1), channel_id=1, source_target_pairs={{0,32},{1,129},{2,34},{3,131},{4,36},{5,133},{6,38},{7,135},{8,40}... | collective-permute-start | bytes 196616 | tf_op jit(solution)/shard_map/ppermute | solution.py:81
  24.8 1.9 %all-to-all-done.near_ref = bf16[8,16,2304]{2,1,0:T(8,128)(2,1)S(1)} async-done(((bf16[8,16,2304]{2,1,0:T(8,128)(2,1)}), bf16[8,16,2304]{2,1,0:T(8,128)(2,1)S(1)}, u32[]{:S(2)}, u32[]{:S(2)}) %all-to-all-start) | async-done | bytes 589856 | tf_op jit(solution)/shard_map/all_to_all | solution.py:62
  26.8 0.8 copy-done
  27.6 3.0 %dispatch.1 = bf16[32,16,2048]{2,1,0:T(8,128)(2,1)} custom-call(bf16[8,16,2304]{2,1,0:T(8,128)(2,1)} %copy-done, s32[1,128]{1,0:T(1,128)} %bitcast.3), custom_call_target="tpu_custom_call" | custom-call | tf_op jit(solution)/shard_map/dispatch/pallas_call | solution.py:181
  30.6 10.3 %all-to-all-start.1 = ((bf16[32,16,2048]{2,1,0:T(8,128)(2,1)}), bf16[32,16,2048]{2,1,0:T(8,128)(2,1)S(1)}, u32[]{:S(2)}, u32[]{:S(2)}) async-start(bf16[32,16,2048]{2,1,0:T(8,128)(2,1)} %dispatch.1), calls=%async_computation.1 | async-start | bytes 4194304 | tf_op jit(solution)/shard_map/all_to_all | solution.py:62
  41.0 1.9 %collective-permute-start.2 = (bf16[2048,384]{1,0:T(8,128)(2,1)}, bf16[2048,384]{1,0:T(8,128)(2,1)}, u32[]{:S(2)}, u32[]{:S(2)}) collective-permute-start(bf16[2048,384]{1,0:T(8,128)(2,1)} %refs_0_.1), channel_id=1, source_target_pairs={{0,1},{1,0},{2,3},{3,2},{4,5},{5,4},{6,7},{7,6},{8,9},{9,8},{10,11... | collective-permute-start | bytes 4718600 | tf_op jit(solution)/shard_map/ppermute | solution.py:73
  42.9 2.4 %collective-permute-start.3 = (bf16[192,2048]{1,0:T(8,128)(2,1)S(1)}, bf16[192,2048]{1,0:T(8,128)(2,1)S(1)}, u32[]{:S(2)}, u32[]{:S(2)}) collective-permute-start(bf16[192,2048]{1,0:T(8,128)(2,1)S(1)} %copy-done.7), channel_id=1, source_target_pairs={{0,1},{1,0},{2,3},{3,2},{4,5},{5,4},{6,7},{7,6},{8,9},{9,8},{10,11... | collective-permute-start | bytes 2359304 | tf_op jit(solution)/shard_map/ppermute | solution.py:73
  45.4 3.4 %collective-permute-start.4 = (bf16[512,128]{1,0:T(8,128)(2,1)S(1)}, bf16[512,128]{1,0:T(8,128)(2,1)S(1)}, u32[]{:S(2)}, u32[]{:S(2)}) collective-permute-start(bf16[512,128]{1,0:T(8,128)(2,1)S(1)} %constant_dynamic-update-slice_fusion), channel_id=1, source_target_pairs={{0,128},{1,33},{2,130},{3,35},{4,132},{5,37},{6,134},{7,39},{8,136... | collective-permute-start | bytes 393224 | tf_op jit(solution)/shard_map/ppermute | solution.py:73
  48.7 4.6 %collective-permute-start.5 = (bf16[512,128]{1,0:T(8,128)(2,1)S(1)}, bf16[512,128]{1,0:T(8,128)(2,1)S(1)}, u32[]{:S(2)}, u32[]{:S(2)}) collective-permute-start(bf16[512,128]{1,0:T(8,128)(2,1)S(1)} %constant_dynamic-update-slice_fusion), channel_id=1, source_target_pairs={{0,256},{1,65},{2,258},{3,67},{4,260},{5,69},{6,262},{7,71},{8,264... | collective-permute-start | bytes 393224 | tf_op jit(solution)/shard_map/ppermute | solution.py:73
  53.4 3.3 %collective-permute-start.6 = (bf16[512,128]{1,0:T(8,128)(2,1)S(1)}, bf16[512,128]{1,0:T(8,128)(2,1)S(1)}, u32[]{:S(2)}, u32[]{:S(2)}) collective-permute-start(bf16[512,128]{1,0:T(8,128)(2,1)S(1)} %constant_dynamic-update-slice_fusion), channel_id=1, source_target_pairs={{0,384},{1,97},{2,386},{3,99},{4,388},{5,101},{6,390},{7,103},{8,3... | collective-permute-start | bytes 393224 | tf_op jit(solution)/shard_map/ppermute | solution.py:73
  56.7 0.9 copy-done.8
  57.6 12.9 %all-to-all-done.1.rows_ref = bf16[32,16,2048]{2,1,0:T(8,128)(2,1)S(1)} async-done(((bf16[32,16,2048]{2,1,0:T(8,128)(2,1)}), bf16[32,16,2048]{2,1,0:T(8,128)(2,1)S(1)}, u32[]{:S(2)}, u32[]{:S(2)}) %all-to-all-start.1) | async-done | bytes 2097184 | tf_op jit(solution)/shard_map/all_to_all | solution.py:62
  70.5 6.8 %expert.1 = bf16[32,16,2048]{2,1,0:T(8,128)(2,1)} custom-call(bf16[32,16,2048]{2,1,0:T(8,128)(2,1)S(1)} %all-to-all-done.1.rows_ref, bf16[2048,384]{1,0:T(8,128)(2,1)} %refs_0_.1, bf16[2048,384]{1,0:T(8,128)(2,1)} %collective-permute-done.2.refs_1_, bf16[192,2048]{1,0:T(8,128)(2,1)} %refs_2_.1, bf16[192,2048]{1,0:T(8,128)(2,1)} %copy-done.8), custom_call_target="tpu_custom_call" | custom-call | tf_op jit(solution)/shard_map/expert/pallas_call | solution.py:275
  78.1 6.6 %all-to-all-start.2 = ((bf16[32,16,2048]{2,1,0:T(8,128)(2,1)}), bf16[32,16,2048]{2,1,0:T(8,128)(2,1)S(1)}, u32[]{:S(2)}, u32[]{:S(2)}) async-start(bf16[32,16,2048]{2,1,0:T(8,128)(2,1)} %expert.1), calls=%async_computation.2 | async-start | bytes 4194304 | tf_op jit(solution)/shard_map/all_to_all | solution.py:62
  84.8 1.0 pad_maximum_fusion.query_ref
  85.8 1.6 %copy-done.2 = bf16[16,64,1024]{2,1,0:T(8,128)(2,1)S(1)} copy-done((bf16[16,64,1024]{2,1,0:T(8,128)(2,1)S(1)}, bf16[16,64,1024]{2,1,0:T(8,128)(2,1)}, u32[]{:S(2)}) %copy-start.2) | copy-done | bytes 2097176
  87.4 5.1 %partial_attention.1 = (bf16[4,144,128]{2,1,0:T(8,128)(2,1)S(1)}, bf16[4,144,128]{2,1,0:T(8,128)(2,1)S(1)}, bf16[4,144,128]{2,1,0:T(8,128)(2,1)S(1)}, bf16[4,144,128]{2,1,0:T(8,128)(2,1)S(1)}) custom-call(s32[16]{0:T(128)S(1)} %copy-done.5, s32[16]{0:T(128)S(1)} %copy-done.6, bf16[2048,128]{1,0:T(8,128)(2,1)S(1)} %pad_maximum_fusion.query_ref, ...), custom_call_target="tpu_custom_call" | custom-call | tf_op jit(solution)/shard_map/partial_attention/pallas_call | solution.py:399
  92.5 3.4 %collective-permute-start.7 = (bf16[4,144,128]{2,1,0:T(8,128)(2,1)S(1)}, bf16[4,144,128]{2,1,0:T(8,128)(2,1)S(1)}, u32[]{:S(2)}, u32[]{:S(2)}) collective-permute-start(bf16[4,144,128]{2,1,0:T(8,128)(2,1)S(1)} %get-tuple-element.30), channel_id=1, source_target_pairs={{0,128},{1,33},{2,130},{3,35},{4,132},{5,37},{6,134},{7,39},{8,136... | collective-permute-start | bytes 442376 | tf_op jit(solution)/shard_map/ppermute | solution.py:73
  95.9 4.6 %collective-permute-start.8 = (bf16[4,144,128]{2,1,0:T(8,128)(2,1)S(1)}, bf16[4,144,128]{2,1,0:T(8,128)(2,1)S(1)}, u32[]{:S(2)}, u32[]{:S(2)}) collective-permute-start(bf16[4,144,128]{2,1,0:T(8,128)(2,1)S(1)} %get-tuple-element.31), channel_id=1, source_target_pairs={{0,256},{1,65},{2,258},{3,67},{4,260},{5,69},{6,262},{7,71},{8,264... | collective-permute-start | bytes 442376 | tf_op jit(solution)/shard_map/ppermute | solution.py:73
  100.5 3.3 %collective-permute-start.9 = (bf16[4,144,128]{2,1,0:T(8,128)(2,1)S(1)}, bf16[4,144,128]{2,1,0:T(8,128)(2,1)S(1)}, u32[]{:S(2)}, u32[]{:S(2)}) collective-permute-start(bf16[4,144,128]{2,1,0:T(8,128)(2,1)S(1)} %get-tuple-element.32), channel_id=1, source_target_pairs={{0,384},{1,97},{2,386},{3,99},{4,388},{5,101},{6,390},{7,103},{8,3... | collective-permute-start | bytes 442376 | tf_op jit(solution)/shard_map/ppermute | solution.py:73
  104.4 10.0 %all-to-all-done.2.rows_ref = bf16[32,16,2048]{2,1,0:T(8,128)(2,1)S(1)} async-done(((bf16[32,16,2048]{2,1,0:T(8,128)(2,1)}), bf16[32,16,2048]{2,1,0:T(8,128)(2,1)S(1)}, u32[]{:S(2)}, u32[]{:S(2)}) %all-to-all-start.2) | async-done | bytes 2097184 | tf_op jit(solution)/shard_map/all_to_all | solution.py:62
  114.4 1.5 %combine.1 = bf16[8,16,2048]{2,1,0:T(8,128)(2,1)} custom-call(bf16[256,512]{1,0:T(8,128)(2,1)S(1)} %mixing.1.mix_ref, bf16[32,16,2048]{2,1,0:T(8,128)(2,1)S(1)} %all-to-all-done.2.rows_ref), custom_call_target="tpu_custom_call" | custom-call | tf_op jit(solution)/shard_map/combine/pallas_call | solution.py:485
  116.0 4.6 %all-to-all-start.3 = ((bf16[8,16,2048]{2,1,0:T(8,128)(2,1)}), bf16[8,16,2048]{2,1,0:T(8,128)(2,1)S(1)}, u32[]{:S(2)}, u32[]{:S(2)}) async-start(bf16[8,16,2048]{2,1,0:T(8,128)(2,1)} %combine.1), calls=%async_computation.3 | async-start | bytes 1048576 | tf_op jit(solution)/shard_map/all_to_all | solution.py:62
  121.2 3.9 %collective-permute-start.10 = (bf16[1,144,128]{2,1,0:T(8,128)(2,1)S(1)}, bf16[1,144,128]{2,1,0:T(8,128)(2,1)S(1)}, u32[]{:S(2)}, u32[]{:S(2)}) collective-permute-start(bf16[1,144,128]{2,1,0:T(8,128)(2,1)S(1)} %get-tuple-element.39), channel_id=1, source_target_pairs={{0,32},{1,129},{2,34},{3,131},{4,36},{5,133},{6,38},{7,135},{8,40}... | collective-permute-start | bytes 110600 | tf_op jit(solution)/shard_map/ppermute | solution.py:73
  125.2 4.3 %collective-permute-start.11 = (bf16[1,144,128]{2,1,0:T(8,128)(2,1)S(1)}, bf16[1,144,128]{2,1,0:T(8,128)(2,1)S(1)}, u32[]{:S(2)}, u32[]{:S(2)}) collective-permute-start(bf16[1,144,128]{2,1,0:T(8,128)(2,1)S(1)} %get-tuple-element.40), channel_id=1, source_target_pairs={{0,64},{1,257},{2,66},{3,259},{4,68},{5,261},{6,70},{7,263},{8,72}... | collective-permute-start | bytes 110600 | tf_op jit(solution)/shard_map/ppermute | solution.py:73
  129.4 3.4 %collective-permute-start.12 = (bf16[1,144,128]{2,1,0:T(8,128)(2,1)S(1)}, bf16[1,144,128]{2,1,0:T(8,128)(2,1)S(1)}, u32[]{:S(2)}, u32[]{:S(2)}) collective-permute-start(bf16[1,144,128]{2,1,0:T(8,128)(2,1)S(1)} %get-tuple-element.41), channel_id=1, source_target_pairs={{0,96},{1,385},{2,98},{3,387},{4,100},{5,389},{6,102},{7,391},{8,1... | collective-permute-start | bytes 110600 | tf_op jit(solution)/shard_map/ppermute | solution.py:73
  132.8 2.5 %collective-permute-done.12.got3_ref = bf16[1,144,128]{2,1,0:T(8,128)(2,1)S(1)} collective-permute-done((bf16[1,144,128]{2,1,0:T(8,128)(2,1)S(1)}, bf16[1,144,128]{2,1,0:T(8,128)(2,1)S(1)}, u32[]{:S(2)}, u32[]{:S(2)}) %collective-permute-start.12) | collective-permute-done | bytes 36896 | tf_op jit(solution)/shard_map/ppermute | solution.py:73
  135.3 0.9 finish.1
  (37 shorter events, 3.4 us)
Async XLA Ops:
  2.5 24.3 %all-to-all-start = ((bf16[8,16,2304]{2,1,0:T(8,128)(2,1)}), bf16[8,16,2304]{2,1,0:T(8,128)(2,1)S(1)}, u32[]{:S(2)}, u32[]{:S(2)}) async-start(bf16[8,16,2304]{2,1,0:T(8,128)(2,1)} %pack.1), calls=%async_computation | async-start | bytes 1179648 | tf_op jit(solution)/shard_map/all_to_all | solution.py:62
  13.6 9.4 %collective-permute-start = (bf16[128,128]{1,0:T(8,128)(2,1)S(1)}, bf16[128,128]{1,0:T(8,128)(2,1)S(1)}, u32[]{:S(2)}, u32[]{:S(2)}) collective-permute-start(bf16[128,128]{1,0:T(8,128)(2,1)S(1)} %reshape.11.query_ref), channel_id=1, source_target_pairs={{0,64},{1,257},{2,66},{3,259},{4,68},{5,261},{6,70},{7,263},{8,72}... | collective-permute-start | bytes 98312 | tf_op jit(solution)/shard_map/ppermute | solution.py:81
  22.9 7.7 %collective-permute-start.1 = (bf16[256,128]{1,0:T(8,128)(2,1)S(1)}, bf16[256,128]{1,0:T(8,128)(2,1)S(1)}, u32[]{:S(2)}, u32[]{:S(2)}) collective-permute-start(bf16[256,128]{1,0:T(8,128)(2,1)S(1)} %pad_maximum_fusion.1), channel_id=1, source_target_pairs={{0,32},{1,129},{2,34},{3,131},{4,36},{5,133},{6,38},{7,135},{8,40}... | collective-permute-start | bytes 196616 | tf_op jit(solution)/shard_map/ppermute | solution.py:81
  26.8 0.8 copy-start
  30.6 12.3 %copy-start.7 = (bf16[192,2048]{1,0:T(8,128)(2,1)S(1)}, bf16[192,2048]{1,0:T(8,128)(2,1)}, u32[]{:S(2)}) copy-start(bf16[192,2048]{1,0:T(8,128)(2,1)} %refs_2_.1) | copy-start | bytes 2359300
  30.6 39.9 %all-to-all-start.1 = ((bf16[32,16,2048]{2,1,0:T(8,128)(2,1)}), bf16[32,16,2048]{2,1,0:T(8,128)(2,1)S(1)}, u32[]{:S(2)}, u32[]{:S(2)}) async-start(bf16[32,16,2048]{2,1,0:T(8,128)(2,1)} %dispatch.1), calls=%async_computation.1 | async-start | bytes 4194304 | tf_op jit(solution)/shard_map/all_to_all | solution.py:62
  41.0 16.7 %collective-permute-start.2 = (bf16[2048,384]{1,0:T(8,128)(2,1)}, bf16[2048,384]{1,0:T(8,128)(2,1)}, u32[]{:S(2)}, u32[]{:S(2)}) collective-permute-start(bf16[2048,384]{1,0:T(8,128)(2,1)} %refs_0_.1), channel_id=1, source_target_pairs={{0,1},{1,0},{2,3},{3,2},{4,5},{5,4},{6,7},{7,6},{8,9},{9,8},{10,11... | collective-permute-start | bytes 4718600 | tf_op jit(solution)/shard_map/ppermute | solution.py:73
  42.9 13.8 %collective-permute-start.3 = (bf16[192,2048]{1,0:T(8,128)(2,1)S(1)}, bf16[192,2048]{1,0:T(8,128)(2,1)S(1)}, u32[]{:S(2)}, u32[]{:S(2)}) collective-permute-start(bf16[192,2048]{1,0:T(8,128)(2,1)S(1)} %copy-done.7), channel_id=1, source_target_pairs={{0,1},{1,0},{2,3},{3,2},{4,5},{5,4},{6,7},{7,6},{8,9},{9,8},{10,11... | collective-permute-start | bytes 2359304 | tf_op jit(solution)/shard_map/ppermute | solution.py:73
  45.4 32.1 %collective-permute-start.4 = (bf16[512,128]{1,0:T(8,128)(2,1)S(1)}, bf16[512,128]{1,0:T(8,128)(2,1)S(1)}, u32[]{:S(2)}, u32[]{:S(2)}) collective-permute-start(bf16[512,128]{1,0:T(8,128)(2,1)S(1)} %constant_dynamic-update-slice_fusion), channel_id=1, source_target_pairs={{0,128},{1,33},{2,130},{3,35},{4,132},{5,37},{6,134},{7,39},{8,136... | collective-permute-start | bytes 393224 | tf_op jit(solution)/shard_map/ppermute | solution.py:73
  48.7 28.7 %collective-permute-start.5 = (bf16[512,128]{1,0:T(8,128)(2,1)S(1)}, bf16[512,128]{1,0:T(8,128)(2,1)S(1)}, u32[]{:S(2)}, u32[]{:S(2)}) collective-permute-start(bf16[512,128]{1,0:T(8,128)(2,1)S(1)} %constant_dynamic-update-slice_fusion), channel_id=1, source_target_pairs={{0,256},{1,65},{2,258},{3,67},{4,260},{5,69},{6,262},{7,71},{8,264... | collective-permute-start | bytes 393224 | tf_op jit(solution)/shard_map/ppermute | solution.py:73
  53.4 24.1 %collective-permute-start.6 = (bf16[512,128]{1,0:T(8,128)(2,1)S(1)}, bf16[512,128]{1,0:T(8,128)(2,1)S(1)}, u32[]{:S(2)}, u32[]{:S(2)}) collective-permute-start(bf16[512,128]{1,0:T(8,128)(2,1)S(1)} %constant_dynamic-update-slice_fusion), channel_id=1, source_target_pairs={{0,384},{1,97},{2,386},{3,99},{4,388},{5,101},{6,390},{7,103},{8,3... | collective-permute-start | bytes 393224 | tf_op jit(solution)/shard_map/ppermute | solution.py:73
  56.7 0.9 copy-start.8
  77.4 8.4 %copy-start.5 = (s32[16]{0:T(128)S(1)}, s32[16]{0:T(128)}, u32[]{:S(2)}) copy-start(s32[16]{0:T(128)} %owner_ref.1) | copy-start | bytes 196
  77.4 8.4 %copy-start.6 = (s32[16]{0:T(128)S(1)}, s32[16]{0:T(128)}, u32[]{:S(2)}) copy-start(s32[16]{0:T(128)} %count_ref.1) | copy-start | bytes 196
  77.5 0.6 copy-start.9
  78.1 36.3 %all-to-all-start.2 = ((bf16[32,16,2048]{2,1,0:T(8,128)(2,1)}), bf16[32,16,2048]{2,1,0:T(8,128)(2,1)S(1)}, u32[]{:S(2)}, u32[]{:S(2)}) async-start(bf16[32,16,2048]{2,1,0:T(8,128)(2,1)} %expert.1), calls=%async_computation.2 | async-start | bytes 4194304 | tf_op jit(solution)/shard_map/all_to_all | solution.py:62
  84.7 19.1 %copy-start.1 = (bf16[8,16,2304]{2,1,0:T(8,128)(2,1)S(1)}, bf16[8,16,2304]{2,1,0:T(8,128)(2,1)}, u32[]{:S(2)}) copy-start(bf16[8,16,2304]{2,1,0:T(8,128)(2,1)} %copy-done) | copy-start | bytes 1769476
  84.7 19.1 %copy-start.4 = (s32[128]{0:T(128)S(1)}, s32[128]{0:T(128)}, u32[]{:S(2)}) copy-start(s32[128]{0:T(128)} %param.14) | copy-start | bytes 1540
  85.8 1.6 %copy-start.2 = (bf16[16,64,1024]{2,1,0:T(8,128)(2,1)S(1)}, bf16[16,64,1024]{2,1,0:T(8,128)(2,1)}, u32[]{:S(2)}) copy-start(bf16[16,64,1024]{2,1,0:T(8,128)(2,1)} %pool_ref.1) | copy-start | bytes 6291460
  92.5 23.5 %collective-permute-start.7 = (bf16[4,144,128]{2,1,0:T(8,128)(2,1)S(1)}, bf16[4,144,128]{2,1,0:T(8,128)(2,1)S(1)}, u32[]{:S(2)}, u32[]{:S(2)}) collective-permute-start(bf16[4,144,128]{2,1,0:T(8,128)(2,1)S(1)} %get-tuple-element.30), channel_id=1, source_target_pairs={{0,128},{1,33},{2,130},{3,35},{4,132},{5,37},{6,134},{7,39},{8,136... | collective-permute-start | bytes 442376 | tf_op jit(solution)/shard_map/ppermute | solution.py:73
  95.9 20.1 %collective-permute-start.8 = (bf16[4,144,128]{2,1,0:T(8,128)(2,1)S(1)}, bf16[4,144,128]{2,1,0:T(8,128)(2,1)S(1)}, u32[]{:S(2)}, u32[]{:S(2)}) collective-permute-start(bf16[4,144,128]{2,1,0:T(8,128)(2,1)S(1)} %get-tuple-element.31), channel_id=1, source_target_pairs={{0,256},{1,65},{2,258},{3,67},{4,260},{5,69},{6,262},{7,71},{8,264... | collective-permute-start | bytes 442376 | tf_op jit(solution)/shard_map/ppermute | solution.py:73
  100.5 15.4 %collective-permute-start.9 = (bf16[4,144,128]{2,1,0:T(8,128)(2,1)S(1)}, bf16[4,144,128]{2,1,0:T(8,128)(2,1)S(1)}, u32[]{:S(2)}, u32[]{:S(2)}) collective-permute-start(bf16[4,144,128]{2,1,0:T(8,128)(2,1)S(1)} %get-tuple-element.32), channel_id=1, source_target_pairs={{0,384},{1,97},{2,386},{3,99},{4,388},{5,101},{6,390},{7,103},{8,3... | collective-permute-start | bytes 442376 | tf_op jit(solution)/shard_map/ppermute | solution.py:73
  104.4 30.9 %copy-start.3 = (bf16[2,1024]{1,0:T(2,128)(2,1)S(1)}, bf16[2,1024]{1,0:T(2,128)(2,1)}, u32[]{:S(2)}) copy-start(bf16[2,1024]{1,0:T(2,128)(2,1)} %new_ref.1) | copy-start | bytes 12292
  116.0 20.2 %all-to-all-start.3 = ((bf16[8,16,2048]{2,1,0:T(8,128)(2,1)}), bf16[8,16,2048]{2,1,0:T(8,128)(2,1)S(1)}, u32[]{:S(2)}, u32[]{:S(2)}) async-start(bf16[8,16,2048]{2,1,0:T(8,128)(2,1)} %combine.1), calls=%async_computation.3 | async-start | bytes 1048576 | tf_op jit(solution)/shard_map/all_to_all | solution.py:62
  121.2 11.6 %collective-permute-start.10 = (bf16[1,144,128]{2,1,0:T(8,128)(2,1)S(1)}, bf16[1,144,128]{2,1,0:T(8,128)(2,1)S(1)}, u32[]{:S(2)}, u32[]{:S(2)}) collective-permute-start(bf16[1,144,128]{2,1,0:T(8,128)(2,1)S(1)} %get-tuple-element.39), channel_id=1, source_target_pairs={{0,32},{1,129},{2,34},{3,131},{4,36},{5,133},{6,38},{7,135},{8,40}... | collective-permute-start | bytes 110600 | tf_op jit(solution)/shard_map/ppermute | solution.py:73
  125.2 7.7 %collective-permute-start.11 = (bf16[1,144,128]{2,1,0:T(8,128)(2,1)S(1)}, bf16[1,144,128]{2,1,0:T(8,128)(2,1)S(1)}, u32[]{:S(2)}, u32[]{:S(2)}) collective-permute-start(bf16[1,144,128]{2,1,0:T(8,128)(2,1)S(1)} %get-tuple-element.40), channel_id=1, source_target_pairs={{0,64},{1,257},{2,66},{3,259},{4,68},{5,261},{6,70},{7,263},{8,72}... | collective-permute-start | bytes 110600 | tf_op jit(solution)/shard_map/ppermute | solution.py:73
  129.4 5.9 %collective-permute-start.12 = (bf16[1,144,128]{2,1,0:T(8,128)(2,1)S(1)}, bf16[1,144,128]{2,1,0:T(8,128)(2,1)S(1)}, u32[]{:S(2)}, u32[]{:S(2)}) collective-permute-start(bf16[1,144,128]{2,1,0:T(8,128)(2,1)S(1)} %get-tuple-element.41), channel_id=1, source_target_pairs={{0,96},{1,385},{2,98},{3,387},{4,100},{5,389},{6,102},{7,391},{8,1... | collective-permute-start | bytes 110600 | tf_op jit(solution)/shard_map/ppermute | solution.py:73
